TPU v7x, 32 devices: a whole 2x2x4 slice. The times are simulated.
32 devices in a mesh: groups: 2 (over x), seq: 8 (over z, y), heads: 2 (over core).
Axes of the slice: x: 2, y: 2, z: 4, core: 2. Of those that a mesh axis runs over, the one named last changes fastest.
Arguments:
- x_in: bfloat16 [2048, 8192], P(('groups', 'seq'), 'heads'), parts along dimension 0, may hold values from -6 to 6
- z_in: bfloat16 [2048, 8192], P(('groups', 'seq'), 'heads'), parts along dimension 0, may hold values from -6 to 6
- bc_in: bfloat16 [2048, 2, 512], P(('groups', 'seq'), None, 'heads'), parts along dimension 0, may hold values from -1.25 to 1.25
- conv_x_weight: bfloat16 [4, 8192], P(None, 'heads'), may hold values from -3 to 3
- conv_x_bias: float32 [8192], P('heads'), may hold values from -3 to 3
- conv_bc_weight: bfloat16 [4, 2, 512], P(None, None, 'heads'), may hold values from -3 to 3
- conv_bc_bias: float32 [2, 512], P(None, 'heads'), may hold values from -0.625 to 0.625
- dt_raw: bfloat16 [2048, 128], P(('groups', 'seq'), 'heads'), parts along dimension 0, may hold values from -3 to 3
- dt_bias: float32 [128], P('heads'), may hold values from -1 to 0.5
- decay: float32 [128], P('heads'), may hold values from 1.953125e-05 to 0.05
- skip_d: float32 [128], P('heads'), may hold values from 0.5 to 1.5
- norm_gain: float32 [8192], P('heads'), may hold values from 0.1 to 1.9
- lengths: int32 [16], P('groups'), parts along dimension 0, may hold values from 1 to 512, 1024 in all
Outputs:
- mixed: bfloat16 [2048, 8192], P(('groups', 'seq'), 'heads'), parts along dimension 0
There are 2 independent parts, one for each index of `groups`. A program takes and returns all parts, laid end to end along the dimension named above; an argument that names none is the same for every part. Nothing has to cross between parts.
Inputs may be any that keep to these rules, and one draw needn't show every extreme that they name: `lengths`: 8 token counts that sum to 1024; the longest rollout has exactly 512 tokens.
All inputs are finite; a program needn't handle non-finite values.
Results may differ from a plain program's by a relative error of at most 0.0098.
Values may be sent and summed in bfloat16 or wider, within the bound.
No kernel may reach another device: no remote copies, remote signals or barrier semaphores. Data moves between devices by JAX's collectives and lax.ppermute only.
A program may use at most 192 MiB of HBM per device.

v0:
```python
import jax
import jax.numpy as jnp
from jax import lax
from jax.sharding import PartitionSpec as P

HEAD_DIM = 64
STATE = 128
BLOCK = 128


def shifted(block, axis, distance):
    devices = range(lax.axis_size(axis))
    route = [(i - distance, i) for i in devices if i - distance in devices]
    return lax.ppermute(block, axis, route)


def prefix_2(x, axis, combine, identity):
    peers, position = (lax.axis_size(axis), lax.axis_index(axis))
    everything = jax.tree.map(lambda part: lax.all_gather(part, axis), x)
    start = jax.tree.map(
        lambda part, zero: jnp.broadcast_to(jnp.asarray(zero, part.dtype), part.shape), x, identity
    )

    def step(k, before):
        reached = k < position
        new = combine(before, jax.tree.map(lambda part: part[k], everything))
        return jax.tree.map(lambda a, b: jnp.where(reached, a, b), new, before)

    return lax.fori_loop(0, peers, step, start)


def seg_ids(ends, pos):
    count = jnp.sum((ends[None, :] <= pos[:, None]).astype(jnp.int32), axis=1)
    return jnp.where(pos >= 0, count, -1)


def conv_act(extended, weight, bias, keep):
    rows = keep.shape[1]
    total = bias
    for k in range(weight.shape[0]):
        piece = extended[k : k + rows].astype(jnp.float32) * weight[k].astype(jnp.float32)
        flag = keep[k].reshape((rows,) + (1,) * (extended.ndim - 1))
        total = total + jnp.where(flag, piece, 0.0)
    return jax.nn.silu(total).astype(jnp.bfloat16)


def contract(form, left, right):
    return jnp.einsum(form, left, right, preferred_element_type=jnp.float32)


def block_terms(xs, rates, decay, bmat, cmat, seg, prev_seg, block):
    count, heads, hdim = xs.shape
    groups, state = (bmat.shape[1], bmat.shape[2])
    per = heads // groups
    blocks = count // block
    xb = xs.reshape(blocks, block, groups, per, hdim)
    rate_b = rates.reshape(blocks, block, groups, per)
    cum = jnp.cumsum(-rate_b * decay.reshape(groups, per), axis=1)
    segb = seg.reshape(blocks, block)
    bb = bmat.reshape(blocks, block, groups, state)
    cb = cmat.reshape(blocks, block, groups, state)
    scores = contract("btgn,bsgn->bgts", cb, bb)
    order = jnp.arange(block)
    mask = (segb[:, :, None] == segb[:, None, :]) & (order[:, None] >= order[None, :])
    cum_t = jnp.transpose(cum, (0, 2, 3, 1))
    diff = cum_t[..., :, None] - cum_t[..., None, :]
    mask5 = mask[:, None, None]
    decays = jnp.where(mask5, jnp.exp(jnp.where(mask5, diff, 0.0)), 0.0)
    rate_t = jnp.transpose(rate_b, (0, 2, 3, 1))
    weights = (decays * scores[:, :, None] * rate_t[..., None, :]).astype(jnp.bfloat16)
    inner = contract("bgkts,bsgkp->btgkp", weights, xb)
    last = cum[:, -1]
    same_end = segb == segb[:, -1:]
    to_end = jnp.where(same_end[:, :, None, None], jnp.exp(last[:, None] - cum), 0.0) * rate_b
    scaled = (to_end[..., None] * xb.astype(jnp.float32)).astype(jnp.bfloat16)
    states = contract("bsgn,bsgkp->bgknp", bb, scaled)
    live = segb == prev_seg[:, None]
    carry = jnp.where(live[:, -1][:, None, None], jnp.exp(last), 0.0)
    entry = jnp.where(live[:, :, None, None], jnp.exp(cum), 0.0)
    return (inner, states, carry, entry, cb, xb)


def combine(earlier, later):
    return (earlier[0] * later[0], later[0][..., None, None] * earlier[1] + later[1])


def prefix_blocks(carry, states):
    return lax.associative_scan(combine, (carry, states), axis=0)


def finish(pieces, prefix, skip, start):
    inner, states, carry, entry, cb, xb = pieces
    blocks, block, groups, per, hdim = xb.shape
    lead_g = jnp.concatenate([jnp.ones_like(prefix[0]), prefix[0][:-1]], axis=0)
    lead_s = jnp.concatenate([jnp.zeros_like(prefix[1]), prefix[1][:-1]], axis=0)
    entering = (lead_s + lead_g[..., None, None] * start[None]).astype(jnp.bfloat16)
    outer = contract("btgn,bgknp->btgkp", cb, entering) * entry[..., None]
    total = inner + outer + skip.reshape(groups, per)[:, :, None] * xb.astype(jnp.float32)
    return total.reshape(blocks * block, groups * per, hdim).astype(jnp.bfloat16)


def gated_norm(y, gate, gain, gsize):
    rows, width = y.shape
    mixed = y.astype(jnp.float32) * jax.nn.silu(gate.astype(jnp.float32))
    grouped = mixed.reshape(rows, width // gsize, gsize)
    meansq = jnp.mean(grouped * grouped, axis=-1, keepdims=True)
    normed = (grouped * lax.rsqrt(meansq + 1e-05)).reshape(rows, width)
    return (normed * gain).astype(jnp.bfloat16)


def shards(
    x_in,
    z_in,
    bc_in,
    conv_x_weight,
    conv_x_bias,
    conv_bc_weight,
    conv_bc_bias,
    dt_raw,
    dt_bias,
    decay,
    skip_d,
    norm_gain,
    lengths,
):
    rows = x_in.shape[0]
    shard = lax.axis_index("seq")
    heads_local = dt_raw.shape[1]
    groups_local = bc_in.shape[2] // STATE
    ends = jnp.cumsum(lengths)
    width = conv_x_weight.shape[0]
    edge_x, edge_bc = shifted((x_in[rows - width + 1 :], bc_in[rows - width + 1 :]), "seq", 1)
    position = shard * rows + jnp.arange(rows, dtype=jnp.int32)
    own = seg_ids(ends, position)
    keep = jnp.stack([seg_ids(ends, position - (width - 1) + k) == own for k in range(width)])
    xc = conv_act(jnp.concatenate([edge_x, x_in], axis=0), conv_x_weight, conv_x_bias, keep)
    bcc = conv_act(jnp.concatenate([edge_bc, bc_in], axis=0), conv_bc_weight, conv_bc_bias, keep)
    xh = xc.reshape(rows, heads_local, HEAD_DIM)
    rates = jax.nn.softplus(dt_raw.astype(jnp.float32) + dt_bias)
    bmat = bcc[:, 0].reshape(rows, groups_local, STATE)
    cmat = bcc[:, 1].reshape(rows, groups_local, STATE)
    prev_seg = seg_ids(ends, shard * rows + jnp.arange(rows // BLOCK, dtype=jnp.int32) * BLOCK - 1)
    pieces = block_terms(xh, rates, decay, bmat, cmat, own, prev_seg, BLOCK)
    prefix = prefix_blocks(pieces[2], pieces[1])
    identity = (jnp.ones_like(prefix[0][0]), jnp.zeros_like(prefix[1][0]))
    before = prefix_2((prefix[0][-1], prefix[1][-1]), "seq", combine, identity)
    y = finish(pieces, prefix, skip_d, before[1])
    gsize = heads_local * HEAD_DIM // groups_local
    return gated_norm(y.reshape(rows, heads_local * HEAD_DIM), z_in, norm_gain, gsize)


def solution(mesh):
    return jax.shard_map(
        shards,
        mesh=mesh,
        in_specs=(
            P(("groups", "seq"), "heads"),
            P(("groups", "seq"), "heads"),
            P(("groups", "seq"), None, "heads"),
            P(None, "heads"),
            P("heads"),
            P(None, None, "heads"),
            P(None, "heads"),
            P(("groups", "seq"), "heads"),
            P("heads"),
            P("heads"),
            P("heads"),
            P("heads"),
            P("groups"),
        ),
        out_specs=P(("groups", "seq"), "heads"),
        check_vma=False,
    )
```

profile of v0, /device:TPU:0, one launch (start us, length us, event | category | flops | bytes accessed | tf_op | source)
XLA Modules:
  0.0 361.9 jit_solution(2412453798349976921)
XLA Ops:
  6.5 0.9 slice.63
  7.4 4.9 %collective-permute-start = (bf16[3,4096]{1,0:T(4,128)(2,1)S(1)}, bf16[3,4096]{1,0:T(4,128)(2,1)S(1)}, u32[]{:S(2)}, u32[]{:S(2)}) collective-permute-start(bf16[3,4096]{1,0:T(4,128)(2,1)S(1)} %slice.63), channel_id=1, source_target_pairs={{0,2},{2,4},{4,6},{6,8},{8,10},{10,12},{12,14},{1,3},{3,5},{5,7},{... | collective-permute-start | bytes 73736 | tf_op jit(solution)/shard_map/ppermute | solution.py:14
  12.3 0.7 slice.71
  13.2 3.4 collective-permute-start.1
  16.7 0.8 reduce-window.4
  17.5 0.6 fusion.37
  19.5 1.6 slice_convert_fusion.3
  21.7 0.8 compare_select_fusion
  22.6 0.7 mul.277
  23.5 1.2 slice_bitcast_fusion
  25.5 0.7 bitcast_convert_fusion.3
  26.2 1.6 copy.85
  29.2 6.1 %multiply_convert_fusion.3 = bf16[128,4096]{0,1:T(8,128)(2,1)S(1)} fusion(bf16[128,4096]{0,1:T(8,128)(2,1)S(1)} %copy.85, bf16[3,4096]{0,1:T(8,128)(2,1)S(1)} %copy.84, f32[4096]{0:T(1024)S(1)} %bitcast.120, f32[4096]{0:T(1024)} %bitcast.121, f32[4096]{0:T(1024)S(1)} %bitcast.119, f32[4096]{0:T(1024)S(1)} %bitcast.118, f32[4096]{0:T(1024)} %param.19, ...), kind=kLoop, calls=%fused_computation.33 | loop fusion | flops 15204352 | bytes 2204032 | tf_op jit(solution)/shard_map/convert_element_type | solution.py:44
  35.3 1.8 convolution_bitcast_fusion
  37.2 1.3 copy.100
  38.5 18.3 %all-gather = f32[8,1,2,32]{3,2,1,0:T(2,128)S(1)} all-gather(f32[1,1,2,32]{3,2,1,0:T(2,128)S(1)} %copy-done.10), channel_id=2, replica_groups=mesh['groups'=2,'seq'=8,'heads'=2] {'seq'}, dimensions={0}, use_global_device_ids=true | all-gather | bytes 2304 | tf_op jit(solution)/shard_map/all_gather | solution.py:19
  57.2 3.3 fusion.1
  60.5 204.6 %all-gather.3.cloned.1.call-done = f32[8,2,32,128,64]{3,4,2,1,0:T(8,128)} async-done(((f32[1,2,32,128,64]{3,4,2,1,0:T(8,128)}), f32[8,2,32,128,64]{3,4,2,1,0:T(8,128)}) %all-gather.3.cloned.1.call-update) | async-done | bytes 16777232 | tf_op jit(solution)/shard_map/all_gather | solution.py:19
  265.1 82.5 %while.14 = (s32[]{:T(128)}, f32[2,32,128,64]{3,2,1,0:T(8,128)}, s32[]{:T(128)}, f32[8,2,32]{2,1,0:T(2,128)S(1)}, f32[8,2,32,128,64]{3,4,2,1,0:T(8,128)}, /*index=5*/s32[]{:T(128)}, s32[]{:T(128)}) while((s32[]{:T(128)}, f32[2,32,128,64]{3,2,1,0:T(8,128)}, s32[]{:T(128)}, f32[8,2,32]{2,1,0:T(2,128)S(1)}, ...), condition=%wide.region_8.9_spmd.clone, body=%wide.region_7.8_spmd.clone.sunk | while | flops 2097156 | bytes 14680937 | solution.py:29
  265.1 1.7 constant_dynamic-slice_fusion.2
  266.8 2.7 copy.113
  269.6 4.7 %fusion.47 = f32[2,32,128,64]{3,2,1,0:T(8,128)} fusion(f32[1,2,32,128,64]{4,3,2,1,0:T(8,128)} %copy.113, f32[2,32,128,64]{3,2,1,0:T(8,128)} %get-tuple-element.222, f32[2,32]{1,0:T(2,128)S(1)} %dynamic-slice_bitcast_fusion.2, pred[]{:T(512)S(6)} %compare.3, pred[]{:T(512)S(6)} %lt.22), kind=kLoop, calls=%fused_computation.1.clone.1 | loop fusion | flops 2097152 | bytes 6291714 | tf_op jit(solution)/shard_map/while/body/eval_jaxpr/jit(_where)/select_n | solution.py:27
  274.3 1.7 constant_dynamic-slice_fusion.2
  276.0 2.7 copy.113
  278.8 6.0 %fusion.47 = f32[2,32,128,64]{3,2,1,0:T(8,128)} fusion(f32[1,2,32,128,64]{4,3,2,1,0:T(8,128)} %copy.113, f32[2,32,128,64]{3,2,1,0:T(8,128)} %get-tuple-element.222, f32[2,32]{1,0:T(2,128)S(1)} %dynamic-slice_bitcast_fusion.2, pred[]{:T(512)S(6)} %compare.3, pred[]{:T(512)S(6)} %lt.22), kind=kLoop, calls=%fused_computation.1.clone.1 | loop fusion | flops 2097152 | bytes 6291714 | tf_op jit(solution)/shard_map/while/body/eval_jaxpr/jit(_where)/select_n | solution.py:27
  284.8 1.7 constant_dynamic-slice_fusion.2
  286.5 2.7 copy.113
  289.2 6.0 %fusion.47 = f32[2,32,128,64]{3,2,1,0:T(8,128)} fusion(f32[1,2,32,128,64]{4,3,2,1,0:T(8,128)} %copy.113, f32[2,32,128,64]{3,2,1,0:T(8,128)} %get-tuple-element.222, f32[2,32]{1,0:T(2,128)S(1)} %dynamic-slice_bitcast_fusion.2, pred[]{:T(512)S(6)} %compare.3, pred[]{:T(512)S(6)} %lt.22), kind=kLoop, calls=%fused_computation.1.clone.1 | loop fusion | flops 2097152 | bytes 6291714 | tf_op jit(solution)/shard_map/while/body/eval_jaxpr/jit(_where)/select_n | solution.py:27
  295.2 1.7 constant_dynamic-slice_fusion.2
  297.0 2.7 copy.113
  299.7 6.0 %fusion.47 = f32[2,32,128,64]{3,2,1,0:T(8,128)} fusion(f32[1,2,32,128,64]{4,3,2,1,0:T(8,128)} %copy.113, f32[2,32,128,64]{3,2,1,0:T(8,128)} %get-tuple-element.222, f32[2,32]{1,0:T(2,128)S(1)} %dynamic-slice_bitcast_fusion.2, pred[]{:T(512)S(6)} %compare.3, pred[]{:T(512)S(6)} %lt.22), kind=kLoop, calls=%fused_computation.1.clone.1 | loop fusion | flops 2097152 | bytes 6291714 | tf_op jit(solution)/shard_map/while/body/eval_jaxpr/jit(_where)/select_n | solution.py:27
  305.7 1.7 constant_dynamic-slice_fusion.2
  307.4 2.7 copy.113
  310.2 6.0 %fusion.47 = f32[2,32,128,64]{3,2,1,0:T(8,128)} fusion(f32[1,2,32,128,64]{4,3,2,1,0:T(8,128)} %copy.113, f32[2,32,128,64]{3,2,1,0:T(8,128)} %get-tuple-element.222, f32[2,32]{1,0:T(2,128)S(1)} %dynamic-slice_bitcast_fusion.2, pred[]{:T(512)S(6)} %compare.3, pred[]{:T(512)S(6)} %lt.22), kind=kLoop, calls=%fused_computation.1.clone.1 | loop fusion | flops 2097152 | bytes 6291714 | tf_op jit(solution)/shard_map/while/body/eval_jaxpr/jit(_where)/select_n | solution.py:27
  316.2 1.7 constant_dynamic-slice_fusion.2
  317.9 2.7 copy.113
  320.7 6.0 %fusion.47 = f32[2,32,128,64]{3,2,1,0:T(8,128)} fusion(f32[1,2,32,128,64]{4,3,2,1,0:T(8,128)} %copy.113, f32[2,32,128,64]{3,2,1,0:T(8,128)} %get-tuple-element.222, f32[2,32]{1,0:T(2,128)S(1)} %dynamic-slice_bitcast_fusion.2, pred[]{:T(512)S(6)} %compare.3, pred[]{:T(512)S(6)} %lt.22), kind=kLoop, calls=%fused_computation.1.clone.1 | loop fusion | flops 2097152 | bytes 6291714 | tf_op jit(solution)/shard_map/while/body/eval_jaxpr/jit(_where)/select_n | solution.py:27
  326.7 1.7 constant_dynamic-slice_fusion.2
  328.4 2.7 copy.113
  331.1 6.0 %fusion.47 = f32[2,32,128,64]{3,2,1,0:T(8,128)} fusion(f32[1,2,32,128,64]{4,3,2,1,0:T(8,128)} %copy.113, f32[2,32,128,64]{3,2,1,0:T(8,128)} %get-tuple-element.222, f32[2,32]{1,0:T(2,128)S(1)} %dynamic-slice_bitcast_fusion.2, pred[]{:T(512)S(6)} %compare.3, pred[]{:T(512)S(6)} %lt.22), kind=kLoop, calls=%fused_computation.1.clone.1 | loop fusion | flops 2097152 | bytes 6291714 | tf_op jit(solution)/shard_map/while/body/eval_jaxpr/jit(_where)/select_n | solution.py:27
  337.1 1.7 constant_dynamic-slice_fusion.2
  338.9 2.7 copy.113
  341.6 6.0 %fusion.47 = f32[2,32,128,64]{3,2,1,0:T(8,128)} fusion(f32[1,2,32,128,64]{4,3,2,1,0:T(8,128)} %copy.113, f32[2,32,128,64]{3,2,1,0:T(8,128)} %get-tuple-element.222, f32[2,32]{1,0:T(2,128)S(1)} %dynamic-slice_bitcast_fusion.2, pred[]{:T(512)S(6)} %compare.3, pred[]{:T(512)S(6)} %lt.22), kind=kLoop, calls=%fused_computation.1.clone.1 | loop fusion | flops 2097152 | bytes 6291714 | tf_op jit(solution)/shard_map/while/body/eval_jaxpr/jit(_where)/select_n | solution.py:27
  347.6 3.1 fusion.11
  351.2 0.7 copy-done
  351.9 0.8 bitcast_reduce_fusion
  352.8 0.9 fusion.10
  353.7 1.3 copy.101
  (61 shorter events, 4.8 us)
Async XLA Ops:
  6.5 21.3 %copy-start.3 = (bf16[128,2,256]{2,1,0:T(2,128)(2,1)S(1)}, bf16[128,2,256]{2,1,0:T(2,128)(2,1)}, u32[]{:S(2)}) copy-start(bf16[128,2,256]{2,1,0:T(2,128)(2,1)} %param.17) | copy-start | bytes 393220
  6.5 21.5 %copy-start.11 = (f32[2,256]{1,0:T(2,128)S(1)}, f32[2,256]{1,0:T(2,128)}, u32[]{:S(2)}) copy-start(f32[2,256]{1,0:T(2,128)} %param.21) | copy-start | bytes 6148
  6.5 258.5 %all-gather.3.cloned.1.call-start = ((), (), s32[]{:S(2)}) async-start(), calls=%async_computation | async-start | bytes 18874368 | tf_op jit(solution)/shard_map/all_gather | solution.py:19
  7.4 21.2 %collective-permute-start = (bf16[3,4096]{1,0:T(4,128)(2,1)S(1)}, bf16[3,4096]{1,0:T(4,128)(2,1)S(1)}, u32[]{:S(2)}, u32[]{:S(2)}) collective-permute-start(bf16[3,4096]{1,0:T(4,128)(2,1)S(1)} %slice.63), channel_id=1, source_target_pairs={{0,2},{2,4},{4,6},{6,8},{8,10},{10,12},{12,14},{1,3},{3,5},{5,7},{... | collective-permute-start | bytes 73736 | tf_op jit(solution)/shard_map/ppermute | solution.py:14
  13.2 14.8 %collective-permute-start.1 = (bf16[3,2,256]{0,2,1:T(8,128)(2,1)S(1)}, bf16[3,2,256]{0,2,1:T(8,128)(2,1)S(1)}, u32[]{:S(2)}, u32[]{:S(2)}) collective-permute-start(bf16[3,2,256]{0,2,1:T(8,128)(2,1)S(1)} %copy.90), channel_id=1, source_target_pairs={{0,2},{2,4},{4,6},{6,8},{8,10},{10,12},{12,14},{1,3},{3,5},{5,7},{... | collective-permute-start | bytes 9224 | tf_op jit(solution)/shard_map/ppermute | solution.py:14
  18.9 6.5 %copy-start.5 = (s32[128]{0:T(128)}, s32[128]{0:T(128)S(1)}, u32[]{:S(2)}) copy-start(s32[128]{0:T(128)S(1)} %get-tuple-element.158) | copy-start | bytes 1540
  25.3 2.7 copy-start.7
  25.3 2.7 copy-start.8
  25.3 2.7 copy-start.9
  35.3 1.9 copy-start.12
  35.3 2.0 copy-start.2
  37.0 1.5 copy-start.10
  37.0 19.8 %copy-start.6 = (s32[128]{0:T(128)S(1)}, s32[128]{0:T(128)}, u32[]{:S(2)}) copy-start(s32[128]{0:T(128)} %copy-done.5) | copy-start | bytes 1540
  347.6 3.1 copy-start.1
  350.7 1.2 copy-start
  351.9 0.8 copy-start.4
Sparse Core Ops, SparseCore 0:
  37.2 227.8 all-gather.2
where the time goes:
time: 363 us; the launch traced here: 362 us
  waiting for transfers between devices  205 us (56%)
  other arithmetic  62.4 us (17%)
  local copies, waits for them, and re-layouts  45.4 us (13%)
  blocking collectives  18.3 us (5%)
  between operations  14.3 us (4%)
  matrix products  8.34 us (2%)
  starting transfers between devices  8.31 us (2%)
    all_gather x1, waiting for transfers between devices, prefix_2(): everything = jax.tree.map(lambda part: lax.all_gather(part, axis), x)  205 us
    select_n x8, other arithmetic, step(): return jax.tree.map(lambda a, b: jnp.where(reached, a, b), new, before)  46.7 us
    dynamic_slice x16, local copies, waits for them, and re-layouts, step(): new = combine(before, jax.tree.map(lambda part: part[k], everything))  35.7 us
    all_gather x1, blocking collectives, prefix_2(): everything = jax.tree.map(lambda part: lax.all_gather(part, axis), x)  18.3 us
    dot_general x4, matrix products, contract(): return jnp.einsum(form, left, right, preferred_element_type=jnp.float32)  8.34 us
    ppermute x2, starting transfers between devices, shifted(): return lax.ppermute(block, axis, route)  8.31 us
  transfers between devices with their start and end apart: 3, of which 1 were waited for; matrix products, arithmetic and copies ran while one was open for 5% of the time, Pallas kernels for 0%

commit v1 on v0

v1 whole, which is shorter than its diff:
```python
import functools

import jax
import jax.numpy as jnp
from jax import lax
from jax.experimental import pallas as pl
from jax.experimental.pallas import tpu as pltpu
from jax.sharding import PartitionSpec as P

HEAD_DIM = 64
STATE = 128
BLOCK = 128
QUAD = 4
HALO = 16
EXTRA = 16
F32 = jnp.float32
BF16 = jnp.bfloat16


def mm(left, right):
    return jnp.dot(left, right, preferred_element_type=F32)


def ends_of(lens_ref):
    total = 0
    ends = []
    for i in range(lens_ref.shape[0]):
        total = total + lens_ref[i]
        ends.append(total)
    return ends


def seg_of(pos, ends):
    count = 0
    for end in ends:
        count = count + jnp.where(end <= pos, 1, 0)
    return jnp.where(pos >= 0, count, -1)


def tokens(start, shape, dim):
    return start + lax.broadcasted_iota(jnp.int32, shape, dim)


def shift_matrix(start, ends, taps):
    shape = (BLOCK, HALO + BLOCK)
    row = lax.broadcasted_iota(jnp.int32, shape, 0)
    col = lax.broadcasted_iota(jnp.int32, shape, 1)
    same = seg_of(start + row, ends) == seg_of(start - HALO + col, ends)
    parts = []
    for k in range(taps - 1):
        parts.append(jnp.where((col == row + (HALO - taps + 1 + k)) & same, 1.0, 0.0))
    return jnp.concatenate(parts, axis=0).astype(BF16)


def conv_half(shift, halo, block, weight, bias):
    taps = weight.shape[0]
    half = weight.astype(F32) * 0.5
    moved = mm(shift, jnp.concatenate([halo, block], axis=0))
    total = bias * 0.5 + block.astype(F32) * half[taps - 1 : taps]
    for k in range(taps - 1):
        total = total + moved[k * BLOCK : (k + 1) * BLOCK] * half[k : k + 1]
    return total


def silu_of_half(half):
    return half + half * jnp.tanh(half)


def rates_of(dt_ref, dtb_ref, dec_ref):
    raw = jnp.transpose(dt_ref[...].astype(F32)) + dtb_ref[...]
    rate = jnp.maximum(raw, 0.0) + jnp.log1p(jnp.exp(-jnp.abs(raw)))
    shape = (BLOCK, BLOCK)
    lower = lax.broadcasted_iota(jnp.int32, shape, 0) >= lax.broadcasted_iota(jnp.int32, shape, 1)
    cum = jnp.dot(
        jnp.where(lower, 1.0, 0.0),
        -rate * dec_ref[...],
        precision=lax.Precision.HIGHEST,
        preferred_element_type=F32,
    )
    return rate, cum


def head_map(heads, first, width):
    shape = (heads, width)
    row = lax.broadcasted_iota(jnp.int32, shape, 0)
    col = lax.broadcasted_iota(jnp.int32, shape, 1)
    return jnp.where(row == first + col // HEAD_DIM, 1.0, 0.0).astype(BF16)


def pair_of(value):
    high = value.astype(BF16)
    low = (value - high.astype(F32)).astype(BF16)
    return high, low


def spread(value, onehot2):
    high, low = pair_of(value)
    return mm(jnp.concatenate([high, low], axis=1), onehot2)


def state_kernel(k, info, lens, x, halo, b_in, halo_b, wx, bx, wb, bb, dt, dtb, dec, msg, xc_out):
    start = info[0] * BLOCK
    quarter = info[1] ^ k
    width = x.shape[1]
    heads = dt.shape[0]
    ends = ends_of(lens)
    shift = shift_matrix(start, ends, wx.shape[0])
    xc = silu_of_half(conv_half(shift, halo[...], x[...], wx[...], bx[...])).astype(BF16)
    xc_out[...] = xc
    bmat = silu_of_half(conv_half(shift, halo_b[...], b_in[...], wb[...], bb[...]))
    bmat_t = jnp.transpose(bmat).astype(BF16)
    rate, cum = rates_of(dt, dtb, dec)
    last = cum[BLOCK - 1 : BLOCK]
    seg_last = seg_of(start + BLOCK - 1, ends)
    same = seg_of(tokens(start, (BLOCK, heads), 0), ends) == seg_last
    factor = jnp.where(same, jnp.exp(last - cum), 0.0) * rate
    onehot = head_map(heads, quarter * (width // HEAD_DIM), width)
    scaled = (xc.astype(F32) * spread(factor, jnp.concatenate([onehot, onehot], axis=0))).astype(BF16)
    msg[0:STATE, :] = mm(bmat_t, scaled).astype(BF16)
    live = seg_last == seg_of(start - 1, ends)
    carry = jnp.where(live, jnp.exp(last), 0.0)
    high, low = pair_of(carry)
    row = lax.broadcasted_iota(jnp.int32, (EXTRA, heads), 0)
    rows = jnp.where(row == 0, high.astype(F32), jnp.where(row == 1, low.astype(F32), 0.0))
    msg[STATE : STATE + EXTRA, :] = mm(rows.astype(BF16), onehot).astype(BF16)


def carry_of(msg):
    return msg[STATE : STATE + 1, :].astype(F32) + msg[STATE + 1 : STATE + 2, :].astype(F32)


def fold_kernel(info, m0, m1, m2, m3, total, decay):
    msgs = (m0, m1, m2, m3)
    for mine in range(QUAD):

        @pl.when(info[1] == mine)
        def _():
            block = [msgs[mine ^ b] for b in range(QUAD)]
            state = block[0][0:STATE, :].astype(F32)
            through = carry_of(block[0])
            for b in range(1, QUAD):
                carry = carry_of(block[b])
                state = block[b][0:STATE, :].astype(F32) + carry * state
                through = through * carry
            total[...] = state.astype(BF16)
            decay[...] = jnp.broadcast_to(through, decay.shape)


def enter_kernel(info, start, m0, m1, m2, m3, o0, o1, o2, o3):
    msgs = (m0, m1, m2, m3)
    outs = (o0, o1, o2, o3)
    for mine in range(QUAD):

        @pl.when(info[1] == mine)
        def _():
            outs[mine][...] = start[...]
            state = start[...].astype(F32)
            for b in range(1, QUAD):
                prev = msgs[mine ^ (b - 1)]
                state = prev[0:STATE, :].astype(F32) + carry_of(prev) * state
                outs[mine ^ b][...] = state.astype(BF16)


def inner_kernel(
    k, info, lens, xc, z, b_in, c_in, halo_b, halo_c, wb, wc, bb, bc, dt, dtb, dec, skip, near, gain, c_out
):
    start = info[0] * BLOCK
    quarter = info[1] ^ k
    width = xc.shape[1]
    heads = dt.shape[0]
    ends = ends_of(lens)
    shift = shift_matrix(start, ends, wb.shape[0])
    bmat = silu_of_half(conv_half(shift, halo_b[...], b_in[...], wb[...], bb[...])).astype(BF16)
    cmat = silu_of_half(conv_half(shift, halo_c[...], c_in[...], wc[...], bc[...])).astype(BF16)
    c_out[...] = cmat
    rate, cum = rates_of(dt, dtb, dec)
    shape = (BLOCK, BLOCK)
    row = lax.broadcasted_iota(jnp.int32, shape, 0)
    col = lax.broadcasted_iota(jnp.int32, shape, 1)
    mask = (row >= col) & (seg_of(start + row, ends) == seg_of(start + col, ends))
    scores = lax.dot_general(cmat, bmat, (((1,), (1,)), ((), ())), preferred_element_type=F32)
    scores = jnp.where(mask, scores, 0.0).astype(BF16)
    onehot = head_map(heads, quarter * (width // HEAD_DIM), width)
    onehot2 = jnp.concatenate([onehot, onehot], axis=0)
    xf = xc[...].astype(F32)
    scaled = (xf * spread(rate * jnp.exp(-cum), onehot2)).astype(BF16)
    grown = jnp.exp(cum)
    grown_c = spread(grown, onehot2)
    skip_c = spread(jnp.broadcast_to(skip[...], (8, heads)), onehot2)[0:1]
    zf = z[...].astype(F32) * 0.5
    gate = silu_of_half(zf)
    near[...] = (mm(scores, scaled) * grown_c + skip_c * xf) * gate
    live = seg_of(tokens(start, (BLOCK, width), 0), ends) == seg_of(start - 1, ends)
    gain[...] = jnp.where(live, grown_c * gate, 0.0)


def finish_kernel(k, info, near0, near1, gain0, gain1, e0, e1, cmat, scale, *rest):
    out = rest[-1]
    width = near0.shape[1]
    c = cmat[...]
    first = near0[...] + gain0[...] * mm(c, e0[...])
    second = near1[...] + gain1[...] * mm(c, e1[...])
    square = jnp.sum(first * first, axis=1, keepdims=True) + jnp.sum(second * second, axis=1, keepdims=True)
    inv = lax.rsqrt(square * (1.0 / (2 * width)) + 1e-05)
    low = ((info[1] ^ k) & 1) == 0
    for mine in range(2):

        @pl.when(low == (mine == 0))
        def _():
            a = slice(mine * width, (mine + 1) * width)
            b = slice((1 - mine) * width, (2 - mine) * width)
            out[:, a] = (first * inv * scale[:, a]).astype(BF16)
            out[:, b] = (second * inv * scale[:, b]).astype(BF16)


def call(kernel, scalars, grid_in, outs, specs_in, specs_out, args, flops, aliases=None, limit=None):
    nbytes = 4 << 20
    return pl.pallas_call(
        kernel,
        grid_spec=pltpu.PrefetchScalarGridSpec(
            num_scalar_prefetch=len(scalars), grid=grid_in, in_specs=specs_in, out_specs=specs_out
        ),
        out_shape=outs,
        input_output_aliases=aliases or {},
        cost_estimate=pl.CostEstimate(flops=flops, bytes_accessed=nbytes, transcendentals=0),
        compiler_params=pltpu.CompilerParams(vmem_limit_bytes=limit or (32 << 20)),
    )(*scalars, *args)


def shards(
    x_in,
    z_in,
    bc_in,
    conv_x_weight,
    conv_x_bias,
    conv_bc_weight,
    conv_bc_bias,
    dt_raw,
    dt_bias,
    decay,
    skip_d,
    norm_gain,
    lengths,
):
    rows, chan = x_in.shape
    heads = dt_raw.shape[1]
    peers = lax.axis_size("seq")
    shard = lax.axis_index("seq").astype(jnp.int32)
    taps = conv_x_weight.shape[0]
    width = chan // QUAD
    groups = bc_in.shape[2] // STATE
    per_group = QUAD // groups
    bcw = bc_in.shape[2]
    reach = peers // 2 // QUAD

    bc2 = bc_in.reshape(rows, 2 * bcw)
    wbc = conv_bc_weight.reshape(taps, 2 * bcw)
    bbc = conv_bc_bias.reshape(1, 2 * bcw)
    bx = conv_x_bias.reshape(1, chan)
    gain = norm_gain.reshape(1, chan)
    dt_t = dt_raw.T
    dtb = dt_bias.reshape(1, heads)
    dec = decay.reshape(1, heads)
    skip = skip_d.reshape(1, heads)
    info = jnp.stack([shard, shard % QUAD])

    edge = jnp.concatenate([x_in[rows - HALO :], bc2[rows - HALO :]], axis=1)
    edge = lax.ppermute(edge, "seq", [(i, (i + 1) % peers) for i in range(peers)])
    scalars = (info, lengths)

    def spec(shape, col):
        return pl.BlockSpec(shape, lambda i, info, *_: (0, col(info)))

    def whole(shape):
        return pl.BlockSpec(shape, lambda i, *_: (0, 0))

    def at(k):
        return lambda info: info[1] ^ k

    def group_at(k, base):
        return lambda info: base + (info[1] ^ k) // per_group

    rate_specs = [whole((heads, rows)), whole((1, heads)), whole((1, heads))]
    rate_args = [dt_t, dtb, dec]
    xw = width // STATE * QUAD

    def state(k):
        return call(
            functools.partial(state_kernel, k),
            scalars,
            (1,),
            [jax.ShapeDtypeStruct((STATE + EXTRA, width), BF16), jax.ShapeDtypeStruct((rows, width), BF16)],
            [
                spec((rows, width), at(k)),
                spec((HALO, width), at(k)),
                spec((rows, STATE), group_at(k, 0)),
                spec((HALO, STATE), group_at(k, xw)),
                spec((taps, width), at(k)),
                spec((1, width), at(k)),
                spec((taps, STATE), group_at(k, 0)),
                spec((1, STATE), group_at(k, 0)),
                *rate_specs,
            ],
            [whole((STATE + EXTRA, width)), whole((rows, width))],
            [x_in, edge, bc2, edge, conv_x_weight, bx, wbc, bbc, *rate_args],
            400_000_000,
        )

    def inner(k, xc):
        return call(
            functools.partial(inner_kernel, k),
            scalars,
            (1,),
            [
                jax.ShapeDtypeStruct((rows, width), F32),
                jax.ShapeDtypeStruct((rows, width), F32),
                jax.ShapeDtypeStruct((rows, STATE), BF16),
            ],
            [
                whole((rows, width)),
                spec((rows, width), at(k)),
                spec((rows, STATE), group_at(k, 0)),
                spec((rows, STATE), group_at(k, groups)),
                spec((HALO, STATE), group_at(k, xw)),
                spec((HALO, STATE), group_at(k, xw + groups)),
                spec((taps, STATE), group_at(k, 0)),
                spec((taps, STATE), group_at(k, groups)),
                spec((1, STATE), group_at(k, 0)),
                spec((1, STATE), group_at(k, groups)),
                *rate_specs,
                whole((1, heads)),
            ],
            [whole((rows, width)), whole((rows, width)), whole((rows, STATE))],
            [xc, z_in, bc2, bc2, edge, edge, wbc, wbc, bbc, bbc, *rate_args, skip],
            400_000_000,
        )

    def swap(value, k):
        return lax.ppermute(value, "seq", [(i, i ^ k) for i in range(peers)])

    def ahead(value):
        return lax.ppermute(value, "seq", [(i, (i + QUAD) % peers) for i in range(peers)])

    msgs, xcs = [None] * QUAD, [None] * QUAD
    for k in (3, 2, 1, 0):
        msgs[k], xcs[k] = state(k)
        if k:
            msgs[k] = swap(msgs[k], k)

    locals_ = [inner(k, xcs[k]) for k in range(QUAD)]

    msg_spec = whole((STATE + EXTRA, width))
    state_spec = whole((STATE, width))
    total, through = call(
        fold_kernel,
        (info,),
        (1,),
        [jax.ShapeDtypeStruct((STATE, width), BF16), jax.ShapeDtypeStruct((8, width), F32)],
        [msg_spec] * QUAD,
        [state_spec, whole((8, width))],
        msgs,
        1_000_000,
    )
    entering = ahead(total)
    for _ in range(reach - 1):
        entering = ahead((total.astype(F32) + through[0:1] * entering.astype(F32)).astype(BF16))
    enter = call(
        enter_kernel,
        (info,),
        (1,),
        [jax.ShapeDtypeStruct((STATE, width), BF16)] * QUAD,
        [state_spec] + [msg_spec] * QUAD,
        [state_spec] * QUAD,
        [entering, *msgs],
        1_000_000,
    )
    enter = [enter[0]] + [swap(enter[k], k) for k in range(1, QUAD)]

    out = None
    for p in range(groups):
        k = 2 * p
        args = [
            locals_[k][0], locals_[k + 1][0], locals_[k][1], locals_[k + 1][1], enter[k], enter[k + 1],
            locals_[k][2], gain,
        ]
        specs = [whole((rows, width))] * 4 + [state_spec] * 2
        specs += [whole((rows, STATE)), spec((1, 2 * width), group_at(k, 0))]
        aliases = {}
        if out is not None:
            aliases = {1 + len(args): 0}
            args.append(out)
            specs.append(pl.BlockSpec(memory_space=pl.ANY))
        out = call(
            functools.partial(finish_kernel, k),
            (info,),
            (1,),
            jax.ShapeDtypeStruct((rows, chan), BF16),
            specs,
            spec((rows, 2 * width), group_at(k, 0)),
            args,
            200_000_000,
            aliases,
        )
    return out


def solution(mesh):
    return jax.shard_map(
        shards,
        mesh=mesh,
        in_specs=(
            P(("groups", "seq"), "heads"),
            P(("groups", "seq"), "heads"),
            P(("groups", "seq"), None, "heads"),
            P(None, "heads"),
            P("heads"),
            P(None, None, "heads"),
            P(None, "heads"),
            P(("groups", "seq"), "heads"),
            P("heads"),
            P("heads"),
            P("heads"),
            P("heads"),
            P("groups"),
        ),
        out_specs=P(("groups", "seq"), "heads"),
        check_vma=False,
    )
```

time: 363 us -> 63.9 us (0.18)
  waiting for transfers between devices: 205 us -> 30.4 us
  other arithmetic: 62.4 us -> 0.09 us
  local copies, waits for them, and re-layouts: 45.4 us -> 4.16 us
  blocking collectives: 18.3 us -> 0 us
  Pallas kernels: 0 us -> 18.2 us
  between operations: 14.3 us -> 0.14 us
  matrix products: 8.34 us -> 0 us
    all_gather x1 -> x0, waiting for transfers between devices: 205 us -> none  [prefix_2(): everything = jax.tree.map(lambda part: lax.all_gather(part, axis), x)]
    select_n x10 -> x0, other arithmetic: 47.6 us -> none  [the longest x8 46.7 us: step(): return jax.tree.map(lambda a, b: jnp.where(reached, a, b), new, before)]
    dynamic_slice x16 -> x0, local copies, waits for them, and re-layouts: 35.7 us -> none  [step(): new = combine(before, jax.tree.map(lambda part: part[k], everything))]
    ppermute x2 -> x8, waiting for transfers between devices: 0.01 us -> 30.4 us  [the longest x1 12.5 us: ahead(): lax.ppermute(value, 'seq', [(i, (i + QUAD) % peers) for i in range(peers)])]
    all_gather x1 -> x0, blocking collectives: 18.3 us -> none  [prefix_2(): everything = jax.tree.map(lambda part: lax.all_gather(part, axis), x)]
    pallas_call x0 -> x12, Pallas kernels: none -> 18.2 us  [call(): pl.pallas_call(kernel, grid_spec=pltpu.PrefetchScalarGridSpec(num_scalar_...]
    dot_general x4 -> x0, matrix products: 8.34 us -> none  [contract(): return jnp.einsum(form, left, right, preferred_element_type=jnp.float32)]
    convert_element_type x4 -> x0, other arithmetic: 8.11 us -> none  [the longest x2 6.67 us: conv_act(): return jax.nn.silu(total).astype(jnp.bfloat16)]
  transfers between devices with their start and end apart: 3 -> 8, of which waited for: 1 -> 5; matrix products, arithmetic and copies ran while one was open for 5% -> 0% of each run, Pallas kernels for 0% -> 20%
where the time goes in v1:
time: 63.9 us; the launch traced here: 63.6 us
  waiting for transfers between devices  30.4 us (48%)
  Pallas kernels  18.2 us (28%)
  starting transfers between devices  10.6 us (17%)
  local copies, waits for them, and re-layouts  4.16 us (7%)
    pallas_call x12, Pallas kernels, call(): pl.pallas_call(kernel, grid_spec=pltpu.PrefetchScalarGridSpec(num_scalar_...  18.2 us
    ppermute x1, waiting for transfers between devices, ahead(): lax.ppermute(value, 'seq', [(i, (i + QUAD) % peers) for i in range(peers)])  12.5 us
    ppermute x6, waiting for transfers between devices, swap(): return lax.ppermute(value, 'seq', [(i, i ^ k) for i in range(peers)])  11.9 us
    ppermute x6, starting transfers between devices, swap(): return lax.ppermute(value, 'seq', [(i, i ^ k) for i in range(peers)])  7.22 us
    ppermute x1, waiting for transfers between devices, shards(): lax.ppermute(edge, 'seq', [(i, (i + 1) % peers) for i in range(peers)])  6.08 us
    unnamed x30, local copies, waits for them, and re-layouts  3.26 us
    ppermute x1, starting transfers between devices, shards(): lax.ppermute(edge, 'seq', [(i, (i + 1) % peers) for i in range(peers)])  3.02 us
  transfers between devices with their start and end apart: 8, of which 5 were waited for; matrix products, arithmetic and copies ran while one was open for 0% of the time, Pallas kernels for 20%

profile of v1, /device:TPU:0, one launch (start us, length us, event | category | flops | bytes accessed | tf_op | source)
XLA Modules:
  0.0 63.6 jit_solution(12907923770257659461)
XLA Ops:
  0.0 0.0 slice-start
  0.0 0.0 slice-start.1
  0.0 0.8 %slice-done.1 = bf16[16,2,256]{2,1,0:T(2,128)(2,1)S(1)} async-done(((bf16[128,2,256]{2,1,0:T(2,128)(2,1)}), bf16[16,2,256]{2,1,0:T(2,128)(2,1)S(1)}, s32[]{:S(2)}) %slice-start.1) | async-done | bytes 16408 | tf_op jit(solution)/shard_map/slice | solution.py:267
  0.8 0.1 slice-done
  0.9 0.0 copy-start.10
  0.9 3.0 %collective-permute-start = (bf16[16,4608]{1,0:T(8,128)(2,1)S(1)}, bf16[16,4608]{1,0:T(8,128)(2,1)S(1)}, u32[]{:S(2)}, u32[]{:S(2)}) collective-permute-start(bf16[16,4608]{1,0:T(8,128)(2,1)S(1)} %pad_maximum_fusion), channel_id=1, source_target_pairs={{0,2},{2,4},{4,6},{6,8},{8,10},{10,12},{12,14},{14,0},{1,3},{3,5},... | collective-permute-start | bytes 442376 | tf_op jit(solution)/shard_map/ppermute | solution.py:268
  3.9 0.0 copy-done.10
  4.0 0.0 copy-start.12
  4.0 0.7 %copy-done.11 = bf16[4,2,256]{2,1,0:T(2,128)(2,1)S(1)} copy-done((bf16[4,2,256]{2,1,0:T(2,128)(2,1)S(1)}, bf16[4,2,256]{2,1,0:T(2,128)(2,1)}, u32[]{:S(2)}) %copy-start.11) | copy-done | bytes 4120
  4.6 0.0 copy-done.12
  4.7 0.1 pad_add_fusion.info
  4.7 6.1 %collective-permute-done.halo.halo_b.halo_c = bf16[16,4608]{1,0:T(8,128)(2,1)S(1)} collective-permute-done((bf16[16,4608]{1,0:T(8,128)(2,1)S(1)}, bf16[16,4608]{1,0:T(8,128)(2,1)S(1)}, u32[]{:S(2)}, u32[]{:S(2)}) %collective-permute-start) | collective-permute-done | bytes 147488 | tf_op jit(solution)/shard_map/ppermute | solution.py:268
  10.8 0.0 copy-done.3
  10.8 0.0 copy-done.4
  10.8 0.0 copy-done.2
  10.9 0.6 copy-done.6
  11.5 0.0 copy-done.7
  11.5 0.0 copy-done.8
  11.5 1.2 %copy-done = bf16[128,4096]{1,0:T(8,128)(2,1)S(1)} copy-done((bf16[128,4096]{1,0:T(8,128)(2,1)S(1)}, bf16[128,4096]{1,0:T(8,128)(2,1)}, u32[]{:S(2)}) %copy-start) | copy-done | bytes 1048600
  12.7 1.6 %shard_map.132 = (bf16[144,1024]{1,0:T(8,128)(2,1)S(1)}, bf16[128,1024]{1,0:T(8,128)(2,1)S(1)}) custom-call(s32[2]{0:T(128)S(1)} %pad_add_fusion.info, s32[8]{0:T(128)S(1)} %copy-done.6, bf16[128,4096]{1,0:T(8,128)(2,1)S(1)} %copy-done, bf16[16,4608]{1,0:T(8,128)(2,1)S(1)} %collective-permute-done.halo.halo_b.halo_c, bf16[128,512]{1,0:T(8,128)(2,1)S(1)} %bitcast.17, ...), custom_call_target="tpu_custom_call" | custom-call | flops 400000000 | bytes 4194304 | tf_op jit(solution)/shard_map/pallas_call | solution.py:218
  14.3 0.1 collective-permute-start.1
  14.4 1.6 %shard_map.127 = (bf16[144,1024]{1,0:T(8,128)(2,1)S(1)}, bf16[128,1024]{1,0:T(8,128)(2,1)S(1)}) custom-call(s32[2]{0:T(128)S(1)} %pad_add_fusion.info, s32[8]{0:T(128)S(1)} %copy-done.6, bf16[128,4096]{1,0:T(8,128)(2,1)S(1)} %copy-done, bf16[16,4608]{1,0:T(8,128)(2,1)S(1)} %collective-permute-done.halo.halo_b.halo_c, bf16[128,512]{1,0:T(8,128)(2,1)S(1)} %bitcast.18, ...), custom_call_target="tpu_custom_call" | custom-call | flops 400000000 | bytes 4194304 | tf_op jit(solution)/shard_map/pallas_call | solution.py:218
  16.0 0.3 collective-permute-start.2
  16.3 1.6 %shard_map.129 = (bf16[144,1024]{1,0:T(8,128)(2,1)S(1)}, bf16[128,1024]{1,0:T(8,128)(2,1)S(1)}) custom-call(s32[2]{0:T(128)S(1)} %pad_add_fusion.info, s32[8]{0:T(128)S(1)} %copy-done.6, bf16[128,4096]{1,0:T(8,128)(2,1)S(1)} %copy-done, bf16[16,4608]{1,0:T(8,128)(2,1)S(1)} %collective-permute-done.halo.halo_b.halo_c, bf16[128,512]{1,0:T(8,128)(2,1)S(1)} %bitcast.19, ...), custom_call_target="tpu_custom_call" | custom-call | flops 400000000 | bytes 4194304 | tf_op jit(solution)/shard_map/pallas_call | solution.py:218
  17.9 3.3 %collective-permute-start.3 = (bf16[144,1024]{1,0:T(8,128)(2,1)S(1)}, bf16[144,1024]{1,0:T(8,128)(2,1)S(1)}, u32[]{:S(2)}, u32[]{:S(2)}) collective-permute-start(bf16[144,1024]{1,0:T(8,128)(2,1)S(1)} %get-tuple-element.37), channel_id=1, source_target_pairs={{0,6},{2,4},{4,2},{6,0},{8,14},{10,12},{12,10},{14,8},{1,7},{3,5},... | collective-permute-start | bytes 884744 | tf_op jit(solution)/shard_map/ppermute | solution.py:339
  21.1 1.6 %shard_map.131 = (bf16[144,1024]{1,0:T(8,128)(2,1)S(1)}, bf16[128,1024]{1,0:T(8,128)(2,1)S(1)}) custom-call(s32[2]{0:T(128)S(1)} %pad_add_fusion.info, s32[8]{0:T(128)S(1)} %copy-done.6, bf16[128,4096]{1,0:T(8,128)(2,1)S(1)} %copy-done, bf16[16,4608]{1,0:T(8,128)(2,1)S(1)} %collective-permute-done.halo.halo_b.halo_c, bf16[128,512]{1,0:T(8,128)(2,1)S(1)} %bitcast.20, ...), custom_call_target="tpu_custom_call" | custom-call | flops 400000000 | bytes 4194304 | tf_op jit(solution)/shard_map/pallas_call | solution.py:218
  22.7 0.0 collective-permute-done.1.m1
  22.7 3.3 %collective-permute-done.2.m2 = bf16[144,1024]{1,0:T(8,128)(2,1)S(1)} collective-permute-done((bf16[144,1024]{1,0:T(8,128)(2,1)S(1)}, bf16[144,1024]{1,0:T(8,128)(2,1)S(1)}, u32[]{:S(2)}, u32[]{:S(2)}) %collective-permute-start.2) | collective-permute-done | bytes 294944 | tf_op jit(solution)/shard_map/ppermute | solution.py:339
  26.0 5.7 %collective-permute-done.3.m3 = bf16[144,1024]{1,0:T(8,128)(2,1)S(1)} collective-permute-done((bf16[144,1024]{1,0:T(8,128)(2,1)S(1)}, bf16[144,1024]{1,0:T(8,128)(2,1)S(1)}, u32[]{:S(2)}, u32[]{:S(2)}) %collective-permute-start.3) | collective-permute-done | bytes 294944 | tf_op jit(solution)/shard_map/ppermute | solution.py:339
  31.7 1.4 %shard_map.133 = (bf16[128,1024]{1,0:T(8,128)(2,1)S(1)}, f32[8,1024]{1,0:T(8,128)}) custom-call(s32[2]{0:T(128)S(1)} %pad_add_fusion.info, bf16[144,1024]{1,0:T(8,128)(2,1)S(1)} %get-tuple-element.34.m0, bf16[144,1024]{1,0:T(8,128)(2,1)S(1)} %collective-permute-done.1.m1, bf16[144,1024]{1,0:T(8,128)(2,1)S(1)} %collective-permute-done.2.m2, ...), custom_call_target="tpu_custom_call" | custom-call | flops 1000000 | bytes 4194304 | tf_op jit(solution)/shard_map/pallas_call | solution.py:218
  33.1 0.4 collective-permute-start.4
  33.4 12.5 %collective-permute-done.4.start = bf16[128,1024]{1,0:T(8,128)(2,1)S(1)} collective-permute-done((bf16[128,1024]{1,0:T(8,128)(2,1)S(1)}, bf16[128,1024]{1,0:T(8,128)(2,1)S(1)}, u32[]{:S(2)}, u32[]{:S(2)}) %collective-permute-start.4) | collective-permute-done | bytes 262176 | tf_op jit(solution)/shard_map/ppermute | solution.py:342
  45.9 0.8 %shard_map.134 = (bf16[128,1024]{1,0:T(8,128)(2,1)S(1)}, bf16[128,1024]{1,0:T(8,128)(2,1)S(1)}, bf16[128,1024]{1,0:T(8,128)(2,1)S(1)}, bf16[128,1024]{1,0:T(8,128)(2,1)S(1)}) custom-call(s32[2]{0:T(128)S(1)} %pad_add_fusion.info, bf16[128,1024]{1,0:T(8,128)(2,1)S(1)} %collective-permute-done.4.start, bf16[144,1024]{1,0:T(8,128)(2,1)S(1)} %get-tuple-element.34.m0, ...), custom_call_target="tpu_custom_call" | custom-call | flops 1000000 | bytes 4194304 | tf_op jit(solution)/shard_map/pallas_call | solution.py:218
  46.7 0.4 collective-permute-start.7
  47.1 0.0 collective-permute-start.5
  47.1 3.2 %collective-permute-start.6 = (bf16[128,1024]{1,0:T(8,128)(2,1)S(1)}, bf16[128,1024]{1,0:T(8,128)(2,1)S(1)}, u32[]{:S(2)}, u32[]{:S(2)}) collective-permute-start(bf16[128,1024]{1,0:T(8,128)(2,1)S(1)} %get-tuple-element.40), channel_id=1, source_target_pairs={{0,6},{2,4},{4,2},{6,0},{8,14},{10,12},{12,10},{14,8},{1,7},{3,5},... | collective-permute-start | bytes 786440 | tf_op jit(solution)/shard_map/ppermute | solution.py:339
  50.3 0.0 copy-done.1
  50.3 0.7 %copy-done.9 = f32[64]{0:T(128)S(1)} copy-done((f32[64]{0:T(128)S(1)}, f32[64]{0:T(128)}, u32[]{:S(2)}) %copy-start.9) | copy-done | bytes 280
  50.9 1.5 %shard_map.135 = (f32[128,1024]{1,0:T(8,128)S(1)}, f32[128,1024]{1,0:T(8,128)S(1)}, bf16[128,128]{1,0:T(8,128)(2,1)S(1)}) custom-call(s32[2]{0:T(128)S(1)} %pad_add_fusion.info, s32[8]{0:T(128)S(1)} %copy-done.6, bf16[128,1024]{1,0:T(8,128)(2,1)S(1)} %get-tuple-element.42.xc, bf16[128,4096]{1,0:T(8,128)(2,1)S(1)} %copy-done.1, ...), custom_call_target="tpu_custom_call" | custom-call | flops 400000000 | bytes 4194304 | tf_op jit(solution)/shard_map/pallas_call | solution.py:218
  52.4 1.6 %shard_map.136 = (f32[128,1024]{1,0:T(8,128)S(1)}, f32[128,1024]{1,0:T(8,128)S(1)}, bf16[128,128]{1,0:T(8,128)(2,1)}) custom-call(s32[2]{0:T(128)S(1)} %pad_add_fusion.info, s32[8]{0:T(128)S(1)} %copy-done.6, bf16[128,1024]{1,0:T(8,128)(2,1)S(1)} %get-tuple-element.44.xc, bf16[128,4096]{1,0:T(8,128)(2,1)S(1)} %copy-done.1, bf16[128,512]{1,0:T(8,128)(2,1)S(1)} %bitcast.23, ...), custom_call_target="tpu_custom_call" | custom-call | flops 400000000 | bytes 4194304 | tf_op jit(solution)/shard_map/pallas_call | solution.py:218
  54.0 1.6 %shard_map.130 = (f32[128,1024]{1,0:T(8,128)S(1)}, f32[128,1024]{1,0:T(8,128)S(1)}, bf16[128,128]{1,0:T(8,128)(2,1)}) custom-call(s32[2]{0:T(128)S(1)} %pad_add_fusion.info, s32[8]{0:T(128)S(1)} %copy-done.6, bf16[128,1024]{1,0:T(8,128)(2,1)S(1)} %get-tuple-element.30.xc, bf16[128,4096]{1,0:T(8,128)(2,1)S(1)} %copy-done.1, bf16[128,512]{1,0:T(8,128)(2,1)S(1)} %bitcast.25, ...), custom_call_target="tpu_custom_call" | custom-call | flops 400000000 | bytes 4194304 | tf_op jit(solution)/shard_map/pallas_call | solution.py:218
  55.6 1.5 %shard_map.128 = (f32[128,1024]{1,0:T(8,128)S(1)}, f32[128,1024]{1,0:T(8,128)S(1)}, bf16[128,128]{1,0:T(8,128)(2,1)S(1)}) custom-call(s32[2]{0:T(128)S(1)} %pad_add_fusion.info, s32[8]{0:T(128)S(1)} %copy-done.6, bf16[128,1024]{1,0:T(8,128)(2,1)S(1)} %get-tuple-element.28.xc, bf16[128,4096]{1,0:T(8,128)(2,1)S(1)} %copy-done.1, ...), custom_call_target="tpu_custom_call" | custom-call | flops 400000000 | bytes 4194304 | tf_op jit(solution)/shard_map/pallas_call | solution.py:218
  57.1 0.0 collective-permute-done.7.e1
  57.1 0.0 copy-done.5
  57.1 1.8 %shard_map.137.rest_0_ = bf16[128,4096]{1,0:T(8,128)(2,1)} custom-call(s32[2]{0:T(128)S(1)} %pad_add_fusion.info, f32[128,1024]{1,0:T(8,128)S(1)} %get-tuple-element.43.near0, f32[128,1024]{1,0:T(8,128)S(1)} %get-tuple-element.45.near1, f32[128,1024]{1,0:T(8,128)S(1)} %get-tuple-element.46.gain0, f32[128,1024]{1,0:T(8,128)S(1)} %get-tuple-element.47.gain1, ...), custom_call_target="tpu_custom_call" | custom-call | flops 200000000 | bytes 4194304 | tf_op jit(solution)/shard_map/pallas_call | solution.py:218
  58.9 0.0 collective-permute-done.5.e0
  58.9 2.9 %collective-permute-done.6.e1 = bf16[128,1024]{1,0:T(8,128)(2,1)S(1)} collective-permute-done((bf16[128,1024]{1,0:T(8,128)(2,1)S(1)}, bf16[128,1024]{1,0:T(8,128)(2,1)S(1)}, u32[]{:S(2)}, u32[]{:S(2)}) %collective-permute-start.6) | collective-permute-done | bytes 262176 | tf_op jit(solution)/shard_map/ppermute | solution.py:339
  61.8 1.8 %shard_map.138 = bf16[128,4096]{1,0:T(8,128)(2,1)} custom-call(s32[2]{0:T(128)S(1)} %pad_add_fusion.info, f32[128,1024]{1,0:T(8,128)S(1)} %get-tuple-element.29.near0, f32[128,1024]{1,0:T(8,128)S(1)} %get-tuple-element.31.near1, f32[128,1024]{1,0:T(8,128)S(1)} %get-tuple-element.32.gain0, ...), custom_call_target="tpu_custom_call", output_to_operand_aliasing={{}: (9, {})} | custom-call | flops 200000000 | bytes 4194304 | tf_op jit(solution)/shard_map/pallas_call | solution.py:218
  (16 shorter events, 0.1 us)
Async XLA Ops:
  0.0 0.9 %slice-start = ((bf16[128,4096]{1,0:T(8,128)(2,1)}), bf16[16,4096]{1,0:T(8,128)(2,1)S(1)}, s32[]{:S(2)}) async-start(bf16[128,4096]{1,0:T(8,128)(2,1)} %x.7), calls=%async_computation | async-start | bytes 262144 | tf_op jit(solution)/shard_map/slice | solution.py:267
  0.0 0.8 %slice-start.1 = ((bf16[128,2,256]{2,1,0:T(2,128)(2,1)}), bf16[16,2,256]{2,1,0:T(2,128)(2,1)S(1)}, s32[]{:S(2)}) async-start(bf16[128,2,256]{2,1,0:T(2,128)(2,1)} %param.15), calls=%async_computation.1 | async-start | bytes 32768 | tf_op jit(solution)/shard_map/slice | solution.py:267
  0.9 3.0 %copy-start.10 = (bf16[128,2,256]{2,1,0:T(2,128)(2,1)S(1)}, bf16[128,2,256]{2,1,0:T(2,128)(2,1)}, u32[]{:S(2)}) copy-start(bf16[128,2,256]{2,1,0:T(2,128)(2,1)} %param.15) | copy-start | bytes 393220
  0.9 9.9 %collective-permute-start = (bf16[16,4608]{1,0:T(8,128)(2,1)S(1)}, bf16[16,4608]{1,0:T(8,128)(2,1)S(1)}, u32[]{:S(2)}, u32[]{:S(2)}) collective-permute-start(bf16[16,4608]{1,0:T(8,128)(2,1)S(1)} %pad_maximum_fusion), channel_id=1, source_target_pairs={{0,2},{2,4},{4,6},{6,8},{8,10},{10,12},{12,14},{14,0},{1,3},{3,5},... | collective-permute-start | bytes 442376 | tf_op jit(solution)/shard_map/ppermute | solution.py:268
  3.9 0.7 %copy-start.11 = (bf16[4,2,256]{2,1,0:T(2,128)(2,1)S(1)}, bf16[4,2,256]{2,1,0:T(2,128)(2,1)}, u32[]{:S(2)}) copy-start(bf16[4,2,256]{2,1,0:T(2,128)(2,1)} %param.18) | copy-start | bytes 12292
  3.9 6.9 %copy-start.3 = (bf16[4,4096]{1,0:T(4,128)(2,1)S(1)}, bf16[4,4096]{1,0:T(4,128)(2,1)}, u32[]{:S(2)}) copy-start(bf16[4,4096]{1,0:T(4,128)(2,1)} %wx.7) | copy-start | bytes 98308
  4.0 0.7 %copy-start.12 = (f32[2,256]{1,0:T(2,128)S(1)}, f32[2,256]{1,0:T(2,128)}, u32[]{:S(2)}) copy-start(f32[2,256]{1,0:T(2,128)} %param.19) | copy-start | bytes 6148
  4.6 6.2 %copy-start.4 = (f32[4096]{0:T(1024)S(1)}, f32[4096]{0:T(1024)}, u32[]{:S(2)}) copy-start(f32[4096]{0:T(1024)} %param.17) | copy-start | bytes 49156
  4.6 6.2 %copy-start.2 = (bf16[128,64]{0,1:T(8,128)(2,1)S(1)}, bf16[128,64]{0,1:T(8,128)(2,1)}, u32[]{:S(2)}) copy-start(bf16[128,64]{0,1:T(8,128)(2,1)} %param.20) | copy-start | bytes 49156
  10.8 0.7 %copy-start.6 = (s32[8]{0:T(128)S(1)}, s32[8]{0:T(128)}, u32[]{:S(2)}) copy-start(s32[8]{0:T(128)} %lens.15) | copy-start | bytes 100
  10.8 0.7 %copy-start.7 = (f32[64]{0:T(128)S(1)}, f32[64]{0:T(128)}, u32[]{:S(2)}) copy-start(f32[64]{0:T(128)} %param.21) | copy-start | bytes 772
  10.8 0.7 %copy-start.8 = (f32[64]{0:T(128)S(1)}, f32[64]{0:T(128)}, u32[]{:S(2)}) copy-start(f32[64]{0:T(128)} %param.22) | copy-start | bytes 772
  11.5 1.2 %copy-start = (bf16[128,4096]{1,0:T(8,128)(2,1)S(1)}, bf16[128,4096]{1,0:T(8,128)(2,1)}, u32[]{:S(2)}) copy-start(bf16[128,4096]{1,0:T(8,128)(2,1)} %x.7) | copy-start | bytes 3145732
  14.3 8.4 %collective-permute-start.1 = (bf16[144,1024]{1,0:T(8,128)(2,1)S(1)}, bf16[144,1024]{1,0:T(8,128)(2,1)S(1)}, u32[]{:S(2)}, u32[]{:S(2)}) collective-permute-start(bf16[144,1024]{1,0:T(8,128)(2,1)S(1)} %get-tuple-element.35), channel_id=1, source_target_pairs={{0,2},{2,0},{4,6},{6,4},{8,10},{10,8},{12,14},{14,12},{1,3},{3,1},... | collective-permute-start | bytes 884744 | tf_op jit(solution)/shard_map/ppermute | solution.py:339
  16.0 10.0 %collective-permute-start.2 = (bf16[144,1024]{1,0:T(8,128)(2,1)S(1)}, bf16[144,1024]{1,0:T(8,128)(2,1)S(1)}, u32[]{:S(2)}, u32[]{:S(2)}) collective-permute-start(bf16[144,1024]{1,0:T(8,128)(2,1)S(1)} %get-tuple-element.36), channel_id=1, source_target_pairs={{0,4},{2,6},{4,0},{6,2},{8,12},{10,14},{12,8},{14,10},{1,5},{3,7},... | collective-permute-start | bytes 884744 | tf_op jit(solution)/shard_map/ppermute | solution.py:339
  17.9 13.9 %collective-permute-start.3 = (bf16[144,1024]{1,0:T(8,128)(2,1)S(1)}, bf16[144,1024]{1,0:T(8,128)(2,1)S(1)}, u32[]{:S(2)}, u32[]{:S(2)}) collective-permute-start(bf16[144,1024]{1,0:T(8,128)(2,1)S(1)} %get-tuple-element.37), channel_id=1, source_target_pairs={{0,6},{2,4},{4,2},{6,0},{8,14},{10,12},{12,10},{14,8},{1,7},{3,5},... | collective-permute-start | bytes 884744 | tf_op jit(solution)/shard_map/ppermute | solution.py:339
  31.7 18.6 %copy-start.1 = (bf16[128,4096]{1,0:T(8,128)(2,1)S(1)}, bf16[128,4096]{1,0:T(8,128)(2,1)}, u32[]{:S(2)}) copy-start(bf16[128,4096]{1,0:T(8,128)(2,1)} %z.7) | copy-start | bytes 3145732
  33.1 12.8 %collective-permute-start.4 = (bf16[128,1024]{1,0:T(8,128)(2,1)S(1)}, bf16[128,1024]{1,0:T(8,128)(2,1)S(1)}, u32[]{:S(2)}, u32[]{:S(2)}) collective-permute-start(bf16[128,1024]{1,0:T(8,128)(2,1)S(1)} %get-tuple-element.38), channel_id=1, source_target_pairs={{0,8},{2,10},{4,12},{6,14},{8,0},{10,2},{12,4},{14,6},{1,9},{3,11}... | collective-permute-start | bytes 786440 | tf_op jit(solution)/shard_map/ppermute | solution.py:342
  46.7 10.4 %collective-permute-start.7 = (bf16[128,1024]{1,0:T(8,128)(2,1)S(1)}, bf16[128,1024]{1,0:T(8,128)(2,1)S(1)}, u32[]{:S(2)}, u32[]{:S(2)}) collective-permute-start(bf16[128,1024]{1,0:T(8,128)(2,1)S(1)} %get-tuple-element.49), channel_id=1, source_target_pairs={{0,2},{2,0},{4,6},{6,4},{8,10},{10,8},{12,14},{14,12},{1,3},{3,1},... | collective-permute-start | bytes 786440 | tf_op jit(solution)/shard_map/ppermute | solution.py:339
  47.1 11.8 %collective-permute-start.5 = (bf16[128,1024]{1,0:T(8,128)(2,1)S(1)}, bf16[128,1024]{1,0:T(8,128)(2,1)S(1)}, u32[]{:S(2)}, u32[]{:S(2)}) collective-permute-start(bf16[128,1024]{1,0:T(8,128)(2,1)S(1)} %get-tuple-element.39), channel_id=1, source_target_pairs={{0,4},{2,6},{4,0},{6,2},{8,12},{10,14},{12,8},{14,10},{1,5},{3,7},... | collective-permute-start | bytes 786440 | tf_op jit(solution)/shard_map/ppermute | solution.py:339
  47.1 14.7 %collective-permute-start.6 = (bf16[128,1024]{1,0:T(8,128)(2,1)S(1)}, bf16[128,1024]{1,0:T(8,128)(2,1)S(1)}, u32[]{:S(2)}, u32[]{:S(2)}) collective-permute-start(bf16[128,1024]{1,0:T(8,128)(2,1)S(1)} %get-tuple-element.40), channel_id=1, source_target_pairs={{0,6},{2,4},{4,2},{6,0},{8,14},{10,12},{12,10},{14,8},{1,7},{3,5},... | collective-permute-start | bytes 786440 | tf_op jit(solution)/shard_map/ppermute | solution.py:339
  50.3 0.7 %copy-start.9 = (f32[64]{0:T(128)S(1)}, f32[64]{0:T(128)}, u32[]{:S(2)}) copy-start(f32[64]{0:T(128)} %param.23) | copy-start | bytes 772
  55.6 1.5 %copy-start.5 = (f32[4096]{0:T(1024)S(1)}, f32[4096]{0:T(1024)}, u32[]{:S(2)}) copy-start(f32[4096]{0:T(1024)} %param.24) | copy-start | bytes 49156

commit v2 on v1

v2 whole, which is shorter than its diff:
```python
import functools

import jax
import jax.numpy as jnp
from jax import lax
from jax.experimental import pallas as pl
from jax.experimental.pallas import tpu as pltpu
from jax.sharding import PartitionSpec as P

HEAD_DIM = 64
STATE = 128
BLOCK = 128
QUAD = 4
HALO = 16
EXTRA = 16
F32 = jnp.float32
BF16 = jnp.bfloat16


def mm(left, right):
    return jnp.dot(left, right, preferred_element_type=F32)


def ends_of(lens_ref):
    total = 0
    ends = []
    for i in range(lens_ref.shape[0]):
        total = total + lens_ref[i]
        ends.append(total)
    return ends


def seg_of(pos, ends):
    count = 0
    for end in ends:
        count = count + jnp.where(end <= pos, 1, 0)
    return jnp.where(pos >= 0, count, -1)


def tokens(start, shape, dim):
    return start + lax.broadcasted_iota(jnp.int32, shape, dim)


def shift_matrix(start, ends, rows, before, taps):
    shape = (rows, before + rows)
    row = lax.broadcasted_iota(jnp.int32, shape, 0)
    col = lax.broadcasted_iota(jnp.int32, shape, 1)
    same = seg_of(start + row, ends) == seg_of(start - before + col, ends)
    parts = []
    for k in range(taps - 1):
        parts.append(jnp.where((col == row + (before - taps + 1 + k)) & same, 1.0, 0.0))
    return jnp.concatenate(parts, axis=0).astype(BF16)


def conv_half(shift, extended, block, weight, bias):
    rows = block.shape[0]
    taps = weight.shape[0]
    half = weight.astype(F32) * 0.5
    moved = mm(shift, extended)
    total = bias * 0.5 + block.astype(F32) * half[taps - 1 : taps]
    for k in range(taps - 1):
        total = total + moved[k * rows : (k + 1) * rows] * half[k : k + 1]
    return total


def silu_of_half(half):
    return half + half * jnp.tanh(half)


def rates_of(dt_ref, dtb_ref, dec_ref):
    raw = jnp.transpose(dt_ref[...].astype(F32)) + dtb_ref[...]
    rate = jnp.maximum(raw, 0.0) + jnp.log1p(jnp.exp(-jnp.abs(raw)))
    shape = (BLOCK, BLOCK)
    lower = lax.broadcasted_iota(jnp.int32, shape, 0) >= lax.broadcasted_iota(jnp.int32, shape, 1)
    cum = jnp.dot(
        jnp.where(lower, 1.0, 0.0),
        -rate * dec_ref[...],
        precision=lax.Precision.HIGHEST,
        preferred_element_type=F32,
    )
    return rate, cum


def head_map(heads, first, width):
    shape = (heads, width)
    row = lax.broadcasted_iota(jnp.int32, shape, 0)
    col = lax.broadcasted_iota(jnp.int32, shape, 1)
    return jnp.where(row == first + col // HEAD_DIM, 1.0, 0.0).astype(BF16)


def pair_of(value):
    high = value.astype(BF16)
    low = (value - high.astype(F32)).astype(BF16)
    return jnp.concatenate([high, low], axis=1)


def twice(onehot):
    return jnp.concatenate([onehot, onehot], axis=0)


def early_kernel(info, lens, x, bc, wx, bx, wbc, bbc, dt, dtb, dec, xc_out, part, first, carries, factors):
    start = info[0] * BLOCK
    heads = dt.shape[0]
    chan = x.shape[1]
    inner = bc.shape[1] // 2
    groups = inner // STATE
    ends = ends_of(lens)
    shift = shift_matrix(start, ends, BLOCK, 0, wx.shape[0])
    b_in = bc[:, 0:inner]
    bmat = silu_of_half(conv_half(shift, b_in, b_in, wbc[:, 0:inner], bbc[:, 0:inner]))
    bmat = jnp.where(tokens(0, bmat.shape, 0) >= HALO, bmat, 0.0)
    bmat_t = jnp.transpose(bmat).astype(BF16)
    rate, cum = rates_of(dt, dtb, dec)
    last = cum[BLOCK - 1 : BLOCK]
    seg_last = seg_of(start + BLOCK - 1, ends)
    same = seg_of(tokens(start, (BLOCK, heads), 0), ends) == seg_last
    factor = pair_of(jnp.where(same, jnp.exp(last - cum), 0.0) * rate)
    factors[:, 0 : 2 * heads] = pair_of(rate * jnp.exp(-cum))
    factors[:, 2 * heads : 4 * heads] = pair_of(jnp.exp(cum))
    live = seg_last == seg_of(start - 1, ends)
    carry = pair_of(jnp.where(live, jnp.exp(last), 0.0)).astype(F32)
    row = lax.broadcasted_iota(jnp.int32, (EXTRA, heads), 0)
    rows = jnp.where(row == 0, carry[:, 0:heads], jnp.where(row == 1, carry[:, heads:], 0.0)).astype(BF16)
    step = 1024
    for at in range(0, chan, step):
        lane = slice(at, at + step)
        g = at // (chan // groups)
        xs = x[:, lane]
        xc = silu_of_half(conv_half(shift, xs, xs, wx[:, lane], bx[:, lane])).astype(BF16)
        xc_out[:, lane] = xc
        onehot = head_map(heads, at // HEAD_DIM, step)
        spread = mm(factor, twice(onehot))
        first[:, lane] = spread[0:HALO]
        carries[:, lane] = mm(rows, onehot).astype(BF16)
        part[:, lane] = mm(bmat_t[g * STATE : (g + 1) * STATE], (xc.astype(F32) * spread).astype(BF16))


def late_kernel(g, info, lens, x, bc, halo, wx, bx, wbc, bbc, part, first, carries, m0, m1, m2, m3, xc_out):
    start = info[0] * BLOCK
    mine = info[1]
    chan = x.shape[1]
    groups = bc.shape[1] // 2 // STATE
    wide = chan // groups
    width = wide // QUAD
    ends = ends_of(lens)
    shift = shift_matrix(start, ends, HALO, HALO, wx.shape[0])
    lane = slice(g * STATE, (g + 1) * STATE)
    top = bc[0:HALO, lane]
    ext = jnp.concatenate([halo[:, chan + g * STATE : chan + (g + 1) * STATE], top], axis=0)
    bmat = silu_of_half(conv_half(shift, ext, top, wbc[:, lane], bbc[:, lane])).astype(BF16)
    for k, msg in enumerate((m0, m1, m2, m3)):
        inside = pl.multiple_of((mine ^ k) * width, width)
        at = pl.ds(pl.multiple_of(g * wide + inside, width), width)
        top = x[0:HALO, at]
        ext = jnp.concatenate([halo[:, at], top], axis=0)
        xc = silu_of_half(conv_half(shift, ext, top, wx[:, at], bx[:, at])).astype(BF16)
        xc_out[:, pl.ds(inside, width)] = xc
        scaled = (xc.astype(F32) * first[:, at]).astype(BF16)
        add = lax.dot_general(bmat, scaled, (((0,), (0,)), ((), ())), preferred_element_type=F32)
        msg[0:STATE, :] = (part[:, at] + add).astype(BF16)
        msg[STATE : STATE + EXTRA, :] = carries[:, at]


def carry_of(msg):
    return msg[STATE : STATE + 1, :].astype(F32) + msg[STATE + 1 : STATE + 2, :].astype(F32)


def fold_kernel(info, m0, m1, m2, m3, total, decay):
    msgs = (m0, m1, m2, m3)
    for mine in range(QUAD):

        @pl.when(info[1] == mine)
        def _():
            block = [msgs[mine ^ b] for b in range(QUAD)]
            state = block[0][0:STATE, :].astype(F32)
            through = carry_of(block[0])
            for b in range(1, QUAD):
                carry = carry_of(block[b])
                state = block[b][0:STATE, :].astype(F32) + carry * state
                through = through * carry
            total[...] = state.astype(BF16)
            decay[...] = jnp.broadcast_to(through, decay.shape)


def enter_kernel(info, start, m0, m1, m2, m3, o0, o1, o2, o3):
    msgs = (m0, m1, m2, m3)
    outs = (o0, o1, o2, o3)
    for mine in range(QUAD):

        @pl.when(info[1] == mine)
        def _():
            outs[mine][...] = start[...]
            state = start[...].astype(F32)
            for b in range(1, QUAD):
                prev = msgs[mine ^ (b - 1)]
                state = prev[0:STATE, :].astype(F32) + carry_of(prev) * state
                outs[mine ^ b][...] = state.astype(BF16)


def inner_kernel(g, info, lens, xc_in, xc_top, z, bc, halo, wbc, bbc, factors, skip, near, gain, c_out):
    start = info[0] * BLOCK
    chan = xc_in.shape[1]
    inner = bc.shape[1] // 2
    groups = inner // STATE
    wide = chan // groups
    heads = skip.shape[1]
    ends = ends_of(lens)
    shift = shift_matrix(start, ends, BLOCK, HALO, wbc.shape[0])

    def conv(base):
        lane = slice(base, base + STATE)
        block = bc[:, lane]
        ext = jnp.concatenate([halo[:, chan + base : chan + base + STATE], block], axis=0)
        return silu_of_half(conv_half(shift, ext, block, wbc[:, lane], bbc[:, lane])).astype(BF16)

    bmat = conv(g * STATE)
    cmat = conv(inner + g * STATE)
    c_out[...] = cmat
    shape = (BLOCK, BLOCK)
    row = lax.broadcasted_iota(jnp.int32, shape, 0)
    col = lax.broadcasted_iota(jnp.int32, shape, 1)
    mask = (row >= col) & (seg_of(start + row, ends) == seg_of(start + col, ends))
    scores = lax.dot_general(cmat, bmat, (((1,), (1,)), ((), ())), preferred_element_type=F32)
    scores = jnp.where(mask, scores, 0.0).astype(BF16)
    skips = pair_of(jnp.broadcast_to(skip[...], (8, heads)))
    step = 1024
    live = seg_of(tokens(start, (BLOCK, step), 0), ends) == seg_of(start - 1, ends)
    for at in range(0, wide, step):
        lane = slice(at, at + step)
        deep = slice(g * wide + at, g * wide + at + step)
        onehot2 = twice(head_map(heads, (g * wide + at) // HEAD_DIM, step))
        xf = jnp.concatenate([xc_top[:, lane], xc_in[HALO:, deep]], axis=0).astype(F32)
        scaled = (xf * mm(factors[:, 0 : 2 * heads], onehot2)).astype(BF16)
        grown = mm(factors[:, 2 * heads : 4 * heads], onehot2)
        skip_c = mm(skips, onehot2)[0:1]
        gate = silu_of_half(z[:, deep].astype(F32) * 0.5)
        near[:, lane] = (mm(scores, scaled) * grown + skip_c * xf) * gate
        gain[:, lane] = jnp.where(live, grown * gate, 0.0)


def finish_kernel(g, info, near, gain, e0, e1, e2, e3, cmat, scale, *rest):
    out, held, sem = rest[-3:]
    mine = info[1]
    wide = near.shape[1]
    width = wide // QUAD
    c = cmat[...]
    values = []
    square = 0.0
    for k, e in enumerate((e0, e1, e2, e3)):
        at = pl.ds(pl.multiple_of((mine ^ k) * width, width), width)
        value = near[:, at] + gain[:, at] * mm(c, e[...])
        square = square + jnp.sum(value * value, axis=1, keepdims=True)
        values.append((at, value))
    inv = lax.rsqrt(square * (1.0 / wide) + 1e-05)
    for k, (at, value) in enumerate(values):
        deep = pl.ds(pl.multiple_of(g * wide + (mine ^ k) * width, width), width)
        held[:, at] = (value * inv * scale[:, deep]).astype(BF16)
    copy = pltpu.make_async_copy(held, out.at[:, g * wide : (g + 1) * wide], sem)
    copy.start()
    copy.wait()


SMEM = pl.BlockSpec(memory_space=pltpu.SMEM)
VMEM = pl.BlockSpec(memory_space=pltpu.VMEM)
ANY = pl.BlockSpec(memory_space=pl.ANY)


def call(kernel, scalars, args, outs, flops, **more):
    return pl.pallas_call(
        kernel,
        in_specs=[SMEM] * len(scalars) + more.pop("specs", [VMEM] * len(args)),
        out_specs=more.pop("out_specs", [VMEM] * len(outs)),
        out_shape=[jax.ShapeDtypeStruct(*out) for out in outs],
        cost_estimate=pl.CostEstimate(flops=flops, bytes_accessed=4 << 20, transcendentals=0),
        compiler_params=pltpu.CompilerParams(vmem_limit_bytes=32 << 20),
        **more,
    )(*scalars, *args)


def tie(first, second):
    return lax.optimization_barrier((first, second))


def shards(
    x_in,
    z_in,
    bc_in,
    conv_x_weight,
    conv_x_bias,
    conv_bc_weight,
    conv_bc_bias,
    dt_raw,
    dt_bias,
    decay,
    skip_d,
    norm_gain,
    lengths,
):
    rows, chan = x_in.shape
    heads = dt_raw.shape[1]
    peers = lax.axis_size("seq")
    shard = lax.axis_index("seq").astype(jnp.int32)
    taps = conv_x_weight.shape[0]
    bcw = bc_in.shape[2]
    groups = bcw // STATE
    wide = chan // groups
    width = wide // QUAD
    reach = peers // 2 // QUAD

    bc = bc_in.reshape(rows, 2 * bcw)
    wbc = conv_bc_weight.reshape(taps, 2 * bcw)
    bbc = conv_bc_bias.reshape(1, 2 * bcw)
    bx = conv_x_bias.reshape(1, chan)
    scale = norm_gain.reshape(1, chan)
    info = jnp.stack([shard, shard % QUAD])
    both = (info, lengths)

    halo = jnp.concatenate([x_in[rows - HALO :], bc[rows - HALO :]], axis=1)
    halo = lax.ppermute(halo, "seq", [(i, (i + 1) % peers) for i in range(peers)])

    def swap(values):
        routes = [[(i, i ^ k) for i in range(peers)] for k in range(QUAD)]
        swapped = {k: lax.ppermute(values[k], "seq", routes[k]) for k in (3, 1, 2)}
        return [values[0], swapped[1], swapped[2], swapped[3]]

    def ahead(value):
        return lax.ppermute(value, "seq", [(i, (i + QUAD) % peers) for i in range(peers)])

    convs = [conv_x_weight, bx, wbc, bbc]
    xc, part, first, carries, factors = call(
        early_kernel,
        both,
        [x_in, bc, *convs, dt_raw.T, dt_bias.reshape(1, heads), decay.reshape(1, heads)],
        [
            ((rows, chan), BF16),
            ((STATE, chan), F32),
            ((HALO, chan), F32),
            ((EXTRA, chan), BF16),
            ((rows, 4 * heads), BF16),
        ],
        600_000_000,
    )
    msgs, tops = [], []
    for g in range(groups):
        *sent, top = call(
            functools.partial(late_kernel, g),
            both,
            [x_in, bc, halo, *convs, part, first, carries],
            [((STATE + EXTRA, width), BF16)] * QUAD + [((HALO, wide), BF16)],
            20_000_000,
        )
        msgs.append(swap(sent))
        tops.append(top)

    local = []
    for g in range(groups):
        args = [xc, tops[g], z_in, bc, halo, wbc, bbc, factors, skip_d.reshape(1, heads)]
        outs = [((rows, wide), F32), ((rows, wide), F32), ((rows, STATE), BF16)]
        local.append(list(call(functools.partial(inner_kernel, g), both, args, outs, 300_000_000)))
        msgs[g][0], local[g][0] = tie(msgs[g][0], local[g][0])

    entering = []
    for g in range(groups):
        total, through = call(
            fold_kernel, (info,), msgs[g], [((STATE, width), BF16), ((8, width), F32)], 1_000_000
        )
        state = ahead(total)
        for _ in range(reach - 1):
            state = ahead((total.astype(F32) + through[0:1] * state.astype(F32)).astype(BF16))
        entering.append(state)

    blocks = []
    for g in range(groups):
        outs = [((STATE, width), BF16)] * QUAD
        blocks.append(swap(call(enter_kernel, (info,), [entering[g], *msgs[g]], outs, 1_000_000)))

    out = None
    for g in range(groups):
        near, gain, cmat = local[g]
        args = [near, gain, *blocks[g], cmat, scale]
        specs = [VMEM] * len(args)
        aliases = {}
        if out is not None:
            aliases = {1 + len(args): 0}
            args.append(out)
            specs.append(ANY)
        (out,) = call(
            functools.partial(finish_kernel, g),
            (info,),
            args,
            [((rows, chan), BF16)],
            100_000_000,
            specs=specs,
            out_specs=[ANY],
            scratch_shapes=[pltpu.VMEM((rows, wide), BF16), pltpu.SemaphoreType.DMA],
            input_output_aliases=aliases,
        )
    return out


def solution(mesh):
    return jax.shard_map(
        shards,
        mesh=mesh,
        in_specs=(
            P(("groups", "seq"), "heads"),
            P(("groups", "seq"), "heads"),
            P(("groups", "seq"), None, "heads"),
            P(None, "heads"),
            P("heads"),
            P(None, None, "heads"),
            P(None, "heads"),
            P(("groups", "seq"), "heads"),
            P("heads"),
            P("heads"),
            P("heads"),
            P("heads"),
            P("groups"),
        ),
        out_specs=P(("groups", "seq"), "heads"),
        check_vma=False,
    )
```

time: 63.9 us -> 56.1 us (0.88)
  waiting for transfers between devices: 30.4 us -> 4.4 us
  starting transfers between devices: 10.6 us -> 25 us
  local copies, waits for them, and re-layouts: 4.16 us -> 9.34 us
  Pallas kernels: 18.2 us -> 16.5 us
    ppermute x7 -> x13, waiting for transfers between devices: 18 us -> 4.39 us  [the longest x12 4.39 us: swap(): swapped = {k: lax.ppermute(values[k], 'seq', routes[k]) for k in (3, 1, 2)}]
    ppermute x1 -> x2, waiting for transfers between devices: 12.5 us -> 0.01 us  [ahead(): lax.ppermute(value, 'seq', [(i, (i + QUAD) % peers) for i in range(peers)])]
    ppermute x7 -> x13, starting transfers between devices: 10.2 us -> 19.5 us  [the longest x12 16.4 us: swap(): swapped = {k: lax.ppermute(values[k], 'seq', routes[k]) for k in (3, 1, 2)}]
    ppermute x1 -> x2, starting transfers between devices: 0.35 us -> 5.58 us  [ahead(): lax.ppermute(value, 'seq', [(i, (i + QUAD) % peers) for i in range(peers)])]
    unnamed x30 -> x24, local copies, waits for them, and re-layouts: 3.26 us -> 7.69 us
    pallas_call x12 -> x11, Pallas kernels: 18.2 us -> 16.5 us  [call(): pl.pallas_call(kernel, in_specs=[SMEM] * len(scalars) + more.pop('specs',...]
    slice x4 -> x2, local copies, waits for them, and re-layouts: 0.9 us -> 1.65 us  [shards(): halo = jnp.concatenate([x_in[rows - HALO:], bc[rows - HALO:]], axis=1)]
  transfers between devices with their start and end apart: 8 -> 15, of which waited for: 5 -> 5; matrix products, arithmetic and copies ran while one was open for 0% -> 4% of each run, Pallas kernels for 20% -> 24%
where the time goes in v2:
time: 56.1 us; the launch traced here: 55.6 us
  starting transfers between devices  25 us (45%)
  Pallas kernels  16.5 us (29%)
  local copies, waits for them, and re-layouts  9.34 us (17%)
  waiting for transfers between devices  4.4 us (8%)
    pallas_call x11, Pallas kernels, call(): pl.pallas_call(kernel, in_specs=[SMEM] * len(scalars) + more.pop('specs',...  16.5 us
    ppermute x12, starting transfers between devices, swap(): swapped = {k: lax.ppermute(values[k], 'seq', routes[k]) for k in (3, 1, 2)}  16.4 us
    unnamed x24, local copies, waits for them, and re-layouts  7.69 us
    ppermute x2, starting transfers between devices, ahead(): lax.ppermute(value, 'seq', [(i, (i + QUAD) % peers) for i in range(peers)])  5.58 us
    ppermute x12, waiting for transfers between devices, swap(): swapped = {k: lax.ppermute(values[k], 'seq', routes[k]) for k in (3, 1, 2)}  4.39 us
    ppermute x1, starting transfers between devices, shards(): lax.ppermute(halo, 'seq', [(i, (i + 1) % peers) for i in range(peers)])  3.02 us
    slice x2, local copies, waits for them, and re-layouts, shards(): halo = jnp.concatenate([x_in[rows - HALO:], bc[rows - HALO:]], axis=1)  1.65 us
  transfers between devices with their start and end apart: 15, of which 5 were waited for; matrix products, arithmetic and copies ran while one was open for 4% of the time, Pallas kernels for 24%

profile of v2, /device:TPU:0, one launch (start us, length us, event | category | flops | bytes accessed | tf_op | source)
XLA Modules:
  0.0 55.6 jit_solution(6945955917777718981)
XLA Ops:
  0.0 0.7 %slice.10 = bf16[16,2,256]{2,1,0:T(2,128)(2,1)S(1)} slice(bf16[128,2,256]{2,1,0:T(2,128)(2,1)} %param.15), slice={[112:128], [0:2], [0:256]} | slice | bytes 32768 | tf_op jit(solution)/shard_map/slice | solution.py:318
  0.7 0.9 %slice.9 = bf16[16,4096]{1,0:T(8,128)(2,1)S(1)} slice(bf16[128,4096]{1,0:T(8,128)(2,1)} %x.5), slice={[112:128], [0:4096]} | slice | bytes 262144 | tf_op jit(solution)/shard_map/slice | solution.py:318
  1.7 3.0 %collective-permute-start = (bf16[16,4608]{1,0:T(8,128)(2,1)S(1)}, bf16[16,4608]{1,0:T(8,128)(2,1)S(1)}, u32[]{:S(2)}, u32[]{:S(2)}) collective-permute-start(bf16[16,4608]{1,0:T(8,128)(2,1)S(1)} %pad_maximum_fusion), channel_id=1, source_target_pairs={{0,2},{2,4},{4,6},{6,8},{8,10},{10,12},{12,14},{14,0},{1,3},{3,5},... | collective-permute-start | bytes 442376 | tf_op jit(solution)/shard_map/ppermute | solution.py:319
  4.7 0.7 %copy.18 = f32[1,1,2,256]{3,1,2,0:T(1,128)S(1)} copy(f32[1,1,2,256]{3,2,1,0:T(2,128)} %bitcast.46) | data formatting | bytes 4096
  5.4 0.7 %copy.17 = bf16[1,4,2,256]{3,1,2,0:T(4,128)(2,1)S(1)} copy(bf16[1,4,2,256]{3,2,1,0:T(2,128)(2,1)} %bitcast.45) | data formatting | bytes 8192
  6.1 0.9 %copy.15 = bf16[16,8,2,256]{3,1,2,0:T(8,128)(2,1)S(1)} copy(bf16[16,8,2,256]{3,2,1,0:T(2,128)(2,1)} %bitcast.42) | data formatting | bytes 262144
  7.0 0.1 pad_add_fusion.info
  7.1 1.2 %copy-done = bf16[128,4096]{1,0:T(8,128)(2,1)S(1)} copy-done((bf16[128,4096]{1,0:T(8,128)(2,1)S(1)}, bf16[128,4096]{1,0:T(8,128)(2,1)}, u32[]{:S(2)}) %copy-start) | copy-done | bytes 1048600
  8.3 0.8 %copy-done.2 = bf16[4,4096]{1,0:T(4,128)(2,1)S(1)} copy-done((bf16[4,4096]{1,0:T(4,128)(2,1)S(1)}, bf16[4,4096]{1,0:T(4,128)(2,1)}, u32[]{:S(2)}) %copy-start.2) | copy-done | bytes 32792
  9.1 0.7 %copy-done.3 = f32[4096]{0:T(1024)S(1)} copy-done((f32[4096]{0:T(1024)S(1)}, f32[4096]{0:T(1024)}, u32[]{:S(2)}) %copy-start.3) | copy-done | bytes 16408
  9.8 0.7 %copy-done.5 = s32[8]{0:T(128)S(1)} copy-done((s32[8]{0:T(128)S(1)}, s32[8]{0:T(128)}, u32[]{:S(2)}) %copy-start.5) | copy-done | bytes 56
  10.5 0.7 %copy-done.7 = bf16[128,64]{0,1:T(8,128)(2,1)S(1)} copy-done((bf16[128,64]{0,1:T(8,128)(2,1)S(1)}, bf16[128,64]{0,1:T(8,128)(2,1)}, u32[]{:S(2)}) %copy-start.7) | copy-done | bytes 16408
  11.2 0.7 %copy-done.8 = f32[64]{0:T(128)S(1)} copy-done((f32[64]{0:T(128)S(1)}, f32[64]{0:T(128)}, u32[]{:S(2)}) %copy-start.8) | copy-done | bytes 280
  11.8 0.7 %copy-done.9 = f32[64]{0:T(128)S(1)} copy-done((f32[64]{0:T(128)S(1)}, f32[64]{0:T(128)}, u32[]{:S(2)}) %copy-start.9) | copy-done | bytes 280
  12.5 2.8 %shard_map.127 = (bf16[128,4096]{1,0:T(8,128)(2,1)S(1)}, f32[128,4096]{1,0:T(8,128)S(1)}, f32[16,4096]{1,0:T(8,128)S(1)}, bf16[16,4096]{1,0:T(8,128)(2,1)S(1)}, bf16[128,256]{1,0:T(8,128)(2,1)S(1)}) custom-call(s32[2]{0:T(128)S(1)} %pad_add_fusion.info, s32[8]{0:T(128)S(1)} %copy-done.5, bf16[128,4096]{1,0:T(8,128)(2,1)S(1)} %copy-done, ...), custom_call_target="tpu_custom_call" | custom-call | flops 600000000 | bytes 4194304 | tf_op jit(solution)/shard_map/pallas_call | solution.py:269
  15.3 0.0 collective-permute-done.halo
  15.3 1.5 %shard_map.132 = (bf16[144,512]{1,0:T(8,128)(2,1)S(1)}, bf16[144,512]{1,0:T(8,128)(2,1)S(1)}, bf16[144,512]{1,0:T(8,128)(2,1)S(1)}, bf16[144,512]{1,0:T(8,128)(2,1)S(1)}, bf16[16,2048]{1,0:T(8,128)(2,1)S(1)}) custom-call(s32[2]{0:T(128)S(1)} %pad_add_fusion.info, s32[8]{0:T(128)S(1)} %copy-done.5, bf16[128,4096]{1,0:T(8,128)(2,1)S(1)} %copy-done, ...), custom_call_target="tpu_custom_call" | custom-call | flops 20000000 | bytes 4194304 | tf_op jit(solution)/shard_map/pallas_call | solution.py:269
  16.8 0.0 copy-start.1
  16.8 0.0 copy-start.6
  16.8 1.6 %collective-permute-start.8 = (bf16[144,512]{1,0:T(8,128)(2,1)S(1)}, bf16[144,512]{1,0:T(8,128)(2,1)S(1)}, u32[]{:S(2)}, u32[]{:S(2)}) collective-permute-start(bf16[144,512]{1,0:T(8,128)(2,1)S(1)} %get-tuple-element.66), channel_id=1, source_target_pairs={{0,2},{2,0},{4,6},{6,4},{8,10},{10,8},{12,14},{14,12},{1,3},{3,1},... | collective-permute-start | bytes 442376 | tf_op jit(solution)/shard_map/ppermute | solution.py:323
  18.4 1.6 %collective-permute-start.9 = (bf16[144,512]{1,0:T(8,128)(2,1)S(1)}, bf16[144,512]{1,0:T(8,128)(2,1)S(1)}, u32[]{:S(2)}, u32[]{:S(2)}) collective-permute-start(bf16[144,512]{1,0:T(8,128)(2,1)S(1)} %get-tuple-element.67), channel_id=1, source_target_pairs={{0,4},{2,6},{4,0},{6,2},{8,12},{10,14},{12,8},{14,10},{1,5},{3,7},... | collective-permute-start | bytes 442376 | tf_op jit(solution)/shard_map/ppermute | solution.py:323
  20.0 0.4 collective-permute-start.10
  20.4 1.5 %shard_map.128 = (bf16[144,512]{1,0:T(8,128)(2,1)S(1)}, bf16[144,512]{1,0:T(8,128)(2,1)S(1)}, bf16[144,512]{1,0:T(8,128)(2,1)S(1)}, bf16[144,512]{1,0:T(8,128)(2,1)S(1)}, bf16[16,2048]{1,0:T(8,128)(2,1)S(1)}) custom-call(s32[2]{0:T(128)S(1)} %pad_add_fusion.info, s32[8]{0:T(128)S(1)} %copy-done.5, bf16[128,4096]{1,0:T(8,128)(2,1)S(1)} %copy-done, ...), custom_call_target="tpu_custom_call" | custom-call | flops 20000000 | bytes 4194304 | tf_op jit(solution)/shard_map/pallas_call | solution.py:269
  21.8 1.6 %collective-permute-start.1 = (bf16[144,512]{1,0:T(8,128)(2,1)S(1)}, bf16[144,512]{1,0:T(8,128)(2,1)S(1)}, u32[]{:S(2)}, u32[]{:S(2)}) collective-permute-start(bf16[144,512]{1,0:T(8,128)(2,1)S(1)} %get-tuple-element.51), channel_id=1, source_target_pairs={{0,2},{2,0},{4,6},{6,4},{8,10},{10,8},{12,14},{14,12},{1,3},{3,1},... | collective-permute-start | bytes 442376 | tf_op jit(solution)/shard_map/ppermute | solution.py:323
  23.4 1.6 %collective-permute-start.2 = (bf16[144,512]{1,0:T(8,128)(2,1)S(1)}, bf16[144,512]{1,0:T(8,128)(2,1)S(1)}, u32[]{:S(2)}, u32[]{:S(2)}) collective-permute-start(bf16[144,512]{1,0:T(8,128)(2,1)S(1)} %get-tuple-element.52), channel_id=1, source_target_pairs={{0,4},{2,6},{4,0},{6,2},{8,12},{10,14},{12,8},{14,10},{1,5},{3,7},... | collective-permute-start | bytes 442376 | tf_op jit(solution)/shard_map/ppermute | solution.py:323
  25.0 0.4 collective-permute-start.3
  25.4 1.6 %shard_map.133 = (f32[128,2048]{1,0:T(8,128)S(1)}, f32[128,2048]{1,0:T(8,128)S(1)}, bf16[128,128]{1,0:T(8,128)(2,1)S(1)}) custom-call(s32[2]{0:T(128)S(1)} %pad_add_fusion.info, s32[8]{0:T(128)S(1)} %copy-done.5, bf16[128,4096]{1,0:T(8,128)(2,1)S(1)} %get-tuple-element.44.xc_in, bf16[16,2048]{1,0:T(8,128)(2,1)S(1)} %get-tuple-element.61.xc_top, ...), custom_call_target="tpu_custom_call" | custom-call | flops 300000000 | bytes 4194304 | tf_op jit(solution)/shard_map/pallas_call | solution.py:269
  27.0 0.7 %collective-permute-done.10.m3 = bf16[144,512]{1,0:T(8,128)(2,1)S(1)} collective-permute-done((bf16[144,512]{1,0:T(8,128)(2,1)S(1)}, bf16[144,512]{1,0:T(8,128)(2,1)S(1)}, u32[]{:S(2)}, u32[]{:S(2)}) %collective-permute-start.10) | collective-permute-done | bytes 147488 | tf_op jit(solution)/shard_map/ppermute | solution.py:323
  27.8 1.3 %shard_map.134 = (bf16[128,512]{1,0:T(8,128)(2,1)S(1)}, f32[8,512]{1,0:T(8,128)}) custom-call(s32[2]{0:T(128)S(1)} %pad_add_fusion.info, bf16[144,512]{1,0:T(8,128)(2,1)S(1)} %get-tuple-element.65.m0, bf16[144,512]{1,0:T(8,128)(2,1)S(1)} %collective-permute-done.8.m1, bf16[144,512]{1,0:T(8,128)(2,1)S(1)} %collective-permute-done.9.m2, ...), custom_call_target="tpu_custom_call" | custom-call | flops 1000000 | bytes 4194304 | tf_op jit(solution)/shard_map/pallas_call | solution.py:269
  29.0 3.2 %collective-permute-start.11 = (bf16[128,512]{1,0:T(8,128)(2,1)S(1)}, bf16[128,512]{1,0:T(8,128)(2,1)S(1)}, u32[]{:S(2)}, u32[]{:S(2)}) collective-permute-start(bf16[128,512]{1,0:T(8,128)(2,1)S(1)} %get-tuple-element.69), channel_id=1, source_target_pairs={{0,8},{2,10},{4,12},{6,14},{8,0},{10,2},{12,4},{14,6},{1,9},{3,11}... | collective-permute-start | bytes 393224 | tf_op jit(solution)/shard_map/ppermute | solution.py:327
  32.2 1.6 %shard_map.129 = (f32[128,2048]{1,0:T(8,128)S(1)}, f32[128,2048]{1,0:T(8,128)S(1)}, bf16[128,128]{1,0:T(8,128)(2,1)S(1)}) custom-call(s32[2]{0:T(128)S(1)} %pad_add_fusion.info, s32[8]{0:T(128)S(1)} %copy-done.5, bf16[128,4096]{1,0:T(8,128)(2,1)S(1)} %get-tuple-element.44.xc_in, bf16[16,2048]{1,0:T(8,128)(2,1)S(1)} %get-tuple-element.45.xc_top, ...), custom_call_target="tpu_custom_call" | custom-call | flops 300000000 | bytes 4194304 | tf_op jit(solution)/shard_map/pallas_call | solution.py:269
  33.8 0.0 collective-permute-done.1.m1
  33.8 0.6 %collective-permute-done.3.m3 = bf16[144,512]{1,0:T(8,128)(2,1)S(1)} collective-permute-done((bf16[144,512]{1,0:T(8,128)(2,1)S(1)}, bf16[144,512]{1,0:T(8,128)(2,1)S(1)}, u32[]{:S(2)}, u32[]{:S(2)}) %collective-permute-start.3) | collective-permute-done | bytes 147488 | tf_op jit(solution)/shard_map/ppermute | solution.py:323
  34.4 1.3 %shard_map.130 = (bf16[128,512]{1,0:T(8,128)(2,1)S(1)}, f32[8,512]{1,0:T(8,128)}) custom-call(s32[2]{0:T(128)S(1)} %pad_add_fusion.info, bf16[144,512]{1,0:T(8,128)(2,1)S(1)} %get-tuple-element.50.m0, bf16[144,512]{1,0:T(8,128)(2,1)S(1)} %collective-permute-done.1.m1, bf16[144,512]{1,0:T(8,128)(2,1)S(1)} %collective-permute-done.2.m2, ...), custom_call_target="tpu_custom_call" | custom-call | flops 1000000 | bytes 4194304 | tf_op jit(solution)/shard_map/pallas_call | solution.py:269
  35.7 2.4 %collective-permute-start.4 = (bf16[128,512]{1,0:T(8,128)(2,1)S(1)}, bf16[128,512]{1,0:T(8,128)(2,1)S(1)}, u32[]{:S(2)}, u32[]{:S(2)}) collective-permute-start(bf16[128,512]{1,0:T(8,128)(2,1)S(1)} %get-tuple-element.54), channel_id=1, source_target_pairs={{0,8},{2,10},{4,12},{6,14},{8,0},{10,2},{12,4},{14,6},{1,9},{3,11}... | collective-permute-start | bytes 393224 | tf_op jit(solution)/shard_map/ppermute | solution.py:327
  38.1 0.7 %shard_map.135 = (bf16[128,512]{1,0:T(8,128)(2,1)S(1)}, bf16[128,512]{1,0:T(8,128)(2,1)S(1)}, bf16[128,512]{1,0:T(8,128)(2,1)S(1)}, bf16[128,512]{1,0:T(8,128)(2,1)S(1)}) custom-call(s32[2]{0:T(128)S(1)} %pad_add_fusion.info, bf16[128,512]{1,0:T(8,128)(2,1)S(1)} %collective-permute-done.11.start, bf16[144,512]{1,0:T(8,128)(2,1)S(1)} %get-tuple-element.65.m0, ...), custom_call_target="tpu_custom_call" | custom-call | flops 1000000 | bytes 4194304 | tf_op jit(solution)/shard_map/pallas_call | solution.py:269
  38.8 1.6 %collective-permute-start.12 = (bf16[128,512]{1,0:T(8,128)(2,1)S(1)}, bf16[128,512]{1,0:T(8,128)(2,1)S(1)}, u32[]{:S(2)}, u32[]{:S(2)}) collective-permute-start(bf16[128,512]{1,0:T(8,128)(2,1)S(1)} %get-tuple-element.71), channel_id=1, source_target_pairs={{0,2},{2,0},{4,6},{6,4},{8,10},{10,8},{12,14},{14,12},{1,3},{3,1},... | collective-permute-start | bytes 393224 | tf_op jit(solution)/shard_map/ppermute | solution.py:323
  40.4 1.5 %collective-permute-start.13 = (bf16[128,512]{1,0:T(8,128)(2,1)S(1)}, bf16[128,512]{1,0:T(8,128)(2,1)S(1)}, u32[]{:S(2)}, u32[]{:S(2)}) collective-permute-start(bf16[128,512]{1,0:T(8,128)(2,1)S(1)} %get-tuple-element.72), channel_id=1, source_target_pairs={{0,4},{2,6},{4,0},{6,2},{8,12},{10,14},{12,8},{14,10},{1,5},{3,7},... | collective-permute-start | bytes 393224 | tf_op jit(solution)/shard_map/ppermute | solution.py:323
  41.9 1.4 %collective-permute-start.14 = (bf16[128,512]{1,0:T(8,128)(2,1)S(1)}, bf16[128,512]{1,0:T(8,128)(2,1)S(1)}, u32[]{:S(2)}, u32[]{:S(2)}) collective-permute-start(bf16[128,512]{1,0:T(8,128)(2,1)S(1)} %get-tuple-element.73), channel_id=1, source_target_pairs={{0,6},{2,4},{4,2},{6,0},{8,14},{10,12},{12,10},{14,8},{1,7},{3,5},... | collective-permute-start | bytes 393224 | tf_op jit(solution)/shard_map/ppermute | solution.py:323
  43.3 0.7 %shard_map.131 = (bf16[128,512]{1,0:T(8,128)(2,1)S(1)}, bf16[128,512]{1,0:T(8,128)(2,1)S(1)}, bf16[128,512]{1,0:T(8,128)(2,1)S(1)}, bf16[128,512]{1,0:T(8,128)(2,1)S(1)}) custom-call(s32[2]{0:T(128)S(1)} %pad_add_fusion.info, bf16[128,512]{1,0:T(8,128)(2,1)S(1)} %collective-permute-done.4.start, bf16[144,512]{1,0:T(8,128)(2,1)S(1)} %get-tuple-element.50.m0, ...), custom_call_target="tpu_custom_call" | custom-call | flops 1000000 | bytes 4194304 | tf_op jit(solution)/shard_map/pallas_call | solution.py:269
  44.0 1.2 %collective-permute-start.5 = (bf16[128,512]{1,0:T(8,128)(2,1)S(1)}, bf16[128,512]{1,0:T(8,128)(2,1)S(1)}, u32[]{:S(2)}, u32[]{:S(2)}) collective-permute-start(bf16[128,512]{1,0:T(8,128)(2,1)S(1)} %get-tuple-element.56), channel_id=1, source_target_pairs={{0,2},{2,0},{4,6},{6,4},{8,10},{10,8},{12,14},{14,12},{1,3},{3,1},... | collective-permute-start | bytes 393224 | tf_op jit(solution)/shard_map/ppermute | solution.py:323
  45.2 1.4 %collective-permute-start.6 = (bf16[128,512]{1,0:T(8,128)(2,1)S(1)}, bf16[128,512]{1,0:T(8,128)(2,1)S(1)}, u32[]{:S(2)}, u32[]{:S(2)}) collective-permute-start(bf16[128,512]{1,0:T(8,128)(2,1)S(1)} %get-tuple-element.57), channel_id=1, source_target_pairs={{0,4},{2,6},{4,0},{6,2},{8,12},{10,14},{12,8},{14,10},{1,5},{3,7},... | collective-permute-start | bytes 393224 | tf_op jit(solution)/shard_map/ppermute | solution.py:323
  46.6 2.2 %collective-permute-start.7 = (bf16[128,512]{1,0:T(8,128)(2,1)S(1)}, bf16[128,512]{1,0:T(8,128)(2,1)S(1)}, u32[]{:S(2)}, u32[]{:S(2)}) collective-permute-start(bf16[128,512]{1,0:T(8,128)(2,1)S(1)} %get-tuple-element.58), channel_id=1, source_target_pairs={{0,6},{2,4},{4,2},{6,0},{8,14},{10,12},{12,10},{14,8},{1,7},{3,5},... | collective-permute-start | bytes 393224 | tf_op jit(solution)/shard_map/ppermute | solution.py:323
  48.8 1.2 %collective-permute-done.14.e3 = bf16[128,512]{1,0:T(8,128)(2,1)S(1)} collective-permute-done((bf16[128,512]{1,0:T(8,128)(2,1)S(1)}, bf16[128,512]{1,0:T(8,128)(2,1)S(1)}, u32[]{:S(2)}, u32[]{:S(2)}) %collective-permute-start.14) | collective-permute-done | bytes 131104 | tf_op jit(solution)/shard_map/ppermute | solution.py:323
  50.1 1.8 %shard_map.136.rest_0_ = bf16[128,4096]{1,0:T(8,128)(2,1)} custom-call(s32[2]{0:T(128)S(1)} %pad_add_fusion.info, f32[128,2048]{1,0:T(8,128)S(1)} %get-tuple-element.63.near, f32[128,2048]{1,0:T(8,128)S(1)} %get-tuple-element.64.gain, bf16[128,512]{1,0:T(8,128)(2,1)S(1)} %get-tuple-element.70.e0, bf16[128,512]{1,0:T(8,128)(2,1)S(1)} %collective-permute-done.12.e1, ...), custom_call_target="tpu_custom_call" | custom-call | flops 100000000 | bytes 4194304 | tf_op jit(solution)/shard_map/pallas_call | solution.py:269
  52.0 0.1 collective-permute-done.6.e2
  52.1 1.7 %collective-permute-done.7.e3 = bf16[128,512]{1,0:T(8,128)(2,1)S(1)} collective-permute-done((bf16[128,512]{1,0:T(8,128)(2,1)S(1)}, bf16[128,512]{1,0:T(8,128)(2,1)S(1)}, u32[]{:S(2)}, u32[]{:S(2)}) %collective-permute-start.7) | collective-permute-done | bytes 131104 | tf_op jit(solution)/shard_map/ppermute | solution.py:323
  53.8 1.8 %shard_map.137 = bf16[128,4096]{1,0:T(8,128)(2,1)} custom-call(s32[2]{0:T(128)S(1)} %pad_add_fusion.info, f32[128,2048]{1,0:T(8,128)S(1)} %get-tuple-element.48.near, f32[128,2048]{1,0:T(8,128)S(1)} %get-tuple-element.49.gain, bf16[128,512]{1,0:T(8,128)(2,1)S(1)} %get-tuple-element.55.e0, ...), custom_call_target="tpu_custom_call", output_to_operand_aliasing={{}: (9, {})} | custom-call | flops 100000000 | bytes 4194304 | tf_op jit(solution)/shard_map/pallas_call | solution.py:269
  (21 shorter events, 0.1 us)
Async XLA Ops:
  1.7 13.6 %collective-permute-start = (bf16[16,4608]{1,0:T(8,128)(2,1)S(1)}, bf16[16,4608]{1,0:T(8,128)(2,1)S(1)}, u32[]{:S(2)}, u32[]{:S(2)}) collective-permute-start(bf16[16,4608]{1,0:T(8,128)(2,1)S(1)} %pad_maximum_fusion), channel_id=1, source_target_pairs={{0,2},{2,4},{4,6},{6,8},{8,10},{10,12},{12,14},{14,0},{1,3},{3,5},... | collective-permute-start | bytes 442376 | tf_op jit(solution)/shard_map/ppermute | solution.py:319
  7.1 1.2 %copy-start = (bf16[128,4096]{1,0:T(8,128)(2,1)S(1)}, bf16[128,4096]{1,0:T(8,128)(2,1)}, u32[]{:S(2)}) copy-start(bf16[128,4096]{1,0:T(8,128)(2,1)} %x.5) | copy-start | bytes 3145732
  8.3 0.8 %copy-start.2 = (bf16[4,4096]{1,0:T(4,128)(2,1)S(1)}, bf16[4,4096]{1,0:T(4,128)(2,1)}, u32[]{:S(2)}) copy-start(bf16[4,4096]{1,0:T(4,128)(2,1)} %wx.5) | copy-start | bytes 98308
  9.1 0.7 %copy-start.3 = (f32[4096]{0:T(1024)S(1)}, f32[4096]{0:T(1024)}, u32[]{:S(2)}) copy-start(f32[4096]{0:T(1024)} %param.17) | copy-start | bytes 49156
  9.8 0.7 %copy-start.5 = (s32[8]{0:T(128)S(1)}, s32[8]{0:T(128)}, u32[]{:S(2)}) copy-start(s32[8]{0:T(128)} %lens.9) | copy-start | bytes 100
  10.4 0.7 %copy-start.7 = (bf16[128,64]{0,1:T(8,128)(2,1)S(1)}, bf16[128,64]{0,1:T(8,128)(2,1)}, u32[]{:S(2)}) copy-start(bf16[128,64]{0,1:T(8,128)(2,1)} %param.20) | copy-start | bytes 49156
  11.2 0.7 %copy-start.8 = (f32[64]{0:T(128)S(1)}, f32[64]{0:T(128)}, u32[]{:S(2)}) copy-start(f32[64]{0:T(128)} %param.21) | copy-start | bytes 772
  11.8 0.7 %copy-start.9 = (f32[64]{0:T(128)S(1)}, f32[64]{0:T(128)}, u32[]{:S(2)}) copy-start(f32[64]{0:T(128)} %param.22) | copy-start | bytes 772
  16.8 8.6 %copy-start.1 = (bf16[128,4096]{1,0:T(8,128)(2,1)S(1)}, bf16[128,4096]{1,0:T(8,128)(2,1)}, u32[]{:S(2)}) copy-start(bf16[128,4096]{1,0:T(8,128)(2,1)} %z.3) | copy-start | bytes 3145732
  16.8 8.6 %copy-start.6 = (f32[64]{0:T(128)S(1)}, f32[64]{0:T(128)}, u32[]{:S(2)}) copy-start(f32[64]{0:T(128)} %param.23) | copy-start | bytes 772
  16.8 8.2 %collective-permute-start.8 = (bf16[144,512]{1,0:T(8,128)(2,1)S(1)}, bf16[144,512]{1,0:T(8,128)(2,1)S(1)}, u32[]{:S(2)}, u32[]{:S(2)}) collective-permute-start(bf16[144,512]{1,0:T(8,128)(2,1)S(1)} %get-tuple-element.66), channel_id=1, source_target_pairs={{0,2},{2,0},{4,6},{6,4},{8,10},{10,8},{12,14},{14,12},{1,3},{3,1},... | collective-permute-start | bytes 442376 | tf_op jit(solution)/shard_map/ppermute | solution.py:323
  18.4 8.6 %collective-permute-start.9 = (bf16[144,512]{1,0:T(8,128)(2,1)S(1)}, bf16[144,512]{1,0:T(8,128)(2,1)S(1)}, u32[]{:S(2)}, u32[]{:S(2)}) collective-permute-start(bf16[144,512]{1,0:T(8,128)(2,1)S(1)} %get-tuple-element.67), channel_id=1, source_target_pairs={{0,4},{2,6},{4,0},{6,2},{8,12},{10,14},{12,8},{14,10},{1,5},{3,7},... | collective-permute-start | bytes 442376 | tf_op jit(solution)/shard_map/ppermute | solution.py:323
  20.0 7.8 %collective-permute-start.10 = (bf16[144,512]{1,0:T(8,128)(2,1)S(1)}, bf16[144,512]{1,0:T(8,128)(2,1)S(1)}, u32[]{:S(2)}, u32[]{:S(2)}) collective-permute-start(bf16[144,512]{1,0:T(8,128)(2,1)S(1)} %get-tuple-element.68), channel_id=1, source_target_pairs={{0,6},{2,4},{4,2},{6,0},{8,14},{10,12},{12,10},{14,8},{1,7},{3,5},... | collective-permute-start | bytes 442376 | tf_op jit(solution)/shard_map/ppermute | solution.py:323
  21.8 12.0 %collective-permute-start.1 = (bf16[144,512]{1,0:T(8,128)(2,1)S(1)}, bf16[144,512]{1,0:T(8,128)(2,1)S(1)}, u32[]{:S(2)}, u32[]{:S(2)}) collective-permute-start(bf16[144,512]{1,0:T(8,128)(2,1)S(1)} %get-tuple-element.51), channel_id=1, source_target_pairs={{0,2},{2,0},{4,6},{6,4},{8,10},{10,8},{12,14},{14,12},{1,3},{3,1},... | collective-permute-start | bytes 442376 | tf_op jit(solution)/shard_map/ppermute | solution.py:323
  23.4 10.4 %collective-permute-start.2 = (bf16[144,512]{1,0:T(8,128)(2,1)S(1)}, bf16[144,512]{1,0:T(8,128)(2,1)S(1)}, u32[]{:S(2)}, u32[]{:S(2)}) collective-permute-start(bf16[144,512]{1,0:T(8,128)(2,1)S(1)} %get-tuple-element.52), channel_id=1, source_target_pairs={{0,4},{2,6},{4,0},{6,2},{8,12},{10,14},{12,8},{14,10},{1,5},{3,7},... | collective-permute-start | bytes 442376 | tf_op jit(solution)/shard_map/ppermute | solution.py:323
  25.0 9.4 %collective-permute-start.3 = (bf16[144,512]{1,0:T(8,128)(2,1)S(1)}, bf16[144,512]{1,0:T(8,128)(2,1)S(1)}, u32[]{:S(2)}, u32[]{:S(2)}) collective-permute-start(bf16[144,512]{1,0:T(8,128)(2,1)S(1)} %get-tuple-element.53), channel_id=1, source_target_pairs={{0,6},{2,4},{4,2},{6,0},{8,14},{10,12},{12,10},{14,8},{1,7},{3,5},... | collective-permute-start | bytes 442376 | tf_op jit(solution)/shard_map/ppermute | solution.py:323
  29.0 9.1 %collective-permute-start.11 = (bf16[128,512]{1,0:T(8,128)(2,1)S(1)}, bf16[128,512]{1,0:T(8,128)(2,1)S(1)}, u32[]{:S(2)}, u32[]{:S(2)}) collective-permute-start(bf16[128,512]{1,0:T(8,128)(2,1)S(1)} %get-tuple-element.69), channel_id=1, source_target_pairs={{0,8},{2,10},{4,12},{6,14},{8,0},{10,2},{12,4},{14,6},{1,9},{3,11}... | collective-permute-start | bytes 393224 | tf_op jit(solution)/shard_map/ppermute | solution.py:327
  32.2 17.9 %copy-start.4 = (f32[4096]{0:T(1024)S(1)}, f32[4096]{0:T(1024)}, u32[]{:S(2)}) copy-start(f32[4096]{0:T(1024)} %param.24) | copy-start | bytes 49156
  35.7 7.6 %collective-permute-start.4 = (bf16[128,512]{1,0:T(8,128)(2,1)S(1)}, bf16[128,512]{1,0:T(8,128)(2,1)S(1)}, u32[]{:S(2)}, u32[]{:S(2)}) collective-permute-start(bf16[128,512]{1,0:T(8,128)(2,1)S(1)} %get-tuple-element.54), channel_id=1, source_target_pairs={{0,8},{2,10},{4,12},{6,14},{8,0},{10,2},{12,4},{14,6},{1,9},{3,11}... | collective-permute-start | bytes 393224 | tf_op jit(solution)/shard_map/ppermute | solution.py:327
  38.8 7.8 %collective-permute-start.12 = (bf16[128,512]{1,0:T(8,128)(2,1)S(1)}, bf16[128,512]{1,0:T(8,128)(2,1)S(1)}, u32[]{:S(2)}, u32[]{:S(2)}) collective-permute-start(bf16[128,512]{1,0:T(8,128)(2,1)S(1)} %get-tuple-element.71), channel_id=1, source_target_pairs={{0,2},{2,0},{4,6},{6,4},{8,10},{10,8},{12,14},{14,12},{1,3},{3,1},... | collective-permute-start | bytes 393224 | tf_op jit(solution)/shard_map/ppermute | solution.py:323
  40.4 8.4 %collective-permute-start.13 = (bf16[128,512]{1,0:T(8,128)(2,1)S(1)}, bf16[128,512]{1,0:T(8,128)(2,1)S(1)}, u32[]{:S(2)}, u32[]{:S(2)}) collective-permute-start(bf16[128,512]{1,0:T(8,128)(2,1)S(1)} %get-tuple-element.72), channel_id=1, source_target_pairs={{0,4},{2,6},{4,0},{6,2},{8,12},{10,14},{12,8},{14,10},{1,5},{3,7},... | collective-permute-start | bytes 393224 | tf_op jit(solution)/shard_map/ppermute | solution.py:323
  41.9 8.2 %collective-permute-start.14 = (bf16[128,512]{1,0:T(8,128)(2,1)S(1)}, bf16[128,512]{1,0:T(8,128)(2,1)S(1)}, u32[]{:S(2)}, u32[]{:S(2)}) collective-permute-start(bf16[128,512]{1,0:T(8,128)(2,1)S(1)} %get-tuple-element.73), channel_id=1, source_target_pairs={{0,6},{2,4},{4,2},{6,0},{8,14},{10,12},{12,10},{14,8},{1,7},{3,5},... | collective-permute-start | bytes 393224 | tf_op jit(solution)/shard_map/ppermute | solution.py:323
  44.0 8.0 %collective-permute-start.5 = (bf16[128,512]{1,0:T(8,128)(2,1)S(1)}, bf16[128,512]{1,0:T(8,128)(2,1)S(1)}, u32[]{:S(2)}, u32[]{:S(2)}) collective-permute-start(bf16[128,512]{1,0:T(8,128)(2,1)S(1)} %get-tuple-element.56), channel_id=1, source_target_pairs={{0,2},{2,0},{4,6},{6,4},{8,10},{10,8},{12,14},{14,12},{1,3},{3,1},... | collective-permute-start | bytes 393224 | tf_op jit(solution)/shard_map/ppermute | solution.py:323
  45.2 6.9 %collective-permute-start.6 = (bf16[128,512]{1,0:T(8,128)(2,1)S(1)}, bf16[128,512]{1,0:T(8,128)(2,1)S(1)}, u32[]{:S(2)}, u32[]{:S(2)}) collective-permute-start(bf16[128,512]{1,0:T(8,128)(2,1)S(1)} %get-tuple-element.57), channel_id=1, source_target_pairs={{0,4},{2,6},{4,0},{6,2},{8,12},{10,14},{12,8},{14,10},{1,5},{3,7},... | collective-permute-start | bytes 393224 | tf_op jit(solution)/shard_map/ppermute | solution.py:323
  46.6 7.2 %collective-permute-start.7 = (bf16[128,512]{1,0:T(8,128)(2,1)S(1)}, bf16[128,512]{1,0:T(8,128)(2,1)S(1)}, u32[]{:S(2)}, u32[]{:S(2)}) collective-permute-start(bf16[128,512]{1,0:T(8,128)(2,1)S(1)} %get-tuple-element.58), channel_id=1, source_target_pairs={{0,6},{2,4},{4,2},{6,0},{8,14},{10,12},{12,10},{14,8},{1,7},{3,5},... | collective-permute-start | bytes 393224 | tf_op jit(solution)/shard_map/ppermute | solution.py:323

commit v3 on v2

v3 whole, which is shorter than its diff:
```python
import functools

import jax
import jax.numpy as jnp
from jax import lax
from jax.experimental import pallas as pl
from jax.experimental.pallas import tpu as pltpu
from jax.sharding import PartitionSpec as P

HEAD_DIM = 64
STATE = 128
BLOCK = 128
QUAD = 4
HALO = 16
EXTRA = 16
F32 = jnp.float32
BF16 = jnp.bfloat16


def mm(left, right):
    return jnp.dot(left, right, preferred_element_type=F32)


def ends_of(lens_ref):
    total = 0
    ends = []
    for i in range(lens_ref.shape[0]):
        total = total + lens_ref[i]
        ends.append(total)
    return ends


def seg_of(pos, ends):
    count = 0
    for end in ends:
        count = count + jnp.where(end <= pos, 1, 0)
    return jnp.where(pos >= 0, count, -1)


def tokens(start, shape, dim):
    return start + lax.broadcasted_iota(jnp.int32, shape, dim)


def shift_matrix(start, ends, rows, before, taps):
    shape = (rows, before + rows)
    row = lax.broadcasted_iota(jnp.int32, shape, 0)
    col = lax.broadcasted_iota(jnp.int32, shape, 1)
    same = seg_of(start + row, ends) == seg_of(start - before + col, ends)
    parts = []
    for k in range(taps - 1):
        parts.append(jnp.where((col == row + (before - taps + 1 + k)) & same, 1.0, 0.0))
    return jnp.concatenate(parts, axis=0).astype(BF16)


def conv_half(shift, extended, block, weight, bias):
    rows = block.shape[0]
    taps = weight.shape[0]
    half = weight.astype(F32) * 0.5
    moved = mm(shift, extended)
    total = bias * 0.5 + block.astype(F32) * half[taps - 1 : taps]
    for k in range(taps - 1):
        total = total + moved[k * rows : (k + 1) * rows] * half[k : k + 1]
    return total


def silu_of_half(half):
    return half + half * jnp.tanh(half)


def rates_of(dt_ref, dtb_ref, dec_ref):
    raw = jnp.transpose(dt_ref[...].astype(F32)) + dtb_ref[...]
    rate = jnp.maximum(raw, 0.0) + jnp.log1p(jnp.exp(-jnp.abs(raw)))
    shape = (BLOCK, BLOCK)
    lower = lax.broadcasted_iota(jnp.int32, shape, 0) >= lax.broadcasted_iota(jnp.int32, shape, 1)
    cum = jnp.dot(
        jnp.where(lower, 1.0, 0.0),
        -rate * dec_ref[...],
        precision=lax.Precision.HIGHEST,
        preferred_element_type=F32,
    )
    return rate, cum


def head_map(heads, first, width):
    shape = (heads, width)
    row = lax.broadcasted_iota(jnp.int32, shape, 0)
    col = lax.broadcasted_iota(jnp.int32, shape, 1)
    return jnp.where(row == first + col // HEAD_DIM, 1.0, 0.0).astype(BF16)


def pair_of(value):
    high = value.astype(BF16)
    low = (value - high.astype(F32)).astype(BF16)
    return jnp.concatenate([high, low], axis=1)


def twice(onehot):
    return jnp.concatenate([onehot, onehot], axis=0)


def edge_kernel(x, bc, out, held, sems):
    rows, chan = x.shape
    inner = bc.shape[2]
    copies = [
        pltpu.make_async_copy(bc.at[rows - HALO : rows], held, sems.at[0]),
        pltpu.make_async_copy(x.at[rows - HALO : rows, :], out.at[:, 0:chan], sems.at[1]),
    ]
    for copy in copies:
        copy.start()
    copies[0].wait()
    value = held[...].astype(F32)
    for i in range(2):
        out[:, chan + i * inner : chan + (i + 1) * inner] = value[:, i, :].astype(BF16)
    copies[1].wait()


def early_kernel(
    info, lens_in, x_in, wx_in, bx_in, dt_in, dtb_in, dec_in, wbc_in, bbc_in, skip_in,
    xc_out, scaled, top, first, carries, factors, shift, mask, wx, bx, wbc, bbc, skip,
    lens, x, dt, dtb, dec, sems,
):
    heads, rows = dt.shape
    chan = x.shape[1]
    step = 1024
    small = [
        (lens_in, lens), (dt_in, dt), (dtb_in, dtb), (dec_in, dec), (wx_in, wx), (bx_in, bx), (wbc_in, wbc),
        (bbc_in, bbc), (skip_in, skip),
    ]
    copies = [pltpu.make_async_copy(s, d, sems.at[i]) for i, (s, d) in enumerate(small)]
    blocks = [
        pltpu.make_async_copy(x_in.at[:, at : at + step], x.at[:, at : at + step], sems.at[len(small) + i])
        for i, at in enumerate(range(0, chan, step))
    ]
    for copy in copies + blocks:
        copy.start()
    for copy in copies:
        copy.wait()
    start = info[0] * BLOCK
    ends = ends_of(lens)
    moves = shift_matrix(start, ends, BLOCK, HALO, wx.shape[0])
    shift[...] = moves
    moves = shift_matrix(start, ends, BLOCK, 0, wx.shape[0])
    shape = (BLOCK, BLOCK)
    row = lax.broadcasted_iota(jnp.int32, shape, 0)
    col = lax.broadcasted_iota(jnp.int32, shape, 1)
    seg_row = seg_of(start + row, ends)
    mask[...] = jnp.where((row >= col) & (seg_row == seg_of(start + col, ends)), 1.0, 0.0)
    rate, cum = rates_of(dt, dtb, dec)
    last = cum[BLOCK - 1 : BLOCK]
    seg_last = seg_of(start + BLOCK - 1, ends)
    seg_head = seg_row[:, 0:heads]
    factor = pair_of(jnp.where(seg_head == seg_last, jnp.exp(last - cum), 0.0) * rate)
    grown = jnp.exp(cum)
    before = seg_of(start - 1, ends)
    factors[:, 0 : 2 * heads] = pair_of(rate * jnp.exp(-cum))
    factors[:, 2 * heads : 4 * heads] = pair_of(grown)
    factors[:, 4 * heads : 6 * heads] = pair_of(jnp.where(seg_head == before, grown, 0.0))
    carry = pair_of(jnp.where(seg_last == before, jnp.exp(last), 0.0)).astype(F32)
    row = lax.broadcasted_iota(jnp.int32, (EXTRA, heads), 0)
    rows = jnp.where(row == 0, carry[:, 0:heads], jnp.where(row == 1, carry[:, heads:], 0.0)).astype(BF16)
    for i, at in enumerate(range(0, chan, step)):
        lane = slice(at, at + step)
        onehot = head_map(heads, at // HEAD_DIM, step)
        spread = mm(factor, twice(onehot))
        first[:, lane] = spread[0:HALO]
        carries[:, lane] = mm(rows, onehot).astype(BF16)
        blocks[i].wait()
        xs = x[:, lane]
        top[:, lane] = xs[0:HALO]
        xc = silu_of_half(conv_half(moves, xs, xs, wx[:, lane], bx[:, lane])).astype(BF16)
        xc_out[:, lane] = xc
        scaled[:, lane] = (xc.astype(F32) * spread).astype(BF16)


def bc_conv(which, g, shift, halo, bc, wbc, bbc):
    taps, _, inner = wbc.shape
    chan = halo.shape[1] - 2 * inner
    base = which * inner + g * STATE
    lane = slice(g * STATE, (g + 1) * STATE)
    block = bc[:, base : base + STATE]
    ext = jnp.concatenate([halo[:, chan + base : chan + base + STATE], block], axis=0)
    weight = jnp.concatenate([wbc[k].astype(F32)[which : which + 1, lane] for k in range(taps)], axis=0)
    return silu_of_half(conv_half(shift[...], ext, block, weight, bbc[which : which + 1, lane]))


def late_kernel(g, info, top, bc, halo, wx, bx, wbc, bbc, shift, scaled, first, carries, m0, m1, m2, m3, xc_out, b_out, held):
    mine = info[1]
    wide, width = xc_out.shape[1], m0.shape[1]
    taps = wx.shape[0]
    deep = slice(g * wide, (g + 1) * wide)
    bmat = bc_conv(0, g, shift, halo, bc, wbc, bbc)
    b_out[...] = bmat.astype(BF16)
    moves = jnp.concatenate([shift[k * BLOCK : k * BLOCK + HALO, 0 : 2 * HALO] for k in range(taps - 1)], axis=0)
    ext = jnp.concatenate([halo[:, deep], top[:, deep]], axis=0)
    xc = silu_of_half(conv_half(moves, ext, top[:, deep], wx[:, deep], bx[:, deep])).astype(BF16)
    xc_out[...] = xc
    head = (xc.astype(F32) * first[:, deep]).astype(BF16)
    operand = jnp.concatenate([head, scaled[HALO:, deep]], axis=0)
    held[0:STATE, :] = mm(jnp.transpose(bmat).astype(BF16), operand).astype(BF16)
    held[STATE : STATE + EXTRA, :] = carries[:, deep]
    for k, msg in enumerate((m0, m1, m2, m3)):
        msg[...] = held[:, pl.ds(pl.multiple_of((mine ^ k) * width, width), width)]


def carry_of(msg):
    return msg[STATE : STATE + 1, :].astype(F32) + msg[STATE + 1 : STATE + 2, :].astype(F32)


def fold_kernel(info, m0, m1, m2, m3, total, *decay):
    msgs = (m0, m1, m2, m3)
    for mine in range(QUAD):

        @pl.when(info[1] == mine)
        def _():
            block = [msgs[mine ^ b] for b in range(QUAD)]
            state = block[0][0:STATE, :].astype(F32)
            through = carry_of(block[0])
            for b in range(1, QUAD):
                carry = carry_of(block[b])
                state = block[b][0:STATE, :].astype(F32) + carry * state
                through = through * carry
            total[...] = state.astype(BF16)
            for out in decay:
                out[...] = jnp.broadcast_to(through, out.shape)


def enter_kernel(info, start, m0, m1, m2, m3, o0, o1, o2, o3):
    msgs = (m0, m1, m2, m3)
    outs = (o0, o1, o2, o3)
    for mine in range(QUAD):

        @pl.when(info[1] == mine)
        def _():
            outs[mine][...] = start[...]
            state = start[...].astype(F32)
            for b in range(1, QUAD):
                prev = msgs[mine ^ (b - 1)]
                state = prev[0:STATE, :].astype(F32) + carry_of(prev) * state
                outs[mine ^ b][...] = state.astype(BF16)


def inner_kernel(
    g, xc_in, xc_top, z_in, bc, bmat, halo, wbc, bbc, shift, mask, factors, skip, near, gain, c_out, z, sem
):
    wide = xc_top.shape[1]
    copy = pltpu.make_async_copy(z_in.at[:, g * wide : (g + 1) * wide], z, sem)
    copy.start()
    heads = skip.shape[1]
    cmat = bc_conv(1, g, shift, halo, bc, wbc, bbc).astype(BF16)
    c_out[...] = cmat
    scores = lax.dot_general(cmat, bmat[...], (((1,), (1,)), ((), ())), preferred_element_type=F32)
    scores = (scores * mask[...]).astype(BF16)
    skips = pair_of(jnp.broadcast_to(skip[...], (8, heads)))
    step = 1024
    copy.wait()
    for at in range(0, wide, step):
        lane = slice(at, at + step)
        deep = slice(g * wide + at, g * wide + at + step)
        onehot2 = twice(head_map(heads, (g * wide + at) // HEAD_DIM, step))
        xf = jnp.concatenate([xc_top[:, lane], xc_in[HALO:, deep]], axis=0).astype(F32)
        scaled = (xf * mm(factors[:, 0 : 2 * heads], onehot2)).astype(BF16)
        grown = mm(factors[:, 2 * heads : 4 * heads], onehot2)
        skip_c = mm(skips, onehot2)[0:1]
        gate = silu_of_half(z[:, lane].astype(F32) * 0.5)
        near[:, lane] = (mm(scores, scaled) * grown + skip_c * xf) * gate
        gain[:, lane] = mm(factors[:, 4 * heads : 6 * heads], onehot2) * gate


def finish_kernel(g, info, near, gain, e0, e1, e2, e3, cmat, scale_in, *rest):
    out, held, scale, sems = rest[-4:]
    mine = info[1]
    rows, wide = near.shape
    width = wide // QUAD
    steps = sems.shape[0] - 1
    part = rows // steps
    fetch = pltpu.make_async_copy(scale_in.at[:, g * wide : (g + 1) * wide], scale, sems.at[steps])
    fetch.start()
    copies = []
    for i in range(steps):
        these = slice(i * part, (i + 1) * part)
        c = cmat[these, :]
        values = []
        square = 0.0
        for k, e in enumerate((e0, e1, e2, e3)):
            at = pl.ds(pl.multiple_of((mine ^ k) * width, width), width)
            value = near[these, at] + gain[these, at] * mm(c, e[...])
            square = square + jnp.sum(value * value, axis=1, keepdims=True)
            values.append((at, value))
        inv = lax.rsqrt(square * (1.0 / wide) + 1e-05)
        if i == 0:
            fetch.wait()
        for at, value in values:
            held[these, at] = (value * inv * scale[:, at]).astype(BF16)
        copy = pltpu.make_async_copy(held.at[these, :], out.at[these, g * wide : (g + 1) * wide], sems.at[i])
        copy.start()
        copies.append(copy)
    for copy in copies:
        copy.wait()


SMEM = pl.BlockSpec(memory_space=pltpu.SMEM)
VMEM = pl.BlockSpec(memory_space=pltpu.VMEM)
ANY = pl.BlockSpec(memory_space=pl.ANY)
HBM = pl.BlockSpec(memory_space=pltpu.HBM)


def call(kernel, scalars, args, outs, flops, limit=32 << 20, **more):
    pinned = more.get("specs", ())
    args = [
        pltpu.with_memory_space_constraint(arg, pltpu.HBM) if i < len(pinned) and pinned[i] is HBM else arg
        for i, arg in enumerate(args)
    ]
    return pl.pallas_call(
        kernel,
        in_specs=[SMEM] * len(scalars) + more.pop("specs", [VMEM] * len(args)),
        out_specs=more.pop("out_specs", [VMEM] * len(outs)),
        out_shape=[jax.ShapeDtypeStruct(*out) for out in outs],
        cost_estimate=pl.CostEstimate(flops=flops, bytes_accessed=4 << 20, transcendentals=0),
        compiler_params=pltpu.CompilerParams(vmem_limit_bytes=limit),
        **more,
    )(*scalars, *args)


def tie(first, second):
    return lax.optimization_barrier((first, second))


def shards(
    x_in,
    z_in,
    bc_in,
    conv_x_weight,
    conv_x_bias,
    conv_bc_weight,
    conv_bc_bias,
    dt_raw,
    dt_bias,
    decay,
    skip_d,
    norm_gain,
    lengths,
):
    rows, chan = x_in.shape
    heads = dt_raw.shape[1]
    peers = lax.axis_size("seq")
    shard = lax.axis_index("seq").astype(jnp.int32)
    taps = conv_x_weight.shape[0]
    bcw = bc_in.shape[2]
    groups = bcw // STATE
    wide = chan // groups
    width = wide // QUAD
    reach = peers // 2 // QUAD

    bx = conv_x_bias.reshape(1, chan)
    scale = norm_gain.reshape(1, chan)
    info = jnp.stack([shard, shard % QUAD])

    (edge,) = call(
        edge_kernel,
        [],
        [x_in, bc_in],
        [((HALO, chan + 2 * bcw), BF16)],
        1_000_000,
        specs=[HBM] * 2,
        scratch_shapes=[pltpu.VMEM((HALO, 2, bcw), BF16), pltpu.SemaphoreType.DMA((2,))],
    )
    halo = lax.ppermute(edge, "seq", [(i, (i + 1) % peers) for i in range(peers)])
    bc = bc_in.reshape(rows, 2 * bcw)

    def swap(values):
        routes = [[(i, i ^ k) for i in range(peers)] for k in range(QUAD)]
        swapped = {k: lax.ppermute(values[k], "seq", routes[k]) for k in (3, 1, 2)}
        return [values[0], swapped[1], swapped[2], swapped[3]]

    def ahead(value):
        return lax.ppermute(value, "seq", [(i, (i + QUAD) % peers) for i in range(peers)])

    early_args = [
        lengths, x_in, conv_x_weight, bx, dt_raw.T, dt_bias.reshape(1, heads), decay.reshape(1, heads),
        conv_bc_weight, conv_bc_bias, skip_d.reshape(1, heads),
    ]
    xc, scaled, top, first, carries, factors, shift, mask, wx, bx, wbc, bbc, skip = call(
        early_kernel,
        [info],
        early_args,
        [
            ((rows, chan), BF16),
            ((rows, chan), BF16),
            ((HALO, chan), BF16),
            ((HALO, chan), F32),
            ((EXTRA, chan), BF16),
            ((rows, 6 * heads), BF16),
            (((taps - 1) * BLOCK, HALO + BLOCK), BF16),
            ((BLOCK, BLOCK), F32),
            ((taps, chan), BF16),
            ((1, chan), F32),
            ((taps, 2, bcw), BF16),
            ((2, bcw), F32),
            ((1, heads), F32),
        ],
        600_000_000,
        specs=[HBM] * len(early_args),
        scratch_shapes=[
            pltpu.SMEM(lengths.shape, jnp.int32),
            pltpu.VMEM((rows, chan), BF16),
            pltpu.VMEM((heads, rows), BF16),
            pltpu.VMEM((1, heads), F32),
            pltpu.VMEM((1, heads), F32),
            pltpu.SemaphoreType.DMA((13,)),
        ],
    )
    msgs, tops, bmats = [], [], []
    for g in range(groups):
        *sent, xc_top, bmat = call(
            functools.partial(late_kernel, g),
            [info],
            [top, bc, halo, wx, bx, wbc, bbc, shift, scaled, first, carries],
            [((STATE + EXTRA, width), BF16)] * QUAD + [((HALO, wide), BF16), ((rows, STATE), BF16)],
            100_000_000,
            scratch_shapes=[pltpu.VMEM((STATE + EXTRA, wide), BF16)],
        )
        msgs.append(swap(sent))
        tops.append(xc_top)
        bmats.append(bmat)

    local = []
    for g in range(groups):
        args = [xc, tops[g], z_in, bc, bmats[g], halo, wbc, bbc, shift, mask, factors, skip]
        outs = [((rows, wide), F32), ((rows, wide), F32), ((rows, STATE), BF16)]
        near = call(
            functools.partial(inner_kernel, g),
            [],
            args,
            outs,
            300_000_000,
            specs=[HBM if arg is z_in else VMEM for arg in args],
            scratch_shapes=[pltpu.VMEM((rows, wide), BF16), pltpu.SemaphoreType.DMA],
        )
        local.append(list(near))
        msgs[g][0], local[g][0] = tie(msgs[g][0], local[g][0])

    entering = []
    for g in range(groups):
        outs = [((STATE, width), BF16)] + [((8, width), F32)] * (reach > 1)
        total, *through = call(fold_kernel, (info,), msgs[g], outs, 1_000_000)
        state = ahead(total)
        for _ in range(reach - 1):
            state = ahead((total.astype(F32) + through[0][0:1] * state.astype(F32)).astype(BF16))
        entering.append(state)

    blocks = []
    for g in range(groups):
        outs = [((STATE, width), BF16)] * QUAD
        blocks.append(swap(call(enter_kernel, (info,), [entering[g], *msgs[g]], outs, 1_000_000)))

    out = None
    for g in range(groups):
        near, gain, cmat = local[g]
        args = [near, gain, *blocks[g], cmat, scale]
        specs = [VMEM] * (len(args) - 1) + [HBM]
        aliases = {}
        if out is not None:
            aliases = {1 + len(args): 0}
            args.append(out)
            specs.append(ANY)
        (out,) = call(
            functools.partial(finish_kernel, g),
            (info,),
            args,
            [((rows, chan), BF16)],
            100_000_000,
            specs=specs,
            out_specs=[ANY],
            scratch_shapes=[
                pltpu.VMEM((rows, wide), BF16),
                pltpu.VMEM((1, wide), F32),
                pltpu.SemaphoreType.DMA((3,)),
            ],
            input_output_aliases=aliases,
        )
    return out


def solution(mesh):
    return jax.shard_map(
        shards,
        mesh=mesh,
        in_specs=(
            P(("groups", "seq"), "heads"),
            P(("groups", "seq"), "heads"),
            P(("groups", "seq"), None, "heads"),
            P(None, "heads"),
            P("heads"),
            P(None, None, "heads"),
            P(None, "heads"),
            P(("groups", "seq"), "heads"),
            P("heads"),
            P("heads"),
            P("heads"),
            P("heads"),
            P("groups"),
        ),
        out_specs=P(("groups", "seq"), "heads"),
        check_vma=False,
    )
```

time: 56.1 us -> 50.4 us (0.90)
  waiting for transfers between devices: 4.4 us -> 14.6 us
  local copies, waits for them, and re-layouts: 9.34 us -> 0.02 us
  starting transfers between devices: 25 us -> 16.1 us
  Pallas kernels: 16.5 us -> 19.1 us
    unnamed x24 -> x3, local copies, waits for them, and re-layouts: 7.69 us -> 0.02 us
    ppermute x2, starting transfers between devices: 5.58 us -> 0.8 us  [ahead(): lax.ppermute(value, 'seq', [(i, (i + QUAD) % peers) for i in range(peers)])]
    ppermute x12, starting transfers between devices: 16.4 us -> 12.3 us  [swap(): swapped = {k: lax.ppermute(values[k], 'seq', routes[k]) for k in (3, 1, 2)}]
    ppermute x12, waiting for transfers between devices: 4.39 us -> 8.21 us  [swap(): swapped = {k: lax.ppermute(values[k], 'seq', routes[k]) for k in (3, 1, 2)}]
    ppermute x2, waiting for transfers between devices: 0.01 us -> 3.69 us  [ahead(): lax.ppermute(value, 'seq', [(i, (i + QUAD) % peers) for i in range(peers)])]
    ppermute x1, waiting for transfers between devices: 0.01 us -> 2.66 us  [shards(): lax.ppermute(edge, 'seq', [(i, (i + 1) % peers) for i in range(peers)])]
    pallas_call x11 -> x12, Pallas kernels: 16.5 us -> 19.1 us  [call(): pl.pallas_call(kernel, in_specs=[SMEM] * len(scalars) + more.pop('specs',...]
    slice x2 -> x0, local copies, waits for them, and re-layouts: 1.65 us -> none  [shards(): halo = jnp.concatenate([x_in[rows - HALO:], bc[rows - HALO:]], axis=1)]
  transfers between devices with their start and end apart: 15 -> 15, of which waited for: 5 -> 8; matrix products, arithmetic and copies ran while one was open for 4% -> 0% of each run, Pallas kernels for 24% -> 29%
where the time goes in v3:
time: 50.4 us; the launch traced here: 50.1 us
  Pallas kernels  19.1 us (38%)
  starting transfers between devices  16.1 us (32%)
  waiting for transfers between devices  14.6 us (29%)
    pallas_call x12, Pallas kernels, call(): pl.pallas_call(kernel, in_specs=[SMEM] * len(scalars) + more.pop('specs',...  19.1 us
    ppermute x12, starting transfers between devices, swap(): swapped = {k: lax.ppermute(values[k], 'seq', routes[k]) for k in (3, 1, 2)}  12.3 us
    ppermute x12, waiting for transfers between devices, swap(): swapped = {k: lax.ppermute(values[k], 'seq', routes[k]) for k in (3, 1, 2)}  8.21 us
    ppermute x2, waiting for transfers between devices, ahead(): lax.ppermute(value, 'seq', [(i, (i + QUAD) % peers) for i in range(peers)])  3.69 us
    ppermute x1, starting transfers between devices, shards(): lax.ppermute(edge, 'seq', [(i, (i + 1) % peers) for i in range(peers)])  3.02 us
    ppermute x1, waiting for transfers between devices, shards(): lax.ppermute(edge, 'seq', [(i, (i + 1) % peers) for i in range(peers)])  2.66 us
  transfers between devices with their start and end apart: 15, of which 8 were waited for; matrix products, arithmetic and copies ran while one was open for 0% of the time, Pallas kernels for 29%

profile of v3, /device:TPU:0, one launch (start us, length us, event | category | flops | bytes accessed | tf_op | source)
XLA Modules:
  0.0 50.1 jit_solution(12203089158494430605)
XLA Ops:
  0.0 0.0 copy-start
  0.0 1.0 %shard_map.128 = bf16[16,4608]{1,0:T(8,128)(2,1)S(1)} custom-call(bf16[128,4096]{1,0:T(8,128)(2,1)} %x.1, bf16[128,2,256]{2,1,0:T(2,128)(2,1)} %bc.1), custom_call_target="tpu_custom_call" | custom-call | flops 1000000 | bytes 4194304 | tf_op jit(solution)/shard_map/pallas_call | solution.py:313
  1.0 3.0 %collective-permute-start = (bf16[16,4608]{1,0:T(8,128)(2,1)S(1)}, bf16[16,4608]{1,0:T(8,128)(2,1)S(1)}, u32[]{:S(2)}, u32[]{:S(2)}) collective-permute-start(bf16[16,4608]{1,0:T(8,128)(2,1)S(1)} %shard_map.128), channel_id=1, source_target_pairs={{0,2},{2,4},{4,6},{6,8},{8,10},{10,12},{12,14},{14,0},{1,3},{3,5},... | collective-permute-start | bytes 442376 | tf_op jit(solution)/shard_map/ppermute | solution.py:367
  4.0 0.0 copy-done
  4.0 0.1 pad_add_fusion.info
  4.1 4.1 %shard_map.127 = (bf16[128,4096]{1,0:T(8,128)(2,1)S(1)}, bf16[128,4096]{1,0:T(8,128)(2,1)S(1)}, bf16[16,4096]{1,0:T(8,128)(2,1)S(1)}, f32[16,4096]{1,0:T(8,128)S...) custom-call(s32[2]{0:T(128)S(1)} %pad_add_fusion.info, ...), custom_call_target="tpu_custom_call" | custom-call | flops 600000000 | bytes 4194304 | tf_op jit(solution)/shard_map/pallas_call | solution.py:313
  8.2 2.7 %collective-permute-done.halo = bf16[16,4608]{1,0:T(8,128)(2,1)S(1)} collective-permute-done((bf16[16,4608]{1,0:T(8,128)(2,1)S(1)}, bf16[16,4608]{1,0:T(8,128)(2,1)S(1)}, u32[]{:S(2)}, u32[]{:S(2)}) %collective-permute-start) | collective-permute-done | bytes 147488 | tf_op jit(solution)/shard_map/ppermute | solution.py:367
  10.9 1.1 %shard_map.133 = (bf16[144,512]{1,0:T(8,128)(2,1)S(1)}, bf16[144,512]{1,0:T(8,128)(2,1)S(1)}, bf16[144,512]{1,0:T(8,128)(2,1)S(1)}, bf16[144,512]{1,0:T(8,128)(2...) custom-call(s32[2]{0:T(128)S(1)} %pad_add_fusion.info, bf16[16,4096]{1,0:T(8,128)(2,1)S(1)} %get-tuple-element.48.top, ...), custom_call_target="tpu_custom_call" | custom-call | flops 100000000 | bytes 4194304 | tf_op jit(solution)/shard_map/pallas_call | solution.py:313
  12.0 0.1 collective-permute-start.8
  12.1 0.4 collective-permute-start.9
  12.6 3.0 %collective-permute-start.10 = (bf16[144,512]{1,0:T(8,128)(2,1)S(1)}, bf16[144,512]{1,0:T(8,128)(2,1)S(1)}, u32[]{:S(2)}, u32[]{:S(2)}) collective-permute-start(bf16[144,512]{1,0:T(8,128)(2,1)S(1)} %get-tuple-element.85), channel_id=1, source_target_pairs={{0,6},{2,4},{4,2},{6,0},{8,14},{10,12},{12,10},{14,8},{1,7},{3,5},... | collective-permute-start | bytes 442376 | tf_op jit(solution)/shard_map/ppermute | solution.py:372
  15.6 1.2 %shard_map.129 = (bf16[144,512]{1,0:T(8,128)(2,1)S(1)}, bf16[144,512]{1,0:T(8,128)(2,1)S(1)}, bf16[144,512]{1,0:T(8,128)(2,1)S(1)}, bf16[144,512]{1,0:T(8,128)(2...) custom-call(s32[2]{0:T(128)S(1)} %pad_add_fusion.info, bf16[16,4096]{1,0:T(8,128)(2,1)S(1)} %get-tuple-element.48.top, ...), custom_call_target="tpu_custom_call" | custom-call | flops 100000000 | bytes 4194304 | tf_op jit(solution)/shard_map/pallas_call | solution.py:313
  16.8 0.1 collective-permute-start.1
  16.9 0.5 collective-permute-start.2
  17.4 1.1 %collective-permute-done.8.m1 = bf16[144,512]{1,0:T(8,128)(2,1)S(1)} collective-permute-done((bf16[144,512]{1,0:T(8,128)(2,1)S(1)}, bf16[144,512]{1,0:T(8,128)(2,1)S(1)}, u32[]{:S(2)}, u32[]{:S(2)}) %collective-permute-start.8) | collective-permute-done | bytes 147488 | tf_op jit(solution)/shard_map/ppermute | solution.py:372
  18.4 1.9 %collective-permute-start.3 = (bf16[144,512]{1,0:T(8,128)(2,1)S(1)}, bf16[144,512]{1,0:T(8,128)(2,1)S(1)}, u32[]{:S(2)}, u32[]{:S(2)}) collective-permute-start(bf16[144,512]{1,0:T(8,128)(2,1)S(1)} %get-tuple-element.70), channel_id=1, source_target_pairs={{0,6},{2,4},{4,2},{6,0},{8,14},{10,12},{12,10},{14,8},{1,7},{3,5},... | collective-permute-start | bytes 442376 | tf_op jit(solution)/shard_map/ppermute | solution.py:372
  20.3 2.1 %shard_map.134 = (f32[128,2048]{1,0:T(8,128)S(1)}, f32[128,2048]{1,0:T(8,128)S(1)}, bf16[128,128]{1,0:T(8,128)(2,1)S(1)}) custom-call(bf16[128,4096]{1,0:T(8,128)(2,1)S(1)} %get-tuple-element.58.xc_in, bf16[16,2048]{1,0:T(8,128)(2,1)S(1)} %get-tuple-element.77.xc_top, bf16[128,4096]{1,0:T(8,128)(2,1)} %z_in.3, bf16[128,512]{1,0:T(8,128)(2,1)S(1)} %bitcast.12, ...), custom_call_target="tpu_custom_call" | custom-call | flops 300000000 | bytes 4194304 | tf_op jit(solution)/shard_map/pallas_call | solution.py:313
  22.5 0.0 collective-permute-done.9.m2
  22.5 1.1 %collective-permute-done.10.m3 = bf16[144,512]{1,0:T(8,128)(2,1)S(1)} collective-permute-done((bf16[144,512]{1,0:T(8,128)(2,1)S(1)}, bf16[144,512]{1,0:T(8,128)(2,1)S(1)}, u32[]{:S(2)}, u32[]{:S(2)}) %collective-permute-start.10) | collective-permute-done | bytes 147488 | tf_op jit(solution)/shard_map/ppermute | solution.py:372
  23.6 0.7 %shard_map.135 = bf16[128,512]{1,0:T(8,128)(2,1)S(1)} custom-call(s32[2]{0:T(128)S(1)} %pad_add_fusion.info, bf16[144,512]{1,0:T(8,128)(2,1)S(1)} %get-tuple-element.82.m0, bf16[144,512]{1,0:T(8,128)(2,1)S(1)} %collective-permute-done.8.m1, bf16[144,512]{1,0:T(8,128)(2,1)S(1)} %collective-permute-done.9.m2, bf16[144,512]{1,0:T(8,128)(2,1)S(1)} %collective-permute-done.10.m3), custom_call_target="tpu_custom_call" | custom-call | flops 1000000 | bytes 4194304 | tf_op jit(solution)/shard_map/pallas_call | solution.py:313
  24.3 0.7 %collective-permute-start.11 = (bf16[128,512]{1,0:T(8,128)(2,1)S(1)}, bf16[128,512]{1,0:T(8,128)(2,1)S(1)}, u32[]{:S(2)}, u32[]{:S(2)}) collective-permute-start(bf16[128,512]{1,0:T(8,128)(2,1)S(1)} %shard_map.135), channel_id=1, source_target_pairs={{0,8},{2,10},{4,12},{6,14},{8,0},{10,2},{12,4},{14,6},{1,9},{3,11}... | collective-permute-start | bytes 393224 | tf_op jit(solution)/shard_map/ppermute | solution.py:376
  25.0 2.2 %shard_map.130 = (f32[128,2048]{1,0:T(8,128)S(1)}, f32[128,2048]{1,0:T(8,128)S(1)}, bf16[128,128]{1,0:T(8,128)(2,1)S(1)}) custom-call(bf16[128,4096]{1,0:T(8,128)(2,1)S(1)} %get-tuple-element.58.xc_in, bf16[16,2048]{1,0:T(8,128)(2,1)S(1)} %get-tuple-element.59.xc_top, bf16[128,4096]{1,0:T(8,128)(2,1)} %z_in.3, bf16[128,512]{1,0:T(8,128)(2,1)S(1)} %bitcast.13, ...), custom_call_target="tpu_custom_call" | custom-call | flops 300000000 | bytes 4194304 | tf_op jit(solution)/shard_map/pallas_call | solution.py:313
  27.2 0.0 collective-permute-done.1.m1
  27.2 0.0 collective-permute-done.2.m2
  27.2 2.8 %collective-permute-done.3.m3 = bf16[144,512]{1,0:T(8,128)(2,1)S(1)} collective-permute-done((bf16[144,512]{1,0:T(8,128)(2,1)S(1)}, bf16[144,512]{1,0:T(8,128)(2,1)S(1)}, u32[]{:S(2)}, u32[]{:S(2)}) %collective-permute-start.3) | collective-permute-done | bytes 147488 | tf_op jit(solution)/shard_map/ppermute | solution.py:372
  30.1 0.7 %shard_map.131 = bf16[128,512]{1,0:T(8,128)(2,1)S(1)} custom-call(s32[2]{0:T(128)S(1)} %pad_add_fusion.info, bf16[144,512]{1,0:T(8,128)(2,1)S(1)} %get-tuple-element.67.m0, bf16[144,512]{1,0:T(8,128)(2,1)S(1)} %collective-permute-done.1.m1, bf16[144,512]{1,0:T(8,128)(2,1)S(1)} %collective-permute-done.2.m2, bf16[144,512]{1,0:T(8,128)(2,1)S(1)} %collective-permute-done.3.m3), custom_call_target="tpu_custom_call" | custom-call | flops 1000000 | bytes 4194304 | tf_op jit(solution)/shard_map/pallas_call | solution.py:313
  30.7 0.1 collective-permute-start.4
  30.8 3.7 %collective-permute-done.11.start = bf16[128,512]{1,0:T(8,128)(2,1)S(1)} collective-permute-done((bf16[128,512]{1,0:T(8,128)(2,1)S(1)}, bf16[128,512]{1,0:T(8,128)(2,1)S(1)}, u32[]{:S(2)}, u32[]{:S(2)}) %collective-permute-start.11) | collective-permute-done | bytes 131104 | tf_op jit(solution)/shard_map/ppermute | solution.py:376
  34.5 0.7 %shard_map.136 = (bf16[128,512]{1,0:T(8,128)(2,1)S(1)}, bf16[128,512]{1,0:T(8,128)(2,1)S(1)}, bf16[128,512]{1,0:T(8,128)(2,1)S(1)}, bf16[128,512]{1,0:T(8,128)(2,1)S(1)}) custom-call(s32[2]{0:T(128)S(1)} %pad_add_fusion.info, bf16[128,512]{1,0:T(8,128)(2,1)S(1)} %collective-permute-done.11.start, bf16[144,512]{1,0:T(8,128)(2,1)S(1)} %get-tuple-element.82.m0, ...), custom_call_target="tpu_custom_call" | custom-call | flops 1000000 | bytes 4194304 | tf_op jit(solution)/shard_map/pallas_call | solution.py:313
  35.2 0.1 collective-permute-start.12
  35.3 0.1 collective-permute-start.13
  35.4 3.4 %collective-permute-start.14 = (bf16[128,512]{1,0:T(8,128)(2,1)S(1)}, bf16[128,512]{1,0:T(8,128)(2,1)S(1)}, u32[]{:S(2)}, u32[]{:S(2)}) collective-permute-start(bf16[128,512]{1,0:T(8,128)(2,1)S(1)} %get-tuple-element.89), channel_id=1, source_target_pairs={{0,6},{2,4},{4,2},{6,0},{8,14},{10,12},{12,10},{14,8},{1,7},{3,5},... | collective-permute-start | bytes 393224 | tf_op jit(solution)/shard_map/ppermute | solution.py:372
  38.8 0.0 collective-permute-done.4.start
  38.8 0.7 %shard_map.132 = (bf16[128,512]{1,0:T(8,128)(2,1)S(1)}, bf16[128,512]{1,0:T(8,128)(2,1)S(1)}, bf16[128,512]{1,0:T(8,128)(2,1)S(1)}, bf16[128,512]{1,0:T(8,128)(2,1)S(1)}) custom-call(s32[2]{0:T(128)S(1)} %pad_add_fusion.info, bf16[128,512]{1,0:T(8,128)(2,1)S(1)} %collective-permute-done.4.start, bf16[144,512]{1,0:T(8,128)(2,1)S(1)} %get-tuple-element.67.m0, ...), custom_call_target="tpu_custom_call" | custom-call | flops 1000000 | bytes 4194304 | tf_op jit(solution)/shard_map/pallas_call | solution.py:313
  39.5 0.1 collective-permute-start.5
  39.6 0.5 collective-permute-start.6
  40.1 0.8 %collective-permute-done.12.e1 = bf16[128,512]{1,0:T(8,128)(2,1)S(1)} collective-permute-done((bf16[128,512]{1,0:T(8,128)(2,1)S(1)}, bf16[128,512]{1,0:T(8,128)(2,1)S(1)}, u32[]{:S(2)}, u32[]{:S(2)}) %collective-permute-start.12) | collective-permute-done | bytes 131104 | tf_op jit(solution)/shard_map/ppermute | solution.py:372
  40.9 2.1 %collective-permute-start.7 = (bf16[128,512]{1,0:T(8,128)(2,1)S(1)}, bf16[128,512]{1,0:T(8,128)(2,1)S(1)}, u32[]{:S(2)}, u32[]{:S(2)}) collective-permute-start(bf16[128,512]{1,0:T(8,128)(2,1)S(1)} %get-tuple-element.74), channel_id=1, source_target_pairs={{0,6},{2,4},{4,2},{6,0},{8,14},{10,12},{12,10},{14,8},{1,7},{3,5},... | collective-permute-start | bytes 393224 | tf_op jit(solution)/shard_map/ppermute | solution.py:372
  43.0 0.0 collective-permute-done.13.e2
  43.0 2.0 %collective-permute-done.14.e3 = bf16[128,512]{1,0:T(8,128)(2,1)S(1)} collective-permute-done((bf16[128,512]{1,0:T(8,128)(2,1)S(1)}, bf16[128,512]{1,0:T(8,128)(2,1)S(1)}, u32[]{:S(2)}, u32[]{:S(2)}) %collective-permute-start.14) | collective-permute-done | bytes 131104 | tf_op jit(solution)/shard_map/ppermute | solution.py:372
  45.0 2.4 %shard_map.137.rest_0_ = bf16[128,4096]{1,0:T(8,128)(2,1)} custom-call(s32[2]{0:T(128)S(1)} %pad_add_fusion.info, f32[128,2048]{1,0:T(8,128)S(1)} %get-tuple-element.80.near, f32[128,2048]{1,0:T(8,128)S(1)} %get-tuple-element.81.gain, bf16[128,512]{1,0:T(8,128)(2,1)S(1)} %get-tuple-element.86.e0, bf16[128,512]{1,0:T(8,128)(2,1)S(1)} %collective-permute-done.12.e1, ...), custom_call_target="tpu_custom_call" | custom-call | flops 100000000 | bytes 4194304 | tf_op jit(solution)/shard_map/pallas_call | solution.py:313
  47.3 0.0 collective-permute-done.5.e1
  47.3 0.0 collective-permute-done.6.e2
  47.4 0.4 collective-permute-done.7.e3
  47.7 2.4 %shard_map.138 = bf16[128,4096]{1,0:T(8,128)(2,1)} custom-call(s32[2]{0:T(128)S(1)} %pad_add_fusion.info, f32[128,2048]{1,0:T(8,128)S(1)} %get-tuple-element.65.near, f32[128,2048]{1,0:T(8,128)S(1)} %get-tuple-element.66.gain, bf16[128,512]{1,0:T(8,128)(2,1)S(1)} %get-tuple-element.71.e0, ...), custom_call_target="tpu_custom_call", output_to_operand_aliasing={{}: (9, {})} | custom-call | flops 100000000 | bytes 4194304 | tf_op jit(solution)/shard_map/pallas_call | solution.py:313
  (1 shorter events, 0.0 us)
Async XLA Ops:
  0.0 4.0 %copy-start = (bf16[128,2,256]{2,1,0:T(2,128)(2,1)S(1)}, bf16[128,2,256]{2,1,0:T(2,128)(2,1)}, u32[]{:S(2)}) copy-start(bf16[128,2,256]{2,1,0:T(2,128)(2,1)} %bc.1) | copy-start | bytes 393220
  1.0 9.9 %collective-permute-start = (bf16[16,4608]{1,0:T(8,128)(2,1)S(1)}, bf16[16,4608]{1,0:T(8,128)(2,1)S(1)}, u32[]{:S(2)}, u32[]{:S(2)}) collective-permute-start(bf16[16,4608]{1,0:T(8,128)(2,1)S(1)} %shard_map.128), channel_id=1, source_target_pairs={{0,2},{2,4},{4,6},{6,8},{8,10},{10,12},{12,14},{14,0},{1,3},{3,5},... | collective-permute-start | bytes 442376 | tf_op jit(solution)/shard_map/ppermute | solution.py:367
  12.0 6.4 %collective-permute-start.8 = (bf16[144,512]{1,0:T(8,128)(2,1)S(1)}, bf16[144,512]{1,0:T(8,128)(2,1)S(1)}, u32[]{:S(2)}, u32[]{:S(2)}) collective-permute-start(bf16[144,512]{1,0:T(8,128)(2,1)S(1)} %get-tuple-element.83), channel_id=1, source_target_pairs={{0,2},{2,0},{4,6},{6,4},{8,10},{10,8},{12,14},{14,12},{1,3},{3,1},... | collective-permute-start | bytes 442376 | tf_op jit(solution)/shard_map/ppermute | solution.py:372
  12.1 10.4 %collective-permute-start.9 = (bf16[144,512]{1,0:T(8,128)(2,1)S(1)}, bf16[144,512]{1,0:T(8,128)(2,1)S(1)}, u32[]{:S(2)}, u32[]{:S(2)}) collective-permute-start(bf16[144,512]{1,0:T(8,128)(2,1)S(1)} %get-tuple-element.84), channel_id=1, source_target_pairs={{0,4},{2,6},{4,0},{6,2},{8,12},{10,14},{12,8},{14,10},{1,5},{3,7},... | collective-permute-start | bytes 442376 | tf_op jit(solution)/shard_map/ppermute | solution.py:372
  12.6 11.1 %collective-permute-start.10 = (bf16[144,512]{1,0:T(8,128)(2,1)S(1)}, bf16[144,512]{1,0:T(8,128)(2,1)S(1)}, u32[]{:S(2)}, u32[]{:S(2)}) collective-permute-start(bf16[144,512]{1,0:T(8,128)(2,1)S(1)} %get-tuple-element.85), channel_id=1, source_target_pairs={{0,6},{2,4},{4,2},{6,0},{8,14},{10,12},{12,10},{14,8},{1,7},{3,5},... | collective-permute-start | bytes 442376 | tf_op jit(solution)/shard_map/ppermute | solution.py:372
  16.8 10.4 %collective-permute-start.1 = (bf16[144,512]{1,0:T(8,128)(2,1)S(1)}, bf16[144,512]{1,0:T(8,128)(2,1)S(1)}, u32[]{:S(2)}, u32[]{:S(2)}) collective-permute-start(bf16[144,512]{1,0:T(8,128)(2,1)S(1)} %get-tuple-element.68), channel_id=1, source_target_pairs={{0,2},{2,0},{4,6},{6,4},{8,10},{10,8},{12,14},{14,12},{1,3},{3,1},... | collective-permute-start | bytes 442376 | tf_op jit(solution)/shard_map/ppermute | solution.py:372
  16.9 10.3 %collective-permute-start.2 = (bf16[144,512]{1,0:T(8,128)(2,1)S(1)}, bf16[144,512]{1,0:T(8,128)(2,1)S(1)}, u32[]{:S(2)}, u32[]{:S(2)}) collective-permute-start(bf16[144,512]{1,0:T(8,128)(2,1)S(1)} %get-tuple-element.69), channel_id=1, source_target_pairs={{0,4},{2,6},{4,0},{6,2},{8,12},{10,14},{12,8},{14,10},{1,5},{3,7},... | collective-permute-start | bytes 442376 | tf_op jit(solution)/shard_map/ppermute | solution.py:372
  18.4 11.6 %collective-permute-start.3 = (bf16[144,512]{1,0:T(8,128)(2,1)S(1)}, bf16[144,512]{1,0:T(8,128)(2,1)S(1)}, u32[]{:S(2)}, u32[]{:S(2)}) collective-permute-start(bf16[144,512]{1,0:T(8,128)(2,1)S(1)} %get-tuple-element.70), channel_id=1, source_target_pairs={{0,6},{2,4},{4,2},{6,0},{8,14},{10,12},{12,10},{14,8},{1,7},{3,5},... | collective-permute-start | bytes 442376 | tf_op jit(solution)/shard_map/ppermute | solution.py:372
  24.3 10.2 %collective-permute-start.11 = (bf16[128,512]{1,0:T(8,128)(2,1)S(1)}, bf16[128,512]{1,0:T(8,128)(2,1)S(1)}, u32[]{:S(2)}, u32[]{:S(2)}) collective-permute-start(bf16[128,512]{1,0:T(8,128)(2,1)S(1)} %shard_map.135), channel_id=1, source_target_pairs={{0,8},{2,10},{4,12},{6,14},{8,0},{10,2},{12,4},{14,6},{1,9},{3,11}... | collective-permute-start | bytes 393224 | tf_op jit(solution)/shard_map/ppermute | solution.py:376
  30.7 8.0 %collective-permute-start.4 = (bf16[128,512]{1,0:T(8,128)(2,1)S(1)}, bf16[128,512]{1,0:T(8,128)(2,1)S(1)}, u32[]{:S(2)}, u32[]{:S(2)}) collective-permute-start(bf16[128,512]{1,0:T(8,128)(2,1)S(1)} %shard_map.131), channel_id=1, source_target_pairs={{0,8},{2,10},{4,12},{6,14},{8,0},{10,2},{12,4},{14,6},{1,9},{3,11}... | collective-permute-start | bytes 393224 | tf_op jit(solution)/shard_map/ppermute | solution.py:376
  35.2 5.7 %collective-permute-start.12 = (bf16[128,512]{1,0:T(8,128)(2,1)S(1)}, bf16[128,512]{1,0:T(8,128)(2,1)S(1)}, u32[]{:S(2)}, u32[]{:S(2)}) collective-permute-start(bf16[128,512]{1,0:T(8,128)(2,1)S(1)} %get-tuple-element.87), channel_id=1, source_target_pairs={{0,2},{2,0},{4,6},{6,4},{8,10},{10,8},{12,14},{14,12},{1,3},{3,1},... | collective-permute-start | bytes 393224 | tf_op jit(solution)/shard_map/ppermute | solution.py:372
  35.3 7.7 %collective-permute-start.13 = (bf16[128,512]{1,0:T(8,128)(2,1)S(1)}, bf16[128,512]{1,0:T(8,128)(2,1)S(1)}, u32[]{:S(2)}, u32[]{:S(2)}) collective-permute-start(bf16[128,512]{1,0:T(8,128)(2,1)S(1)} %get-tuple-element.88), channel_id=1, source_target_pairs={{0,4},{2,6},{4,0},{6,2},{8,12},{10,14},{12,8},{14,10},{1,5},{3,7},... | collective-permute-start | bytes 393224 | tf_op jit(solution)/shard_map/ppermute | solution.py:372
  35.4 9.6 %collective-permute-start.14 = (bf16[128,512]{1,0:T(8,128)(2,1)S(1)}, bf16[128,512]{1,0:T(8,128)(2,1)S(1)}, u32[]{:S(2)}, u32[]{:S(2)}) collective-permute-start(bf16[128,512]{1,0:T(8,128)(2,1)S(1)} %get-tuple-element.89), channel_id=1, source_target_pairs={{0,6},{2,4},{4,2},{6,0},{8,14},{10,12},{12,10},{14,8},{1,7},{3,5},... | collective-permute-start | bytes 393224 | tf_op jit(solution)/shard_map/ppermute | solution.py:372
  39.5 7.9 %collective-permute-start.5 = (bf16[128,512]{1,0:T(8,128)(2,1)S(1)}, bf16[128,512]{1,0:T(8,128)(2,1)S(1)}, u32[]{:S(2)}, u32[]{:S(2)}) collective-permute-start(bf16[128,512]{1,0:T(8,128)(2,1)S(1)} %get-tuple-element.72), channel_id=1, source_target_pairs={{0,2},{2,0},{4,6},{6,4},{8,10},{10,8},{12,14},{14,12},{1,3},{3,1},... | collective-permute-start | bytes 393224 | tf_op jit(solution)/shard_map/ppermute | solution.py:372
  39.6 7.8 %collective-permute-start.6 = (bf16[128,512]{1,0:T(8,128)(2,1)S(1)}, bf16[128,512]{1,0:T(8,128)(2,1)S(1)}, u32[]{:S(2)}, u32[]{:S(2)}) collective-permute-start(bf16[128,512]{1,0:T(8,128)(2,1)S(1)} %get-tuple-element.73), channel_id=1, source_target_pairs={{0,4},{2,6},{4,0},{6,2},{8,12},{10,14},{12,8},{14,10},{1,5},{3,7},... | collective-permute-start | bytes 393224 | tf_op jit(solution)/shard_map/ppermute | solution.py:372
  40.9 6.8 %collective-permute-start.7 = (bf16[128,512]{1,0:T(8,128)(2,1)S(1)}, bf16[128,512]{1,0:T(8,128)(2,1)S(1)}, u32[]{:S(2)}, u32[]{:S(2)}) collective-permute-start(bf16[128,512]{1,0:T(8,128)(2,1)S(1)} %get-tuple-element.74), channel_id=1, source_target_pairs={{0,6},{2,4},{4,2},{6,0},{8,14},{10,12},{12,10},{14,8},{1,7},{3,5},... | collective-permute-start | bytes 393224 | tf_op jit(solution)/shard_map/ppermute | solution.py:372

commit v4 on v3

--- a/solution.py
+++ b/solution.py
@@ -11,8 +11,9 @@
 STATE = 128
 BLOCK = 128
 QUAD = 4
-HALO = 16
-EXTRA = 16
+HALO = 8
+EXTRA = 8
+FIRST = 16
 F32 = jnp.float32
 BF16 = jnp.bfloat16
 
@@ -115,8 +116,8 @@
 
 
 def early_kernel(
-    info, lens_in, x_in, wx_in, bx_in, dt_in, dtb_in, dec_in, wbc_in, bbc_in, skip_in,
-    xc_out, scaled, top, first, carries, factors, shift, mask, wx, bx, wbc, bbc, skip,
+    info, lens_in, x_in, wx_in, bx_in, dt_in, dtb_in, dec_in, wbc_in, bbc_in, skip_in, scale_in,
+    xc_out, scaled, top, first, carries, factors, shift, mask, wx, bx, wbc, bbc, skip, scale,
     lens, x, dt, dtb, dec, sems,
 ):
     heads, rows = dt.shape
@@ -124,7 +125,7 @@
     step = 1024
     small = [
         (lens_in, lens), (dt_in, dt), (dtb_in, dtb), (dec_in, dec), (wx_in, wx), (bx_in, bx), (wbc_in, wbc),
-        (bbc_in, bbc), (skip_in, skip),
+        (bbc_in, bbc), (skip_in, skip), (scale_in, scale),
     ]
     copies = [pltpu.make_async_copy(s, d, sems.at[i]) for i, (s, d) in enumerate(small)]
     blocks = [
@@ -162,14 +163,18 @@
         lane = slice(at, at + step)
         onehot = head_map(heads, at // HEAD_DIM, step)
         spread = mm(factor, twice(onehot))
-        first[:, lane] = spread[0:HALO]
+        first[:, lane] = spread[0:FIRST]
         carries[:, lane] = mm(rows, onehot).astype(BF16)
         blocks[i].wait()
         xs = x[:, lane]
-        top[:, lane] = xs[0:HALO]
+        top[:, lane] = xs[0:FIRST]
         xc = silu_of_half(conv_half(moves, xs, xs, wx[:, lane], bx[:, lane])).astype(BF16)
         xc_out[:, lane] = xc
         scaled[:, lane] = (xc.astype(F32) * spread).astype(BF16)
+
+
+def joined(above, below):
+    return jnp.concatenate([above.astype(F32), below.astype(F32)], axis=0).astype(BF16)
 
 
 def bc_conv(which, g, shift, halo, bc, wbc, bbc):
@@ -178,7 +183,7 @@
     base = which * inner + g * STATE
     lane = slice(g * STATE, (g + 1) * STATE)
     block = bc[:, base : base + STATE]
-    ext = jnp.concatenate([halo[:, chan + base : chan + base + STATE], block], axis=0)
+    ext = joined(halo[:, chan + base : chan + base + STATE], block)
     weight = jnp.concatenate([wbc[k].astype(F32)[which : which + 1, lane] for k in range(taps)], axis=0)
     return silu_of_half(conv_half(shift[...], ext, block, weight, bbc[which : which + 1, lane]))
 
@@ -190,12 +195,13 @@
     deep = slice(g * wide, (g + 1) * wide)
     bmat = bc_conv(0, g, shift, halo, bc, wbc, bbc)
     b_out[...] = bmat.astype(BF16)
-    moves = jnp.concatenate([shift[k * BLOCK : k * BLOCK + HALO, 0 : 2 * HALO] for k in range(taps - 1)], axis=0)
-    ext = jnp.concatenate([halo[:, deep], top[:, deep]], axis=0)
+    cols = slice(0, HALO + FIRST)
+    moves = jnp.concatenate([shift[k * BLOCK : k * BLOCK + FIRST, cols] for k in range(taps - 1)], axis=0)
+    ext = joined(halo[:, deep], top[:, deep])
     xc = silu_of_half(conv_half(moves, ext, top[:, deep], wx[:, deep], bx[:, deep])).astype(BF16)
     xc_out[...] = xc
     head = (xc.astype(F32) * first[:, deep]).astype(BF16)
-    operand = jnp.concatenate([head, scaled[HALO:, deep]], axis=0)
+    operand = jnp.concatenate([head, scaled[FIRST:, deep]], axis=0)
     held[0:STATE, :] = mm(jnp.transpose(bmat).astype(BF16), operand).astype(BF16)
     held[STATE : STATE + EXTRA, :] = carries[:, deep]
     for k, msg in enumerate((m0, m1, m2, m3)):
@@ -257,7 +263,7 @@
         lane = slice(at, at + step)
         deep = slice(g * wide + at, g * wide + at + step)
         onehot2 = twice(head_map(heads, (g * wide + at) // HEAD_DIM, step))
-        xf = jnp.concatenate([xc_top[:, lane], xc_in[HALO:, deep]], axis=0).astype(F32)
+        xf = jnp.concatenate([xc_top[:, lane], xc_in[FIRST:, deep]], axis=0).astype(F32)
         scaled = (xf * mm(factors[:, 0 : 2 * heads], onehot2)).astype(BF16)
         grown = mm(factors[:, 2 * heads : 4 * heads], onehot2)
         skip_c = mm(skips, onehot2)[0:1]
@@ -266,32 +272,29 @@
         gain[:, lane] = mm(factors[:, 4 * heads : 6 * heads], onehot2) * gate
 
 
-def finish_kernel(g, info, near, gain, e0, e1, e2, e3, cmat, scale_in, *rest):
-    out, held, scale, sems = rest[-4:]
+def finish_kernel(g, info, near, gain, e0, e1, e2, e3, cmat, scale, *rest):
+    out, ready, held, sems = rest[-4:]
     mine = info[1]
     rows, wide = near.shape
     width = wide // QUAD
-    steps = sems.shape[0] - 1
+    steps = sems.shape[0]
     part = rows // steps
-    fetch = pltpu.make_async_copy(scale_in.at[:, g * wide : (g + 1) * wide], scale, sems.at[steps])
-    fetch.start()
+    square = [0.0] * steps
+    ats = [pl.ds(pl.multiple_of((mine ^ k) * width, width), width) for k in range(QUAD)]
+    c = cmat[...]
+    for at, e in zip(ats, (e0, e1, e2, e3)):
+        far = mm(c, e[...])
+        for i in range(steps):
+            these = slice(i * part, (i + 1) * part)
+            value = near[these, at] + gain[these, at] * far[these]
+            square[i] = square[i] + jnp.sum(value * value, axis=1, keepdims=True)
+            held[these, at] = value
     copies = []
     for i in range(steps):
         these = slice(i * part, (i + 1) * part)
-        c = cmat[these, :]
-        values = []
-        square = 0.0
-        for k, e in enumerate((e0, e1, e2, e3)):
-            at = pl.ds(pl.multiple_of((mine ^ k) * width, width), width)
-            value = near[these, at] + gain[these, at] * mm(c, e[...])
-            square = square + jnp.sum(value * value, axis=1, keepdims=True)
-            values.append((at, value))
-        inv = lax.rsqrt(square * (1.0 / wide) + 1e-05)
-        if i == 0:
-            fetch.wait()
-        for at, value in values:
-            held[these, at] = (value * inv * scale[:, at]).astype(BF16)
-        copy = pltpu.make_async_copy(held.at[these, :], out.at[these, g * wide : (g + 1) * wide], sems.at[i])
+        inv = lax.rsqrt(square[i] * (1.0 / wide) + 1e-05)
+        ready[these, :] = (held[these, :] * inv * scale[:, g * wide : (g + 1) * wide]).astype(BF16)
+        copy = pltpu.make_async_copy(ready.at[these, :], out.at[these, g * wide : (g + 1) * wide], sems.at[i])
         copy.start()
         copies.append(copy)
     for copy in copies:
@@ -377,17 +380,17 @@
 
     early_args = [
         lengths, x_in, conv_x_weight, bx, dt_raw.T, dt_bias.reshape(1, heads), decay.reshape(1, heads),
-        conv_bc_weight, conv_bc_bias, skip_d.reshape(1, heads),
+        conv_bc_weight, conv_bc_bias, skip_d.reshape(1, heads), scale,
     ]
-    xc, scaled, top, first, carries, factors, shift, mask, wx, bx, wbc, bbc, skip = call(
+    xc, scaled, top, first, carries, factors, shift, mask, wx, bx, wbc, bbc, skip, scale = call(
         early_kernel,
         [info],
         early_args,
         [
             ((rows, chan), BF16),
             ((rows, chan), BF16),
-            ((HALO, chan), BF16),
-            ((HALO, chan), F32),
+            ((FIRST, chan), BF16),
+            ((FIRST, chan), F32),
             ((EXTRA, chan), BF16),
             ((rows, 6 * heads), BF16),
             (((taps - 1) * BLOCK, HALO + BLOCK), BF16),
@@ -397,6 +400,7 @@
             ((taps, 2, bcw), BF16),
             ((2, bcw), F32),
             ((1, heads), F32),
+            ((1, chan), F32),
         ],
         600_000_000,
         specs=[HBM] * len(early_args),
@@ -406,7 +410,7 @@
             pltpu.VMEM((heads, rows), BF16),
             pltpu.VMEM((1, heads), F32),
             pltpu.VMEM((1, heads), F32),
-            pltpu.SemaphoreType.DMA((13,)),
+            pltpu.SemaphoreType.DMA((14,)),
         ],
     )
     msgs, tops, bmats = [], [], []
@@ -415,7 +419,7 @@
             functools.partial(late_kernel, g),
             [info],
             [top, bc, halo, wx, bx, wbc, bbc, shift, scaled, first, carries],
-            [((STATE + EXTRA, width), BF16)] * QUAD + [((HALO, wide), BF16), ((rows, STATE), BF16)],
+            [((STATE + EXTRA, width), BF16)] * QUAD + [((FIRST, wide), BF16), ((rows, STATE), BF16)],
             100_000_000,
             scratch_shapes=[pltpu.VMEM((STATE + EXTRA, wide), BF16)],
         )
@@ -457,7 +461,7 @@
     for g in range(groups):
         near, gain, cmat = local[g]
         args = [near, gain, *blocks[g], cmat, scale]
-        specs = [VMEM] * (len(args) - 1) + [HBM]
+        specs = [VMEM] * len(args)
         aliases = {}
         if out is not None:
             aliases = {1 + len(args): 0}
@@ -473,8 +477,8 @@
             out_specs=[ANY],
             scratch_shapes=[
                 pltpu.VMEM((rows, wide), BF16),
-                pltpu.VMEM((1, wide), F32),
-                pltpu.SemaphoreType.DMA((3,)),
+                pltpu.VMEM((rows, wide), F32),
+                pltpu.SemaphoreType.DMA((4,)),
             ],
             input_output_aliases=aliases,
         )

time: 50.4 us -> 48.3 us (0.958)
  waiting for transfers between devices: 14.6 us -> 10.8 us
  starting transfers between devices: 16.1 us -> 19.1 us
  Pallas kernels: 19.1 us -> 17.9 us
    ppermute x2, starting transfers between devices: 0.8 us -> 3.49 us  [ahead(): lax.ppermute(value, 'seq', [(i, (i + QUAD) % peers) for i in range(peers)])]
    ppermute x1, waiting for transfers between devices: 2.66 us -> 1.1 us  [shards(): lax.ppermute(edge, 'seq', [(i, (i + 1) % peers) for i in range(peers)])]
    ppermute x2, waiting for transfers between devices: 3.69 us -> 2.5 us  [ahead(): lax.ppermute(value, 'seq', [(i, (i + QUAD) % peers) for i in range(peers)])]
    pallas_call x12, Pallas kernels: 19.1 us -> 17.9 us  [call(): pl.pallas_call(kernel, in_specs=[SMEM] * len(scalars) + more.pop('specs',...]
    ppermute x12, waiting for transfers between devices: 8.21 us -> 7.15 us  [swap(): swapped = {k: lax.ppermute(values[k], 'seq', routes[k]) for k in (3, 1, 2)}]
  transfers between devices with their start and end apart: 15 -> 15, of which waited for: 8 -> 7; matrix products, arithmetic and copies ran while one was open for 0% -> 0% of each run, Pallas kernels for 29% -> 29%
where the time goes in v4:
time: 48.3 us; the launch traced here: 48 us
  starting transfers between devices  19.1 us (40%)
  Pallas kernels  17.9 us (37%)
  waiting for transfers between devices  10.8 us (22%)
    pallas_call x12, Pallas kernels, call(): pl.pallas_call(kernel, in_specs=[SMEM] * len(scalars) + more.pop('specs',...  17.9 us
    ppermute x12, starting transfers between devices, swap(): swapped = {k: lax.ppermute(values[k], 'seq', routes[k]) for k in (3, 1, 2)}  12.6 us
    ppermute x12, waiting for transfers between devices, swap(): swapped = {k: lax.ppermute(values[k], 'seq', routes[k]) for k in (3, 1, 2)}  7.15 us
    ppermute x2, starting transfers between devices, ahead(): lax.ppermute(value, 'seq', [(i, (i + QUAD) % peers) for i in range(peers)])  3.49 us
    ppermute x1, starting transfers between devices, shards(): lax.ppermute(edge, 'seq', [(i, (i + 1) % peers) for i in range(peers)])  3.02 us
    ppermute x2, waiting for transfers between devices, ahead(): lax.ppermute(value, 'seq', [(i, (i + QUAD) % peers) for i in range(peers)])  2.5 us
    ppermute x1, waiting for transfers between devices, shards(): lax.ppermute(edge, 'seq', [(i, (i + 1) % peers) for i in range(peers)])  1.1 us
  transfers between devices with their start and end apart: 15, of which 7 were waited for; matrix products, arithmetic and copies ran while one was open for 0% of the time, Pallas kernels for 29%

profile of v4, /device:TPU:0, one launch (start us, length us, event | category | flops | bytes accessed | tf_op | source)
XLA Modules:
  0.0 48.0 jit_solution(4530448163417770408)
XLA Ops:
  0.0 0.0 copy-start
  0.0 0.9 %shard_map.128 = bf16[8,4608]{1,0:T(8,128)(2,1)S(1)} custom-call(bf16[128,4096]{1,0:T(8,128)(2,1)} %x.1, bf16[128,2,256]{2,1,0:T(2,128)(2,1)} %bc.1), custom_call_target="tpu_custom_call" | custom-call | flops 1000000 | bytes 4194304 | tf_op jit(solution)/shard_map/pallas_call | solution.py:316
  0.9 3.0 %collective-permute-start = (bf16[8,4608]{1,0:T(8,128)(2,1)S(1)}, bf16[8,4608]{1,0:T(8,128)(2,1)S(1)}, u32[]{:S(2)}, u32[]{:S(2)}) collective-permute-start(bf16[8,4608]{1,0:T(8,128)(2,1)S(1)} %shard_map.128), channel_id=1, source_target_pairs={{0,2},{2,4},{4,6},{6,8},{8,10},{10,12},{12,14},{14,0},{1,3},{3,5},... | collective-permute-start | bytes 221192 | tf_op jit(solution)/shard_map/ppermute | solution.py:370
  3.9 0.1 pad_add_fusion.info
  4.0 0.0 copy-done
  4.0 4.2 %shard_map.127 = (bf16[128,4096]{1,0:T(8,128)(2,1)S(1)}, bf16[128,4096]{1,0:T(8,128)(2,1)S(1)}, bf16[16,4096]{1,0:T(8,128)(2,1)S(1)}, f32[16,4096]{1,0:T(8,128)S...) custom-call(s32[2]{0:T(128)S(1)} %pad_add_fusion.info, ...), custom_call_target="tpu_custom_call" | custom-call | flops 600000000 | bytes 4194304 | tf_op jit(solution)/shard_map/pallas_call | solution.py:316
  8.2 1.1 %collective-permute-done.halo = bf16[8,4608]{1,0:T(8,128)(2,1)S(1)} collective-permute-done((bf16[8,4608]{1,0:T(8,128)(2,1)S(1)}, bf16[8,4608]{1,0:T(8,128)(2,1)S(1)}, u32[]{:S(2)}, u32[]{:S(2)}) %collective-permute-start) | collective-permute-done | bytes 73760 | tf_op jit(solution)/shard_map/ppermute | solution.py:370
  9.3 1.1 %shard_map.133 = (bf16[136,512]{1,0:T(8,128)(2,1)S(1)}, bf16[136,512]{1,0:T(8,128)(2,1)S(1)}, bf16[136,512]{1,0:T(8,128)(2,1)S(1)}, bf16[136,512]{1,0:T(8,128)(2...) custom-call(s32[2]{0:T(128)S(1)} %pad_add_fusion.info, bf16[16,4096]{1,0:T(8,128)(2,1)S(1)} %get-tuple-element.49.top, ...), custom_call_target="tpu_custom_call" | custom-call | flops 100000000 | bytes 4194304 | tf_op jit(solution)/shard_map/pallas_call | solution.py:316
  10.5 0.5 %collective-permute-start.8 = (bf16[136,512]{1,0:T(8,128)(2,1)S(1)}, bf16[136,512]{1,0:T(8,128)(2,1)S(1)}, u32[]{:S(2)}, u32[]{:S(2)}) collective-permute-start(bf16[136,512]{1,0:T(8,128)(2,1)S(1)} %get-tuple-element.85), channel_id=1, source_target_pairs={{0,2},{2,0},{4,6},{6,4},{8,10},{10,8},{12,14},{14,12},{1,3},{3,1},... | collective-permute-start | bytes 417800 | tf_op jit(solution)/shard_map/ppermute | solution.py:375
  11.0 1.6 %collective-permute-start.9 = (bf16[136,512]{1,0:T(8,128)(2,1)S(1)}, bf16[136,512]{1,0:T(8,128)(2,1)S(1)}, u32[]{:S(2)}, u32[]{:S(2)}) collective-permute-start(bf16[136,512]{1,0:T(8,128)(2,1)S(1)} %get-tuple-element.86), channel_id=1, source_target_pairs={{0,4},{2,6},{4,0},{6,2},{8,12},{10,14},{12,8},{14,10},{1,5},{3,7},... | collective-permute-start | bytes 417800 | tf_op jit(solution)/shard_map/ppermute | solution.py:375
  12.5 1.5 %collective-permute-start.10 = (bf16[136,512]{1,0:T(8,128)(2,1)S(1)}, bf16[136,512]{1,0:T(8,128)(2,1)S(1)}, u32[]{:S(2)}, u32[]{:S(2)}) collective-permute-start(bf16[136,512]{1,0:T(8,128)(2,1)S(1)} %get-tuple-element.87), channel_id=1, source_target_pairs={{0,6},{2,4},{4,2},{6,0},{8,14},{10,12},{12,10},{14,8},{1,7},{3,5},... | collective-permute-start | bytes 417800 | tf_op jit(solution)/shard_map/ppermute | solution.py:375
  14.0 1.1 %shard_map.129 = (bf16[136,512]{1,0:T(8,128)(2,1)S(1)}, bf16[136,512]{1,0:T(8,128)(2,1)S(1)}, bf16[136,512]{1,0:T(8,128)(2,1)S(1)}, bf16[136,512]{1,0:T(8,128)(2...) custom-call(s32[2]{0:T(128)S(1)} %pad_add_fusion.info, bf16[16,4096]{1,0:T(8,128)(2,1)S(1)} %get-tuple-element.49.top, ...), custom_call_target="tpu_custom_call" | custom-call | flops 100000000 | bytes 4194304 | tf_op jit(solution)/shard_map/pallas_call | solution.py:316
  15.2 0.5 %collective-permute-start.1 = (bf16[136,512]{1,0:T(8,128)(2,1)S(1)}, bf16[136,512]{1,0:T(8,128)(2,1)S(1)}, u32[]{:S(2)}, u32[]{:S(2)}) collective-permute-start(bf16[136,512]{1,0:T(8,128)(2,1)S(1)} %get-tuple-element.69), channel_id=1, source_target_pairs={{0,2},{2,0},{4,6},{6,4},{8,10},{10,8},{12,14},{14,12},{1,3},{3,1},... | collective-permute-start | bytes 417800 | tf_op jit(solution)/shard_map/ppermute | solution.py:375
  15.7 1.6 %collective-permute-start.2 = (bf16[136,512]{1,0:T(8,128)(2,1)S(1)}, bf16[136,512]{1,0:T(8,128)(2,1)S(1)}, u32[]{:S(2)}, u32[]{:S(2)}) collective-permute-start(bf16[136,512]{1,0:T(8,128)(2,1)S(1)} %get-tuple-element.70), channel_id=1, source_target_pairs={{0,4},{2,6},{4,0},{6,2},{8,12},{10,14},{12,8},{14,10},{1,5},{3,7},... | collective-permute-start | bytes 417800 | tf_op jit(solution)/shard_map/ppermute | solution.py:375
  17.2 0.0 collective-permute-done.8.m1
  17.3 1.5 %collective-permute-start.3 = (bf16[136,512]{1,0:T(8,128)(2,1)S(1)}, bf16[136,512]{1,0:T(8,128)(2,1)S(1)}, u32[]{:S(2)}, u32[]{:S(2)}) collective-permute-start(bf16[136,512]{1,0:T(8,128)(2,1)S(1)} %get-tuple-element.71), channel_id=1, source_target_pairs={{0,6},{2,4},{4,2},{6,0},{8,14},{10,12},{12,10},{14,8},{1,7},{3,5},... | collective-permute-start | bytes 417800 | tf_op jit(solution)/shard_map/ppermute | solution.py:375
  18.7 2.1 %shard_map.134 = (f32[128,2048]{1,0:T(8,128)S(1)}, f32[128,2048]{1,0:T(8,128)S(1)}, bf16[128,128]{1,0:T(8,128)(2,1)S(1)}) custom-call(bf16[128,4096]{1,0:T(8,128)(2,1)S(1)} %get-tuple-element.59.xc_in, bf16[16,2048]{1,0:T(8,128)(2,1)S(1)} %get-tuple-element.79.xc_top, bf16[128,4096]{1,0:T(8,128)(2,1)} %z_in.3, bf16[128,512]{1,0:T(8,128)(2,1)S(1)} %bitcast.12, ...), custom_call_target="tpu_custom_call" | custom-call | flops 300000000 | bytes 4194304 | tf_op jit(solution)/shard_map/pallas_call | solution.py:316
  20.9 0.0 collective-permute-done.9.m2
  20.9 0.7 %collective-permute-done.10.m3 = bf16[136,512]{1,0:T(8,128)(2,1)S(1)} collective-permute-done((bf16[136,512]{1,0:T(8,128)(2,1)S(1)}, bf16[136,512]{1,0:T(8,128)(2,1)S(1)}, u32[]{:S(2)}, u32[]{:S(2)}) %collective-permute-start.10) | collective-permute-done | bytes 139296 | tf_op jit(solution)/shard_map/ppermute | solution.py:375
  21.5 0.7 %shard_map.135 = bf16[128,512]{1,0:T(8,128)(2,1)S(1)} custom-call(s32[2]{0:T(128)S(1)} %pad_add_fusion.info, bf16[136,512]{1,0:T(8,128)(2,1)S(1)} %get-tuple-element.84.m0, bf16[136,512]{1,0:T(8,128)(2,1)S(1)} %collective-permute-done.8.m1, bf16[136,512]{1,0:T(8,128)(2,1)S(1)} %collective-permute-done.9.m2, bf16[136,512]{1,0:T(8,128)(2,1)S(1)} %collective-permute-done.10.m3), custom_call_target="tpu_custom_call" | custom-call | flops 1000000 | bytes 4194304 | tf_op jit(solution)/shard_map/pallas_call | solution.py:316
  22.2 1.7 %collective-permute-start.11 = (bf16[128,512]{1,0:T(8,128)(2,1)S(1)}, bf16[128,512]{1,0:T(8,128)(2,1)S(1)}, u32[]{:S(2)}, u32[]{:S(2)}) collective-permute-start(bf16[128,512]{1,0:T(8,128)(2,1)S(1)} %shard_map.135), channel_id=1, source_target_pairs={{0,8},{2,10},{4,12},{6,14},{8,0},{10,2},{12,4},{14,6},{1,9},{3,11}... | collective-permute-start | bytes 393224 | tf_op jit(solution)/shard_map/ppermute | solution.py:379
  23.9 2.2 %shard_map.130 = (f32[128,2048]{1,0:T(8,128)S(1)}, f32[128,2048]{1,0:T(8,128)S(1)}, bf16[128,128]{1,0:T(8,128)(2,1)S(1)}) custom-call(bf16[128,4096]{1,0:T(8,128)(2,1)S(1)} %get-tuple-element.59.xc_in, bf16[16,2048]{1,0:T(8,128)(2,1)S(1)} %get-tuple-element.60.xc_top, bf16[128,4096]{1,0:T(8,128)(2,1)} %z_in.3, bf16[128,512]{1,0:T(8,128)(2,1)S(1)} %bitcast.13, ...), custom_call_target="tpu_custom_call" | custom-call | flops 300000000 | bytes 4194304 | tf_op jit(solution)/shard_map/pallas_call | solution.py:316
  26.1 0.0 collective-permute-done.1.m1
  26.1 0.0 collective-permute-done.2.m2
  26.1 0.9 %collective-permute-done.3.m3 = bf16[136,512]{1,0:T(8,128)(2,1)S(1)} collective-permute-done((bf16[136,512]{1,0:T(8,128)(2,1)S(1)}, bf16[136,512]{1,0:T(8,128)(2,1)S(1)}, u32[]{:S(2)}, u32[]{:S(2)}) %collective-permute-start.3) | collective-permute-done | bytes 139296 | tf_op jit(solution)/shard_map/ppermute | solution.py:375
  27.0 0.7 %shard_map.131 = bf16[128,512]{1,0:T(8,128)(2,1)S(1)} custom-call(s32[2]{0:T(128)S(1)} %pad_add_fusion.info, bf16[136,512]{1,0:T(8,128)(2,1)S(1)} %get-tuple-element.68.m0, bf16[136,512]{1,0:T(8,128)(2,1)S(1)} %collective-permute-done.1.m1, bf16[136,512]{1,0:T(8,128)(2,1)S(1)} %collective-permute-done.2.m2, bf16[136,512]{1,0:T(8,128)(2,1)S(1)} %collective-permute-done.3.m3), custom_call_target="tpu_custom_call" | custom-call | flops 1000000 | bytes 4194304 | tf_op jit(solution)/shard_map/pallas_call | solution.py:316
  27.7 1.8 %collective-permute-start.4 = (bf16[128,512]{1,0:T(8,128)(2,1)S(1)}, bf16[128,512]{1,0:T(8,128)(2,1)S(1)}, u32[]{:S(2)}, u32[]{:S(2)}) collective-permute-start(bf16[128,512]{1,0:T(8,128)(2,1)S(1)} %shard_map.131), channel_id=1, source_target_pairs={{0,8},{2,10},{4,12},{6,14},{8,0},{10,2},{12,4},{14,6},{1,9},{3,11}... | collective-permute-start | bytes 393224 | tf_op jit(solution)/shard_map/ppermute | solution.py:379
  29.5 2.5 %collective-permute-done.11.start = bf16[128,512]{1,0:T(8,128)(2,1)S(1)} collective-permute-done((bf16[128,512]{1,0:T(8,128)(2,1)S(1)}, bf16[128,512]{1,0:T(8,128)(2,1)S(1)}, u32[]{:S(2)}, u32[]{:S(2)}) %collective-permute-start.11) | collective-permute-done | bytes 131104 | tf_op jit(solution)/shard_map/ppermute | solution.py:379
  32.0 0.7 %shard_map.136 = (bf16[128,512]{1,0:T(8,128)(2,1)S(1)}, bf16[128,512]{1,0:T(8,128)(2,1)S(1)}, bf16[128,512]{1,0:T(8,128)(2,1)S(1)}, bf16[128,512]{1,0:T(8,128)(2,1)S(1)}) custom-call(s32[2]{0:T(128)S(1)} %pad_add_fusion.info, bf16[128,512]{1,0:T(8,128)(2,1)S(1)} %collective-permute-done.11.start, bf16[136,512]{1,0:T(8,128)(2,1)S(1)} %get-tuple-element.84.m0, ...), custom_call_target="tpu_custom_call" | custom-call | flops 1000000 | bytes 4194304 | tf_op jit(solution)/shard_map/pallas_call | solution.py:316
  32.6 0.6 %collective-permute-start.12 = (bf16[128,512]{1,0:T(8,128)(2,1)S(1)}, bf16[128,512]{1,0:T(8,128)(2,1)S(1)}, u32[]{:S(2)}, u32[]{:S(2)}) collective-permute-start(bf16[128,512]{1,0:T(8,128)(2,1)S(1)} %get-tuple-element.89), channel_id=1, source_target_pairs={{0,2},{2,0},{4,6},{6,4},{8,10},{10,8},{12,14},{14,12},{1,3},{3,1},... | collective-permute-start | bytes 393224 | tf_op jit(solution)/shard_map/ppermute | solution.py:375
  33.2 0.0 collective-permute-start.13
  33.2 3.0 %collective-permute-start.14 = (bf16[128,512]{1,0:T(8,128)(2,1)S(1)}, bf16[128,512]{1,0:T(8,128)(2,1)S(1)}, u32[]{:S(2)}, u32[]{:S(2)}) collective-permute-start(bf16[128,512]{1,0:T(8,128)(2,1)S(1)} %get-tuple-element.91), channel_id=1, source_target_pairs={{0,6},{2,4},{4,2},{6,0},{8,14},{10,12},{12,10},{14,8},{1,7},{3,5},... | collective-permute-start | bytes 393224 | tf_op jit(solution)/shard_map/ppermute | solution.py:375
  36.2 0.0 collective-permute-done.4.start
  36.2 0.7 %shard_map.132 = (bf16[128,512]{1,0:T(8,128)(2,1)S(1)}, bf16[128,512]{1,0:T(8,128)(2,1)S(1)}, bf16[128,512]{1,0:T(8,128)(2,1)S(1)}, bf16[128,512]{1,0:T(8,128)(2,1)S(1)}) custom-call(s32[2]{0:T(128)S(1)} %pad_add_fusion.info, bf16[128,512]{1,0:T(8,128)(2,1)S(1)} %collective-permute-done.4.start, bf16[136,512]{1,0:T(8,128)(2,1)S(1)} %get-tuple-element.68.m0, ...), custom_call_target="tpu_custom_call" | custom-call | flops 1000000 | bytes 4194304 | tf_op jit(solution)/shard_map/pallas_call | solution.py:316
  36.9 0.6 %collective-permute-start.5 = (bf16[128,512]{1,0:T(8,128)(2,1)S(1)}, bf16[128,512]{1,0:T(8,128)(2,1)S(1)}, u32[]{:S(2)}, u32[]{:S(2)}) collective-permute-start(bf16[128,512]{1,0:T(8,128)(2,1)S(1)} %get-tuple-element.73), channel_id=1, source_target_pairs={{0,2},{2,0},{4,6},{6,4},{8,10},{10,8},{12,14},{14,12},{1,3},{3,1},... | collective-permute-start | bytes 393224 | tf_op jit(solution)/shard_map/ppermute | solution.py:375
  37.5 0.5 %collective-permute-start.6 = (bf16[128,512]{1,0:T(8,128)(2,1)S(1)}, bf16[128,512]{1,0:T(8,128)(2,1)S(1)}, u32[]{:S(2)}, u32[]{:S(2)}) collective-permute-start(bf16[128,512]{1,0:T(8,128)(2,1)S(1)} %get-tuple-element.74), channel_id=1, source_target_pairs={{0,4},{2,6},{4,0},{6,2},{8,12},{10,14},{12,8},{14,10},{1,5},{3,7},... | collective-permute-start | bytes 393224 | tf_op jit(solution)/shard_map/ppermute | solution.py:375
  38.0 1.6 %collective-permute-done.12.e1 = bf16[128,512]{1,0:T(8,128)(2,1)S(1)} collective-permute-done((bf16[128,512]{1,0:T(8,128)(2,1)S(1)}, bf16[128,512]{1,0:T(8,128)(2,1)S(1)}, u32[]{:S(2)}, u32[]{:S(2)}) %collective-permute-start.12) | collective-permute-done | bytes 131104 | tf_op jit(solution)/shard_map/ppermute | solution.py:375
  39.6 0.8 %collective-permute-start.7 = (bf16[128,512]{1,0:T(8,128)(2,1)S(1)}, bf16[128,512]{1,0:T(8,128)(2,1)S(1)}, u32[]{:S(2)}, u32[]{:S(2)}) collective-permute-start(bf16[128,512]{1,0:T(8,128)(2,1)S(1)} %get-tuple-element.75), channel_id=1, source_target_pairs={{0,6},{2,4},{4,2},{6,0},{8,14},{10,12},{12,10},{14,8},{1,7},{3,5},... | collective-permute-start | bytes 393224 | tf_op jit(solution)/shard_map/ppermute | solution.py:375
  40.5 0.0 collective-permute-done.13.e2
  40.5 2.2 %collective-permute-done.14.e3 = bf16[128,512]{1,0:T(8,128)(2,1)S(1)} collective-permute-done((bf16[128,512]{1,0:T(8,128)(2,1)S(1)}, bf16[128,512]{1,0:T(8,128)(2,1)S(1)}, u32[]{:S(2)}, u32[]{:S(2)}) %collective-permute-start.14) | collective-permute-done | bytes 131104 | tf_op jit(solution)/shard_map/ppermute | solution.py:375
  42.6 1.8 %shard_map.137.rest_0_ = bf16[128,4096]{1,0:T(8,128)(2,1)} custom-call(s32[2]{0:T(128)S(1)} %pad_add_fusion.info, f32[128,2048]{1,0:T(8,128)S(1)} %get-tuple-element.82.near, f32[128,2048]{1,0:T(8,128)S(1)} %get-tuple-element.83.gain, bf16[128,512]{1,0:T(8,128)(2,1)S(1)} %get-tuple-element.88.e0, bf16[128,512]{1,0:T(8,128)(2,1)S(1)} %collective-permute-done.12.e1, ...), custom_call_target="tpu_custom_call" | custom-call | flops 100000000 | bytes 4194304 | tf_op jit(solution)/shard_map/pallas_call | solution.py:316
  44.4 0.0 collective-permute-done.5.e1
  44.4 0.0 collective-permute-done.6.e2
  44.4 1.8 %collective-permute-done.7.e3 = bf16[128,512]{1,0:T(8,128)(2,1)S(1)} collective-permute-done((bf16[128,512]{1,0:T(8,128)(2,1)S(1)}, bf16[128,512]{1,0:T(8,128)(2,1)S(1)}, u32[]{:S(2)}, u32[]{:S(2)}) %collective-permute-start.7) | collective-permute-done | bytes 131104 | tf_op jit(solution)/shard_map/ppermute | solution.py:375
  46.2 1.8 %shard_map.138 = bf16[128,4096]{1,0:T(8,128)(2,1)} custom-call(s32[2]{0:T(128)S(1)} %pad_add_fusion.info, f32[128,2048]{1,0:T(8,128)S(1)} %get-tuple-element.66.near, f32[128,2048]{1,0:T(8,128)S(1)} %get-tuple-element.67.gain, bf16[128,512]{1,0:T(8,128)(2,1)S(1)} %get-tuple-element.72.e0, ...), custom_call_target="tpu_custom_call", output_to_operand_aliasing={{}: (9, {})} | custom-call | flops 100000000 | bytes 4194304 | tf_op jit(solution)/shard_map/pallas_call | solution.py:316
  (1 shorter events, 0.0 us)
Async XLA Ops:
  0.0 4.0 %copy-start = (bf16[128,2,256]{2,1,0:T(2,128)(2,1)S(1)}, bf16[128,2,256]{2,1,0:T(2,128)(2,1)}, u32[]{:S(2)}) copy-start(bf16[128,2,256]{2,1,0:T(2,128)(2,1)} %bc.1) | copy-start | bytes 393220
  0.9 8.4 %collective-permute-start = (bf16[8,4608]{1,0:T(8,128)(2,1)S(1)}, bf16[8,4608]{1,0:T(8,128)(2,1)S(1)}, u32[]{:S(2)}, u32[]{:S(2)}) collective-permute-start(bf16[8,4608]{1,0:T(8,128)(2,1)S(1)} %shard_map.128), channel_id=1, source_target_pairs={{0,2},{2,4},{4,6},{6,8},{8,10},{10,12},{12,14},{14,0},{1,3},{3,5},... | collective-permute-start | bytes 221192 | tf_op jit(solution)/shard_map/ppermute | solution.py:370
  10.5 6.8 %collective-permute-start.8 = (bf16[136,512]{1,0:T(8,128)(2,1)S(1)}, bf16[136,512]{1,0:T(8,128)(2,1)S(1)}, u32[]{:S(2)}, u32[]{:S(2)}) collective-permute-start(bf16[136,512]{1,0:T(8,128)(2,1)S(1)} %get-tuple-element.85), channel_id=1, source_target_pairs={{0,2},{2,0},{4,6},{6,4},{8,10},{10,8},{12,14},{14,12},{1,3},{3,1},... | collective-permute-start | bytes 417800 | tf_op jit(solution)/shard_map/ppermute | solution.py:375
  11.0 9.9 %collective-permute-start.9 = (bf16[136,512]{1,0:T(8,128)(2,1)S(1)}, bf16[136,512]{1,0:T(8,128)(2,1)S(1)}, u32[]{:S(2)}, u32[]{:S(2)}) collective-permute-start(bf16[136,512]{1,0:T(8,128)(2,1)S(1)} %get-tuple-element.86), channel_id=1, source_target_pairs={{0,4},{2,6},{4,0},{6,2},{8,12},{10,14},{12,8},{14,10},{1,5},{3,7},... | collective-permute-start | bytes 417800 | tf_op jit(solution)/shard_map/ppermute | solution.py:375
  12.5 9.0 %collective-permute-start.10 = (bf16[136,512]{1,0:T(8,128)(2,1)S(1)}, bf16[136,512]{1,0:T(8,128)(2,1)S(1)}, u32[]{:S(2)}, u32[]{:S(2)}) collective-permute-start(bf16[136,512]{1,0:T(8,128)(2,1)S(1)} %get-tuple-element.87), channel_id=1, source_target_pairs={{0,6},{2,4},{4,2},{6,0},{8,14},{10,12},{12,10},{14,8},{1,7},{3,5},... | collective-permute-start | bytes 417800 | tf_op jit(solution)/shard_map/ppermute | solution.py:375
  15.2 10.9 %collective-permute-start.1 = (bf16[136,512]{1,0:T(8,128)(2,1)S(1)}, bf16[136,512]{1,0:T(8,128)(2,1)S(1)}, u32[]{:S(2)}, u32[]{:S(2)}) collective-permute-start(bf16[136,512]{1,0:T(8,128)(2,1)S(1)} %get-tuple-element.69), channel_id=1, source_target_pairs={{0,2},{2,0},{4,6},{6,4},{8,10},{10,8},{12,14},{14,12},{1,3},{3,1},... | collective-permute-start | bytes 417800 | tf_op jit(solution)/shard_map/ppermute | solution.py:375
  15.7 10.4 %collective-permute-start.2 = (bf16[136,512]{1,0:T(8,128)(2,1)S(1)}, bf16[136,512]{1,0:T(8,128)(2,1)S(1)}, u32[]{:S(2)}, u32[]{:S(2)}) collective-permute-start(bf16[136,512]{1,0:T(8,128)(2,1)S(1)} %get-tuple-element.70), channel_id=1, source_target_pairs={{0,4},{2,6},{4,0},{6,2},{8,12},{10,14},{12,8},{14,10},{1,5},{3,7},... | collective-permute-start | bytes 417800 | tf_op jit(solution)/shard_map/ppermute | solution.py:375
  17.3 9.8 %collective-permute-start.3 = (bf16[136,512]{1,0:T(8,128)(2,1)S(1)}, bf16[136,512]{1,0:T(8,128)(2,1)S(1)}, u32[]{:S(2)}, u32[]{:S(2)}) collective-permute-start(bf16[136,512]{1,0:T(8,128)(2,1)S(1)} %get-tuple-element.71), channel_id=1, source_target_pairs={{0,6},{2,4},{4,2},{6,0},{8,14},{10,12},{12,10},{14,8},{1,7},{3,5},... | collective-permute-start | bytes 417800 | tf_op jit(solution)/shard_map/ppermute | solution.py:375
  22.2 9.7 %collective-permute-start.11 = (bf16[128,512]{1,0:T(8,128)(2,1)S(1)}, bf16[128,512]{1,0:T(8,128)(2,1)S(1)}, u32[]{:S(2)}, u32[]{:S(2)}) collective-permute-start(bf16[128,512]{1,0:T(8,128)(2,1)S(1)} %shard_map.135), channel_id=1, source_target_pairs={{0,8},{2,10},{4,12},{6,14},{8,0},{10,2},{12,4},{14,6},{1,9},{3,11}... | collective-permute-start | bytes 393224 | tf_op jit(solution)/shard_map/ppermute | solution.py:379
  27.7 8.5 %collective-permute-start.4 = (bf16[128,512]{1,0:T(8,128)(2,1)S(1)}, bf16[128,512]{1,0:T(8,128)(2,1)S(1)}, u32[]{:S(2)}, u32[]{:S(2)}) collective-permute-start(bf16[128,512]{1,0:T(8,128)(2,1)S(1)} %shard_map.131), channel_id=1, source_target_pairs={{0,8},{2,10},{4,12},{6,14},{8,0},{10,2},{12,4},{14,6},{1,9},{3,11}... | collective-permute-start | bytes 393224 | tf_op jit(solution)/shard_map/ppermute | solution.py:379
  32.6 7.0 %collective-permute-start.12 = (bf16[128,512]{1,0:T(8,128)(2,1)S(1)}, bf16[128,512]{1,0:T(8,128)(2,1)S(1)}, u32[]{:S(2)}, u32[]{:S(2)}) collective-permute-start(bf16[128,512]{1,0:T(8,128)(2,1)S(1)} %get-tuple-element.89), channel_id=1, source_target_pairs={{0,2},{2,0},{4,6},{6,4},{8,10},{10,8},{12,14},{14,12},{1,3},{3,1},... | collective-permute-start | bytes 393224 | tf_op jit(solution)/shard_map/ppermute | solution.py:375
  33.2 7.3 %collective-permute-start.13 = (bf16[128,512]{1,0:T(8,128)(2,1)S(1)}, bf16[128,512]{1,0:T(8,128)(2,1)S(1)}, u32[]{:S(2)}, u32[]{:S(2)}) collective-permute-start(bf16[128,512]{1,0:T(8,128)(2,1)S(1)} %get-tuple-element.90), channel_id=1, source_target_pairs={{0,4},{2,6},{4,0},{6,2},{8,12},{10,14},{12,8},{14,10},{1,5},{3,7},... | collective-permute-start | bytes 393224 | tf_op jit(solution)/shard_map/ppermute | solution.py:375
  33.2 9.4 %collective-permute-start.14 = (bf16[128,512]{1,0:T(8,128)(2,1)S(1)}, bf16[128,512]{1,0:T(8,128)(2,1)S(1)}, u32[]{:S(2)}, u32[]{:S(2)}) collective-permute-start(bf16[128,512]{1,0:T(8,128)(2,1)S(1)} %get-tuple-element.91), channel_id=1, source_target_pairs={{0,6},{2,4},{4,2},{6,0},{8,14},{10,12},{12,10},{14,8},{1,7},{3,5},... | collective-permute-start | bytes 393224 | tf_op jit(solution)/shard_map/ppermute | solution.py:375
  36.9 7.5 %collective-permute-start.5 = (bf16[128,512]{1,0:T(8,128)(2,1)S(1)}, bf16[128,512]{1,0:T(8,128)(2,1)S(1)}, u32[]{:S(2)}, u32[]{:S(2)}) collective-permute-start(bf16[128,512]{1,0:T(8,128)(2,1)S(1)} %get-tuple-element.73), channel_id=1, source_target_pairs={{0,2},{2,0},{4,6},{6,4},{8,10},{10,8},{12,14},{14,12},{1,3},{3,1},... | collective-permute-start | bytes 393224 | tf_op jit(solution)/shard_map/ppermute | solution.py:375
  37.5 7.0 %collective-permute-start.6 = (bf16[128,512]{1,0:T(8,128)(2,1)S(1)}, bf16[128,512]{1,0:T(8,128)(2,1)S(1)}, u32[]{:S(2)}, u32[]{:S(2)}) collective-permute-start(bf16[128,512]{1,0:T(8,128)(2,1)S(1)} %get-tuple-element.74), channel_id=1, source_target_pairs={{0,4},{2,6},{4,0},{6,2},{8,12},{10,14},{12,8},{14,10},{1,5},{3,7},... | collective-permute-start | bytes 393224 | tf_op jit(solution)/shard_map/ppermute | solution.py:375
  39.6 6.6 %collective-permute-start.7 = (bf16[128,512]{1,0:T(8,128)(2,1)S(1)}, bf16[128,512]{1,0:T(8,128)(2,1)S(1)}, u32[]{:S(2)}, u32[]{:S(2)}) collective-permute-start(bf16[128,512]{1,0:T(8,128)(2,1)S(1)} %get-tuple-element.75), channel_id=1, source_target_pairs={{0,6},{2,4},{4,2},{6,0},{8,14},{10,12},{12,10},{14,8},{1,7},{3,5},... | collective-permute-start | bytes 393224 | tf_op jit(solution)/shard_map/ppermute | solution.py:375

commit v5 on v4

--- a/solution.py
+++ b/solution.py
@@ -189,7 +189,7 @@
 
 
 def late_kernel(g, info, top, bc, halo, wx, bx, wbc, bbc, shift, scaled, first, carries, m0, m1, m2, m3, xc_out, b_out, held):
-    mine = info[1]
+    mine = info[2]
     wide, width = xc_out.shape[1], m0.shape[1]
     taps = wx.shape[0]
     deep = slice(g * wide, (g + 1) * wide)
@@ -274,7 +274,7 @@
 
 def finish_kernel(g, info, near, gain, e0, e1, e2, e3, cmat, scale, *rest):
     out, ready, held, sems = rest[-4:]
-    mine = info[1]
+    mine = info[2]
     rows, wide = near.shape
     width = wide // QUAD
     steps = sems.shape[0]
@@ -356,7 +356,8 @@
 
     bx = conv_x_bias.reshape(1, chan)
     scale = norm_gain.reshape(1, chan)
-    info = jnp.stack([shard, shard % QUAD])
+    owner = (shard % QUAD) ^ (shard // QUAD % 2 * 2)
+    info = jnp.stack([shard, shard % QUAD, owner])
 
     (edge,) = call(
         edge_kernel,
@@ -376,7 +377,7 @@
         return [values[0], swapped[1], swapped[2], swapped[3]]
 
     def ahead(value):
-        return lax.ppermute(value, "seq", [(i, (i + QUAD) % peers) for i in range(peers)])
+        return lax.ppermute(value, "seq", [(i, (i + QUAD) % peers ^ 2) for i in range(peers)])
 
     early_args = [
         lengths, x_in, conv_x_weight, bx, dt_raw.T, dt_bias.reshape(1, heads), decay.reshape(1, heads),

time: 48.3 us -> 46.9 us (0.971)
  waiting for transfers between devices: 10.8 us -> 6.14 us
  starting transfers between devices: 19.1 us -> 22.3 us
    ppermute x12, waiting for transfers between devices: 7.15 us -> 3.88 us  [swap(): swapped = {k: lax.ppermute(values[k], 'seq', routes[k]) for k in (3, 1, 2)}]
    ppermute x2, starting transfers between devices: 3.49 us -> 5.39 us  [ahead(): lax.ppermute(value, 'seq', [(i, (i + QUAD) % peers ^ 2) for i in range(pe...]
    ppermute x12, starting transfers between devices: 12.6 us -> 13.9 us  [swap(): swapped = {k: lax.ppermute(values[k], 'seq', routes[k]) for k in (3, 1, 2)}]
    ppermute x2, waiting for transfers between devices: 2.5 us -> 1.17 us  [ahead(): lax.ppermute(value, 'seq', [(i, (i + QUAD) % peers ^ 2) for i in range(pe...]
  transfers between devices with their start and end apart: 15 -> 15, of which waited for: 7 -> 6; matrix products, arithmetic and copies ran while one was open for 0% -> 0% of each run, Pallas kernels for 29% -> 30%
where the time goes in v5:
time: 46.9 us; the launch traced here: 46.7 us
  starting transfers between devices  22.3 us (48%)
  Pallas kernels  17.9 us (38%)
  waiting for transfers between devices  6.14 us (13%)
    pallas_call x12, Pallas kernels, call(): pl.pallas_call(kernel, in_specs=[SMEM] * len(scalars) + more.pop('specs',...  17.9 us
    ppermute x12, starting transfers between devices, swap(): swapped = {k: lax.ppermute(values[k], 'seq', routes[k]) for k in (3, 1, 2)}  13.9 us
    ppermute x2, starting transfers between devices, ahead(): lax.ppermute(value, 'seq', [(i, (i + QUAD) % peers ^ 2) for i in range(pe...  5.39 us
    ppermute x12, waiting for transfers between devices, swap(): swapped = {k: lax.ppermute(values[k], 'seq', routes[k]) for k in (3, 1, 2)}  3.88 us
    ppermute x1, starting transfers between devices, shards(): lax.ppermute(edge, 'seq', [(i, (i + 1) % peers) for i in range(peers)])  3.02 us
    ppermute x2, waiting for transfers between devices, ahead(): lax.ppermute(value, 'seq', [(i, (i + QUAD) % peers ^ 2) for i in range(pe...  1.17 us
    ppermute x1, waiting for transfers between devices, shards(): lax.ppermute(edge, 'seq', [(i, (i + 1) % peers) for i in range(peers)])  1.09 us
  transfers between devices with their start and end apart: 15, of which 6 were waited for; matrix products, arithmetic and copies ran while one was open for 0% of the time, Pallas kernels for 30%

profile of v5, /device:TPU:0, one launch (start us, length us, event | category | flops | bytes accessed | tf_op | source)
XLA Modules:
  0.0 46.7 jit_solution(2375436952938281677)
XLA Ops:
  0.0 0.0 copy-start
  0.0 0.9 %shard_map.128 = bf16[8,4608]{1,0:T(8,128)(2,1)S(1)} custom-call(bf16[128,4096]{1,0:T(8,128)(2,1)} %x.1, bf16[128,2,256]{2,1,0:T(2,128)(2,1)} %bc.1), custom_call_target="tpu_custom_call" | custom-call | flops 1000000 | bytes 4194304 | tf_op jit(solution)/shard_map/pallas_call | solution.py:316
  0.9 3.0 %collective-permute-start = (bf16[8,4608]{1,0:T(8,128)(2,1)S(1)}, bf16[8,4608]{1,0:T(8,128)(2,1)S(1)}, u32[]{:S(2)}, u32[]{:S(2)}) collective-permute-start(bf16[8,4608]{1,0:T(8,128)(2,1)S(1)} %shard_map.128), channel_id=1, source_target_pairs={{0,2},{2,4},{4,6},{6,8},{8,10},{10,12},{12,14},{14,0},{1,3},{3,5},... | collective-permute-start | bytes 221192 | tf_op jit(solution)/shard_map/ppermute | solution.py:371
  3.9 0.1 pad_add_fusion.info
  4.0 0.0 copy-done
  4.0 4.2 %shard_map.127 = (bf16[128,4096]{1,0:T(8,128)(2,1)S(1)}, bf16[128,4096]{1,0:T(8,128)(2,1)S(1)}, bf16[16,4096]{1,0:T(8,128)(2,1)S(1)}, f32[16,4096]{1,0:T(8,128)S...) custom-call(s32[3]{0:T(128)S(1)} %pad_add_fusion.info, ...), custom_call_target="tpu_custom_call" | custom-call | flops 600000000 | bytes 4194304 | tf_op jit(solution)/shard_map/pallas_call | solution.py:316
  8.2 1.1 %collective-permute-done.halo = bf16[8,4608]{1,0:T(8,128)(2,1)S(1)} collective-permute-done((bf16[8,4608]{1,0:T(8,128)(2,1)S(1)}, bf16[8,4608]{1,0:T(8,128)(2,1)S(1)}, u32[]{:S(2)}, u32[]{:S(2)}) %collective-permute-start) | collective-permute-done | bytes 73760 | tf_op jit(solution)/shard_map/ppermute | solution.py:371
  9.3 1.1 %shard_map.133 = (bf16[136,512]{1,0:T(8,128)(2,1)S(1)}, bf16[136,512]{1,0:T(8,128)(2,1)S(1)}, bf16[136,512]{1,0:T(8,128)(2,1)S(1)}, bf16[136,512]{1,0:T(8,128)(2...) custom-call(s32[3]{0:T(128)S(1)} %pad_add_fusion.info, bf16[16,4096]{1,0:T(8,128)(2,1)S(1)} %get-tuple-element.49.top, ...), custom_call_target="tpu_custom_call" | custom-call | flops 100000000 | bytes 4194304 | tf_op jit(solution)/shard_map/pallas_call | solution.py:316
  10.5 0.5 %collective-permute-start.8 = (bf16[136,512]{1,0:T(8,128)(2,1)S(1)}, bf16[136,512]{1,0:T(8,128)(2,1)S(1)}, u32[]{:S(2)}, u32[]{:S(2)}) collective-permute-start(bf16[136,512]{1,0:T(8,128)(2,1)S(1)} %get-tuple-element.85), channel_id=1, source_target_pairs={{0,2},{2,0},{4,6},{6,4},{8,10},{10,8},{12,14},{14,12},{1,3},{3,1},... | collective-permute-start | bytes 417800 | tf_op jit(solution)/shard_map/ppermute | solution.py:376
  11.0 1.6 %collective-permute-start.9 = (bf16[136,512]{1,0:T(8,128)(2,1)S(1)}, bf16[136,512]{1,0:T(8,128)(2,1)S(1)}, u32[]{:S(2)}, u32[]{:S(2)}) collective-permute-start(bf16[136,512]{1,0:T(8,128)(2,1)S(1)} %get-tuple-element.86), channel_id=1, source_target_pairs={{0,4},{2,6},{4,0},{6,2},{8,12},{10,14},{12,8},{14,10},{1,5},{3,7},... | collective-permute-start | bytes 417800 | tf_op jit(solution)/shard_map/ppermute | solution.py:376
  12.6 1.5 %collective-permute-start.10 = (bf16[136,512]{1,0:T(8,128)(2,1)S(1)}, bf16[136,512]{1,0:T(8,128)(2,1)S(1)}, u32[]{:S(2)}, u32[]{:S(2)}) collective-permute-start(bf16[136,512]{1,0:T(8,128)(2,1)S(1)} %get-tuple-element.87), channel_id=1, source_target_pairs={{0,6},{2,4},{4,2},{6,0},{8,14},{10,12},{12,10},{14,8},{1,7},{3,5},... | collective-permute-start | bytes 417800 | tf_op jit(solution)/shard_map/ppermute | solution.py:376
  14.0 1.1 %shard_map.129 = (bf16[136,512]{1,0:T(8,128)(2,1)S(1)}, bf16[136,512]{1,0:T(8,128)(2,1)S(1)}, bf16[136,512]{1,0:T(8,128)(2,1)S(1)}, bf16[136,512]{1,0:T(8,128)(2...) custom-call(s32[3]{0:T(128)S(1)} %pad_add_fusion.info, bf16[16,4096]{1,0:T(8,128)(2,1)S(1)} %get-tuple-element.49.top, ...), custom_call_target="tpu_custom_call" | custom-call | flops 100000000 | bytes 4194304 | tf_op jit(solution)/shard_map/pallas_call | solution.py:316
  15.2 0.5 %collective-permute-start.1 = (bf16[136,512]{1,0:T(8,128)(2,1)S(1)}, bf16[136,512]{1,0:T(8,128)(2,1)S(1)}, u32[]{:S(2)}, u32[]{:S(2)}) collective-permute-start(bf16[136,512]{1,0:T(8,128)(2,1)S(1)} %get-tuple-element.69), channel_id=1, source_target_pairs={{0,2},{2,0},{4,6},{6,4},{8,10},{10,8},{12,14},{14,12},{1,3},{3,1},... | collective-permute-start | bytes 417800 | tf_op jit(solution)/shard_map/ppermute | solution.py:376
  15.7 1.6 %collective-permute-start.2 = (bf16[136,512]{1,0:T(8,128)(2,1)S(1)}, bf16[136,512]{1,0:T(8,128)(2,1)S(1)}, u32[]{:S(2)}, u32[]{:S(2)}) collective-permute-start(bf16[136,512]{1,0:T(8,128)(2,1)S(1)} %get-tuple-element.70), channel_id=1, source_target_pairs={{0,4},{2,6},{4,0},{6,2},{8,12},{10,14},{12,8},{14,10},{1,5},{3,7},... | collective-permute-start | bytes 417800 | tf_op jit(solution)/shard_map/ppermute | solution.py:376
  17.3 0.0 collective-permute-done.8.m1
  17.3 1.5 %collective-permute-start.3 = (bf16[136,512]{1,0:T(8,128)(2,1)S(1)}, bf16[136,512]{1,0:T(8,128)(2,1)S(1)}, u32[]{:S(2)}, u32[]{:S(2)}) collective-permute-start(bf16[136,512]{1,0:T(8,128)(2,1)S(1)} %get-tuple-element.71), channel_id=1, source_target_pairs={{0,6},{2,4},{4,2},{6,0},{8,14},{10,12},{12,10},{14,8},{1,7},{3,5},... | collective-permute-start | bytes 417800 | tf_op jit(solution)/shard_map/ppermute | solution.py:376
  18.7 2.1 %shard_map.134 = (f32[128,2048]{1,0:T(8,128)S(1)}, f32[128,2048]{1,0:T(8,128)S(1)}, bf16[128,128]{1,0:T(8,128)(2,1)S(1)}) custom-call(bf16[128,4096]{1,0:T(8,128)(2,1)S(1)} %get-tuple-element.59.xc_in, bf16[16,2048]{1,0:T(8,128)(2,1)S(1)} %get-tuple-element.79.xc_top, bf16[128,4096]{1,0:T(8,128)(2,1)} %z_in.3, bf16[128,512]{1,0:T(8,128)(2,1)S(1)} %bitcast.13, ...), custom_call_target="tpu_custom_call" | custom-call | flops 300000000 | bytes 4194304 | tf_op jit(solution)/shard_map/pallas_call | solution.py:316
  20.9 0.0 collective-permute-done.9.m2
  20.9 0.7 %collective-permute-done.10.m3 = bf16[136,512]{1,0:T(8,128)(2,1)S(1)} collective-permute-done((bf16[136,512]{1,0:T(8,128)(2,1)S(1)}, bf16[136,512]{1,0:T(8,128)(2,1)S(1)}, u32[]{:S(2)}, u32[]{:S(2)}) %collective-permute-start.10) | collective-permute-done | bytes 139296 | tf_op jit(solution)/shard_map/ppermute | solution.py:376
  21.5 0.7 %shard_map.135 = bf16[128,512]{1,0:T(8,128)(2,1)S(1)} custom-call(s32[3]{0:T(128)S(1)} %pad_add_fusion.info, bf16[136,512]{1,0:T(8,128)(2,1)S(1)} %get-tuple-element.84.m0, bf16[136,512]{1,0:T(8,128)(2,1)S(1)} %collective-permute-done.8.m1, bf16[136,512]{1,0:T(8,128)(2,1)S(1)} %collective-permute-done.9.m2, bf16[136,512]{1,0:T(8,128)(2,1)S(1)} %collective-permute-done.10.m3), custom_call_target="tpu_custom_call" | custom-call | flops 1000000 | bytes 4194304 | tf_op jit(solution)/shard_map/pallas_call | solution.py:316
  22.2 2.7 %collective-permute-start.11 = (bf16[128,512]{1,0:T(8,128)(2,1)S(1)}, bf16[128,512]{1,0:T(8,128)(2,1)S(1)}, u32[]{:S(2)}, u32[]{:S(2)}) collective-permute-start(bf16[128,512]{1,0:T(8,128)(2,1)S(1)} %shard_map.135), channel_id=1, source_target_pairs={{0,12},{2,14},{4,8},{6,10},{8,4},{10,6},{12,0},{14,2},{1,13},{3,15... | collective-permute-start | bytes 393224 | tf_op jit(solution)/shard_map/ppermute | solution.py:380
  24.9 2.2 %shard_map.130 = (f32[128,2048]{1,0:T(8,128)S(1)}, f32[128,2048]{1,0:T(8,128)S(1)}, bf16[128,128]{1,0:T(8,128)(2,1)S(1)}) custom-call(bf16[128,4096]{1,0:T(8,128)(2,1)S(1)} %get-tuple-element.59.xc_in, bf16[16,2048]{1,0:T(8,128)(2,1)S(1)} %get-tuple-element.60.xc_top, bf16[128,4096]{1,0:T(8,128)(2,1)} %z_in.3, bf16[128,512]{1,0:T(8,128)(2,1)S(1)} %bitcast.14, ...), custom_call_target="tpu_custom_call" | custom-call | flops 300000000 | bytes 4194304 | tf_op jit(solution)/shard_map/pallas_call | solution.py:316
  27.1 0.0 collective-permute-done.1.m1
  27.1 0.0 collective-permute-done.2.m2
  27.1 0.0 collective-permute-done.3.m3
  27.1 0.7 %shard_map.131 = bf16[128,512]{1,0:T(8,128)(2,1)S(1)} custom-call(s32[3]{0:T(128)S(1)} %pad_add_fusion.info, bf16[136,512]{1,0:T(8,128)(2,1)S(1)} %get-tuple-element.68.m0, bf16[136,512]{1,0:T(8,128)(2,1)S(1)} %collective-permute-done.1.m1, bf16[136,512]{1,0:T(8,128)(2,1)S(1)} %collective-permute-done.2.m2, bf16[136,512]{1,0:T(8,128)(2,1)S(1)} %collective-permute-done.3.m3), custom_call_target="tpu_custom_call" | custom-call | flops 1000000 | bytes 4194304 | tf_op jit(solution)/shard_map/pallas_call | solution.py:316
  27.8 2.7 %collective-permute-start.4 = (bf16[128,512]{1,0:T(8,128)(2,1)S(1)}, bf16[128,512]{1,0:T(8,128)(2,1)S(1)}, u32[]{:S(2)}, u32[]{:S(2)}) collective-permute-start(bf16[128,512]{1,0:T(8,128)(2,1)S(1)} %shard_map.131), channel_id=1, source_target_pairs={{0,12},{2,14},{4,8},{6,10},{8,4},{10,6},{12,0},{14,2},{1,13},{3,15... | collective-permute-start | bytes 393224 | tf_op jit(solution)/shard_map/ppermute | solution.py:380
  30.5 0.0 collective-permute-done.11.start
  30.5 0.7 %shard_map.136 = (bf16[128,512]{1,0:T(8,128)(2,1)S(1)}, bf16[128,512]{1,0:T(8,128)(2,1)S(1)}, bf16[128,512]{1,0:T(8,128)(2,1)S(1)}, bf16[128,512]{1,0:T(8,128)(2,1)S(1)}) custom-call(s32[3]{0:T(128)S(1)} %pad_add_fusion.info, bf16[128,512]{1,0:T(8,128)(2,1)S(1)} %collective-permute-done.11.start, bf16[136,512]{1,0:T(8,128)(2,1)S(1)} %get-tuple-element.84.m0, ...), custom_call_target="tpu_custom_call" | custom-call | flops 1000000 | bytes 4194304 | tf_op jit(solution)/shard_map/pallas_call | solution.py:316
  31.2 0.4 collective-permute-start.12
  31.6 2.5 %collective-permute-start.13 = (bf16[128,512]{1,0:T(8,128)(2,1)S(1)}, bf16[128,512]{1,0:T(8,128)(2,1)S(1)}, u32[]{:S(2)}, u32[]{:S(2)}) collective-permute-start(bf16[128,512]{1,0:T(8,128)(2,1)S(1)} %get-tuple-element.90), channel_id=1, source_target_pairs={{0,4},{2,6},{4,0},{6,2},{8,12},{10,14},{12,8},{14,10},{1,5},{3,7},... | collective-permute-start | bytes 393224 | tf_op jit(solution)/shard_map/ppermute | solution.py:376
  34.1 0.6 %collective-permute-start.14 = (bf16[128,512]{1,0:T(8,128)(2,1)S(1)}, bf16[128,512]{1,0:T(8,128)(2,1)S(1)}, u32[]{:S(2)}, u32[]{:S(2)}) collective-permute-start(bf16[128,512]{1,0:T(8,128)(2,1)S(1)} %get-tuple-element.91), channel_id=1, source_target_pairs={{0,6},{2,4},{4,2},{6,0},{8,14},{10,12},{12,10},{14,8},{1,7},{3,5},... | collective-permute-start | bytes 393224 | tf_op jit(solution)/shard_map/ppermute | solution.py:376
  34.7 1.2 %collective-permute-done.4.start = bf16[128,512]{1,0:T(8,128)(2,1)S(1)} collective-permute-done((bf16[128,512]{1,0:T(8,128)(2,1)S(1)}, bf16[128,512]{1,0:T(8,128)(2,1)S(1)}, u32[]{:S(2)}, u32[]{:S(2)}) %collective-permute-start.4) | collective-permute-done | bytes 131104 | tf_op jit(solution)/shard_map/ppermute | solution.py:380
  35.9 0.7 %shard_map.132 = (bf16[128,512]{1,0:T(8,128)(2,1)S(1)}, bf16[128,512]{1,0:T(8,128)(2,1)S(1)}, bf16[128,512]{1,0:T(8,128)(2,1)S(1)}, bf16[128,512]{1,0:T(8,128)(2,1)S(1)}) custom-call(s32[3]{0:T(128)S(1)} %pad_add_fusion.info, bf16[128,512]{1,0:T(8,128)(2,1)S(1)} %collective-permute-done.4.start, bf16[136,512]{1,0:T(8,128)(2,1)S(1)} %get-tuple-element.68.m0, ...), custom_call_target="tpu_custom_call" | custom-call | flops 1000000 | bytes 4194304 | tf_op jit(solution)/shard_map/pallas_call | solution.py:316
  36.6 0.1 collective-permute-start.5
  36.7 1.6 %collective-permute-start.6 = (bf16[128,512]{1,0:T(8,128)(2,1)S(1)}, bf16[128,512]{1,0:T(8,128)(2,1)S(1)}, u32[]{:S(2)}, u32[]{:S(2)}) collective-permute-start(bf16[128,512]{1,0:T(8,128)(2,1)S(1)} %get-tuple-element.74), channel_id=1, source_target_pairs={{0,4},{2,6},{4,0},{6,2},{8,12},{10,14},{12,8},{14,10},{1,5},{3,7},... | collective-permute-start | bytes 393224 | tf_op jit(solution)/shard_map/ppermute | solution.py:376
  38.3 0.3 collective-permute-done.12.e1
  38.6 1.5 %collective-permute-start.7 = (bf16[128,512]{1,0:T(8,128)(2,1)S(1)}, bf16[128,512]{1,0:T(8,128)(2,1)S(1)}, u32[]{:S(2)}, u32[]{:S(2)}) collective-permute-start(bf16[128,512]{1,0:T(8,128)(2,1)S(1)} %get-tuple-element.75), channel_id=1, source_target_pairs={{0,6},{2,4},{4,2},{6,0},{8,14},{10,12},{12,10},{14,8},{1,7},{3,5},... | collective-permute-start | bytes 393224 | tf_op jit(solution)/shard_map/ppermute | solution.py:376
  40.2 0.0 collective-permute-done.13.e2
  40.2 1.7 %collective-permute-done.14.e3 = bf16[128,512]{1,0:T(8,128)(2,1)S(1)} collective-permute-done((bf16[128,512]{1,0:T(8,128)(2,1)S(1)}, bf16[128,512]{1,0:T(8,128)(2,1)S(1)}, u32[]{:S(2)}, u32[]{:S(2)}) %collective-permute-start.14) | collective-permute-done | bytes 131104 | tf_op jit(solution)/shard_map/ppermute | solution.py:376
  41.9 1.8 %shard_map.137.rest_0_ = bf16[128,4096]{1,0:T(8,128)(2,1)} custom-call(s32[3]{0:T(128)S(1)} %pad_add_fusion.info, f32[128,2048]{1,0:T(8,128)S(1)} %get-tuple-element.82.near, f32[128,2048]{1,0:T(8,128)S(1)} %get-tuple-element.83.gain, bf16[128,512]{1,0:T(8,128)(2,1)S(1)} %get-tuple-element.88.e0, bf16[128,512]{1,0:T(8,128)(2,1)S(1)} %collective-permute-done.12.e1, ...), custom_call_target="tpu_custom_call" | custom-call | flops 100000000 | bytes 4194304 | tf_op jit(solution)/shard_map/pallas_call | solution.py:316
  43.7 0.0 collective-permute-done.5.e1
  43.7 0.0 collective-permute-done.6.e2
  43.7 1.2 %collective-permute-done.7.e3 = bf16[128,512]{1,0:T(8,128)(2,1)S(1)} collective-permute-done((bf16[128,512]{1,0:T(8,128)(2,1)S(1)}, bf16[128,512]{1,0:T(8,128)(2,1)S(1)}, u32[]{:S(2)}, u32[]{:S(2)}) %collective-permute-start.7) | collective-permute-done | bytes 131104 | tf_op jit(solution)/shard_map/ppermute | solution.py:376
  44.9 1.8 %shard_map.138 = bf16[128,4096]{1,0:T(8,128)(2,1)} custom-call(s32[3]{0:T(128)S(1)} %pad_add_fusion.info, f32[128,2048]{1,0:T(8,128)S(1)} %get-tuple-element.66.near, f32[128,2048]{1,0:T(8,128)S(1)} %get-tuple-element.67.gain, bf16[128,512]{1,0:T(8,128)(2,1)S(1)} %get-tuple-element.72.e0, ...), custom_call_target="tpu_custom_call", output_to_operand_aliasing={{}: (9, {})} | custom-call | flops 100000000 | bytes 4194304 | tf_op jit(solution)/shard_map/pallas_call | solution.py:316
  (1 shorter events, 0.0 us)
Async XLA Ops:
  0.0 4.0 %copy-start = (bf16[128,2,256]{2,1,0:T(2,128)(2,1)S(1)}, bf16[128,2,256]{2,1,0:T(2,128)(2,1)}, u32[]{:S(2)}) copy-start(bf16[128,2,256]{2,1,0:T(2,128)(2,1)} %bc.1) | copy-start | bytes 393220
  0.9 8.4 %collective-permute-start = (bf16[8,4608]{1,0:T(8,128)(2,1)S(1)}, bf16[8,4608]{1,0:T(8,128)(2,1)S(1)}, u32[]{:S(2)}, u32[]{:S(2)}) collective-permute-start(bf16[8,4608]{1,0:T(8,128)(2,1)S(1)} %shard_map.128), channel_id=1, source_target_pairs={{0,2},{2,4},{4,6},{6,8},{8,10},{10,12},{12,14},{14,0},{1,3},{3,5},... | collective-permute-start | bytes 221192 | tf_op jit(solution)/shard_map/ppermute | solution.py:371
  10.5 6.8 %collective-permute-start.8 = (bf16[136,512]{1,0:T(8,128)(2,1)S(1)}, bf16[136,512]{1,0:T(8,128)(2,1)S(1)}, u32[]{:S(2)}, u32[]{:S(2)}) collective-permute-start(bf16[136,512]{1,0:T(8,128)(2,1)S(1)} %get-tuple-element.85), channel_id=1, source_target_pairs={{0,2},{2,0},{4,6},{6,4},{8,10},{10,8},{12,14},{14,12},{1,3},{3,1},... | collective-permute-start | bytes 417800 | tf_op jit(solution)/shard_map/ppermute | solution.py:376
  11.0 9.9 %collective-permute-start.9 = (bf16[136,512]{1,0:T(8,128)(2,1)S(1)}, bf16[136,512]{1,0:T(8,128)(2,1)S(1)}, u32[]{:S(2)}, u32[]{:S(2)}) collective-permute-start(bf16[136,512]{1,0:T(8,128)(2,1)S(1)} %get-tuple-element.86), channel_id=1, source_target_pairs={{0,4},{2,6},{4,0},{6,2},{8,12},{10,14},{12,8},{14,10},{1,5},{3,7},... | collective-permute-start | bytes 417800 | tf_op jit(solution)/shard_map/ppermute | solution.py:376
  12.6 9.0 %collective-permute-start.10 = (bf16[136,512]{1,0:T(8,128)(2,1)S(1)}, bf16[136,512]{1,0:T(8,128)(2,1)S(1)}, u32[]{:S(2)}, u32[]{:S(2)}) collective-permute-start(bf16[136,512]{1,0:T(8,128)(2,1)S(1)} %get-tuple-element.87), channel_id=1, source_target_pairs={{0,6},{2,4},{4,2},{6,0},{8,14},{10,12},{12,10},{14,8},{1,7},{3,5},... | collective-permute-start | bytes 417800 | tf_op jit(solution)/shard_map/ppermute | solution.py:376
  15.2 11.9 %collective-permute-start.1 = (bf16[136,512]{1,0:T(8,128)(2,1)S(1)}, bf16[136,512]{1,0:T(8,128)(2,1)S(1)}, u32[]{:S(2)}, u32[]{:S(2)}) collective-permute-start(bf16[136,512]{1,0:T(8,128)(2,1)S(1)} %get-tuple-element.69), channel_id=1, source_target_pairs={{0,2},{2,0},{4,6},{6,4},{8,10},{10,8},{12,14},{14,12},{1,3},{3,1},... | collective-permute-start | bytes 417800 | tf_op jit(solution)/shard_map/ppermute | solution.py:376
  15.7 11.4 %collective-permute-start.2 = (bf16[136,512]{1,0:T(8,128)(2,1)S(1)}, bf16[136,512]{1,0:T(8,128)(2,1)S(1)}, u32[]{:S(2)}, u32[]{:S(2)}) collective-permute-start(bf16[136,512]{1,0:T(8,128)(2,1)S(1)} %get-tuple-element.70), channel_id=1, source_target_pairs={{0,4},{2,6},{4,0},{6,2},{8,12},{10,14},{12,8},{14,10},{1,5},{3,7},... | collective-permute-start | bytes 417800 | tf_op jit(solution)/shard_map/ppermute | solution.py:376
  17.3 9.9 %collective-permute-start.3 = (bf16[136,512]{1,0:T(8,128)(2,1)S(1)}, bf16[136,512]{1,0:T(8,128)(2,1)S(1)}, u32[]{:S(2)}, u32[]{:S(2)}) collective-permute-start(bf16[136,512]{1,0:T(8,128)(2,1)S(1)} %get-tuple-element.71), channel_id=1, source_target_pairs={{0,6},{2,4},{4,2},{6,0},{8,14},{10,12},{12,10},{14,8},{1,7},{3,5},... | collective-permute-start | bytes 417800 | tf_op jit(solution)/shard_map/ppermute | solution.py:376
  22.2 8.3 %collective-permute-start.11 = (bf16[128,512]{1,0:T(8,128)(2,1)S(1)}, bf16[128,512]{1,0:T(8,128)(2,1)S(1)}, u32[]{:S(2)}, u32[]{:S(2)}) collective-permute-start(bf16[128,512]{1,0:T(8,128)(2,1)S(1)} %shard_map.135), channel_id=1, source_target_pairs={{0,12},{2,14},{4,8},{6,10},{8,4},{10,6},{12,0},{14,2},{1,13},{3,15... | collective-permute-start | bytes 393224 | tf_op jit(solution)/shard_map/ppermute | solution.py:380
  27.8 8.1 %collective-permute-start.4 = (bf16[128,512]{1,0:T(8,128)(2,1)S(1)}, bf16[128,512]{1,0:T(8,128)(2,1)S(1)}, u32[]{:S(2)}, u32[]{:S(2)}) collective-permute-start(bf16[128,512]{1,0:T(8,128)(2,1)S(1)} %shard_map.131), channel_id=1, source_target_pairs={{0,12},{2,14},{4,8},{6,10},{8,4},{10,6},{12,0},{14,2},{1,13},{3,15... | collective-permute-start | bytes 393224 | tf_op jit(solution)/shard_map/ppermute | solution.py:380
  31.2 7.5 %collective-permute-start.12 = (bf16[128,512]{1,0:T(8,128)(2,1)S(1)}, bf16[128,512]{1,0:T(8,128)(2,1)S(1)}, u32[]{:S(2)}, u32[]{:S(2)}) collective-permute-start(bf16[128,512]{1,0:T(8,128)(2,1)S(1)} %get-tuple-element.89), channel_id=1, source_target_pairs={{0,2},{2,0},{4,6},{6,4},{8,10},{10,8},{12,14},{14,12},{1,3},{3,1},... | collective-permute-start | bytes 393224 | tf_op jit(solution)/shard_map/ppermute | solution.py:376
  31.6 8.6 %collective-permute-start.13 = (bf16[128,512]{1,0:T(8,128)(2,1)S(1)}, bf16[128,512]{1,0:T(8,128)(2,1)S(1)}, u32[]{:S(2)}, u32[]{:S(2)}) collective-permute-start(bf16[128,512]{1,0:T(8,128)(2,1)S(1)} %get-tuple-element.90), channel_id=1, source_target_pairs={{0,4},{2,6},{4,0},{6,2},{8,12},{10,14},{12,8},{14,10},{1,5},{3,7},... | collective-permute-start | bytes 393224 | tf_op jit(solution)/shard_map/ppermute | solution.py:376
  34.1 7.8 %collective-permute-start.14 = (bf16[128,512]{1,0:T(8,128)(2,1)S(1)}, bf16[128,512]{1,0:T(8,128)(2,1)S(1)}, u32[]{:S(2)}, u32[]{:S(2)}) collective-permute-start(bf16[128,512]{1,0:T(8,128)(2,1)S(1)} %get-tuple-element.91), channel_id=1, source_target_pairs={{0,6},{2,4},{4,2},{6,0},{8,14},{10,12},{12,10},{14,8},{1,7},{3,5},... | collective-permute-start | bytes 393224 | tf_op jit(solution)/shard_map/ppermute | solution.py:376
  36.6 7.1 %collective-permute-start.5 = (bf16[128,512]{1,0:T(8,128)(2,1)S(1)}, bf16[128,512]{1,0:T(8,128)(2,1)S(1)}, u32[]{:S(2)}, u32[]{:S(2)}) collective-permute-start(bf16[128,512]{1,0:T(8,128)(2,1)S(1)} %get-tuple-element.73), channel_id=1, source_target_pairs={{0,2},{2,0},{4,6},{6,4},{8,10},{10,8},{12,14},{14,12},{1,3},{3,1},... | collective-permute-start | bytes 393224 | tf_op jit(solution)/shard_map/ppermute | solution.py:376
  36.7 6.9 %collective-permute-start.6 = (bf16[128,512]{1,0:T(8,128)(2,1)S(1)}, bf16[128,512]{1,0:T(8,128)(2,1)S(1)}, u32[]{:S(2)}, u32[]{:S(2)}) collective-permute-start(bf16[128,512]{1,0:T(8,128)(2,1)S(1)} %get-tuple-element.74), channel_id=1, source_target_pairs={{0,4},{2,6},{4,0},{6,2},{8,12},{10,14},{12,8},{14,10},{1,5},{3,7},... | collective-permute-start | bytes 393224 | tf_op jit(solution)/shard_map/ppermute | solution.py:376
  38.6 6.2 %collective-permute-start.7 = (bf16[128,512]{1,0:T(8,128)(2,1)S(1)}, bf16[128,512]{1,0:T(8,128)(2,1)S(1)}, u32[]{:S(2)}, u32[]{:S(2)}) collective-permute-start(bf16[128,512]{1,0:T(8,128)(2,1)S(1)} %get-tuple-element.75), channel_id=1, source_target_pairs={{0,6},{2,4},{4,2},{6,0},{8,14},{10,12},{12,10},{14,8},{1,7},{3,5},... | collective-permute-start | bytes 393224 | tf_op jit(solution)/shard_map/ppermute | solution.py:376

commit v6 on v5

v6 whole, which is shorter than its diff:
```python
import functools

import jax
import jax.numpy as jnp
from jax import lax
from jax.experimental import pallas as pl
from jax.experimental.pallas import tpu as pltpu
from jax.sharding import PartitionSpec as P

HEAD_DIM = 64
STATE = 128
BLOCK = 128
QUAD = 4
HALO = 8
TILE = 8
EXTRA = 16
FIRST = 16
F32 = jnp.float32
BF16 = jnp.bfloat16


def mm(left, right):
    return jnp.dot(left, right, preferred_element_type=F32)


def ends_of(lens_ref):
    total = 0
    ends = []
    for i in range(lens_ref.shape[0]):
        total = total + lens_ref[i]
        ends.append(total)
    return ends


def seg_of(pos, ends):
    count = 0
    for end in ends:
        count = count + jnp.where(end <= pos, 1, 0)
    return jnp.where(pos >= 0, count, -1)


def tokens(start, shape, dim):
    return start + lax.broadcasted_iota(jnp.int32, shape, dim)


def shift_matrix(start, ends, rows, before, taps):
    shape = (rows, before + rows)
    row = lax.broadcasted_iota(jnp.int32, shape, 0)
    col = lax.broadcasted_iota(jnp.int32, shape, 1)
    same = seg_of(start + row, ends) == seg_of(start - before + col, ends)
    parts = []
    for k in range(taps - 1):
        parts.append(jnp.where((col == row + (before - taps + 1 + k)) & same, 1.0, 0.0))
    return jnp.concatenate(parts, axis=0).astype(BF16)


def conv_half(shift, extended, block, weight, bias):
    rows = block.shape[0]
    taps = weight.shape[0]
    half = weight.astype(F32) * 0.5
    moved = mm(shift, extended)
    total = bias * 0.5 + block.astype(F32) * half[taps - 1 : taps]
    for k in range(taps - 1):
        total = total + moved[k * rows : (k + 1) * rows] * half[k : k + 1]
    return total


def silu_of_half(half):
    return half + half * jnp.tanh(half)


def rates_of(dt_ref, dtb_ref, dec_ref):
    raw = jnp.transpose(dt_ref[...].astype(F32)) + dtb_ref[...]
    rate = jnp.maximum(raw, 0.0) + jnp.log1p(jnp.exp(-jnp.abs(raw)))
    shape = (BLOCK, BLOCK)
    lower = lax.broadcasted_iota(jnp.int32, shape, 0) >= lax.broadcasted_iota(jnp.int32, shape, 1)
    cum = jnp.dot(
        jnp.where(lower, 1.0, 0.0),
        -rate * dec_ref[...],
        precision=lax.Precision.HIGHEST,
        preferred_element_type=F32,
    )
    return rate, cum


def head_map(heads, first, width):
    shape = (heads, width)
    row = lax.broadcasted_iota(jnp.int32, shape, 0)
    col = lax.broadcasted_iota(jnp.int32, shape, 1)
    return jnp.where(row == first + col // HEAD_DIM, 1.0, 0.0).astype(BF16)


def pair_of(value):
    high = value.astype(BF16)
    low = (value - high.astype(F32)).astype(BF16)
    return jnp.concatenate([high, low], axis=1)


def twice(onehot):
    return jnp.concatenate([onehot, onehot], axis=0)


def next_matrix(start, ends, taps):
    shape = (TILE, BLOCK)
    row = lax.broadcasted_iota(jnp.int32, shape, 0)
    col = lax.broadcasted_iota(jnp.int32, shape, 1)
    same = seg_of(start + BLOCK + row, ends) == seg_of(start + col, ends)
    parts = []
    for k in range(taps - 1):
        parts.append(jnp.where((col == row + (BLOCK - taps + 1 + k)) & same, 1.0, 0.0))
    return jnp.concatenate(parts, axis=0).astype(BF16)


def conv_both(moves, block, weight, bias):
    taps = weight.shape[0]
    half = weight.astype(F32) * 0.5
    moved = mm(moves, block)
    total = bias * 0.5 + block.astype(F32) * half[taps - 1 : taps]
    after = 0.0
    base = (taps - 1) * BLOCK
    for k in range(taps - 1):
        total = total + moved[k * BLOCK : (k + 1) * BLOCK] * half[k : k + 1]
        after = after + moved[base + k * TILE : base + (k + 1) * TILE] * half[k : k + 1]
    return total, after


def bc_weight(which, lane, wbc):
    return jnp.concatenate([wbc[k].astype(F32)[which : which + 1, lane] for k in range(wbc.shape[0])], axis=0)


def send_states(g, mine, x, bc, wx, bx, wbc, bbc, moves, factor, carry, xc_out, msgs, held):
    taps = wx.shape[0]
    chan = x.shape[1]
    wide = xc_out.shape[1]
    heads = carry.shape[1] // 2
    width = wide // QUAD
    lane = slice(g * STATE, (g + 1) * STATE)
    btotal, bafter = conv_both(moves[...], bc[:, lane], bc_weight(0, lane, wbc), bbc[0:1, lane])
    bmat = silu_of_half(btotal)
    bmat = jnp.where(tokens(0, bmat.shape, 0) >= taps - 1, bmat, 0.0)
    bmat_t = jnp.transpose(bmat).astype(BF16)
    bparts = jnp.concatenate([btotal[0:TILE], bafter] + [jnp.zeros_like(bafter)] * (width // STATE - 2), axis=1)
    bparts = pltpu.roll(bparts, taps - 1, 0)
    step = 1024
    for at in range(0, wide, step):
        here = slice(at, at + step)
        deep = slice(g * wide + at, g * wide + at + step)
        onehot2 = twice(head_map(heads, (g * wide + at) // HEAD_DIM, step))
        total, after = conv_both(moves[...], x[:, deep], wx[:, deep], bx[:, deep])
        xc = silu_of_half(total).astype(BF16)
        xc_out[:, here] = xc
        spread = mm(factor[...], onehot2)
        held[0:STATE, here] = mm(bmat_t, (xc.astype(F32) * spread).astype(BF16)).astype(BF16)
        row = lax.broadcasted_iota(jnp.int32, (TILE, step), 0)
        passed = mm(carry[...], onehot2[0 : 2 * heads])
        high = passed.astype(BF16).astype(F32)
        upper = jnp.where(row < 2 + taps - 1, pltpu.roll(total[0:TILE], 2, 0), pltpu.roll(after, 1 + taps, 0))
        upper = jnp.where(row == 0, high, jnp.where(row == 1, passed - high, upper))
        lower = jnp.where(row < taps - 1, spread[0:TILE], jnp.concatenate([bparts] * (step // width), axis=1))
        held[STATE : STATE + EXTRA, here] = jnp.concatenate([upper, lower], axis=0).astype(BF16)
    for k, msg in enumerate(msgs):
        msg[...] = held[:, pl.ds(pl.multiple_of((mine ^ k) * width, width), width)]


def first_kernel(
    info, lens_in, x_in, bc_in, wx_in, bx_in, dt_in, dtb_in, dec_in, wbc_in, bbc_in, skip_in, scale_in,
    x, bc, moves, shift, mask, factors, factor, carry, wx, bx, wbc, bbc, skip, scale, xc_out, m0, m1, m2, m3,
    lens, raw, dt, dtb, dec, held, sems,
):
    heads = dt.shape[0]
    wide = xc_out.shape[1]
    inner = bc.shape[1] // 2
    pairs = [
        (lens_in, lens), (dt_in, dt), (dtb_in, dtb), (dec_in, dec), (bc_in, raw), (wx_in, wx), (bx_in, bx),
        (wbc_in, wbc), (bbc_in, bbc), (x_in.at[:, 0:wide], x.at[:, 0:wide]), (x_in.at[:, wide:], x.at[:, wide:]),
        (skip_in, skip), (scale_in, scale),
    ]
    copies = [pltpu.make_async_copy(src, dst, sems.at[i]) for i, (src, dst) in enumerate(pairs)]
    for copy in copies:
        copy.start()
    for copy in copies[0:4]:
        copy.wait()
    start = info[0] * BLOCK
    taps = wx.shape[0]
    ends = ends_of(lens)
    moves[0 : (taps - 1) * BLOCK, :] = shift_matrix(start, ends, BLOCK, 0, taps)
    moves[(taps - 1) * BLOCK :, :] = next_matrix(start, ends, taps)
    shift[...] = shift_matrix(start, ends, BLOCK, HALO, taps)
    shape = (BLOCK, BLOCK)
    row = lax.broadcasted_iota(jnp.int32, shape, 0)
    col = lax.broadcasted_iota(jnp.int32, shape, 1)
    seg_row = seg_of(start + row, ends)
    mask[...] = jnp.where((row >= col) & (seg_row == seg_of(start + col, ends)), 1.0, 0.0)
    rate, cum = rates_of(dt, dtb, dec)
    last = cum[BLOCK - 1 : BLOCK]
    seg_last = seg_of(start + BLOCK - 1, ends)
    seg_head = seg_row[:, 0:heads]
    factor[...] = pair_of(jnp.where(seg_head == seg_last, jnp.exp(last - cum), 0.0) * rate)
    grown = jnp.exp(cum)
    before = seg_of(start - 1, ends)
    factors[:, 0 : 2 * heads] = pair_of(rate * jnp.exp(-cum))
    factors[:, 2 * heads : 4 * heads] = pair_of(grown)
    factors[:, 4 * heads : 6 * heads] = pair_of(jnp.where(seg_head == before, grown, 0.0))
    passed = jnp.where(seg_last == before, jnp.exp(last), 0.0)
    carry[...] = pair_of(jnp.broadcast_to(passed, (TILE, heads)))
    for copy in copies[4:9]:
        copy.wait()
    value = raw[...].astype(F32)
    for i in range(2):
        bc[:, i * inner : (i + 1) * inner] = value[:, i, :].astype(BF16)
    copies[9].wait()
    send_states(0, info[2], x, bc, wx, bx, wbc, bbc, moves, factor, carry, xc_out, (m0, m1, m2, m3), held)
    for copy in copies[10:]:
        copy.wait()


def other_kernel(g, info, x, bc, wx, bx, wbc, bbc, moves, factor, carry, xc_out, edge, m0, m1, m2, m3, held):
    send_states(g, info[2], x, bc, wx, bx, wbc, bbc, moves, factor, carry, xc_out, (m0, m1, m2, m3), held)
    rows, chan = x.shape
    edge[:, 0:chan] = x[rows - HALO : rows, :]
    edge[:, chan:] = bc[rows - HALO : rows, :]


def extra_of(msg):
    value = msg[STATE : STATE + EXTRA, :].astype(F32)
    return value[0:TILE], value[TILE:EXTRA]


def top_state(taps, here, prior):
    upper, lower = here
    total = pltpu.roll(upper, TILE - 2, 0)
    btotal = pltpu.roll(lower[:, 0:STATE], TILE - taps + 1, 0)
    if prior is not None:
        total = total + pltpu.roll(prior[0], TILE - 1 - taps, 0)
        btotal = btotal + pltpu.roll(prior[1][:, STATE : 2 * STATE], TILE - taps + 1, 0)
    xc = silu_of_half(total).astype(BF16).astype(F32)
    scaled = jnp.where(tokens(0, xc.shape, 0) < taps - 1, xc * lower, 0.0)
    bmat = jnp.where(tokens(0, btotal.shape, 0) < taps - 1, silu_of_half(btotal), 0.0)
    scaled = jnp.concatenate([scaled, jnp.zeros_like(scaled)], axis=0).astype(BF16)
    bmat = jnp.concatenate([bmat, jnp.zeros_like(bmat)], axis=0).astype(BF16)
    return lax.dot_general(bmat, scaled, (((0,), (0,)), ((), ())), preferred_element_type=F32)


def carry_row(extra):
    return extra[0][0:1] + extra[0][1:2]


def fold_kernel(taps, more, info, *refs):
    msgs, rest = refs[0:QUAD], refs[QUAD:]
    total, fixed = rest[more], rest[more + 1]
    for mine in range(QUAD):

        @pl.when(info[1] == mine)
        def _():
            block = [msgs[mine ^ b] for b in range(QUAD)]
            extra = [extra_of(msg) for msg in block]
            prior = extra_of(rest[0]) if more else None
            state = block[0][0:STATE, :].astype(F32) + top_state(taps, extra[0], prior)
            through = carry_row(extra[0])
            for b in range(1, QUAD):
                own = block[b][0:STATE, :].astype(F32) + top_state(taps, extra[b], extra[b - 1])
                if b < QUAD - 1:
                    fixed[(b - 1) * STATE : b * STATE, :] = own.astype(BF16)
                state = own + carry_row(extra[b]) * state
                through = through * carry_row(extra[b])
            total[0:STATE, :] = state.astype(BF16)
            total[STATE : STATE + EXTRA, :] = block[QUAD - 1][STATE : STATE + EXTRA, :]
            for out in rest[more + 2 :]:
                out[...] = jnp.broadcast_to(through, out.shape)


def enter_kernel(taps, info, start, fixed, m0, m1, m2, m3, o0, o1, o2, o3):
    msgs = (m0, m1, m2, m3)
    outs = (o0, o1, o2, o3)
    prior = extra_of(start)
    for mine in range(QUAD):

        @pl.when(info[1] == mine)
        def _():
            outs[mine][...] = start[0:STATE, :]
            head = extra_of(msgs[mine])
            state = msgs[mine][0:STATE, :].astype(F32) + top_state(taps, head, prior)
            state = state + carry_row(head) * start[0:STATE, :].astype(F32)
            outs[mine ^ 1][...] = state.astype(BF16)
            for b in range(2, QUAD):
                own = fixed[(b - 2) * STATE : (b - 1) * STATE, :].astype(F32)
                state = own + carry_row(extra_of(msgs[mine ^ (b - 1)])) * state
                outs[mine ^ b][...] = state.astype(BF16)


def joined(above, below):
    return jnp.concatenate([above.astype(F32), below.astype(F32)], axis=0).astype(BF16)


def bc_conv(which, g, shift, halo, bc, wbc, bbc):
    inner = wbc.shape[2]
    chan = halo.shape[1] - 2 * inner
    base = which * inner + g * STATE
    lane = slice(g * STATE, (g + 1) * STATE)
    block = bc[:, base : base + STATE]
    ext = joined(halo[:, chan + base : chan + base + STATE], block)
    half = conv_half(shift[...], ext, block, bc_weight(which, lane, wbc), bbc[which : which + 1, lane])
    return silu_of_half(half).astype(BF16)


def inner_kernel(
    g, xc_in, x, z_in, bc, halo, wx, bx, wbc, bbc, shift, mask, factors, skip, near, gain, c_out, z, sem
):
    wide = xc_in.shape[1]
    copy = pltpu.make_async_copy(z_in.at[:, g * wide : (g + 1) * wide], z, sem)
    copy.start()
    heads = skip.shape[1]
    taps = wx.shape[0]
    cmat = bc_conv(1, g, shift, halo, bc, wbc, bbc)
    c_out[...] = cmat
    bmat = bc_conv(0, g, shift, halo, bc, wbc, bbc)
    scores = lax.dot_general(cmat, bmat, (((1,), (1,)), ((), ())), preferred_element_type=F32)
    scores = (scores * mask[...]).astype(BF16)
    skips = pair_of(jnp.broadcast_to(skip[...], (8, heads)))
    cols = slice(0, HALO + FIRST)
    moves = jnp.concatenate([shift[k * BLOCK : k * BLOCK + FIRST, cols] for k in range(taps - 1)], axis=0)
    step = 1024
    copy.wait()
    for at in range(0, wide, step):
        lane = slice(at, at + step)
        deep = slice(g * wide + at, g * wide + at + step)
        onehot2 = twice(head_map(heads, (g * wide + at) // HEAD_DIM, step))
        top = x[0:FIRST, deep]
        xc_top = silu_of_half(conv_half(moves, joined(halo[:, deep], top), top, wx[:, deep], bx[:, deep]))
        xf = jnp.concatenate([xc_top.astype(BF16), xc_in[FIRST:, lane]], axis=0).astype(F32)
        scaled = (xf * mm(factors[:, 0 : 2 * heads], onehot2)).astype(BF16)
        grown = mm(factors[:, 2 * heads : 4 * heads], onehot2)
        skip_c = mm(skips, onehot2)[0:1]
        gate = silu_of_half(z[:, lane].astype(F32) * 0.5)
        near[:, lane] = (mm(scores, scaled) * grown + skip_c * xf) * gate
        gain[:, lane] = mm(factors[:, 4 * heads : 6 * heads], onehot2) * gate


def finish_kernel(g, info, near, gain, e0, e1, e2, e3, cmat, scale, *rest):
    out, ready, held, sems = rest[-4:]
    mine = info[2]
    rows, wide = near.shape
    width = wide // QUAD
    steps = sems.shape[0]
    part = rows // steps
    square = [0.0] * steps
    ats = [pl.ds(pl.multiple_of((mine ^ k) * width, width), width) for k in range(QUAD)]
    c = cmat[...]
    for at, e in zip(ats, (e0, e1, e2, e3)):
        far = mm(c, e[...])
        for i in range(steps):
            these = slice(i * part, (i + 1) * part)
            value = near[these, at] + gain[these, at] * far[these]
            square[i] = square[i] + jnp.sum(value * value, axis=1, keepdims=True)
            held[these, at] = value
    copies = []
    for i in range(steps):
        these = slice(i * part, (i + 1) * part)
        inv = lax.rsqrt(square[i] * (1.0 / wide) + 1e-05)
        ready[these, :] = (held[these, :] * inv * scale[:, g * wide : (g + 1) * wide]).astype(BF16)
        copy = pltpu.make_async_copy(ready.at[these, :], out.at[these, g * wide : (g + 1) * wide], sems.at[i])
        copy.start()
        copies.append(copy)
    for copy in copies:
        copy.wait()


SMEM = pl.BlockSpec(memory_space=pltpu.SMEM)
VMEM = pl.BlockSpec(memory_space=pltpu.VMEM)
ANY = pl.BlockSpec(memory_space=pl.ANY)
HBM = pl.BlockSpec(memory_space=pltpu.HBM)


def call(kernel, scalars, args, outs, flops, limit=32 << 20, **more):
    pinned = more.get("specs", ())
    args = [
        pltpu.with_memory_space_constraint(arg, pltpu.HBM) if i < len(pinned) and pinned[i] is HBM else arg
        for i, arg in enumerate(args)
    ]
    return pl.pallas_call(
        kernel,
        in_specs=[SMEM] * len(scalars) + more.pop("specs", [VMEM] * len(args)),
        out_specs=more.pop("out_specs", [VMEM] * len(outs)),
        out_shape=[jax.ShapeDtypeStruct(*out) for out in outs],
        cost_estimate=pl.CostEstimate(flops=flops, bytes_accessed=4 << 20, transcendentals=0),
        compiler_params=pltpu.CompilerParams(vmem_limit_bytes=limit),
        **more,
    )(*scalars, *args)


def tie(first, second):
    return lax.optimization_barrier((first, second))


def shards(
    x_in,
    z_in,
    bc_in,
    conv_x_weight,
    conv_x_bias,
    conv_bc_weight,
    conv_bc_bias,
    dt_raw,
    dt_bias,
    decay,
    skip_d,
    norm_gain,
    lengths,
):
    rows, chan = x_in.shape
    heads = dt_raw.shape[1]
    peers = lax.axis_size("seq")
    shard = lax.axis_index("seq").astype(jnp.int32)
    taps = conv_x_weight.shape[0]
    bcw = bc_in.shape[2]
    groups = bcw // STATE
    wide = chan // groups
    width = wide // QUAD
    reach = peers // 2 // QUAD

    bx = conv_x_bias.reshape(1, chan)
    scale = norm_gain.reshape(1, chan)
    owner = (shard % QUAD) ^ (shard // QUAD % 2 * 2)
    info = jnp.stack([shard, shard % QUAD, owner])

    def swap(values):
        routes = [[(i, i ^ k) for i in range(peers)] for k in range(QUAD)]
        swapped = {k: lax.ppermute(values[k], "seq", routes[k]) for k in (3, 1, 2)}
        return [values[0], swapped[1], swapped[2], swapped[3]]

    def ahead(value):
        return lax.ppermute(value, "seq", [(i, (i + QUAD) % peers ^ 2) for i in range(peers)])

    first_args = [
        lengths, x_in, bc_in, conv_x_weight, bx, dt_raw.T, dt_bias.reshape(1, heads), decay.reshape(1, heads),
        conv_bc_weight, conv_bc_bias, skip_d.reshape(1, heads), scale,
    ]
    sent = ((STATE + EXTRA, width), BF16)
    held = pltpu.VMEM((STATE + EXTRA, wide), BF16)
    x, bc, moves, shift, mask, factors, factor, carry, wx, bx, wbc, bbc, skip, scale, xc, *msg = call(
        first_kernel,
        [info],
        first_args,
        [
            ((rows, chan), BF16),
            ((rows, 2 * bcw), BF16),
            (((taps - 1) * (BLOCK + TILE), BLOCK), BF16),
            (((taps - 1) * BLOCK, HALO + BLOCK), BF16),
            ((BLOCK, BLOCK), F32),
            ((rows, 6 * heads), BF16),
            ((rows, 2 * heads), BF16),
            ((TILE, 2 * heads), BF16),
            ((taps, chan), BF16),
            ((1, chan), F32),
            ((taps, 2, bcw), BF16),
            ((2, bcw), F32),
            ((1, heads), F32),
            ((1, chan), F32),
            ((rows, wide), BF16),
            *[sent] * QUAD,
        ],
        600_000_000,
        specs=[HBM] * len(first_args),
        scratch_shapes=[
            pltpu.SMEM(lengths.shape, jnp.int32),
            pltpu.VMEM((rows, 2, bcw), BF16),
            pltpu.VMEM((heads, rows), BF16),
            pltpu.VMEM((1, heads), F32),
            pltpu.VMEM((1, heads), F32),
            held,
            pltpu.SemaphoreType.DMA((13,)),
        ],
    )
    xcs, msgs = [xc], [swap(msg)]
    for g in range(1, groups):
        xc, edge, *msg = call(
            functools.partial(other_kernel, g),
            [info],
            [x, bc, wx, bx, wbc, bbc, moves, factor, carry],
            [((rows, wide), BF16), ((HALO, chan + 2 * bcw), BF16), *[sent] * QUAD],
            300_000_000,
            scratch_shapes=[held],
        )
        xcs.append(xc)
        msgs.append(swap(msg))
    halo = lax.ppermute(edge, "seq", [(i, (i + 1) % peers) for i in range(peers)])

    local = []
    for g in range(groups):
        args = [xcs[g], x, z_in, bc, halo, wx, bx, wbc, bbc, shift, mask, factors, skip]
        outs = [((rows, wide), F32), ((rows, wide), F32), ((rows, STATE), BF16)]
        near = call(
            functools.partial(inner_kernel, g),
            [],
            args,
            outs,
            300_000_000,
            specs=[HBM if arg is z_in else VMEM for arg in args],
            scratch_shapes=[pltpu.VMEM((rows, wide), BF16), pltpu.SemaphoreType.DMA],
        )
        local.append(list(near))

    entering, fixes = [], []
    for g in range(groups):
        outs = [sent, (((QUAD - 2) * STATE, width), BF16)]
        args = list(msgs[g])
        if reach > 1:
            outs.append(((8, width), F32))
            args.append(ahead(lax.dynamic_index_in_dim(jnp.stack(args), shard % QUAD ^ (QUAD - 1), 0, False)))
        total, fixed, *through = call(
            functools.partial(fold_kernel, taps, len(args) - QUAD), (info,), args, outs, 1_000_000
        )
        state = ahead(total)
        for _ in range(reach - 1):
            own = total[0:STATE].astype(F32) + through[0][0:1] * state[0:STATE].astype(F32)
            state = ahead(jnp.concatenate([own.astype(BF16), total[STATE:]], axis=0))
        entering.append(state)
        fixes.append(fixed)

    blocks = []
    for g in range(groups):
        outs = [((STATE, width), BF16)] * QUAD
        kernel = functools.partial(enter_kernel, taps)
        blocks.append(swap(call(kernel, (info,), [entering[g], fixes[g], *msgs[g]], outs, 1_000_000)))

    out = None
    for g in range(groups):
        near, gain, cmat = local[g]
        args = [near, gain, *blocks[g], cmat, scale]
        specs = [VMEM] * len(args)
        aliases = {}
        if out is not None:
            aliases = {1 + len(args): 0}
            args.append(out)
            specs.append(ANY)
        (out,) = call(
            functools.partial(finish_kernel, g),
            (info,),
            args,
            [((rows, chan), BF16)],
            100_000_000,
            specs=specs,
            out_specs=[ANY],
            scratch_shapes=[
                pltpu.VMEM((rows, wide), BF16),
                pltpu.VMEM((rows, wide), F32),
                pltpu.SemaphoreType.DMA((4,)),
            ],
            input_output_aliases=aliases,
        )
    return out


def solution(mesh):
    return jax.shard_map(
        shards,
        mesh=mesh,
        in_specs=(
            P(("groups", "seq"), "heads"),
            P(("groups", "seq"), "heads"),
            P(("groups", "seq"), None, "heads"),
            P(None, "heads"),
            P("heads"),
            P(None, None, "heads"),
            P(None, "heads"),
            P(("groups", "seq"), "heads"),
            P("heads"),
            P("heads"),
            P("heads"),
            P("heads"),
            P("groups"),
        ),
        out_specs=P(("groups", "seq"), "heads"),
        check_vma=False,
    )
```

time: 46.9 us -> 48.8 us (1.041)
  starting transfers between devices: 22.3 us -> 27.5 us
  waiting for transfers between devices: 6.14 us -> 4.1 us
  Pallas kernels: 17.9 us -> 16.7 us
    ppermute x2, starting transfers between devices: 5.39 us -> 10.6 us  [ahead(): lax.ppermute(value, 'seq', [(i, (i + QUAD) % peers ^ 2) for i in range(pe...]
    ppermute x12, waiting for transfers between devices: 3.88 us -> 1.12 us  [swap(): swapped = {k: lax.ppermute(values[k], 'seq', routes[k]) for k in (3, 1, 2)}]
    ppermute x1, starting transfers between devices: 3.02 us -> 0.51 us  [shards(): lax.ppermute(edge, 'seq', [(i, (i + 1) % peers) for i in range(peers)])]
    ppermute x12, starting transfers between devices: 13.9 us -> 16.4 us  [swap(): swapped = {k: lax.ppermute(values[k], 'seq', routes[k]) for k in (3, 1, 2)}]
    ppermute x1, waiting for transfers between devices: 1.09 us -> 2.98 us  [shards(): lax.ppermute(edge, 'seq', [(i, (i + 1) % peers) for i in range(peers)])]
    pallas_call x12 -> x10, Pallas kernels: 17.9 us -> 16.7 us  [call(): pl.pallas_call(kernel, in_specs=[SMEM] * len(scalars) + more.pop('specs',...]
    ppermute x2, waiting for transfers between devices: 1.17 us -> 0.01 us  [ahead(): lax.ppermute(value, 'seq', [(i, (i + QUAD) % peers ^ 2) for i in range(pe...]
  transfers between devices with their start and end apart: 15 -> 15, of which waited for: 6 -> 3; matrix products, arithmetic and copies ran while one was open for 0% -> 0% of each run, Pallas kernels for 30% -> 23%
where the time goes in v6:
time: 48.8 us; the launch traced here: 48.6 us
  starting transfers between devices  27.5 us (56%)
  Pallas kernels  16.7 us (34%)
  waiting for transfers between devices  4.1 us (8%)
    pallas_call x10, Pallas kernels, call(): pl.pallas_call(kernel, in_specs=[SMEM] * len(scalars) + more.pop('specs',...  16.7 us
    ppermute x12, starting transfers between devices, swap(): swapped = {k: lax.ppermute(values[k], 'seq', routes[k]) for k in (3, 1, 2)}  16.4 us
    ppermute x2, starting transfers between devices, ahead(): lax.ppermute(value, 'seq', [(i, (i + QUAD) % peers ^ 2) for i in range(pe...  10.6 us
    ppermute x1, waiting for transfers between devices, shards(): lax.ppermute(edge, 'seq', [(i, (i + 1) % peers) for i in range(peers)])  2.98 us
    ppermute x12, waiting for transfers between devices, swap(): swapped = {k: lax.ppermute(values[k], 'seq', routes[k]) for k in (3, 1, 2)}  1.12 us
  transfers between devices with their start and end apart: 15, of which 3 were waited for; matrix products, arithmetic and copies ran while one was open for 0% of the time, Pallas kernels for 23%

profile of v6, /device:TPU:0, one launch (start us, length us, event | category | flops | bytes accessed | tf_op | source)
XLA Modules:
  0.0 48.6 jit_solution(4460425323929532676)
XLA Ops:
  0.0 0.1 pad_add_fusion.info
  0.1 3.6 %shard_map.127 = (bf16[128,4096]{1,0:T(8,128)(2,1)S(1)}, bf16[128,512]{1,0:T(8,128)(2,1)S(1)}, bf16[408,128]{1,0:T(8,128)(2,1)S(1)}, bf16[384,136]{1,0:T(8,128)(...) custom-call(s32[3]{0:T(128)S(1)} %pad_add_fusion.info, ...), custom_call_target="tpu_custom_call" | custom-call | flops 600000000 | bytes 4194304 | tf_op jit(solution)/shard_map/pallas_call | solution.py:380
  3.7 4.0 %collective-permute-start.10 = (bf16[144,512]{1,0:T(8,128)(2,1)S(1)}, bf16[144,512]{1,0:T(8,128)(2,1)S(1)}, u32[]{:S(2)}, u32[]{:S(2)}) collective-permute-start(bf16[144,512]{1,0:T(8,128)(2,1)S(1)} %get-tuple-element.83), channel_id=1, source_target_pairs={{0,6},{2,4},{4,2},{6,0},{8,14},{10,12},{12,10},{14,8},{1,7},{3,5},... | collective-permute-start | bytes 442376 | tf_op jit(solution)/shard_map/ppermute | solution.py:428
  7.7 0.5 %collective-permute-start.8 = (bf16[144,512]{1,0:T(8,128)(2,1)S(1)}, bf16[144,512]{1,0:T(8,128)(2,1)S(1)}, u32[]{:S(2)}, u32[]{:S(2)}) collective-permute-start(bf16[144,512]{1,0:T(8,128)(2,1)S(1)} %get-tuple-element.81), channel_id=1, source_target_pairs={{0,2},{2,0},{4,6},{6,4},{8,10},{10,8},{12,14},{14,12},{1,3},{3,1},... | collective-permute-start | bytes 442376 | tf_op jit(solution)/shard_map/ppermute | solution.py:428
  8.2 0.1 collective-permute-start.9
  8.3 1.8 %shard_map.128 = (bf16[128,2048]{1,0:T(8,128)(2,1)S(1)}, bf16[8,4608]{1,0:T(8,128)(2,1)S(1)}, bf16[144,512]{1,0:T(8,128)(2,1)S(1)}, bf16[144,512]{1,0:T(8,128)(2...) custom-call(s32[3]{0:T(128)S(1)} %pad_add_fusion.info, bf16[128,4096]{1,0:T(8,128)(2,1)S(1)} %get-tuple-element.48.x, ...), custom_call_target="tpu_custom_call" | custom-call | flops 300000000 | bytes 4194304 | tf_op jit(solution)/shard_map/pallas_call | solution.py:380
  10.1 1.9 %collective-permute-start.1 = (bf16[144,512]{1,0:T(8,128)(2,1)S(1)}, bf16[144,512]{1,0:T(8,128)(2,1)S(1)}, u32[]{:S(2)}, u32[]{:S(2)}) collective-permute-start(bf16[144,512]{1,0:T(8,128)(2,1)S(1)} %get-tuple-element.66), channel_id=1, source_target_pairs={{0,2},{2,0},{4,6},{6,4},{8,10},{10,8},{12,14},{14,12},{1,3},{3,1},... | collective-permute-start | bytes 442376 | tf_op jit(solution)/shard_map/ppermute | solution.py:428
  12.0 1.6 %collective-permute-start.2 = (bf16[144,512]{1,0:T(8,128)(2,1)S(1)}, bf16[144,512]{1,0:T(8,128)(2,1)S(1)}, u32[]{:S(2)}, u32[]{:S(2)}) collective-permute-start(bf16[144,512]{1,0:T(8,128)(2,1)S(1)} %get-tuple-element.67), channel_id=1, source_target_pairs={{0,4},{2,6},{4,0},{6,2},{8,12},{10,14},{12,8},{14,10},{1,5},{3,7},... | collective-permute-start | bytes 442376 | tf_op jit(solution)/shard_map/ppermute | solution.py:428
  13.6 0.0 collective-permute-done.10.refs_3_.m3
  13.6 1.7 %collective-permute-start.3 = (bf16[144,512]{1,0:T(8,128)(2,1)S(1)}, bf16[144,512]{1,0:T(8,128)(2,1)S(1)}, u32[]{:S(2)}, u32[]{:S(2)}) collective-permute-start(bf16[144,512]{1,0:T(8,128)(2,1)S(1)} %get-tuple-element.68), channel_id=1, source_target_pairs={{0,6},{2,4},{4,2},{6,0},{8,14},{10,12},{12,10},{14,8},{1,7},{3,5},... | collective-permute-start | bytes 442376 | tf_op jit(solution)/shard_map/ppermute | solution.py:428
  15.3 0.0 collective-permute-done.8.refs_1_.m1
  15.3 0.7 %collective-permute-done.9.refs_2_.m2 = bf16[144,512]{1,0:T(8,128)(2,1)S(1)} collective-permute-done((bf16[144,512]{1,0:T(8,128)(2,1)S(1)}, bf16[144,512]{1,0:T(8,128)(2,1)S(1)}, u32[]{:S(2)}, u32[]{:S(2)}) %collective-permute-start.9) | collective-permute-done | bytes 147488 | tf_op jit(solution)/shard_map/ppermute | solution.py:428
  16.0 0.9 %shard_map.133 = (bf16[144,512]{1,0:T(8,128)(2,1)S(1)}, bf16[256,512]{1,0:T(8,128)(2,1)S(1)}) custom-call(s32[3]{0:T(128)S(1)} %pad_add_fusion.info, bf16[144,512]{1,0:T(8,128)(2,1)S(1)} %get-tuple-element.80.refs_0_.m0, bf16[144,512]{1,0:T(8,128)(2,1)S(1)} %collective-permute-done.8.refs_1_.m1, bf16[144,512]{1,0:T(8,128)(2,1)S(1)} %collective-permute-done.9.refs_2_.m2, ...), custom_call_target="tpu_custom_call" | custom-call | flops 1000000 | bytes 4194304 | tf_op jit(solution)/shard_map/pallas_call | solution.py:380
  17.0 3.7 %collective-permute-start.11 = (bf16[144,512]{1,0:T(8,128)(2,1)S(1)}, bf16[144,512]{1,0:T(8,128)(2,1)S(1)}, u32[]{:S(2)}, u32[]{:S(2)}) collective-permute-start(bf16[144,512]{1,0:T(8,128)(2,1)S(1)} %get-tuple-element.84), channel_id=1, source_target_pairs={{0,12},{2,14},{4,8},{6,10},{8,4},{10,6},{12,0},{14,2},{1,13},{3,15... | collective-permute-start | bytes 442376 | tf_op jit(solution)/shard_map/ppermute | solution.py:432
  20.6 0.0 collective-permute-done.1.refs_1_.m1
  20.6 0.0 collective-permute-done.2.refs_2_.m2
  20.6 0.4 collective-permute-done.3.refs_3_.m3
  21.0 0.9 %shard_map.130 = (bf16[144,512]{1,0:T(8,128)(2,1)S(1)}, bf16[256,512]{1,0:T(8,128)(2,1)S(1)}) custom-call(s32[3]{0:T(128)S(1)} %pad_add_fusion.info, bf16[144,512]{1,0:T(8,128)(2,1)S(1)} %get-tuple-element.65.refs_0_.m0, bf16[144,512]{1,0:T(8,128)(2,1)S(1)} %collective-permute-done.1.refs_1_.m1, bf16[144,512]{1,0:T(8,128)(2,1)S(1)} %collective-permute-done.2.refs_2_.m2, ...), custom_call_target="tpu_custom_call" | custom-call | flops 1000000 | bytes 4194304 | tf_op jit(solution)/shard_map/pallas_call | solution.py:380
  22.0 7.0 %collective-permute-start.4 = (bf16[144,512]{1,0:T(8,128)(2,1)S(1)}, bf16[144,512]{1,0:T(8,128)(2,1)S(1)}, u32[]{:S(2)}, u32[]{:S(2)}) collective-permute-start(bf16[144,512]{1,0:T(8,128)(2,1)S(1)} %get-tuple-element.69), channel_id=1, source_target_pairs={{0,12},{2,14},{4,8},{6,10},{8,4},{10,6},{12,0},{14,2},{1,13},{3,15... | collective-permute-start | bytes 442376 | tf_op jit(solution)/shard_map/ppermute | solution.py:432
  29.0 0.0 collective-permute-done.11.start
  29.0 0.8 %shard_map.134 = (bf16[128,512]{1,0:T(8,128)(2,1)S(1)}, bf16[128,512]{1,0:T(8,128)(2,1)S(1)}, bf16[128,512]{1,0:T(8,128)(2,1)S(1)}, bf16[128,512]{1,0:T(8,128)(2,1)S(1)}) custom-call(s32[3]{0:T(128)S(1)} %pad_add_fusion.info, bf16[144,512]{1,0:T(8,128)(2,1)S(1)} %collective-permute-done.11.start, bf16[256,512]{1,0:T(8,128)(2,1)S(1)} %get-tuple-element.85.fixed, ...), custom_call_target="tpu_custom_call" | custom-call | flops 1000000 | bytes 4194304 | tf_op jit(solution)/shard_map/pallas_call | solution.py:380
  29.8 1.6 %collective-permute-start.12 = (bf16[128,512]{1,0:T(8,128)(2,1)S(1)}, bf16[128,512]{1,0:T(8,128)(2,1)S(1)}, u32[]{:S(2)}, u32[]{:S(2)}) collective-permute-start(bf16[128,512]{1,0:T(8,128)(2,1)S(1)} %get-tuple-element.87), channel_id=1, source_target_pairs={{0,2},{2,0},{4,6},{6,4},{8,10},{10,8},{12,14},{14,12},{1,3},{3,1},... | collective-permute-start | bytes 393224 | tf_op jit(solution)/shard_map/ppermute | solution.py:428
  31.4 0.5 %collective-permute-start = (bf16[8,4608]{1,0:T(8,128)(2,1)S(1)}, bf16[8,4608]{1,0:T(8,128)(2,1)S(1)}, u32[]{:S(2)}, u32[]{:S(2)}) collective-permute-start(bf16[8,4608]{1,0:T(8,128)(2,1)S(1)} %get-tuple-element.58), channel_id=1, source_target_pairs={{0,2},{2,4},{4,6},{6,8},{8,10},{10,12},{12,14},{14,0},{1,3},{3,5},... | collective-permute-start | bytes 221192 | tf_op jit(solution)/shard_map/ppermute | solution.py:486
  31.9 0.0 collective-permute-start.13
  31.9 1.5 %collective-permute-start.14 = (bf16[128,512]{1,0:T(8,128)(2,1)S(1)}, bf16[128,512]{1,0:T(8,128)(2,1)S(1)}, u32[]{:S(2)}, u32[]{:S(2)}) collective-permute-start(bf16[128,512]{1,0:T(8,128)(2,1)S(1)} %get-tuple-element.89), channel_id=1, source_target_pairs={{0,6},{2,4},{4,2},{6,0},{8,14},{10,12},{12,10},{14,8},{1,7},{3,5},... | collective-permute-start | bytes 393224 | tf_op jit(solution)/shard_map/ppermute | solution.py:428
  33.4 0.0 collective-permute-done.4.start
  33.4 0.8 %shard_map.131 = (bf16[128,512]{1,0:T(8,128)(2,1)S(1)}, bf16[128,512]{1,0:T(8,128)(2,1)S(1)}, bf16[128,512]{1,0:T(8,128)(2,1)S(1)}, bf16[128,512]{1,0:T(8,128)(2,1)S(1)}) custom-call(s32[3]{0:T(128)S(1)} %pad_add_fusion.info, bf16[144,512]{1,0:T(8,128)(2,1)S(1)} %collective-permute-done.4.start, bf16[256,512]{1,0:T(8,128)(2,1)S(1)} %get-tuple-element.70.fixed, ...), custom_call_target="tpu_custom_call" | custom-call | flops 1000000 | bytes 4194304 | tf_op jit(solution)/shard_map/pallas_call | solution.py:380
  34.2 2.1 %collective-permute-start.5 = (bf16[128,512]{1,0:T(8,128)(2,1)S(1)}, bf16[128,512]{1,0:T(8,128)(2,1)S(1)}, u32[]{:S(2)}, u32[]{:S(2)}) collective-permute-start(bf16[128,512]{1,0:T(8,128)(2,1)S(1)} %get-tuple-element.72), channel_id=1, source_target_pairs={{0,2},{2,0},{4,6},{6,4},{8,10},{10,8},{12,14},{14,12},{1,3},{3,1},... | collective-permute-start | bytes 393224 | tf_op jit(solution)/shard_map/ppermute | solution.py:428
  36.3 3.0 %collective-permute-done.halo = bf16[8,4608]{1,0:T(8,128)(2,1)S(1)} collective-permute-done((bf16[8,4608]{1,0:T(8,128)(2,1)S(1)}, bf16[8,4608]{1,0:T(8,128)(2,1)S(1)}, u32[]{:S(2)}, u32[]{:S(2)}) %collective-permute-start) | collective-permute-done | bytes 73760 | tf_op jit(solution)/shard_map/ppermute | solution.py:486
  39.3 0.0 collective-permute-start.6
  39.3 0.0 collective-permute-done.12.e1
  39.3 1.4 %collective-permute-start.7 = (bf16[128,512]{1,0:T(8,128)(2,1)S(1)}, bf16[128,512]{1,0:T(8,128)(2,1)S(1)}, u32[]{:S(2)}, u32[]{:S(2)}) collective-permute-start(bf16[128,512]{1,0:T(8,128)(2,1)S(1)} %get-tuple-element.74), channel_id=1, source_target_pairs={{0,6},{2,4},{4,2},{6,0},{8,14},{10,12},{12,10},{14,8},{1,7},{3,5},... | collective-permute-start | bytes 393224 | tf_op jit(solution)/shard_map/ppermute | solution.py:428
  40.7 2.0 %shard_map.132 = (f32[128,2048]{1,0:T(8,128)S(1)}, f32[128,2048]{1,0:T(8,128)S(1)}, bf16[128,128]{1,0:T(8,128)(2,1)S(1)}) custom-call(bf16[128,2048]{1,0:T(8,128)(2,1)S(1)} %get-tuple-element.77.xc_in, bf16[128,4096]{1,0:T(8,128)(2,1)S(1)} %get-tuple-element.48.x, bf16[128,4096]{1,0:T(8,128)(2,1)} %z_in.3, bf16[128,512]{1,0:T(8,128)(2,1)S(1)} %get-tuple-element.49.bc, ...), custom_call_target="tpu_custom_call" | custom-call | flops 300000000 | bytes 4194304 | tf_op jit(solution)/shard_map/pallas_call | solution.py:380
  42.7 2.3 %shard_map.129 = (f32[128,2048]{1,0:T(8,128)S(1)}, f32[128,2048]{1,0:T(8,128)S(1)}, bf16[128,128]{1,0:T(8,128)(2,1)S(1)}) custom-call(bf16[128,2048]{1,0:T(8,128)(2,1)S(1)} %get-tuple-element.57.xc_in, bf16[128,4096]{1,0:T(8,128)(2,1)S(1)} %get-tuple-element.48.x, bf16[128,4096]{1,0:T(8,128)(2,1)} %z_in.3, bf16[128,512]{1,0:T(8,128)(2,1)S(1)} %get-tuple-element.49.bc, ...), custom_call_target="tpu_custom_call" | custom-call | flops 300000000 | bytes 4194304 | tf_op jit(solution)/shard_map/pallas_call | solution.py:380
  44.9 0.0 collective-permute-done.13.e2
  44.9 0.0 collective-permute-done.14.e3
  45.0 1.8 %shard_map.135.rest_0_ = bf16[128,4096]{1,0:T(8,128)(2,1)} custom-call(s32[3]{0:T(128)S(1)} %pad_add_fusion.info, f32[128,2048]{1,0:T(8,128)S(1)} %get-tuple-element.78.near, f32[128,2048]{1,0:T(8,128)S(1)} %get-tuple-element.79.gain, bf16[128,512]{1,0:T(8,128)(2,1)S(1)} %get-tuple-element.86.e0, bf16[128,512]{1,0:T(8,128)(2,1)S(1)} %collective-permute-done.12.e1, ...), custom_call_target="tpu_custom_call" | custom-call | flops 100000000 | bytes 4194304 | tf_op jit(solution)/shard_map/pallas_call | solution.py:380
  46.7 0.0 collective-permute-done.5.e1
  46.8 0.0 collective-permute-done.6.e2
  46.8 0.0 collective-permute-done.7.e3
  46.8 1.8 %shard_map.136 = bf16[128,4096]{1,0:T(8,128)(2,1)} custom-call(s32[3]{0:T(128)S(1)} %pad_add_fusion.info, f32[128,2048]{1,0:T(8,128)S(1)} %get-tuple-element.63.near, f32[128,2048]{1,0:T(8,128)S(1)} %get-tuple-element.64.gain, bf16[128,512]{1,0:T(8,128)(2,1)S(1)} %get-tuple-element.71.e0, ...), custom_call_target="tpu_custom_call", output_to_operand_aliasing={{}: (9, {})} | custom-call | flops 100000000 | bytes 4194304 | tf_op jit(solution)/shard_map/pallas_call | solution.py:380
Async XLA Ops:
  3.7 9.9 %collective-permute-start.10 = (bf16[144,512]{1,0:T(8,128)(2,1)S(1)}, bf16[144,512]{1,0:T(8,128)(2,1)S(1)}, u32[]{:S(2)}, u32[]{:S(2)}) collective-permute-start(bf16[144,512]{1,0:T(8,128)(2,1)S(1)} %get-tuple-element.83), channel_id=1, source_target_pairs={{0,6},{2,4},{4,2},{6,0},{8,14},{10,12},{12,10},{14,8},{1,7},{3,5},... | collective-permute-start | bytes 442376 | tf_op jit(solution)/shard_map/ppermute | solution.py:428
  7.7 7.6 %collective-permute-start.8 = (bf16[144,512]{1,0:T(8,128)(2,1)S(1)}, bf16[144,512]{1,0:T(8,128)(2,1)S(1)}, u32[]{:S(2)}, u32[]{:S(2)}) collective-permute-start(bf16[144,512]{1,0:T(8,128)(2,1)S(1)} %get-tuple-element.81), channel_id=1, source_target_pairs={{0,2},{2,0},{4,6},{6,4},{8,10},{10,8},{12,14},{14,12},{1,3},{3,1},... | collective-permute-start | bytes 442376 | tf_op jit(solution)/shard_map/ppermute | solution.py:428
  8.2 7.8 %collective-permute-start.9 = (bf16[144,512]{1,0:T(8,128)(2,1)S(1)}, bf16[144,512]{1,0:T(8,128)(2,1)S(1)}, u32[]{:S(2)}, u32[]{:S(2)}) collective-permute-start(bf16[144,512]{1,0:T(8,128)(2,1)S(1)} %get-tuple-element.82), channel_id=1, source_target_pairs={{0,4},{2,6},{4,0},{6,2},{8,12},{10,14},{12,8},{14,10},{1,5},{3,7},... | collective-permute-start | bytes 442376 | tf_op jit(solution)/shard_map/ppermute | solution.py:428
  10.1 10.5 %collective-permute-start.1 = (bf16[144,512]{1,0:T(8,128)(2,1)S(1)}, bf16[144,512]{1,0:T(8,128)(2,1)S(1)}, u32[]{:S(2)}, u32[]{:S(2)}) collective-permute-start(bf16[144,512]{1,0:T(8,128)(2,1)S(1)} %get-tuple-element.66), channel_id=1, source_target_pairs={{0,2},{2,0},{4,6},{6,4},{8,10},{10,8},{12,14},{14,12},{1,3},{3,1},... | collective-permute-start | bytes 442376 | tf_op jit(solution)/shard_map/ppermute | solution.py:428
  12.0 8.6 %collective-permute-start.2 = (bf16[144,512]{1,0:T(8,128)(2,1)S(1)}, bf16[144,512]{1,0:T(8,128)(2,1)S(1)}, u32[]{:S(2)}, u32[]{:S(2)}) collective-permute-start(bf16[144,512]{1,0:T(8,128)(2,1)S(1)} %get-tuple-element.67), channel_id=1, source_target_pairs={{0,4},{2,6},{4,0},{6,2},{8,12},{10,14},{12,8},{14,10},{1,5},{3,7},... | collective-permute-start | bytes 442376 | tf_op jit(solution)/shard_map/ppermute | solution.py:428
  13.6 7.4 %collective-permute-start.3 = (bf16[144,512]{1,0:T(8,128)(2,1)S(1)}, bf16[144,512]{1,0:T(8,128)(2,1)S(1)}, u32[]{:S(2)}, u32[]{:S(2)}) collective-permute-start(bf16[144,512]{1,0:T(8,128)(2,1)S(1)} %get-tuple-element.68), channel_id=1, source_target_pairs={{0,6},{2,4},{4,2},{6,0},{8,14},{10,12},{12,10},{14,8},{1,7},{3,5},... | collective-permute-start | bytes 442376 | tf_op jit(solution)/shard_map/ppermute | solution.py:428
  17.0 12.0 %collective-permute-start.11 = (bf16[144,512]{1,0:T(8,128)(2,1)S(1)}, bf16[144,512]{1,0:T(8,128)(2,1)S(1)}, u32[]{:S(2)}, u32[]{:S(2)}) collective-permute-start(bf16[144,512]{1,0:T(8,128)(2,1)S(1)} %get-tuple-element.84), channel_id=1, source_target_pairs={{0,12},{2,14},{4,8},{6,10},{8,4},{10,6},{12,0},{14,2},{1,13},{3,15... | collective-permute-start | bytes 442376 | tf_op jit(solution)/shard_map/ppermute | solution.py:432
  22.0 11.4 %collective-permute-start.4 = (bf16[144,512]{1,0:T(8,128)(2,1)S(1)}, bf16[144,512]{1,0:T(8,128)(2,1)S(1)}, u32[]{:S(2)}, u32[]{:S(2)}) collective-permute-start(bf16[144,512]{1,0:T(8,128)(2,1)S(1)} %get-tuple-element.69), channel_id=1, source_target_pairs={{0,12},{2,14},{4,8},{6,10},{8,4},{10,6},{12,0},{14,2},{1,13},{3,15... | collective-permute-start | bytes 442376 | tf_op jit(solution)/shard_map/ppermute | solution.py:432
  29.8 9.5 %collective-permute-start.12 = (bf16[128,512]{1,0:T(8,128)(2,1)S(1)}, bf16[128,512]{1,0:T(8,128)(2,1)S(1)}, u32[]{:S(2)}, u32[]{:S(2)}) collective-permute-start(bf16[128,512]{1,0:T(8,128)(2,1)S(1)} %get-tuple-element.87), channel_id=1, source_target_pairs={{0,2},{2,0},{4,6},{6,4},{8,10},{10,8},{12,14},{14,12},{1,3},{3,1},... | collective-permute-start | bytes 393224 | tf_op jit(solution)/shard_map/ppermute | solution.py:428
  31.4 7.9 %collective-permute-start = (bf16[8,4608]{1,0:T(8,128)(2,1)S(1)}, bf16[8,4608]{1,0:T(8,128)(2,1)S(1)}, u32[]{:S(2)}, u32[]{:S(2)}) collective-permute-start(bf16[8,4608]{1,0:T(8,128)(2,1)S(1)} %get-tuple-element.58), channel_id=1, source_target_pairs={{0,2},{2,4},{4,6},{6,8},{8,10},{10,12},{12,14},{14,0},{1,3},{3,5},... | collective-permute-start | bytes 221192 | tf_op jit(solution)/shard_map/ppermute | solution.py:486
  31.9 13.0 %collective-permute-start.13 = (bf16[128,512]{1,0:T(8,128)(2,1)S(1)}, bf16[128,512]{1,0:T(8,128)(2,1)S(1)}, u32[]{:S(2)}, u32[]{:S(2)}) collective-permute-start(bf16[128,512]{1,0:T(8,128)(2,1)S(1)} %get-tuple-element.88), channel_id=1, source_target_pairs={{0,4},{2,6},{4,0},{6,2},{8,12},{10,14},{12,8},{14,10},{1,5},{3,7},... | collective-permute-start | bytes 393224 | tf_op jit(solution)/shard_map/ppermute | solution.py:428
  31.9 13.0 %collective-permute-start.14 = (bf16[128,512]{1,0:T(8,128)(2,1)S(1)}, bf16[128,512]{1,0:T(8,128)(2,1)S(1)}, u32[]{:S(2)}, u32[]{:S(2)}) collective-permute-start(bf16[128,512]{1,0:T(8,128)(2,1)S(1)} %get-tuple-element.89), channel_id=1, source_target_pairs={{0,6},{2,4},{4,2},{6,0},{8,14},{10,12},{12,10},{14,8},{1,7},{3,5},... | collective-permute-start | bytes 393224 | tf_op jit(solution)/shard_map/ppermute | solution.py:428
  34.2 12.5 %collective-permute-start.5 = (bf16[128,512]{1,0:T(8,128)(2,1)S(1)}, bf16[128,512]{1,0:T(8,128)(2,1)S(1)}, u32[]{:S(2)}, u32[]{:S(2)}) collective-permute-start(bf16[128,512]{1,0:T(8,128)(2,1)S(1)} %get-tuple-element.72), channel_id=1, source_target_pairs={{0,2},{2,0},{4,6},{6,4},{8,10},{10,8},{12,14},{14,12},{1,3},{3,1},... | collective-permute-start | bytes 393224 | tf_op jit(solution)/shard_map/ppermute | solution.py:428
  39.3 7.5 %collective-permute-start.6 = (bf16[128,512]{1,0:T(8,128)(2,1)S(1)}, bf16[128,512]{1,0:T(8,128)(2,1)S(1)}, u32[]{:S(2)}, u32[]{:S(2)}) collective-permute-start(bf16[128,512]{1,0:T(8,128)(2,1)S(1)} %get-tuple-element.73), channel_id=1, source_target_pairs={{0,4},{2,6},{4,0},{6,2},{8,12},{10,14},{12,8},{14,10},{1,5},{3,7},... | collective-permute-start | bytes 393224 | tf_op jit(solution)/shard_map/ppermute | solution.py:428
  39.3 7.5 %collective-permute-start.7 = (bf16[128,512]{1,0:T(8,128)(2,1)S(1)}, bf16[128,512]{1,0:T(8,128)(2,1)S(1)}, u32[]{:S(2)}, u32[]{:S(2)}) collective-permute-start(bf16[128,512]{1,0:T(8,128)(2,1)S(1)} %get-tuple-element.74), channel_id=1, source_target_pairs={{0,6},{2,4},{4,2},{6,0},{8,14},{10,12},{12,10},{14,8},{1,7},{3,5},... | collective-permute-start | bytes 393224 | tf_op jit(solution)/shard_map/ppermute | solution.py:428

commit v7 on v6

--- a/solution.py
+++ b/solution.py
@@ -11,10 +11,8 @@
 STATE = 128
 BLOCK = 128
 QUAD = 4
-HALO = 8
 TILE = 8
 EXTRA = 16
-FIRST = 16
 F32 = jnp.float32
 BF16 = jnp.bfloat16
 
@@ -135,11 +133,14 @@
     heads = carry.shape[1] // 2
     width = wide // QUAD
     lane = slice(g * STATE, (g + 1) * STATE)
+    inner = wbc.shape[2]
     btotal, bafter = conv_both(moves[...], bc[:, lane], bc_weight(0, lane, wbc), bbc[0:1, lane])
+    cblock = bc[:, inner + g * STATE : inner + (g + 1) * STATE]
+    ctotal, cafter = conv_both(moves[...], cblock, bc_weight(1, lane, wbc), bbc[1:2, lane])
     bmat = silu_of_half(btotal)
     bmat = jnp.where(tokens(0, bmat.shape, 0) >= taps - 1, bmat, 0.0)
     bmat_t = jnp.transpose(bmat).astype(BF16)
-    bparts = jnp.concatenate([btotal[0:TILE], bafter] + [jnp.zeros_like(bafter)] * (width // STATE - 2), axis=1)
+    bparts = jnp.concatenate([btotal[0:TILE], bafter, ctotal[0:TILE], cafter], axis=1)
     bparts = pltpu.roll(bparts, taps - 1, 0)
     step = 1024
     for at in range(0, wide, step):
@@ -164,7 +165,7 @@
 
 def first_kernel(
     info, lens_in, x_in, bc_in, wx_in, bx_in, dt_in, dtb_in, dec_in, wbc_in, bbc_in, skip_in, scale_in,
-    x, bc, moves, shift, mask, factors, factor, carry, wx, bx, wbc, bbc, skip, scale, xc_out, m0, m1, m2, m3,
+    x, bc, moves, mask, live, factors, factor, carry, wx, bx, wbc, bbc, skip, scale, xc_out, m0, m1, m2, m3,
     lens, raw, dt, dtb, dec, held, sems,
 ):
     heads = dt.shape[0]
@@ -185,7 +186,6 @@
     ends = ends_of(lens)
     moves[0 : (taps - 1) * BLOCK, :] = shift_matrix(start, ends, BLOCK, 0, taps)
     moves[(taps - 1) * BLOCK :, :] = next_matrix(start, ends, taps)
-    shift[...] = shift_matrix(start, ends, BLOCK, HALO, taps)
     shape = (BLOCK, BLOCK)
     row = lax.broadcasted_iota(jnp.int32, shape, 0)
     col = lax.broadcasted_iota(jnp.int32, shape, 1)
@@ -200,7 +200,7 @@
     before = seg_of(start - 1, ends)
     factors[:, 0 : 2 * heads] = pair_of(rate * jnp.exp(-cum))
     factors[:, 2 * heads : 4 * heads] = pair_of(grown)
-    factors[:, 4 * heads : 6 * heads] = pair_of(jnp.where(seg_head == before, grown, 0.0))
+    live[...] = jnp.where(seg_row == before, 1.0, 0.0)
     passed = jnp.where(seg_last == before, jnp.exp(last), 0.0)
     carry[...] = pair_of(jnp.broadcast_to(passed, (TILE, heads)))
     for copy in copies[4:9]:
@@ -214,11 +214,8 @@
         copy.wait()
 
 
-def other_kernel(g, info, x, bc, wx, bx, wbc, bbc, moves, factor, carry, xc_out, edge, m0, m1, m2, m3, held):
+def other_kernel(g, info, x, bc, wx, bx, wbc, bbc, moves, factor, carry, xc_out, m0, m1, m2, m3, held):
     send_states(g, info[2], x, bc, wx, bx, wbc, bbc, moves, factor, carry, xc_out, (m0, m1, m2, m3), held)
-    rows, chan = x.shape
-    edge[:, 0:chan] = x[rows - HALO : rows, :]
-    edge[:, chan:] = bc[rows - HALO : rows, :]
 
 
 def extra_of(msg):
@@ -229,16 +226,21 @@
 def top_state(taps, here, prior):
     upper, lower = here
     total = pltpu.roll(upper, TILE - 2, 0)
-    btotal = pltpu.roll(lower[:, 0:STATE], TILE - taps + 1, 0)
+    parts = pltpu.roll(lower, TILE - taps + 1, 0)
+    btotal, ctotal = parts[:, 0:STATE], parts[:, 2 * STATE : 3 * STATE]
     if prior is not None:
         total = total + pltpu.roll(prior[0], TILE - 1 - taps, 0)
-        btotal = btotal + pltpu.roll(prior[1][:, STATE : 2 * STATE], TILE - taps + 1, 0)
+        parts = pltpu.roll(prior[1], TILE - taps + 1, 0)
+        btotal, ctotal = btotal + parts[:, STATE : 2 * STATE], ctotal + parts[:, 3 * STATE : 4 * STATE]
     xc = silu_of_half(total).astype(BF16).astype(F32)
-    scaled = jnp.where(tokens(0, xc.shape, 0) < taps - 1, xc * lower, 0.0)
-    bmat = jnp.where(tokens(0, btotal.shape, 0) < taps - 1, silu_of_half(btotal), 0.0)
+    xc = jnp.where(tokens(0, xc.shape, 0) < taps - 1, xc, 0.0)
+    both = silu_of_half(jnp.concatenate([btotal, ctotal], axis=1))
+    both = jnp.where(tokens(0, both.shape, 0) < taps - 1, both, 0.0)
+    rows = jnp.concatenate([xc, jnp.concatenate([both, jnp.zeros_like(both)], axis=1)], axis=0).astype(BF16)
+    scaled, bmat = xc * lower, both[:, 0:STATE]
     scaled = jnp.concatenate([scaled, jnp.zeros_like(scaled)], axis=0).astype(BF16)
     bmat = jnp.concatenate([bmat, jnp.zeros_like(bmat)], axis=0).astype(BF16)
-    return lax.dot_general(bmat, scaled, (((0,), (0,)), ((), ())), preferred_element_type=F32)
+    return lax.dot_general(bmat, scaled, (((0,), (0,)), ((), ())), preferred_element_type=F32), rows
 
 
 def carry_row(extra):
@@ -254,13 +256,14 @@
         def _():
             block = [msgs[mine ^ b] for b in range(QUAD)]
             extra = [extra_of(msg) for msg in block]
-            prior = extra_of(rest[0]) if more else None
-            state = block[0][0:STATE, :].astype(F32) + top_state(taps, extra[0], prior)
+            add, _ = top_state(taps, extra[0], extra_of(rest[0]) if more else None)
+            state = block[0][0:STATE, :].astype(F32) + add
             through = carry_row(extra[0])
             for b in range(1, QUAD):
-                own = block[b][0:STATE, :].astype(F32) + top_state(taps, extra[b], extra[b - 1])
-                if b < QUAD - 1:
-                    fixed[(b - 1) * STATE : b * STATE, :] = own.astype(BF16)
+                add, rows = top_state(taps, extra[b], extra[b - 1])
+                own = block[b][0:STATE, :].astype(F32) + add
+                fixed[b - 1, 0:STATE, :] = own.astype(BF16)
+                fixed[b - 1, STATE : STATE + EXTRA, :] = rows
                 state = own + carry_row(extra[b]) * state
                 through = through * carry_row(extra[b])
             total[0:STATE, :] = state.astype(BF16)
@@ -272,71 +275,65 @@
 def enter_kernel(taps, info, start, fixed, m0, m1, m2, m3, o0, o1, o2, o3):
     msgs = (m0, m1, m2, m3)
     outs = (o0, o1, o2, o3)
+    lower = slice(STATE, STATE + EXTRA)
     prior = extra_of(start)
     for mine in range(QUAD):
 
         @pl.when(info[1] == mine)
         def _():
-            outs[mine][...] = start[0:STATE, :]
             head = extra_of(msgs[mine])
-            state = msgs[mine][0:STATE, :].astype(F32) + top_state(taps, head, prior)
+            add, rows = top_state(taps, head, prior)
+            outs[mine][0:STATE, :] = start[0:STATE, :]
+            outs[mine][lower, :] = rows
+            state = msgs[mine][0:STATE, :].astype(F32) + add
             state = state + carry_row(head) * start[0:STATE, :].astype(F32)
-            outs[mine ^ 1][...] = state.astype(BF16)
-            for b in range(2, QUAD):
-                own = fixed[(b - 2) * STATE : (b - 1) * STATE, :].astype(F32)
-                state = own + carry_row(extra_of(msgs[mine ^ (b - 1)])) * state
-                outs[mine ^ b][...] = state.astype(BF16)
-
-
-def joined(above, below):
-    return jnp.concatenate([above.astype(F32), below.astype(F32)], axis=0).astype(BF16)
-
-
-def bc_conv(which, g, shift, halo, bc, wbc, bbc):
-    inner = wbc.shape[2]
-    chan = halo.shape[1] - 2 * inner
-    base = which * inner + g * STATE
-    lane = slice(g * STATE, (g + 1) * STATE)
-    block = bc[:, base : base + STATE]
-    ext = joined(halo[:, chan + base : chan + base + STATE], block)
-    half = conv_half(shift[...], ext, block, bc_weight(which, lane, wbc), bbc[which : which + 1, lane])
-    return silu_of_half(half).astype(BF16)
-
-
-def inner_kernel(
-    g, xc_in, x, z_in, bc, halo, wx, bx, wbc, bbc, shift, mask, factors, skip, near, gain, c_out, z, sem
-):
+            for b in range(1, QUAD):
+                outs[mine ^ b][0:STATE, :] = state.astype(BF16)
+                outs[mine ^ b][lower, :] = fixed[b - 1, lower, :]
+                if b < QUAD - 1:
+                    own = fixed[b - 1, 0:STATE, :].astype(F32)
+                    state = own + carry_row(extra_of(msgs[mine ^ b])) * state
+
+
+def inner_kernel(g, xc_in, z_in, bc, wbc, bbc, moves, mask, factors, skip, near, gain, c_out, rate_top, kept_top, z, sem):
     wide = xc_in.shape[1]
     copy = pltpu.make_async_copy(z_in.at[:, g * wide : (g + 1) * wide], z, sem)
     copy.start()
     heads = skip.shape[1]
-    taps = wx.shape[0]
-    cmat = bc_conv(1, g, shift, halo, bc, wbc, bbc)
+    taps = wbc.shape[0]
+    lane = slice(g * STATE, (g + 1) * STATE)
+    shift = moves[0 : (taps - 1) * BLOCK, :]
+
+    def conv(which):
+        base = which * wbc.shape[2] + g * STATE
+        block = bc[:, base : base + STATE]
+        half = conv_half(shift, block, block, bc_weight(which, lane, wbc), bbc[which : which + 1, lane])
+        return silu_of_half(half).astype(BF16)
+
+    cmat = conv(1)
     c_out[...] = cmat
-    bmat = bc_conv(0, g, shift, halo, bc, wbc, bbc)
-    scores = lax.dot_general(cmat, bmat, (((1,), (1,)), ((), ())), preferred_element_type=F32)
-    scores = (scores * mask[...]).astype(BF16)
+    scores = lax.dot_general(cmat, conv(0), (((1,), (1,)), ((), ())), preferred_element_type=F32)
+    scores = jnp.where(tokens(0, scores.shape, 1) < taps - 1, 0.0, scores * mask[...]).astype(BF16)
     skips = pair_of(jnp.broadcast_to(skip[...], (8, heads)))
-    cols = slice(0, HALO + FIRST)
-    moves = jnp.concatenate([shift[k * BLOCK : k * BLOCK + FIRST, cols] for k in range(taps - 1)], axis=0)
     step = 1024
     copy.wait()
     for at in range(0, wide, step):
         lane = slice(at, at + step)
-        deep = slice(g * wide + at, g * wide + at + step)
         onehot2 = twice(head_map(heads, (g * wide + at) // HEAD_DIM, step))
-        top = x[0:FIRST, deep]
-        xc_top = silu_of_half(conv_half(moves, joined(halo[:, deep], top), top, wx[:, deep], bx[:, deep]))
-        xf = jnp.concatenate([xc_top.astype(BF16), xc_in[FIRST:, lane]], axis=0).astype(F32)
-        scaled = (xf * mm(factors[:, 0 : 2 * heads], onehot2)).astype(BF16)
+        xf = xc_in[:, lane].astype(F32)
+        xf = jnp.where(tokens(0, xf.shape, 0) < taps - 1, 0.0, xf)
+        rates = mm(factors[:, 0 : 2 * heads], onehot2)
+        rate_top[:, lane] = rates[0:TILE]
+        scaled = (xf * rates).astype(BF16)
         grown = mm(factors[:, 2 * heads : 4 * heads], onehot2)
         skip_c = mm(skips, onehot2)[0:1]
         gate = silu_of_half(z[:, lane].astype(F32) * 0.5)
+        kept_top[:, lane] = skip_c * gate[0:TILE]
         near[:, lane] = (mm(scores, scaled) * grown + skip_c * xf) * gate
-        gain[:, lane] = mm(factors[:, 4 * heads : 6 * heads], onehot2) * gate
-
-
-def finish_kernel(g, info, near, gain, e0, e1, e2, e3, cmat, scale, *rest):
+        gain[:, lane] = grown * gate
+
+
+def finish_kernel(g, taps, info, near, gain, cmat, rate_top, kept_top, mask, live, scale, *rest):
     out, ready, held, sems = rest[-4:]
     mine = info[2]
     rows, wide = near.shape
@@ -345,12 +342,22 @@
     part = rows // steps
     square = [0.0] * steps
     ats = [pl.ds(pl.multiple_of((mine ^ k) * width, width), width) for k in range(QUAD)]
-    c = cmat[...]
-    for at, e in zip(ats, (e0, e1, e2, e3)):
-        far = mm(c, e[...])
+    first = rest[0][STATE : STATE + EXTRA, 0 : 2 * STATE].astype(F32)[TILE:EXTRA]
+    c = cmat[...].astype(F32)
+    top = jnp.where(tokens(0, (TILE, STATE), 0) < taps - 1, first[:, STATE:], c[0:TILE])
+    c = jnp.concatenate([top, c[TILE:]], axis=0)
+    bmat = jnp.concatenate([first[:, 0:STATE], jnp.zeros((TILE, STATE), F32)], axis=0).astype(BF16)
+    scores = lax.dot_general(c.astype(BF16), bmat, (((1,), (1,)), ((), ())), preferred_element_type=F32)
+    left = jnp.concatenate([c * live[...], scores * mask[:, 0 : 2 * TILE]], axis=1).astype(BF16)
+    for at, e in zip(ats, rest):
+        xc = e[STATE : STATE + EXTRA, :].astype(F32)[0:TILE]
+        sent = jnp.concatenate([xc * rate_top[:, at], jnp.zeros_like(xc)], axis=0).astype(BF16)
+        far = mm(left, jnp.concatenate([e[0:STATE, :], sent], axis=0))
         for i in range(steps):
             these = slice(i * part, (i + 1) * part)
             value = near[these, at] + gain[these, at] * far[these]
+            if i == 0:
+                value = value + jnp.concatenate([xc * kept_top[:, at], jnp.zeros((part - TILE, width), F32)], axis=0)
             square[i] = square[i] + jnp.sum(value * value, axis=1, keepdims=True)
             held[these, at] = value
     copies = []
@@ -437,7 +444,7 @@
     ]
     sent = ((STATE + EXTRA, width), BF16)
     held = pltpu.VMEM((STATE + EXTRA, wide), BF16)
-    x, bc, moves, shift, mask, factors, factor, carry, wx, bx, wbc, bbc, skip, scale, xc, *msg = call(
+    x, bc, moves, mask, live, factors, factor, carry, wx, bx, wbc, bbc, skip, scale, xc, *msg = call(
         first_kernel,
         [info],
         first_args,
@@ -445,9 +452,9 @@
             ((rows, chan), BF16),
             ((rows, 2 * bcw), BF16),
             (((taps - 1) * (BLOCK + TILE), BLOCK), BF16),
-            (((taps - 1) * BLOCK, HALO + BLOCK), BF16),
             ((BLOCK, BLOCK), F32),
-            ((rows, 6 * heads), BF16),
+            ((BLOCK, BLOCK), F32),
+            ((rows, 4 * heads), BF16),
             ((rows, 2 * heads), BF16),
             ((TILE, 2 * heads), BF16),
             ((taps, chan), BF16),
@@ -473,22 +480,21 @@
     )
     xcs, msgs = [xc], [swap(msg)]
     for g in range(1, groups):
-        xc, edge, *msg = call(
+        xc, *msg = call(
             functools.partial(other_kernel, g),
             [info],
             [x, bc, wx, bx, wbc, bbc, moves, factor, carry],
-            [((rows, wide), BF16), ((HALO, chan + 2 * bcw), BF16), *[sent] * QUAD],
+            [((rows, wide), BF16), *[sent] * QUAD],
             300_000_000,
             scratch_shapes=[held],
         )
         xcs.append(xc)
         msgs.append(swap(msg))
-    halo = lax.ppermute(edge, "seq", [(i, (i + 1) % peers) for i in range(peers)])
 
     local = []
     for g in range(groups):
-        args = [xcs[g], x, z_in, bc, halo, wx, bx, wbc, bbc, shift, mask, factors, skip]
-        outs = [((rows, wide), F32), ((rows, wide), F32), ((rows, STATE), BF16)]
+        args = [xcs[g], z_in, bc, wbc, bbc, moves, mask, factors, skip]
+        outs = [((rows, wide), F32)] * 2 + [((rows, STATE), BF16)] + [((TILE, wide), F32)] * 2
         near = call(
             functools.partial(inner_kernel, g),
             [],
@@ -499,10 +505,11 @@
             scratch_shapes=[pltpu.VMEM((rows, wide), BF16), pltpu.SemaphoreType.DMA],
         )
         local.append(list(near))
+    msgs[-1][0], local[0][0] = tie(msgs[-1][0], local[0][0])
 
     entering, fixes = [], []
     for g in range(groups):
-        outs = [sent, (((QUAD - 2) * STATE, width), BF16)]
+        outs = [sent, ((QUAD - 1, STATE + EXTRA, width), BF16)]
         args = list(msgs[g])
         if reach > 1:
             outs.append(((8, width), F32))
@@ -519,14 +526,15 @@
 
     blocks = []
     for g in range(groups):
-        outs = [((STATE, width), BF16)] * QUAD
+        outs = [sent] * QUAD
         kernel = functools.partial(enter_kernel, taps)
         blocks.append(swap(call(kernel, (info,), [entering[g], fixes[g], *msgs[g]], outs, 1_000_000)))
 
+    blocks[0][1], local[-1][0] = tie(blocks[0][1], local[-1][0])
+
     out = None
     for g in range(groups):
-        near, gain, cmat = local[g]
-        args = [near, gain, *blocks[g], cmat, scale]
+        args = [*local[g], mask, live, scale, *blocks[g]]
         specs = [VMEM] * len(args)
         aliases = {}
         if out is not None:
@@ -534,7 +542,7 @@
             args.append(out)
             specs.append(ANY)
         (out,) = call(
-            functools.partial(finish_kernel, g),
+            functools.partial(finish_kernel, g, taps),
             (info,),
             args,
             [((rows, chan), BF16)],

time: 48.8 us -> 46.5 us (0.953)
  starting transfers between devices: 27.5 us -> 23.4 us
  waiting for transfers between devices: 4.1 us -> 5.89 us
    ppermute x12, waiting for transfers between devices: 1.12 us -> 5.88 us  [swap(): swapped = {k: lax.ppermute(values[k], 'seq', routes[k]) for k in (3, 1, 2)}]
    ppermute x2, starting transfers between devices: 10.6 us -> 7.66 us  [ahead(): lax.ppermute(value, 'seq', [(i, (i + QUAD) % peers ^ 2) for i in range(pe...]
    ppermute x1 -> x0, waiting for transfers between devices: 2.98 us -> none  [shards(): lax.ppermute(edge, 'seq', [(i, (i + 1) % peers) for i in range(peers)])]
    ppermute x12, starting transfers between devices: 16.4 us -> 15.7 us  [swap(): swapped = {k: lax.ppermute(values[k], 'seq', routes[k]) for k in (3, 1, 2)}]
    ppermute x1 -> x0, starting transfers between devices: 0.51 us -> none  [shards(): lax.ppermute(edge, 'seq', [(i, (i + 1) % peers) for i in range(peers)])]
  transfers between devices with their start and end apart: 15 -> 14, of which waited for: 3 -> 5; matrix products, arithmetic and copies ran while one was open for 0% -> 0% of each run, Pallas kernels for 23% -> 24%
where the time goes in v7:
time: 46.5 us; the launch traced here: 46.3 us
  starting transfers between devices  23.4 us (50%)
  Pallas kernels  16.8 us (36%)
  waiting for transfers between devices  5.89 us (13%)
    pallas_call x10, Pallas kernels, call(): pl.pallas_call(kernel, in_specs=[SMEM] * len(scalars) + more.pop('specs',...  16.8 us
    ppermute x12, starting transfers between devices, swap(): swapped = {k: lax.ppermute(values[k], 'seq', routes[k]) for k in (3, 1, 2)}  15.7 us
    ppermute x2, starting transfers between devices, ahead(): lax.ppermute(value, 'seq', [(i, (i + QUAD) % peers ^ 2) for i in range(pe...  7.66 us
    ppermute x12, waiting for transfers between devices, swap(): swapped = {k: lax.ppermute(values[k], 'seq', routes[k]) for k in (3, 1, 2)}  5.88 us
  transfers between devices with their start and end apart: 14, of which 5 were waited for; matrix products, arithmetic and copies ran while one was open for 0% of the time, Pallas kernels for 24%

profile of v7, /device:TPU:0, one launch (start us, length us, event | category | flops | bytes accessed | tf_op | source)
XLA Modules:
  0.0 46.3 jit_solution(7879331642389186640)
XLA Ops:
  0.0 0.1 pad_add_fusion.info
  0.1 3.6 %shard_map.127 = (bf16[128,4096]{1,0:T(8,128)(2,1)S(1)}, bf16[128,512]{1,0:T(8,128)(2,1)S(1)}, bf16[408,128]{1,0:T(8,128)(2,1)S(1)}, f32[128,128]{1,0:T(8,128)S(...) custom-call(s32[3]{0:T(128)S(1)} %pad_add_fusion.info, ...), custom_call_target="tpu_custom_call" | custom-call | flops 600000000 | bytes 4194304 | tf_op jit(solution)/shard_map/pallas_call | solution.py:387
  3.7 3.0 %collective-permute-start = (bf16[144,512]{1,0:T(8,128)(2,1)S(1)}, bf16[144,512]{1,0:T(8,128)(2,1)S(1)}, u32[]{:S(2)}, u32[]{:S(2)}) collective-permute-start(bf16[144,512]{1,0:T(8,128)(2,1)S(1)} %get-tuple-element.56), channel_id=1, source_target_pairs={{0,2},{2,0},{4,6},{6,4},{8,10},{10,8},{12,14},{14,12},{1,3},{3,1},... | collective-permute-start | bytes 442376 | tf_op jit(solution)/shard_map/ppermute | solution.py:435
  6.7 1.6 %collective-permute-start.1 = (bf16[144,512]{1,0:T(8,128)(2,1)S(1)}, bf16[144,512]{1,0:T(8,128)(2,1)S(1)}, u32[]{:S(2)}, u32[]{:S(2)}) collective-permute-start(bf16[144,512]{1,0:T(8,128)(2,1)S(1)} %get-tuple-element.57), channel_id=1, source_target_pairs={{0,4},{2,6},{4,0},{6,2},{8,12},{10,14},{12,8},{14,10},{1,5},{3,7},... | collective-permute-start | bytes 442376 | tf_op jit(solution)/shard_map/ppermute | solution.py:435
  8.3 0.0 collective-permute-start.2
  8.3 1.8 %shard_map.130 = (bf16[128,2048]{1,0:T(8,128)(2,1)S(1)}, bf16[144,512]{1,0:T(8,128)(2,1)S(1)}, bf16[144,512]{1,0:T(8,128)(2,1)S(1)}, bf16[144,512]{1,0:T(8,128)(2,1)S(1)}, bf16[144,512]{1,0:T(8,128)(2,1)S(1)}) custom-call(s32[3]{0:T(128)S(1)} %pad_add_fusion.info, bf16[128,4096]{1,0:T(8,128)(2,1)S(1)} %get-tuple-element.62.x, ...), custom_call_target="tpu_custom_call" | custom-call | flops 300000000 | bytes 4194304 | tf_op jit(solution)/shard_map/pallas_call | solution.py:387
  10.2 2.0 %collective-permute-start.5 = (bf16[144,512]{1,0:T(8,128)(2,1)S(1)}, bf16[144,512]{1,0:T(8,128)(2,1)S(1)}, u32[]{:S(2)}, u32[]{:S(2)}) collective-permute-start(bf16[144,512]{1,0:T(8,128)(2,1)S(1)} %get-tuple-element.87), channel_id=1, source_target_pairs={{0,2},{2,0},{4,6},{6,4},{8,10},{10,8},{12,14},{14,12},{1,3},{3,1},... | collective-permute-start | bytes 442376 | tf_op jit(solution)/shard_map/ppermute | solution.py:435
  12.1 1.6 %collective-permute-start.6 = (bf16[144,512]{1,0:T(8,128)(2,1)S(1)}, bf16[144,512]{1,0:T(8,128)(2,1)S(1)}, u32[]{:S(2)}, u32[]{:S(2)}) collective-permute-start(bf16[144,512]{1,0:T(8,128)(2,1)S(1)} %get-tuple-element.88), channel_id=1, source_target_pairs={{0,4},{2,6},{4,0},{6,2},{8,12},{10,14},{12,8},{14,10},{1,5},{3,7},... | collective-permute-start | bytes 442376 | tf_op jit(solution)/shard_map/ppermute | solution.py:435
  13.7 0.0 collective-permute-done.refs_1_.m1
  13.7 0.0 collective-permute-start.7
  13.7 0.0 collective-permute-done.1.refs_2_.m2
  13.7 2.3 %collective-permute-done.2.refs_3_.m3 = bf16[144,512]{1,0:T(8,128)(2,1)S(1)} collective-permute-done((bf16[144,512]{1,0:T(8,128)(2,1)S(1)}, bf16[144,512]{1,0:T(8,128)(2,1)S(1)}, u32[]{:S(2)}, u32[]{:S(2)}) %collective-permute-start.2) | collective-permute-done | bytes 147488 | tf_op jit(solution)/shard_map/ppermute | solution.py:435
  16.0 0.9 %shard_map.128 = (bf16[144,512]{1,0:T(8,128)(2,1)S(1)}, bf16[3,144,512]{2,1,0:T(8,128)(2,1)S(1)}) custom-call(s32[3]{0:T(128)S(1)} %pad_add_fusion.info, bf16[144,512]{1,0:T(8,128)(2,1)S(1)} %get-tuple-element.55.refs_0_.m0, bf16[144,512]{1,0:T(8,128)(2,1)S(1)} %collective-permute-done.refs_1_.m1, bf16[144,512]{1,0:T(8,128)(2,1)S(1)} %collective-permute-done.1.refs_2_.m2, ...), custom_call_target="tpu_custom_call" | custom-call | flops 1000000 | bytes 4194304 | tf_op jit(solution)/shard_map/pallas_call | solution.py:387
  17.0 4.2 %collective-permute-start.3 = (bf16[144,512]{1,0:T(8,128)(2,1)S(1)}, bf16[144,512]{1,0:T(8,128)(2,1)S(1)}, u32[]{:S(2)}, u32[]{:S(2)}) collective-permute-start(bf16[144,512]{1,0:T(8,128)(2,1)S(1)} %get-tuple-element.59), channel_id=1, source_target_pairs={{0,12},{2,14},{4,8},{6,10},{8,4},{10,6},{12,0},{14,2},{1,13},{3,15... | collective-permute-start | bytes 442376 | tf_op jit(solution)/shard_map/ppermute | solution.py:439
  21.2 2.0 %shard_map.132 = (f32[128,2048]{1,0:T(8,128)S(1)}, f32[128,2048]{1,0:T(8,128)S(1)}, bf16[128,128]{1,0:T(8,128)(2,1)S(1)}, f32[8,2048]{1,0:T(8,128)S(1)}, f32[8,2048]{1,0:T(8,128)S(1)}) custom-call(bf16[128,2048]{1,0:T(8,128)(2,1)S(1)} %get-tuple-element.84.xc_in, bf16[128,4096]{1,0:T(8,128)(2,1)} %z_in.3, bf16[128,512]{1,0:T(8,128)(2,1)S(1)} %get-tuple-element.63.bc, ...), custom_call_target="tpu_custom_call" | custom-call | flops 300000000 | bytes 4194304 | tf_op jit(solution)/shard_map/pallas_call | solution.py:387
  23.2 0.0 collective-permute-done.5.refs_1_.m1
  23.3 0.0 collective-permute-done.6.refs_2_.m2
  23.3 0.0 collective-permute-done.7.refs_3_.m3
  23.3 0.9 %shard_map.133 = (bf16[144,512]{1,0:T(8,128)(2,1)S(1)}, bf16[3,144,512]{2,1,0:T(8,128)(2,1)S(1)}) custom-call(s32[3]{0:T(128)S(1)} %pad_add_fusion.info, bf16[144,512]{1,0:T(8,128)(2,1)S(1)} %get-tuple-element.86.refs_0_.m0, bf16[144,512]{1,0:T(8,128)(2,1)S(1)} %collective-permute-done.5.refs_1_.m1, bf16[144,512]{1,0:T(8,128)(2,1)S(1)} %collective-permute-done.6.refs_2_.m2, ...), custom_call_target="tpu_custom_call" | custom-call | flops 1000000 | bytes 4194304 | tf_op jit(solution)/shard_map/pallas_call | solution.py:387
  24.2 3.4 %collective-permute-start.8 = (bf16[144,512]{1,0:T(8,128)(2,1)S(1)}, bf16[144,512]{1,0:T(8,128)(2,1)S(1)}, u32[]{:S(2)}, u32[]{:S(2)}) collective-permute-start(bf16[144,512]{1,0:T(8,128)(2,1)S(1)} %get-tuple-element.90), channel_id=1, source_target_pairs={{0,12},{2,14},{4,8},{6,10},{8,4},{10,6},{12,0},{14,2},{1,13},{3,15... | collective-permute-start | bytes 442376 | tf_op jit(solution)/shard_map/ppermute | solution.py:439
  27.6 0.0 collective-permute-done.3.start
  27.6 0.8 %shard_map.129 = (bf16[144,512]{1,0:T(8,128)(2,1)S(1)}, bf16[144,512]{1,0:T(8,128)(2,1)S(1)}, bf16[144,512]{1,0:T(8,128)(2,1)S(1)}, bf16[144,512]{1,0:T(8,128)(2,1)S(1)}) custom-call(s32[3]{0:T(128)S(1)} %pad_add_fusion.info, bf16[144,512]{1,0:T(8,128)(2,1)S(1)} %collective-permute-done.3.start, bf16[3,144,512]{2,1,0:T(8,128)(2,1)S(1)} %get-tuple-element.60.fixed, ...), custom_call_target="tpu_custom_call" | custom-call | flops 1000000 | bytes 4194304 | tf_op jit(solution)/shard_map/pallas_call | solution.py:387
  28.5 3.2 %collective-permute-start.4 = (bf16[144,512]{1,0:T(8,128)(2,1)S(1)}, bf16[144,512]{1,0:T(8,128)(2,1)S(1)}, u32[]{:S(2)}, u32[]{:S(2)}) collective-permute-start(bf16[144,512]{1,0:T(8,128)(2,1)S(1)} %get-tuple-element.61), channel_id=1, source_target_pairs={{0,2},{2,0},{4,6},{6,4},{8,10},{10,8},{12,14},{14,12},{1,3},{3,1},... | collective-permute-start | bytes 442376 | tf_op jit(solution)/shard_map/ppermute | solution.py:435
  31.7 0.3 collective-permute-start.12
  32.0 1.2 %collective-permute-start.13 = (bf16[144,512]{1,0:T(8,128)(2,1)S(1)}, bf16[144,512]{1,0:T(8,128)(2,1)S(1)}, u32[]{:S(2)}, u32[]{:S(2)}) collective-permute-start(bf16[144,512]{1,0:T(8,128)(2,1)S(1)} %get-tuple-element.104), channel_id=1, source_target_pairs={{0,6},{2,4},{4,2},{6,0},{8,14},{10,12},{12,10},{14,8},{1,7},{3,5},... | collective-permute-start | bytes 442376 | tf_op jit(solution)/shard_map/ppermute | solution.py:435
  33.2 0.0 collective-permute-done.8.start
  33.2 0.8 %shard_map.134 = (bf16[144,512]{1,0:T(8,128)(2,1)S(1)}, bf16[144,512]{1,0:T(8,128)(2,1)S(1)}, bf16[144,512]{1,0:T(8,128)(2,1)S(1)}, bf16[144,512]{1,0:T(8,128)(2,1)S(1)}) custom-call(s32[3]{0:T(128)S(1)} %pad_add_fusion.info, bf16[144,512]{1,0:T(8,128)(2,1)S(1)} %collective-permute-done.8.start, bf16[3,144,512]{2,1,0:T(8,128)(2,1)S(1)} %get-tuple-element.91.fixed, ...), custom_call_target="tpu_custom_call" | custom-call | flops 1000000 | bytes 4194304 | tf_op jit(solution)/shard_map/pallas_call | solution.py:387
  34.1 2.0 %collective-permute-start.9 = (bf16[144,512]{1,0:T(8,128)(2,1)S(1)}, bf16[144,512]{1,0:T(8,128)(2,1)S(1)}, u32[]{:S(2)}, u32[]{:S(2)}) collective-permute-start(bf16[144,512]{1,0:T(8,128)(2,1)S(1)} %get-tuple-element.93), channel_id=1, source_target_pairs={{0,2},{2,0},{4,6},{6,4},{8,10},{10,8},{12,14},{14,12},{1,3},{3,1},... | collective-permute-start | bytes 442376 | tf_op jit(solution)/shard_map/ppermute | solution.py:435
  36.1 0.3 collective-permute-start.10
  36.4 0.7 %collective-permute-done.4.rest_1_ = bf16[144,512]{1,0:T(8,128)(2,1)S(1)} collective-permute-done((bf16[144,512]{1,0:T(8,128)(2,1)S(1)}, bf16[144,512]{1,0:T(8,128)(2,1)S(1)}, u32[]{:S(2)}, u32[]{:S(2)}) %collective-permute-start.4) | collective-permute-done | bytes 147488 | tf_op jit(solution)/shard_map/ppermute | solution.py:435
  37.2 0.5 %collective-permute-start.11 = (bf16[144,512]{1,0:T(8,128)(2,1)S(1)}, bf16[144,512]{1,0:T(8,128)(2,1)S(1)}, u32[]{:S(2)}, u32[]{:S(2)}) collective-permute-start(bf16[144,512]{1,0:T(8,128)(2,1)S(1)} %get-tuple-element.95), channel_id=1, source_target_pairs={{0,6},{2,4},{4,2},{6,0},{8,14},{10,12},{12,10},{14,8},{1,7},{3,5},... | collective-permute-start | bytes 442376 | tf_op jit(solution)/shard_map/ppermute | solution.py:435
  37.6 2.0 %shard_map.131 = (f32[128,2048]{1,0:T(8,128)S(1)}, f32[128,2048]{1,0:T(8,128)S(1)}, bf16[128,128]{1,0:T(8,128)(2,1)S(1)}, f32[8,2048]{1,0:T(8,128)S(1)}, f32[8,2048]{1,0:T(8,128)S(1)}) custom-call(bf16[128,2048]{1,0:T(8,128)(2,1)S(1)} %get-tuple-element.71.xc_in, bf16[128,4096]{1,0:T(8,128)(2,1)} %z_in.3, bf16[128,512]{1,0:T(8,128)(2,1)S(1)} %get-tuple-element.63.bc, ...), custom_call_target="tpu_custom_call" | custom-call | flops 300000000 | bytes 4194304 | tf_op jit(solution)/shard_map/pallas_call | solution.py:387
  39.6 0.0 collective-permute-done.12.rest_2_
  39.6 0.0 collective-permute-done.13.rest_3_
  39.6 1.9 %shard_map.135.rest_4_ = bf16[128,4096]{1,0:T(8,128)(2,1)} custom-call(s32[3]{0:T(128)S(1)} %pad_add_fusion.info, f32[128,2048]{1,0:T(8,128)S(1)} %get-tuple-element.96.near, f32[128,2048]{1,0:T(8,128)S(1)} %get-tuple-element.97.gain, bf16[128,128]{1,0:T(8,128)(2,1)S(1)} %get-tuple-element.98.cmat, f32[8,2048]{1,0:T(8,128)S(1)} %get-tuple-element.99.rate_top, ...), custom_call_target="tpu_custom_call" | custom-call | flops 100000000 | bytes 4194304 | tf_op jit(solution)/shard_map/pallas_call | solution.py:387
  41.5 0.3 collective-permute-done.9.rest_1_
  41.8 1.4 %collective-permute-done.10.rest_2_ = bf16[144,512]{1,0:T(8,128)(2,1)S(1)} collective-permute-done((bf16[144,512]{1,0:T(8,128)(2,1)S(1)}, bf16[144,512]{1,0:T(8,128)(2,1)S(1)}, u32[]{:S(2)}, u32[]{:S(2)}) %collective-permute-start.10) | collective-permute-done | bytes 147488 | tf_op jit(solution)/shard_map/ppermute | solution.py:435
  43.2 1.2 %collective-permute-done.11.rest_3_ = bf16[144,512]{1,0:T(8,128)(2,1)S(1)} collective-permute-done((bf16[144,512]{1,0:T(8,128)(2,1)S(1)}, bf16[144,512]{1,0:T(8,128)(2,1)S(1)}, u32[]{:S(2)}, u32[]{:S(2)}) %collective-permute-start.11) | collective-permute-done | bytes 147488 | tf_op jit(solution)/shard_map/ppermute | solution.py:435
  44.4 1.9 %shard_map.136 = bf16[128,4096]{1,0:T(8,128)(2,1)} custom-call(s32[3]{0:T(128)S(1)} %pad_add_fusion.info, f32[128,2048]{1,0:T(8,128)S(1)} %get-tuple-element.76.near, f32[128,2048]{1,0:T(8,128)S(1)} %get-tuple-element.77.gain, bf16[128,128]{1,0:T(8,128)(2,1)S(1)} %get-tuple-element.78.cmat, ...), custom_call_target="tpu_custom_call", output_to_operand_aliasing={{}: (13, {})} | custom-call | flops 100000000 | bytes 4194304 | tf_op jit(solution)/shard_map/pallas_call | solution.py:387
Async XLA Ops:
  3.7 10.0 %collective-permute-start = (bf16[144,512]{1,0:T(8,128)(2,1)S(1)}, bf16[144,512]{1,0:T(8,128)(2,1)S(1)}, u32[]{:S(2)}, u32[]{:S(2)}) collective-permute-start(bf16[144,512]{1,0:T(8,128)(2,1)S(1)} %get-tuple-element.56), channel_id=1, source_target_pairs={{0,2},{2,0},{4,6},{6,4},{8,10},{10,8},{12,14},{14,12},{1,3},{3,1},... | collective-permute-start | bytes 442376 | tf_op jit(solution)/shard_map/ppermute | solution.py:435
  6.7 7.0 %collective-permute-start.1 = (bf16[144,512]{1,0:T(8,128)(2,1)S(1)}, bf16[144,512]{1,0:T(8,128)(2,1)S(1)}, u32[]{:S(2)}, u32[]{:S(2)}) collective-permute-start(bf16[144,512]{1,0:T(8,128)(2,1)S(1)} %get-tuple-element.57), channel_id=1, source_target_pairs={{0,4},{2,6},{4,0},{6,2},{8,12},{10,14},{12,8},{14,10},{1,5},{3,7},... | collective-permute-start | bytes 442376 | tf_op jit(solution)/shard_map/ppermute | solution.py:435
  8.3 7.7 %collective-permute-start.2 = (bf16[144,512]{1,0:T(8,128)(2,1)S(1)}, bf16[144,512]{1,0:T(8,128)(2,1)S(1)}, u32[]{:S(2)}, u32[]{:S(2)}) collective-permute-start(bf16[144,512]{1,0:T(8,128)(2,1)S(1)} %get-tuple-element.58), channel_id=1, source_target_pairs={{0,6},{2,4},{4,2},{6,0},{8,14},{10,12},{12,10},{14,8},{1,7},{3,5},... | collective-permute-start | bytes 442376 | tf_op jit(solution)/shard_map/ppermute | solution.py:435
  10.2 13.1 %collective-permute-start.5 = (bf16[144,512]{1,0:T(8,128)(2,1)S(1)}, bf16[144,512]{1,0:T(8,128)(2,1)S(1)}, u32[]{:S(2)}, u32[]{:S(2)}) collective-permute-start(bf16[144,512]{1,0:T(8,128)(2,1)S(1)} %get-tuple-element.87), channel_id=1, source_target_pairs={{0,2},{2,0},{4,6},{6,4},{8,10},{10,8},{12,14},{14,12},{1,3},{3,1},... | collective-permute-start | bytes 442376 | tf_op jit(solution)/shard_map/ppermute | solution.py:435
  12.1 11.1 %collective-permute-start.6 = (bf16[144,512]{1,0:T(8,128)(2,1)S(1)}, bf16[144,512]{1,0:T(8,128)(2,1)S(1)}, u32[]{:S(2)}, u32[]{:S(2)}) collective-permute-start(bf16[144,512]{1,0:T(8,128)(2,1)S(1)} %get-tuple-element.88), channel_id=1, source_target_pairs={{0,4},{2,6},{4,0},{6,2},{8,12},{10,14},{12,8},{14,10},{1,5},{3,7},... | collective-permute-start | bytes 442376 | tf_op jit(solution)/shard_map/ppermute | solution.py:435
  13.7 9.5 %collective-permute-start.7 = (bf16[144,512]{1,0:T(8,128)(2,1)S(1)}, bf16[144,512]{1,0:T(8,128)(2,1)S(1)}, u32[]{:S(2)}, u32[]{:S(2)}) collective-permute-start(bf16[144,512]{1,0:T(8,128)(2,1)S(1)} %get-tuple-element.89), channel_id=1, source_target_pairs={{0,6},{2,4},{4,2},{6,0},{8,14},{10,12},{12,10},{14,8},{1,7},{3,5},... | collective-permute-start | bytes 442376 | tf_op jit(solution)/shard_map/ppermute | solution.py:435
  17.0 10.7 %collective-permute-start.3 = (bf16[144,512]{1,0:T(8,128)(2,1)S(1)}, bf16[144,512]{1,0:T(8,128)(2,1)S(1)}, u32[]{:S(2)}, u32[]{:S(2)}) collective-permute-start(bf16[144,512]{1,0:T(8,128)(2,1)S(1)} %get-tuple-element.59), channel_id=1, source_target_pairs={{0,12},{2,14},{4,8},{6,10},{8,4},{10,6},{12,0},{14,2},{1,13},{3,15... | collective-permute-start | bytes 442376 | tf_op jit(solution)/shard_map/ppermute | solution.py:439
  24.2 9.0 %collective-permute-start.8 = (bf16[144,512]{1,0:T(8,128)(2,1)S(1)}, bf16[144,512]{1,0:T(8,128)(2,1)S(1)}, u32[]{:S(2)}, u32[]{:S(2)}) collective-permute-start(bf16[144,512]{1,0:T(8,128)(2,1)S(1)} %get-tuple-element.90), channel_id=1, source_target_pairs={{0,12},{2,14},{4,8},{6,10},{8,4},{10,6},{12,0},{14,2},{1,13},{3,15... | collective-permute-start | bytes 442376 | tf_op jit(solution)/shard_map/ppermute | solution.py:439
  28.5 8.7 %collective-permute-start.4 = (bf16[144,512]{1,0:T(8,128)(2,1)S(1)}, bf16[144,512]{1,0:T(8,128)(2,1)S(1)}, u32[]{:S(2)}, u32[]{:S(2)}) collective-permute-start(bf16[144,512]{1,0:T(8,128)(2,1)S(1)} %get-tuple-element.61), channel_id=1, source_target_pairs={{0,2},{2,0},{4,6},{6,4},{8,10},{10,8},{12,14},{14,12},{1,3},{3,1},... | collective-permute-start | bytes 442376 | tf_op jit(solution)/shard_map/ppermute | solution.py:435
  31.7 8.0 %collective-permute-start.12 = (bf16[144,512]{1,0:T(8,128)(2,1)S(1)}, bf16[144,512]{1,0:T(8,128)(2,1)S(1)}, u32[]{:S(2)}, u32[]{:S(2)}) collective-permute-start(bf16[144,512]{1,0:T(8,128)(2,1)S(1)} %get-tuple-element.103), channel_id=1, source_target_pairs={{0,4},{2,6},{4,0},{6,2},{8,12},{10,14},{12,8},{14,10},{1,5},{3,7},... | collective-permute-start | bytes 442376 | tf_op jit(solution)/shard_map/ppermute | solution.py:435
  32.0 7.6 %collective-permute-start.13 = (bf16[144,512]{1,0:T(8,128)(2,1)S(1)}, bf16[144,512]{1,0:T(8,128)(2,1)S(1)}, u32[]{:S(2)}, u32[]{:S(2)}) collective-permute-start(bf16[144,512]{1,0:T(8,128)(2,1)S(1)} %get-tuple-element.104), channel_id=1, source_target_pairs={{0,6},{2,4},{4,2},{6,0},{8,14},{10,12},{12,10},{14,8},{1,7},{3,5},... | collective-permute-start | bytes 442376 | tf_op jit(solution)/shard_map/ppermute | solution.py:435
  34.1 7.7 %collective-permute-start.9 = (bf16[144,512]{1,0:T(8,128)(2,1)S(1)}, bf16[144,512]{1,0:T(8,128)(2,1)S(1)}, u32[]{:S(2)}, u32[]{:S(2)}) collective-permute-start(bf16[144,512]{1,0:T(8,128)(2,1)S(1)} %get-tuple-element.93), channel_id=1, source_target_pairs={{0,2},{2,0},{4,6},{6,4},{8,10},{10,8},{12,14},{14,12},{1,3},{3,1},... | collective-permute-start | bytes 442376 | tf_op jit(solution)/shard_map/ppermute | solution.py:435
  36.1 7.1 %collective-permute-start.10 = (bf16[144,512]{1,0:T(8,128)(2,1)S(1)}, bf16[144,512]{1,0:T(8,128)(2,1)S(1)}, u32[]{:S(2)}, u32[]{:S(2)}) collective-permute-start(bf16[144,512]{1,0:T(8,128)(2,1)S(1)} %get-tuple-element.94), channel_id=1, source_target_pairs={{0,4},{2,6},{4,0},{6,2},{8,12},{10,14},{12,8},{14,10},{1,5},{3,7},... | collective-permute-start | bytes 442376 | tf_op jit(solution)/shard_map/ppermute | solution.py:435
  37.2 7.2 %collective-permute-start.11 = (bf16[144,512]{1,0:T(8,128)(2,1)S(1)}, bf16[144,512]{1,0:T(8,128)(2,1)S(1)}, u32[]{:S(2)}, u32[]{:S(2)}) collective-permute-start(bf16[144,512]{1,0:T(8,128)(2,1)S(1)} %get-tuple-element.95), channel_id=1, source_target_pairs={{0,6},{2,4},{4,2},{6,0},{8,14},{10,12},{12,10},{14,8},{1,7},{3,5},... | collective-permute-start | bytes 442376 | tf_op jit(solution)/shard_map/ppermute | solution.py:435

commit v8 on v7

--- a/solution.py
+++ b/solution.py
@@ -236,7 +236,8 @@
     xc = jnp.where(tokens(0, xc.shape, 0) < taps - 1, xc, 0.0)
     both = silu_of_half(jnp.concatenate([btotal, ctotal], axis=1))
     both = jnp.where(tokens(0, both.shape, 0) < taps - 1, both, 0.0)
-    rows = jnp.concatenate([xc, jnp.concatenate([both, jnp.zeros_like(both)], axis=1)], axis=0).astype(BF16)
+    rows = pltpu.roll(jnp.concatenate([both, jnp.zeros_like(both)], axis=1), taps - 1, 0)
+    rows = jnp.where(tokens(0, rows.shape, 0) < taps - 1, xc, rows).astype(BF16)
     scaled, bmat = xc * lower, both[:, 0:STATE]
     scaled = jnp.concatenate([scaled, jnp.zeros_like(scaled)], axis=0).astype(BF16)
     bmat = jnp.concatenate([bmat, jnp.zeros_like(bmat)], axis=0).astype(BF16)
@@ -263,7 +264,7 @@
                 add, rows = top_state(taps, extra[b], extra[b - 1])
                 own = block[b][0:STATE, :].astype(F32) + add
                 fixed[b - 1, 0:STATE, :] = own.astype(BF16)
-                fixed[b - 1, STATE : STATE + EXTRA, :] = rows
+                fixed[b - 1, STATE : STATE + TILE, :] = rows
                 state = own + carry_row(extra[b]) * state
                 through = through * carry_row(extra[b])
             total[0:STATE, :] = state.astype(BF16)
@@ -275,7 +276,7 @@
 def enter_kernel(taps, info, start, fixed, m0, m1, m2, m3, o0, o1, o2, o3):
     msgs = (m0, m1, m2, m3)
     outs = (o0, o1, o2, o3)
-    lower = slice(STATE, STATE + EXTRA)
+    lower = slice(STATE, STATE + TILE)
     prior = extra_of(start)
     for mine in range(QUAD):
 
@@ -342,7 +343,8 @@
     part = rows // steps
     square = [0.0] * steps
     ats = [pl.ds(pl.multiple_of((mine ^ k) * width, width), width) for k in range(QUAD)]
-    first = rest[0][STATE : STATE + EXTRA, 0 : 2 * STATE].astype(F32)[TILE:EXTRA]
+    first = pltpu.roll(rest[0][STATE : STATE + TILE, 0 : 2 * STATE].astype(F32), TILE - taps + 1, 0)
+    first = jnp.where(tokens(0, first.shape, 0) < taps - 1, first, 0.0)
     c = cmat[...].astype(F32)
     top = jnp.where(tokens(0, (TILE, STATE), 0) < taps - 1, first[:, STATE:], c[0:TILE])
     c = jnp.concatenate([top, c[TILE:]], axis=0)
@@ -350,7 +352,8 @@
     scores = lax.dot_general(c.astype(BF16), bmat, (((1,), (1,)), ((), ())), preferred_element_type=F32)
     left = jnp.concatenate([c * live[...], scores * mask[:, 0 : 2 * TILE]], axis=1).astype(BF16)
     for at, e in zip(ats, rest):
-        xc = e[STATE : STATE + EXTRA, :].astype(F32)[0:TILE]
+        xc = e[STATE : STATE + TILE, :].astype(F32)
+        xc = jnp.where(tokens(0, xc.shape, 0) < taps - 1, xc, 0.0)
         sent = jnp.concatenate([xc * rate_top[:, at], jnp.zeros_like(xc)], axis=0).astype(BF16)
         far = mm(left, jnp.concatenate([e[0:STATE, :], sent], axis=0))
         for i in range(steps):
@@ -436,7 +439,7 @@
         return [values[0], swapped[1], swapped[2], swapped[3]]
 
     def ahead(value):
-        return lax.ppermute(value, "seq", [(i, (i + QUAD) % peers ^ 2) for i in range(peers)])
+        return lax.ppermute(value, "seq", [(i, i + QUAD ^ 2) for i in range(peers - QUAD)])
 
     first_args = [
         lengths, x_in, bc_in, conv_x_weight, bx, dt_raw.T, dt_bias.reshape(1, heads), decay.reshape(1, heads),
@@ -509,7 +512,7 @@
 
     entering, fixes = [], []
     for g in range(groups):
-        outs = [sent, ((QUAD - 1, STATE + EXTRA, width), BF16)]
+        outs = [sent, ((QUAD - 1, STATE + TILE, width), BF16)]
         args = list(msgs[g])
         if reach > 1:
             outs.append(((8, width), F32))
@@ -526,7 +529,7 @@
 
     blocks = []
     for g in range(groups):
-        outs = [sent] * QUAD
+        outs = [((STATE + TILE, width), BF16)] * QUAD
         kernel = functools.partial(enter_kernel, taps)
         blocks.append(swap(call(kernel, (info,), [entering[g], fixes[g], *msgs[g]], outs, 1_000_000)))
 
@@ -552,7 +555,7 @@
             scratch_shapes=[
                 pltpu.VMEM((rows, wide), BF16),
                 pltpu.VMEM((rows, wide), F32),
-                pltpu.SemaphoreType.DMA((4,)),
+                pltpu.SemaphoreType.DMA((2,)),
             ],
             input_output_aliases=aliases,
         )

time: 46.5 us -> 45.7 us (0.983)
  waiting for transfers between devices: 5.89 us -> 4.65 us
    ppermute x12, waiting for transfers between devices: 5.88 us -> 4.64 us  [swap(): swapped = {k: lax.ppermute(values[k], 'seq', routes[k]) for k in (3, 1, 2)}]
  transfers between devices with their start and end apart: 14 -> 14, of which waited for: 5 -> 4; matrix products, arithmetic and copies ran while one was open for 0% -> 0% of each run, Pallas kernels for 24% -> 25%
where the time goes in v8:
time: 45.7 us; the launch traced here: 45.4 us
  starting transfers between devices  23.8 us (52%)
  Pallas kernels  16.8 us (37%)
  waiting for transfers between devices  4.65 us (10%)
    pallas_call x10, Pallas kernels, call(): pl.pallas_call(kernel, in_specs=[SMEM] * len(scalars) + more.pop('specs',...  16.8 us
    ppermute x12, starting transfers between devices, swap(): swapped = {k: lax.ppermute(values[k], 'seq', routes[k]) for k in (3, 1, 2)}  15.8 us
    ppermute x2, starting transfers between devices, ahead(): lax.ppermute(value, 'seq', [(i, i + QUAD ^ 2) for i in range(peers - QUAD)])  7.93 us
    ppermute x12, waiting for transfers between devices, swap(): swapped = {k: lax.ppermute(values[k], 'seq', routes[k]) for k in (3, 1, 2)}  4.64 us
  transfers between devices with their start and end apart: 14, of which 4 were waited for; matrix products, arithmetic and copies ran while one was open for 0% of the time, Pallas kernels for 25%

profile of v8, /device:TPU:0, one launch (start us, length us, event | category | flops | bytes accessed | tf_op | source)
XLA Modules:
  0.0 45.4 jit_solution(17508695733037175948)
XLA Ops:
  0.0 0.1 pad_add_fusion.info
  0.1 3.6 %shard_map.127 = (bf16[128,4096]{1,0:T(8,128)(2,1)S(1)}, bf16[128,512]{1,0:T(8,128)(2,1)S(1)}, bf16[408,128]{1,0:T(8,128)(2,1)S(1)}, f32[128,128]{1,0:T(8,128)S(...) custom-call(s32[3]{0:T(128)S(1)} %pad_add_fusion.info, ...), custom_call_target="tpu_custom_call" | custom-call | flops 600000000 | bytes 4194304 | tf_op jit(solution)/shard_map/pallas_call | solution.py:390
  3.7 3.0 %collective-permute-start = (bf16[144,512]{1,0:T(8,128)(2,1)S(1)}, bf16[144,512]{1,0:T(8,128)(2,1)S(1)}, u32[]{:S(2)}, u32[]{:S(2)}) collective-permute-start(bf16[144,512]{1,0:T(8,128)(2,1)S(1)} %get-tuple-element.56), channel_id=1, source_target_pairs={{0,2},{2,0},{4,6},{6,4},{8,10},{10,8},{12,14},{14,12},{1,3},{3,1},... | collective-permute-start | bytes 442376 | tf_op jit(solution)/shard_map/ppermute | solution.py:438
  6.7 1.6 %collective-permute-start.1 = (bf16[144,512]{1,0:T(8,128)(2,1)S(1)}, bf16[144,512]{1,0:T(8,128)(2,1)S(1)}, u32[]{:S(2)}, u32[]{:S(2)}) collective-permute-start(bf16[144,512]{1,0:T(8,128)(2,1)S(1)} %get-tuple-element.57), channel_id=1, source_target_pairs={{0,4},{2,6},{4,0},{6,2},{8,12},{10,14},{12,8},{14,10},{1,5},{3,7},... | collective-permute-start | bytes 442376 | tf_op jit(solution)/shard_map/ppermute | solution.py:438
  8.3 0.0 collective-permute-start.2
  8.3 1.8 %shard_map.130 = (bf16[128,2048]{1,0:T(8,128)(2,1)S(1)}, bf16[144,512]{1,0:T(8,128)(2,1)S(1)}, bf16[144,512]{1,0:T(8,128)(2,1)S(1)}, bf16[144,512]{1,0:T(8,128)(2,1)S(1)}, bf16[144,512]{1,0:T(8,128)(2,1)S(1)}) custom-call(s32[3]{0:T(128)S(1)} %pad_add_fusion.info, bf16[128,4096]{1,0:T(8,128)(2,1)S(1)} %get-tuple-element.62.x, ...), custom_call_target="tpu_custom_call" | custom-call | flops 300000000 | bytes 4194304 | tf_op jit(solution)/shard_map/pallas_call | solution.py:390
  10.2 2.0 %collective-permute-start.5 = (bf16[144,512]{1,0:T(8,128)(2,1)S(1)}, bf16[144,512]{1,0:T(8,128)(2,1)S(1)}, u32[]{:S(2)}, u32[]{:S(2)}) collective-permute-start(bf16[144,512]{1,0:T(8,128)(2,1)S(1)} %get-tuple-element.87), channel_id=1, source_target_pairs={{0,2},{2,0},{4,6},{6,4},{8,10},{10,8},{12,14},{14,12},{1,3},{3,1},... | collective-permute-start | bytes 442376 | tf_op jit(solution)/shard_map/ppermute | solution.py:438
  12.1 1.6 %collective-permute-start.6 = (bf16[144,512]{1,0:T(8,128)(2,1)S(1)}, bf16[144,512]{1,0:T(8,128)(2,1)S(1)}, u32[]{:S(2)}, u32[]{:S(2)}) collective-permute-start(bf16[144,512]{1,0:T(8,128)(2,1)S(1)} %get-tuple-element.88), channel_id=1, source_target_pairs={{0,4},{2,6},{4,0},{6,2},{8,12},{10,14},{12,8},{14,10},{1,5},{3,7},... | collective-permute-start | bytes 442376 | tf_op jit(solution)/shard_map/ppermute | solution.py:438
  13.7 0.0 collective-permute-done.refs_1_.m1
  13.7 0.0 collective-permute-start.7
  13.7 0.0 collective-permute-done.1.refs_2_.m2
  13.7 2.3 %collective-permute-done.2.refs_3_.m3 = bf16[144,512]{1,0:T(8,128)(2,1)S(1)} collective-permute-done((bf16[144,512]{1,0:T(8,128)(2,1)S(1)}, bf16[144,512]{1,0:T(8,128)(2,1)S(1)}, u32[]{:S(2)}, u32[]{:S(2)}) %collective-permute-start.2) | collective-permute-done | bytes 147488 | tf_op jit(solution)/shard_map/ppermute | solution.py:438
  16.0 0.9 %shard_map.128 = (bf16[144,512]{1,0:T(8,128)(2,1)S(1)}, bf16[3,136,512]{2,1,0:T(8,128)(2,1)S(1)}) custom-call(s32[3]{0:T(128)S(1)} %pad_add_fusion.info, bf16[144,512]{1,0:T(8,128)(2,1)S(1)} %get-tuple-element.55.refs_0_.m0, bf16[144,512]{1,0:T(8,128)(2,1)S(1)} %collective-permute-done.refs_1_.m1, bf16[144,512]{1,0:T(8,128)(2,1)S(1)} %collective-permute-done.1.refs_2_.m2, ...), custom_call_target="tpu_custom_call" | custom-call | flops 1000000 | bytes 4194304 | tf_op jit(solution)/shard_map/pallas_call | solution.py:390
  17.0 6.1 %collective-permute-start.3 = (bf16[144,512]{1,0:T(8,128)(2,1)S(1)}, bf16[144,512]{1,0:T(8,128)(2,1)S(1)}, u32[]{:S(2)}, u32[]{:S(2)}) collective-permute-start(bf16[144,512]{1,0:T(8,128)(2,1)S(1)} %get-tuple-element.59), channel_id=1, source_target_pairs={{0,12},{2,14},{4,8},{6,10},{1,13},{3,15},{5,9},{7,11},{16,28},{18,... | collective-permute-start | bytes 442376 | tf_op jit(solution)/shard_map/ppermute | solution.py:442
  23.1 2.0 %shard_map.132 = (f32[128,2048]{1,0:T(8,128)S(1)}, f32[128,2048]{1,0:T(8,128)S(1)}, bf16[128,128]{1,0:T(8,128)(2,1)S(1)}, f32[8,2048]{1,0:T(8,128)S(1)}, f32[8,2048]{1,0:T(8,128)S(1)}) custom-call(bf16[128,2048]{1,0:T(8,128)(2,1)S(1)} %get-tuple-element.84.xc_in, bf16[128,4096]{1,0:T(8,128)(2,1)} %z_in.3, bf16[128,512]{1,0:T(8,128)(2,1)S(1)} %get-tuple-element.63.bc, ...), custom_call_target="tpu_custom_call" | custom-call | flops 300000000 | bytes 4194304 | tf_op jit(solution)/shard_map/pallas_call | solution.py:390
  25.1 0.0 collective-permute-done.5.refs_1_.m1
  25.1 0.0 collective-permute-done.6.refs_2_.m2
  25.1 0.0 collective-permute-done.7.refs_3_.m3
  25.1 0.9 %shard_map.133 = (bf16[144,512]{1,0:T(8,128)(2,1)S(1)}, bf16[3,136,512]{2,1,0:T(8,128)(2,1)S(1)}) custom-call(s32[3]{0:T(128)S(1)} %pad_add_fusion.info, bf16[144,512]{1,0:T(8,128)(2,1)S(1)} %get-tuple-element.86.refs_0_.m0, bf16[144,512]{1,0:T(8,128)(2,1)S(1)} %collective-permute-done.5.refs_1_.m1, bf16[144,512]{1,0:T(8,128)(2,1)S(1)} %collective-permute-done.6.refs_2_.m2, ...), custom_call_target="tpu_custom_call" | custom-call | flops 1000000 | bytes 4194304 | tf_op jit(solution)/shard_map/pallas_call | solution.py:390
  26.1 1.8 %collective-permute-start.8 = (bf16[144,512]{1,0:T(8,128)(2,1)S(1)}, bf16[144,512]{1,0:T(8,128)(2,1)S(1)}, u32[]{:S(2)}, u32[]{:S(2)}) collective-permute-start(bf16[144,512]{1,0:T(8,128)(2,1)S(1)} %get-tuple-element.90), channel_id=1, source_target_pairs={{0,12},{2,14},{4,8},{6,10},{1,13},{3,15},{5,9},{7,11},{16,28},{18,... | collective-permute-start | bytes 442376 | tf_op jit(solution)/shard_map/ppermute | solution.py:442
  27.9 0.0 collective-permute-done.3.start
  27.9 0.8 %shard_map.129 = (bf16[136,512]{1,0:T(8,128)(2,1)S(1)}, bf16[136,512]{1,0:T(8,128)(2,1)S(1)}, bf16[136,512]{1,0:T(8,128)(2,1)S(1)}, bf16[136,512]{1,0:T(8,128)(2,1)S(1)}) custom-call(s32[3]{0:T(128)S(1)} %pad_add_fusion.info, bf16[144,512]{1,0:T(8,128)(2,1)S(1)} %collective-permute-done.3.start, bf16[3,136,512]{2,1,0:T(8,128)(2,1)S(1)} %get-tuple-element.60.fixed, ...), custom_call_target="tpu_custom_call" | custom-call | flops 1000000 | bytes 4194304 | tf_op jit(solution)/shard_map/pallas_call | solution.py:390
  28.8 3.2 %collective-permute-start.4 = (bf16[136,512]{1,0:T(8,128)(2,1)S(1)}, bf16[136,512]{1,0:T(8,128)(2,1)S(1)}, u32[]{:S(2)}, u32[]{:S(2)}) collective-permute-start(bf16[136,512]{1,0:T(8,128)(2,1)S(1)} %get-tuple-element.61), channel_id=1, source_target_pairs={{0,2},{2,0},{4,6},{6,4},{8,10},{10,8},{12,14},{14,12},{1,3},{3,1},... | collective-permute-start | bytes 417800 | tf_op jit(solution)/shard_map/ppermute | solution.py:438
  32.0 0.0 collective-permute-start.12
  32.0 1.5 %collective-permute-start.13 = (bf16[136,512]{1,0:T(8,128)(2,1)S(1)}, bf16[136,512]{1,0:T(8,128)(2,1)S(1)}, u32[]{:S(2)}, u32[]{:S(2)}) collective-permute-start(bf16[136,512]{1,0:T(8,128)(2,1)S(1)} %get-tuple-element.104), channel_id=1, source_target_pairs={{0,6},{2,4},{4,2},{6,0},{8,14},{10,12},{12,10},{14,8},{1,7},{3,5},... | collective-permute-start | bytes 417800 | tf_op jit(solution)/shard_map/ppermute | solution.py:438
  33.5 0.0 collective-permute-done.8.start
  33.5 0.8 %shard_map.134 = (bf16[136,512]{1,0:T(8,128)(2,1)S(1)}, bf16[136,512]{1,0:T(8,128)(2,1)S(1)}, bf16[136,512]{1,0:T(8,128)(2,1)S(1)}, bf16[136,512]{1,0:T(8,128)(2,1)S(1)}) custom-call(s32[3]{0:T(128)S(1)} %pad_add_fusion.info, bf16[144,512]{1,0:T(8,128)(2,1)S(1)} %collective-permute-done.8.start, bf16[3,136,512]{2,1,0:T(8,128)(2,1)S(1)} %get-tuple-element.91.fixed, ...), custom_call_target="tpu_custom_call" | custom-call | flops 1000000 | bytes 4194304 | tf_op jit(solution)/shard_map/pallas_call | solution.py:390
  34.4 2.0 %collective-permute-start.9 = (bf16[136,512]{1,0:T(8,128)(2,1)S(1)}, bf16[136,512]{1,0:T(8,128)(2,1)S(1)}, u32[]{:S(2)}, u32[]{:S(2)}) collective-permute-start(bf16[136,512]{1,0:T(8,128)(2,1)S(1)} %get-tuple-element.93), channel_id=1, source_target_pairs={{0,2},{2,0},{4,6},{6,4},{8,10},{10,8},{12,14},{14,12},{1,3},{3,1},... | collective-permute-start | bytes 417800 | tf_op jit(solution)/shard_map/ppermute | solution.py:438
  36.4 0.0 collective-permute-start.10
  36.4 0.6 %collective-permute-done.4.rest_1_ = bf16[136,512]{1,0:T(8,128)(2,1)S(1)} collective-permute-done((bf16[136,512]{1,0:T(8,128)(2,1)S(1)}, bf16[136,512]{1,0:T(8,128)(2,1)S(1)}, u32[]{:S(2)}, u32[]{:S(2)}) %collective-permute-start.4) | collective-permute-done | bytes 139296 | tf_op jit(solution)/shard_map/ppermute | solution.py:438
  37.0 1.0 %collective-permute-start.11 = (bf16[136,512]{1,0:T(8,128)(2,1)S(1)}, bf16[136,512]{1,0:T(8,128)(2,1)S(1)}, u32[]{:S(2)}, u32[]{:S(2)}) collective-permute-start(bf16[136,512]{1,0:T(8,128)(2,1)S(1)} %get-tuple-element.95), channel_id=1, source_target_pairs={{0,6},{2,4},{4,2},{6,0},{8,14},{10,12},{12,10},{14,8},{1,7},{3,5},... | collective-permute-start | bytes 417800 | tf_op jit(solution)/shard_map/ppermute | solution.py:438
  37.9 2.0 %shard_map.131 = (f32[128,2048]{1,0:T(8,128)S(1)}, f32[128,2048]{1,0:T(8,128)S(1)}, bf16[128,128]{1,0:T(8,128)(2,1)S(1)}, f32[8,2048]{1,0:T(8,128)S(1)}, f32[8,2048]{1,0:T(8,128)S(1)}) custom-call(bf16[128,2048]{1,0:T(8,128)(2,1)S(1)} %get-tuple-element.71.xc_in, bf16[128,4096]{1,0:T(8,128)(2,1)} %z_in.3, bf16[128,512]{1,0:T(8,128)(2,1)S(1)} %get-tuple-element.63.bc, ...), custom_call_target="tpu_custom_call" | custom-call | flops 300000000 | bytes 4194304 | tf_op jit(solution)/shard_map/pallas_call | solution.py:390
  39.9 0.0 collective-permute-done.12.rest_2_
  39.9 0.7 %collective-permute-done.13.rest_3_ = bf16[136,512]{1,0:T(8,128)(2,1)S(1)} collective-permute-done((bf16[136,512]{1,0:T(8,128)(2,1)S(1)}, bf16[136,512]{1,0:T(8,128)(2,1)S(1)}, u32[]{:S(2)}, u32[]{:S(2)}) %collective-permute-start.13) | collective-permute-done | bytes 139296 | tf_op jit(solution)/shard_map/ppermute | solution.py:438
  40.6 1.9 %shard_map.135.rest_4_ = bf16[128,4096]{1,0:T(8,128)(2,1)} custom-call(s32[3]{0:T(128)S(1)} %pad_add_fusion.info, f32[128,2048]{1,0:T(8,128)S(1)} %get-tuple-element.96.near, f32[128,2048]{1,0:T(8,128)S(1)} %get-tuple-element.97.gain, bf16[128,128]{1,0:T(8,128)(2,1)S(1)} %get-tuple-element.98.cmat, f32[8,2048]{1,0:T(8,128)S(1)} %get-tuple-element.99.rate_top, ...), custom_call_target="tpu_custom_call" | custom-call | flops 100000000 | bytes 4194304 | tf_op jit(solution)/shard_map/pallas_call | solution.py:390
  42.5 0.0 collective-permute-done.9.rest_1_
  42.5 0.0 collective-permute-done.10.rest_2_
  42.5 1.0 %collective-permute-done.11.rest_3_ = bf16[136,512]{1,0:T(8,128)(2,1)S(1)} collective-permute-done((bf16[136,512]{1,0:T(8,128)(2,1)S(1)}, bf16[136,512]{1,0:T(8,128)(2,1)S(1)}, u32[]{:S(2)}, u32[]{:S(2)}) %collective-permute-start.11) | collective-permute-done | bytes 139296 | tf_op jit(solution)/shard_map/ppermute | solution.py:438
  43.6 1.9 %shard_map.136 = bf16[128,4096]{1,0:T(8,128)(2,1)} custom-call(s32[3]{0:T(128)S(1)} %pad_add_fusion.info, f32[128,2048]{1,0:T(8,128)S(1)} %get-tuple-element.76.near, f32[128,2048]{1,0:T(8,128)S(1)} %get-tuple-element.77.gain, bf16[128,128]{1,0:T(8,128)(2,1)S(1)} %get-tuple-element.78.cmat, ...), custom_call_target="tpu_custom_call", output_to_operand_aliasing={{}: (13, {})} | custom-call | flops 100000000 | bytes 4194304 | tf_op jit(solution)/shard_map/pallas_call | solution.py:390
Async XLA Ops:
  3.7 10.0 %collective-permute-start = (bf16[144,512]{1,0:T(8,128)(2,1)S(1)}, bf16[144,512]{1,0:T(8,128)(2,1)S(1)}, u32[]{:S(2)}, u32[]{:S(2)}) collective-permute-start(bf16[144,512]{1,0:T(8,128)(2,1)S(1)} %get-tuple-element.56), channel_id=1, source_target_pairs={{0,2},{2,0},{4,6},{6,4},{8,10},{10,8},{12,14},{14,12},{1,3},{3,1},... | collective-permute-start | bytes 442376 | tf_op jit(solution)/shard_map/ppermute | solution.py:438
  6.7 7.0 %collective-permute-start.1 = (bf16[144,512]{1,0:T(8,128)(2,1)S(1)}, bf16[144,512]{1,0:T(8,128)(2,1)S(1)}, u32[]{:S(2)}, u32[]{:S(2)}) collective-permute-start(bf16[144,512]{1,0:T(8,128)(2,1)S(1)} %get-tuple-element.57), channel_id=1, source_target_pairs={{0,4},{2,6},{4,0},{6,2},{8,12},{10,14},{12,8},{14,10},{1,5},{3,7},... | collective-permute-start | bytes 442376 | tf_op jit(solution)/shard_map/ppermute | solution.py:438
  8.3 7.7 %collective-permute-start.2 = (bf16[144,512]{1,0:T(8,128)(2,1)S(1)}, bf16[144,512]{1,0:T(8,128)(2,1)S(1)}, u32[]{:S(2)}, u32[]{:S(2)}) collective-permute-start(bf16[144,512]{1,0:T(8,128)(2,1)S(1)} %get-tuple-element.58), channel_id=1, source_target_pairs={{0,6},{2,4},{4,2},{6,0},{8,14},{10,12},{12,10},{14,8},{1,7},{3,5},... | collective-permute-start | bytes 442376 | tf_op jit(solution)/shard_map/ppermute | solution.py:438
  10.2 14.9 %collective-permute-start.5 = (bf16[144,512]{1,0:T(8,128)(2,1)S(1)}, bf16[144,512]{1,0:T(8,128)(2,1)S(1)}, u32[]{:S(2)}, u32[]{:S(2)}) collective-permute-start(bf16[144,512]{1,0:T(8,128)(2,1)S(1)} %get-tuple-element.87), channel_id=1, source_target_pairs={{0,2},{2,0},{4,6},{6,4},{8,10},{10,8},{12,14},{14,12},{1,3},{3,1},... | collective-permute-start | bytes 442376 | tf_op jit(solution)/shard_map/ppermute | solution.py:438
  12.1 13.0 %collective-permute-start.6 = (bf16[144,512]{1,0:T(8,128)(2,1)S(1)}, bf16[144,512]{1,0:T(8,128)(2,1)S(1)}, u32[]{:S(2)}, u32[]{:S(2)}) collective-permute-start(bf16[144,512]{1,0:T(8,128)(2,1)S(1)} %get-tuple-element.88), channel_id=1, source_target_pairs={{0,4},{2,6},{4,0},{6,2},{8,12},{10,14},{12,8},{14,10},{1,5},{3,7},... | collective-permute-start | bytes 442376 | tf_op jit(solution)/shard_map/ppermute | solution.py:438
  13.7 11.4 %collective-permute-start.7 = (bf16[144,512]{1,0:T(8,128)(2,1)S(1)}, bf16[144,512]{1,0:T(8,128)(2,1)S(1)}, u32[]{:S(2)}, u32[]{:S(2)}) collective-permute-start(bf16[144,512]{1,0:T(8,128)(2,1)S(1)} %get-tuple-element.89), channel_id=1, source_target_pairs={{0,6},{2,4},{4,2},{6,0},{8,14},{10,12},{12,10},{14,8},{1,7},{3,5},... | collective-permute-start | bytes 442376 | tf_op jit(solution)/shard_map/ppermute | solution.py:438
  17.0 10.9 %collective-permute-start.3 = (bf16[144,512]{1,0:T(8,128)(2,1)S(1)}, bf16[144,512]{1,0:T(8,128)(2,1)S(1)}, u32[]{:S(2)}, u32[]{:S(2)}) collective-permute-start(bf16[144,512]{1,0:T(8,128)(2,1)S(1)} %get-tuple-element.59), channel_id=1, source_target_pairs={{0,12},{2,14},{4,8},{6,10},{1,13},{3,15},{5,9},{7,11},{16,28},{18,... | collective-permute-start | bytes 442376 | tf_op jit(solution)/shard_map/ppermute | solution.py:442
  26.1 7.4 %collective-permute-start.8 = (bf16[144,512]{1,0:T(8,128)(2,1)S(1)}, bf16[144,512]{1,0:T(8,128)(2,1)S(1)}, u32[]{:S(2)}, u32[]{:S(2)}) collective-permute-start(bf16[144,512]{1,0:T(8,128)(2,1)S(1)} %get-tuple-element.90), channel_id=1, source_target_pairs={{0,12},{2,14},{4,8},{6,10},{1,13},{3,15},{5,9},{7,11},{16,28},{18,... | collective-permute-start | bytes 442376 | tf_op jit(solution)/shard_map/ppermute | solution.py:442
  28.8 8.2 %collective-permute-start.4 = (bf16[136,512]{1,0:T(8,128)(2,1)S(1)}, bf16[136,512]{1,0:T(8,128)(2,1)S(1)}, u32[]{:S(2)}, u32[]{:S(2)}) collective-permute-start(bf16[136,512]{1,0:T(8,128)(2,1)S(1)} %get-tuple-element.61), channel_id=1, source_target_pairs={{0,2},{2,0},{4,6},{6,4},{8,10},{10,8},{12,14},{14,12},{1,3},{3,1},... | collective-permute-start | bytes 417800 | tf_op jit(solution)/shard_map/ppermute | solution.py:438
  32.0 8.0 %collective-permute-start.12 = (bf16[136,512]{1,0:T(8,128)(2,1)S(1)}, bf16[136,512]{1,0:T(8,128)(2,1)S(1)}, u32[]{:S(2)}, u32[]{:S(2)}) collective-permute-start(bf16[136,512]{1,0:T(8,128)(2,1)S(1)} %get-tuple-element.103), channel_id=1, source_target_pairs={{0,4},{2,6},{4,0},{6,2},{8,12},{10,14},{12,8},{14,10},{1,5},{3,7},... | collective-permute-start | bytes 417800 | tf_op jit(solution)/shard_map/ppermute | solution.py:438
  32.0 8.7 %collective-permute-start.13 = (bf16[136,512]{1,0:T(8,128)(2,1)S(1)}, bf16[136,512]{1,0:T(8,128)(2,1)S(1)}, u32[]{:S(2)}, u32[]{:S(2)}) collective-permute-start(bf16[136,512]{1,0:T(8,128)(2,1)S(1)} %get-tuple-element.104), channel_id=1, source_target_pairs={{0,6},{2,4},{4,2},{6,0},{8,14},{10,12},{12,10},{14,8},{1,7},{3,5},... | collective-permute-start | bytes 417800 | tf_op jit(solution)/shard_map/ppermute | solution.py:438
  34.4 8.2 %collective-permute-start.9 = (bf16[136,512]{1,0:T(8,128)(2,1)S(1)}, bf16[136,512]{1,0:T(8,128)(2,1)S(1)}, u32[]{:S(2)}, u32[]{:S(2)}) collective-permute-start(bf16[136,512]{1,0:T(8,128)(2,1)S(1)} %get-tuple-element.93), channel_id=1, source_target_pairs={{0,2},{2,0},{4,6},{6,4},{8,10},{10,8},{12,14},{14,12},{1,3},{3,1},... | collective-permute-start | bytes 417800 | tf_op jit(solution)/shard_map/ppermute | solution.py:438
  36.4 6.2 %collective-permute-start.10 = (bf16[136,512]{1,0:T(8,128)(2,1)S(1)}, bf16[136,512]{1,0:T(8,128)(2,1)S(1)}, u32[]{:S(2)}, u32[]{:S(2)}) collective-permute-start(bf16[136,512]{1,0:T(8,128)(2,1)S(1)} %get-tuple-element.94), channel_id=1, source_target_pairs={{0,4},{2,6},{4,0},{6,2},{8,12},{10,14},{12,8},{14,10},{1,5},{3,7},... | collective-permute-start | bytes 417800 | tf_op jit(solution)/shard_map/ppermute | solution.py:438
  37.0 6.6 %collective-permute-start.11 = (bf16[136,512]{1,0:T(8,128)(2,1)S(1)}, bf16[136,512]{1,0:T(8,128)(2,1)S(1)}, u32[]{:S(2)}, u32[]{:S(2)}) collective-permute-start(bf16[136,512]{1,0:T(8,128)(2,1)S(1)} %get-tuple-element.95), channel_id=1, source_target_pairs={{0,6},{2,4},{4,2},{6,0},{8,14},{10,12},{12,10},{14,8},{1,7},{3,5},... | collective-permute-start | bytes 417800 | tf_op jit(solution)/shard_map/ppermute | solution.py:438

commit v9 on v7

--- a/solution.py
+++ b/solution.py
@@ -99,7 +99,7 @@
 
 
 def next_matrix(start, ends, taps):
-    shape = (TILE, BLOCK)
+    shape = (2 * TILE, BLOCK)
     row = lax.broadcasted_iota(jnp.int32, shape, 0)
     col = lax.broadcasted_iota(jnp.int32, shape, 1)
     same = seg_of(start + BLOCK + row, ends) == seg_of(start + col, ends)
@@ -118,7 +118,7 @@
     base = (taps - 1) * BLOCK
     for k in range(taps - 1):
         total = total + moved[k * BLOCK : (k + 1) * BLOCK] * half[k : k + 1]
-        after = after + moved[base + k * TILE : base + (k + 1) * TILE] * half[k : k + 1]
+        after = after + moved[base + 2 * k * TILE : base + (2 * k + 1) * TILE] * half[k : k + 1]
     return total, after
 
 
@@ -153,7 +153,7 @@
         spread = mm(factor[...], onehot2)
         held[0:STATE, here] = mm(bmat_t, (xc.astype(F32) * spread).astype(BF16)).astype(BF16)
         row = lax.broadcasted_iota(jnp.int32, (TILE, step), 0)
-        passed = mm(carry[...], onehot2[0 : 2 * heads])
+        passed = mm(carry[...], onehot2[0 : 2 * heads])[0:TILE]
         high = passed.astype(BF16).astype(F32)
         upper = jnp.where(row < 2 + taps - 1, pltpu.roll(total[0:TILE], 2, 0), pltpu.roll(after, 1 + taps, 0))
         upper = jnp.where(row == 0, high, jnp.where(row == 1, passed - high, upper))
@@ -202,7 +202,7 @@
     factors[:, 2 * heads : 4 * heads] = pair_of(grown)
     live[...] = jnp.where(seg_row == before, 1.0, 0.0)
     passed = jnp.where(seg_last == before, jnp.exp(last), 0.0)
-    carry[...] = pair_of(jnp.broadcast_to(passed, (TILE, heads)))
+    carry[...] = pair_of(jnp.broadcast_to(passed, (2 * TILE, heads)))
     for copy in copies[4:9]:
         copy.wait()
     value = raw[...].astype(F32)
@@ -436,7 +436,7 @@
         return [values[0], swapped[1], swapped[2], swapped[3]]
 
     def ahead(value):
-        return lax.ppermute(value, "seq", [(i, (i + QUAD) % peers ^ 2) for i in range(peers)])
+        return lax.ppermute(value, "seq", [(i, i + QUAD ^ 2) for i in range(peers - QUAD)])
 
     first_args = [
         lengths, x_in, bc_in, conv_x_weight, bx, dt_raw.T, dt_bias.reshape(1, heads), decay.reshape(1, heads),
@@ -451,12 +451,12 @@
         [
             ((rows, chan), BF16),
             ((rows, 2 * bcw), BF16),
-            (((taps - 1) * (BLOCK + TILE), BLOCK), BF16),
+            (((taps - 1) * (BLOCK + 2 * TILE), BLOCK), BF16),
             ((BLOCK, BLOCK), F32),
             ((BLOCK, BLOCK), F32),
             ((rows, 4 * heads), BF16),
             ((rows, 2 * heads), BF16),
-            ((TILE, 2 * heads), BF16),
+            ((2 * TILE, 2 * heads), BF16),
             ((taps, chan), BF16),
             ((1, chan), F32),
             ((taps, 2, bcw), BF16),

time: 46.5 us -> 46.3 us (level)
  transfers between devices with their start and end apart: 14 -> 14, of which waited for: 5 -> 4; matrix products, arithmetic and copies ran while one was open for 0% -> 0% of each run, Pallas kernels for 24% -> 25%
where the time goes in v9:
time: 46.3 us; the launch traced here: 46 us
  starting transfers between devices  23.4 us (51%)
  Pallas kernels  16.9 us (37%)
  waiting for transfers between devices  5.44 us (12%)
    pallas_call x10, Pallas kernels, call(): pl.pallas_call(kernel, in_specs=[SMEM] * len(scalars) + more.pop('specs',...  16.9 us
    ppermute x12, starting transfers between devices, swap(): swapped = {k: lax.ppermute(values[k], 'seq', routes[k]) for k in (3, 1, 2)}  15.5 us
    ppermute x2, starting transfers between devices, ahead(): lax.ppermute(value, 'seq', [(i, i + QUAD ^ 2) for i in range(peers - QUAD)])  7.93 us
    ppermute x12, waiting for transfers between devices, swap(): swapped = {k: lax.ppermute(values[k], 'seq', routes[k]) for k in (3, 1, 2)}  5.44 us
  transfers between devices with their start and end apart: 14, of which 4 were waited for; matrix products, arithmetic and copies ran while one was open for 0% of the time, Pallas kernels for 25%

profile of v9, /device:TPU:0, one launch (start us, length us, event | category | flops | bytes accessed | tf_op | source)
XLA Modules:
  0.0 46.0 jit_solution(8463548948973036060)
XLA Ops:
  0.0 0.1 pad_add_fusion.info
  0.1 3.6 %shard_map.127 = (bf16[128,4096]{1,0:T(8,128)(2,1)S(1)}, bf16[128,512]{1,0:T(8,128)(2,1)S(1)}, bf16[432,128]{1,0:T(8,128)(2,1)S(1)}, f32[128,128]{1,0:T(8,128)S(...) custom-call(s32[3]{0:T(128)S(1)} %pad_add_fusion.info, ...), custom_call_target="tpu_custom_call" | custom-call | flops 600000000 | bytes 4194304 | tf_op jit(solution)/shard_map/pallas_call | solution.py:387
  3.7 3.0 %collective-permute-start = (bf16[144,512]{1,0:T(8,128)(2,1)S(1)}, bf16[144,512]{1,0:T(8,128)(2,1)S(1)}, u32[]{:S(2)}, u32[]{:S(2)}) collective-permute-start(bf16[144,512]{1,0:T(8,128)(2,1)S(1)} %get-tuple-element.56), channel_id=1, source_target_pairs={{0,2},{2,0},{4,6},{6,4},{8,10},{10,8},{12,14},{14,12},{1,3},{3,1},... | collective-permute-start | bytes 442376 | tf_op jit(solution)/shard_map/ppermute | solution.py:435
  6.7 1.6 %collective-permute-start.1 = (bf16[144,512]{1,0:T(8,128)(2,1)S(1)}, bf16[144,512]{1,0:T(8,128)(2,1)S(1)}, u32[]{:S(2)}, u32[]{:S(2)}) collective-permute-start(bf16[144,512]{1,0:T(8,128)(2,1)S(1)} %get-tuple-element.57), channel_id=1, source_target_pairs={{0,4},{2,6},{4,0},{6,2},{8,12},{10,14},{12,8},{14,10},{1,5},{3,7},... | collective-permute-start | bytes 442376 | tf_op jit(solution)/shard_map/ppermute | solution.py:435
  8.3 0.0 collective-permute-start.2
  8.3 1.9 %shard_map.130 = (bf16[128,2048]{1,0:T(8,128)(2,1)S(1)}, bf16[144,512]{1,0:T(8,128)(2,1)S(1)}, bf16[144,512]{1,0:T(8,128)(2,1)S(1)}, bf16[144,512]{1,0:T(8,128)(2,1)S(1)}, bf16[144,512]{1,0:T(8,128)(2,1)S(1)}) custom-call(s32[3]{0:T(128)S(1)} %pad_add_fusion.info, bf16[128,4096]{1,0:T(8,128)(2,1)S(1)} %get-tuple-element.62.x, ...), custom_call_target="tpu_custom_call" | custom-call | flops 300000000 | bytes 4194304 | tf_op jit(solution)/shard_map/pallas_call | solution.py:387
  10.3 2.0 %collective-permute-start.5 = (bf16[144,512]{1,0:T(8,128)(2,1)S(1)}, bf16[144,512]{1,0:T(8,128)(2,1)S(1)}, u32[]{:S(2)}, u32[]{:S(2)}) collective-permute-start(bf16[144,512]{1,0:T(8,128)(2,1)S(1)} %get-tuple-element.87), channel_id=1, source_target_pairs={{0,2},{2,0},{4,6},{6,4},{8,10},{10,8},{12,14},{14,12},{1,3},{3,1},... | collective-permute-start | bytes 442376 | tf_op jit(solution)/shard_map/ppermute | solution.py:435
  12.2 1.6 %collective-permute-start.6 = (bf16[144,512]{1,0:T(8,128)(2,1)S(1)}, bf16[144,512]{1,0:T(8,128)(2,1)S(1)}, u32[]{:S(2)}, u32[]{:S(2)}) collective-permute-start(bf16[144,512]{1,0:T(8,128)(2,1)S(1)} %get-tuple-element.88), channel_id=1, source_target_pairs={{0,4},{2,6},{4,0},{6,2},{8,12},{10,14},{12,8},{14,10},{1,5},{3,7},... | collective-permute-start | bytes 442376 | tf_op jit(solution)/shard_map/ppermute | solution.py:435
  13.8 0.0 collective-permute-done.refs_1_.m1
  13.8 0.0 collective-permute-start.7
  13.8 0.0 collective-permute-done.1.refs_2_.m2
  13.8 2.2 %collective-permute-done.2.refs_3_.m3 = bf16[144,512]{1,0:T(8,128)(2,1)S(1)} collective-permute-done((bf16[144,512]{1,0:T(8,128)(2,1)S(1)}, bf16[144,512]{1,0:T(8,128)(2,1)S(1)}, u32[]{:S(2)}, u32[]{:S(2)}) %collective-permute-start.2) | collective-permute-done | bytes 147488 | tf_op jit(solution)/shard_map/ppermute | solution.py:435
  16.1 0.9 %shard_map.128 = (bf16[144,512]{1,0:T(8,128)(2,1)S(1)}, bf16[3,144,512]{2,1,0:T(8,128)(2,1)S(1)}) custom-call(s32[3]{0:T(128)S(1)} %pad_add_fusion.info, bf16[144,512]{1,0:T(8,128)(2,1)S(1)} %get-tuple-element.55.refs_0_.m0, bf16[144,512]{1,0:T(8,128)(2,1)S(1)} %collective-permute-done.refs_1_.m1, bf16[144,512]{1,0:T(8,128)(2,1)S(1)} %collective-permute-done.1.refs_2_.m2, ...), custom_call_target="tpu_custom_call" | custom-call | flops 1000000 | bytes 4194304 | tf_op jit(solution)/shard_map/pallas_call | solution.py:387
  17.0 6.1 %collective-permute-start.3 = (bf16[144,512]{1,0:T(8,128)(2,1)S(1)}, bf16[144,512]{1,0:T(8,128)(2,1)S(1)}, u32[]{:S(2)}, u32[]{:S(2)}) collective-permute-start(bf16[144,512]{1,0:T(8,128)(2,1)S(1)} %get-tuple-element.59), channel_id=1, source_target_pairs={{0,12},{2,14},{4,8},{6,10},{1,13},{3,15},{5,9},{7,11},{16,28},{18,... | collective-permute-start | bytes 442376 | tf_op jit(solution)/shard_map/ppermute | solution.py:439
  23.1 2.0 %shard_map.132 = (f32[128,2048]{1,0:T(8,128)S(1)}, f32[128,2048]{1,0:T(8,128)S(1)}, bf16[128,128]{1,0:T(8,128)(2,1)S(1)}, f32[8,2048]{1,0:T(8,128)S(1)}, f32[8,2048]{1,0:T(8,128)S(1)}) custom-call(bf16[128,2048]{1,0:T(8,128)(2,1)S(1)} %get-tuple-element.84.xc_in, bf16[128,4096]{1,0:T(8,128)(2,1)} %z_in.3, bf16[128,512]{1,0:T(8,128)(2,1)S(1)} %get-tuple-element.63.bc, ...), custom_call_target="tpu_custom_call" | custom-call | flops 300000000 | bytes 4194304 | tf_op jit(solution)/shard_map/pallas_call | solution.py:387
  25.1 0.0 collective-permute-done.5.refs_1_.m1
  25.1 0.0 collective-permute-done.6.refs_2_.m2
  25.1 0.0 collective-permute-done.7.refs_3_.m3
  25.2 0.9 %shard_map.133 = (bf16[144,512]{1,0:T(8,128)(2,1)S(1)}, bf16[3,144,512]{2,1,0:T(8,128)(2,1)S(1)}) custom-call(s32[3]{0:T(128)S(1)} %pad_add_fusion.info, bf16[144,512]{1,0:T(8,128)(2,1)S(1)} %get-tuple-element.86.refs_0_.m0, bf16[144,512]{1,0:T(8,128)(2,1)S(1)} %collective-permute-done.5.refs_1_.m1, bf16[144,512]{1,0:T(8,128)(2,1)S(1)} %collective-permute-done.6.refs_2_.m2, ...), custom_call_target="tpu_custom_call" | custom-call | flops 1000000 | bytes 4194304 | tf_op jit(solution)/shard_map/pallas_call | solution.py:387
  26.1 1.8 %collective-permute-start.8 = (bf16[144,512]{1,0:T(8,128)(2,1)S(1)}, bf16[144,512]{1,0:T(8,128)(2,1)S(1)}, u32[]{:S(2)}, u32[]{:S(2)}) collective-permute-start(bf16[144,512]{1,0:T(8,128)(2,1)S(1)} %get-tuple-element.90), channel_id=1, source_target_pairs={{0,12},{2,14},{4,8},{6,10},{1,13},{3,15},{5,9},{7,11},{16,28},{18,... | collective-permute-start | bytes 442376 | tf_op jit(solution)/shard_map/ppermute | solution.py:439
  27.9 0.0 collective-permute-done.3.start
  28.0 0.8 %shard_map.129 = (bf16[144,512]{1,0:T(8,128)(2,1)S(1)}, bf16[144,512]{1,0:T(8,128)(2,1)S(1)}, bf16[144,512]{1,0:T(8,128)(2,1)S(1)}, bf16[144,512]{1,0:T(8,128)(2,1)S(1)}) custom-call(s32[3]{0:T(128)S(1)} %pad_add_fusion.info, bf16[144,512]{1,0:T(8,128)(2,1)S(1)} %collective-permute-done.3.start, bf16[3,144,512]{2,1,0:T(8,128)(2,1)S(1)} %get-tuple-element.60.fixed, ...), custom_call_target="tpu_custom_call" | custom-call | flops 1000000 | bytes 4194304 | tf_op jit(solution)/shard_map/pallas_call | solution.py:387
  28.8 3.2 %collective-permute-start.4 = (bf16[144,512]{1,0:T(8,128)(2,1)S(1)}, bf16[144,512]{1,0:T(8,128)(2,1)S(1)}, u32[]{:S(2)}, u32[]{:S(2)}) collective-permute-start(bf16[144,512]{1,0:T(8,128)(2,1)S(1)} %get-tuple-element.61), channel_id=1, source_target_pairs={{0,2},{2,0},{4,6},{6,4},{8,10},{10,8},{12,14},{14,12},{1,3},{3,1},... | collective-permute-start | bytes 442376 | tf_op jit(solution)/shard_map/ppermute | solution.py:435
  32.0 0.0 collective-permute-start.12
  32.0 1.5 %collective-permute-start.13 = (bf16[144,512]{1,0:T(8,128)(2,1)S(1)}, bf16[144,512]{1,0:T(8,128)(2,1)S(1)}, u32[]{:S(2)}, u32[]{:S(2)}) collective-permute-start(bf16[144,512]{1,0:T(8,128)(2,1)S(1)} %get-tuple-element.104), channel_id=1, source_target_pairs={{0,6},{2,4},{4,2},{6,0},{8,14},{10,12},{12,10},{14,8},{1,7},{3,5},... | collective-permute-start | bytes 442376 | tf_op jit(solution)/shard_map/ppermute | solution.py:435
  33.5 0.0 collective-permute-done.8.start
  33.5 0.8 %shard_map.134 = (bf16[144,512]{1,0:T(8,128)(2,1)S(1)}, bf16[144,512]{1,0:T(8,128)(2,1)S(1)}, bf16[144,512]{1,0:T(8,128)(2,1)S(1)}, bf16[144,512]{1,0:T(8,128)(2,1)S(1)}) custom-call(s32[3]{0:T(128)S(1)} %pad_add_fusion.info, bf16[144,512]{1,0:T(8,128)(2,1)S(1)} %collective-permute-done.8.start, bf16[3,144,512]{2,1,0:T(8,128)(2,1)S(1)} %get-tuple-element.91.fixed, ...), custom_call_target="tpu_custom_call" | custom-call | flops 1000000 | bytes 4194304 | tf_op jit(solution)/shard_map/pallas_call | solution.py:387
  34.4 2.0 %collective-permute-start.9 = (bf16[144,512]{1,0:T(8,128)(2,1)S(1)}, bf16[144,512]{1,0:T(8,128)(2,1)S(1)}, u32[]{:S(2)}, u32[]{:S(2)}) collective-permute-start(bf16[144,512]{1,0:T(8,128)(2,1)S(1)} %get-tuple-element.93), channel_id=1, source_target_pairs={{0,2},{2,0},{4,6},{6,4},{8,10},{10,8},{12,14},{14,12},{1,3},{3,1},... | collective-permute-start | bytes 442376 | tf_op jit(solution)/shard_map/ppermute | solution.py:435
  36.4 0.0 collective-permute-start.10
  36.4 0.9 %collective-permute-done.4.rest_1_ = bf16[144,512]{1,0:T(8,128)(2,1)S(1)} collective-permute-done((bf16[144,512]{1,0:T(8,128)(2,1)S(1)}, bf16[144,512]{1,0:T(8,128)(2,1)S(1)}, u32[]{:S(2)}, u32[]{:S(2)}) %collective-permute-start.4) | collective-permute-done | bytes 147488 | tf_op jit(solution)/shard_map/ppermute | solution.py:435
  37.3 0.6 %collective-permute-start.11 = (bf16[144,512]{1,0:T(8,128)(2,1)S(1)}, bf16[144,512]{1,0:T(8,128)(2,1)S(1)}, u32[]{:S(2)}, u32[]{:S(2)}) collective-permute-start(bf16[144,512]{1,0:T(8,128)(2,1)S(1)} %get-tuple-element.95), channel_id=1, source_target_pairs={{0,6},{2,4},{4,2},{6,0},{8,14},{10,12},{12,10},{14,8},{1,7},{3,5},... | collective-permute-start | bytes 442376 | tf_op jit(solution)/shard_map/ppermute | solution.py:435
  37.9 2.0 %shard_map.131 = (f32[128,2048]{1,0:T(8,128)S(1)}, f32[128,2048]{1,0:T(8,128)S(1)}, bf16[128,128]{1,0:T(8,128)(2,1)S(1)}, f32[8,2048]{1,0:T(8,128)S(1)}, f32[8,2048]{1,0:T(8,128)S(1)}) custom-call(bf16[128,2048]{1,0:T(8,128)(2,1)S(1)} %get-tuple-element.71.xc_in, bf16[128,4096]{1,0:T(8,128)(2,1)} %z_in.3, bf16[128,512]{1,0:T(8,128)(2,1)S(1)} %get-tuple-element.63.bc, ...), custom_call_target="tpu_custom_call" | custom-call | flops 300000000 | bytes 4194304 | tf_op jit(solution)/shard_map/pallas_call | solution.py:387
  39.9 0.0 collective-permute-done.12.rest_2_
  39.9 1.1 %collective-permute-done.13.rest_3_ = bf16[144,512]{1,0:T(8,128)(2,1)S(1)} collective-permute-done((bf16[144,512]{1,0:T(8,128)(2,1)S(1)}, bf16[144,512]{1,0:T(8,128)(2,1)S(1)}, u32[]{:S(2)}, u32[]{:S(2)}) %collective-permute-start.13) | collective-permute-done | bytes 147488 | tf_op jit(solution)/shard_map/ppermute | solution.py:435
  41.0 1.9 %shard_map.135.rest_4_ = bf16[128,4096]{1,0:T(8,128)(2,1)} custom-call(s32[3]{0:T(128)S(1)} %pad_add_fusion.info, f32[128,2048]{1,0:T(8,128)S(1)} %get-tuple-element.96.near, f32[128,2048]{1,0:T(8,128)S(1)} %get-tuple-element.97.gain, bf16[128,128]{1,0:T(8,128)(2,1)S(1)} %get-tuple-element.98.cmat, f32[8,2048]{1,0:T(8,128)S(1)} %get-tuple-element.99.rate_top, ...), custom_call_target="tpu_custom_call" | custom-call | flops 100000000 | bytes 4194304 | tf_op jit(solution)/shard_map/pallas_call | solution.py:387
  42.9 0.0 collective-permute-done.9.rest_1_
  42.9 0.0 collective-permute-done.10.rest_2_
  43.0 1.2 %collective-permute-done.11.rest_3_ = bf16[144,512]{1,0:T(8,128)(2,1)S(1)} collective-permute-done((bf16[144,512]{1,0:T(8,128)(2,1)S(1)}, bf16[144,512]{1,0:T(8,128)(2,1)S(1)}, u32[]{:S(2)}, u32[]{:S(2)}) %collective-permute-start.11) | collective-permute-done | bytes 147488 | tf_op jit(solution)/shard_map/ppermute | solution.py:435
  44.1 1.9 %shard_map.136 = bf16[128,4096]{1,0:T(8,128)(2,1)} custom-call(s32[3]{0:T(128)S(1)} %pad_add_fusion.info, f32[128,2048]{1,0:T(8,128)S(1)} %get-tuple-element.76.near, f32[128,2048]{1,0:T(8,128)S(1)} %get-tuple-element.77.gain, bf16[128,128]{1,0:T(8,128)(2,1)S(1)} %get-tuple-element.78.cmat, ...), custom_call_target="tpu_custom_call", output_to_operand_aliasing={{}: (13, {})} | custom-call | flops 100000000 | bytes 4194304 | tf_op jit(solution)/shard_map/pallas_call | solution.py:387
Async XLA Ops:
  3.7 10.1 %collective-permute-start = (bf16[144,512]{1,0:T(8,128)(2,1)S(1)}, bf16[144,512]{1,0:T(8,128)(2,1)S(1)}, u32[]{:S(2)}, u32[]{:S(2)}) collective-permute-start(bf16[144,512]{1,0:T(8,128)(2,1)S(1)} %get-tuple-element.56), channel_id=1, source_target_pairs={{0,2},{2,0},{4,6},{6,4},{8,10},{10,8},{12,14},{14,12},{1,3},{3,1},... | collective-permute-start | bytes 442376 | tf_op jit(solution)/shard_map/ppermute | solution.py:435
  6.7 7.1 %collective-permute-start.1 = (bf16[144,512]{1,0:T(8,128)(2,1)S(1)}, bf16[144,512]{1,0:T(8,128)(2,1)S(1)}, u32[]{:S(2)}, u32[]{:S(2)}) collective-permute-start(bf16[144,512]{1,0:T(8,128)(2,1)S(1)} %get-tuple-element.57), channel_id=1, source_target_pairs={{0,4},{2,6},{4,0},{6,2},{8,12},{10,14},{12,8},{14,10},{1,5},{3,7},... | collective-permute-start | bytes 442376 | tf_op jit(solution)/shard_map/ppermute | solution.py:435
  8.3 7.7 %collective-permute-start.2 = (bf16[144,512]{1,0:T(8,128)(2,1)S(1)}, bf16[144,512]{1,0:T(8,128)(2,1)S(1)}, u32[]{:S(2)}, u32[]{:S(2)}) collective-permute-start(bf16[144,512]{1,0:T(8,128)(2,1)S(1)} %get-tuple-element.58), channel_id=1, source_target_pairs={{0,6},{2,4},{4,2},{6,0},{8,14},{10,12},{12,10},{14,8},{1,7},{3,5},... | collective-permute-start | bytes 442376 | tf_op jit(solution)/shard_map/ppermute | solution.py:435
  10.3 14.9 %collective-permute-start.5 = (bf16[144,512]{1,0:T(8,128)(2,1)S(1)}, bf16[144,512]{1,0:T(8,128)(2,1)S(1)}, u32[]{:S(2)}, u32[]{:S(2)}) collective-permute-start(bf16[144,512]{1,0:T(8,128)(2,1)S(1)} %get-tuple-element.87), channel_id=1, source_target_pairs={{0,2},{2,0},{4,6},{6,4},{8,10},{10,8},{12,14},{14,12},{1,3},{3,1},... | collective-permute-start | bytes 442376 | tf_op jit(solution)/shard_map/ppermute | solution.py:435
  12.2 12.9 %collective-permute-start.6 = (bf16[144,512]{1,0:T(8,128)(2,1)S(1)}, bf16[144,512]{1,0:T(8,128)(2,1)S(1)}, u32[]{:S(2)}, u32[]{:S(2)}) collective-permute-start(bf16[144,512]{1,0:T(8,128)(2,1)S(1)} %get-tuple-element.88), channel_id=1, source_target_pairs={{0,4},{2,6},{4,0},{6,2},{8,12},{10,14},{12,8},{14,10},{1,5},{3,7},... | collective-permute-start | bytes 442376 | tf_op jit(solution)/shard_map/ppermute | solution.py:435
  13.8 11.3 %collective-permute-start.7 = (bf16[144,512]{1,0:T(8,128)(2,1)S(1)}, bf16[144,512]{1,0:T(8,128)(2,1)S(1)}, u32[]{:S(2)}, u32[]{:S(2)}) collective-permute-start(bf16[144,512]{1,0:T(8,128)(2,1)S(1)} %get-tuple-element.89), channel_id=1, source_target_pairs={{0,6},{2,4},{4,2},{6,0},{8,14},{10,12},{12,10},{14,8},{1,7},{3,5},... | collective-permute-start | bytes 442376 | tf_op jit(solution)/shard_map/ppermute | solution.py:435
  17.0 11.0 %collective-permute-start.3 = (bf16[144,512]{1,0:T(8,128)(2,1)S(1)}, bf16[144,512]{1,0:T(8,128)(2,1)S(1)}, u32[]{:S(2)}, u32[]{:S(2)}) collective-permute-start(bf16[144,512]{1,0:T(8,128)(2,1)S(1)} %get-tuple-element.59), channel_id=1, source_target_pairs={{0,12},{2,14},{4,8},{6,10},{1,13},{3,15},{5,9},{7,11},{16,28},{18,... | collective-permute-start | bytes 442376 | tf_op jit(solution)/shard_map/ppermute | solution.py:439
  26.1 7.4 %collective-permute-start.8 = (bf16[144,512]{1,0:T(8,128)(2,1)S(1)}, bf16[144,512]{1,0:T(8,128)(2,1)S(1)}, u32[]{:S(2)}, u32[]{:S(2)}) collective-permute-start(bf16[144,512]{1,0:T(8,128)(2,1)S(1)} %get-tuple-element.90), channel_id=1, source_target_pairs={{0,12},{2,14},{4,8},{6,10},{1,13},{3,15},{5,9},{7,11},{16,28},{18,... | collective-permute-start | bytes 442376 | tf_op jit(solution)/shard_map/ppermute | solution.py:439
  28.8 8.5 %collective-permute-start.4 = (bf16[144,512]{1,0:T(8,128)(2,1)S(1)}, bf16[144,512]{1,0:T(8,128)(2,1)S(1)}, u32[]{:S(2)}, u32[]{:S(2)}) collective-permute-start(bf16[144,512]{1,0:T(8,128)(2,1)S(1)} %get-tuple-element.61), channel_id=1, source_target_pairs={{0,2},{2,0},{4,6},{6,4},{8,10},{10,8},{12,14},{14,12},{1,3},{3,1},... | collective-permute-start | bytes 442376 | tf_op jit(solution)/shard_map/ppermute | solution.py:435
  32.0 8.0 %collective-permute-start.12 = (bf16[144,512]{1,0:T(8,128)(2,1)S(1)}, bf16[144,512]{1,0:T(8,128)(2,1)S(1)}, u32[]{:S(2)}, u32[]{:S(2)}) collective-permute-start(bf16[144,512]{1,0:T(8,128)(2,1)S(1)} %get-tuple-element.103), channel_id=1, source_target_pairs={{0,4},{2,6},{4,0},{6,2},{8,12},{10,14},{12,8},{14,10},{1,5},{3,7},... | collective-permute-start | bytes 442376 | tf_op jit(solution)/shard_map/ppermute | solution.py:435
  32.0 9.0 %collective-permute-start.13 = (bf16[144,512]{1,0:T(8,128)(2,1)S(1)}, bf16[144,512]{1,0:T(8,128)(2,1)S(1)}, u32[]{:S(2)}, u32[]{:S(2)}) collective-permute-start(bf16[144,512]{1,0:T(8,128)(2,1)S(1)} %get-tuple-element.104), channel_id=1, source_target_pairs={{0,6},{2,4},{4,2},{6,0},{8,14},{10,12},{12,10},{14,8},{1,7},{3,5},... | collective-permute-start | bytes 442376 | tf_op jit(solution)/shard_map/ppermute | solution.py:435
  34.4 8.6 %collective-permute-start.9 = (bf16[144,512]{1,0:T(8,128)(2,1)S(1)}, bf16[144,512]{1,0:T(8,128)(2,1)S(1)}, u32[]{:S(2)}, u32[]{:S(2)}) collective-permute-start(bf16[144,512]{1,0:T(8,128)(2,1)S(1)} %get-tuple-element.93), channel_id=1, source_target_pairs={{0,2},{2,0},{4,6},{6,4},{8,10},{10,8},{12,14},{14,12},{1,3},{3,1},... | collective-permute-start | bytes 442376 | tf_op jit(solution)/shard_map/ppermute | solution.py:435
  36.4 6.6 %collective-permute-start.10 = (bf16[144,512]{1,0:T(8,128)(2,1)S(1)}, bf16[144,512]{1,0:T(8,128)(2,1)S(1)}, u32[]{:S(2)}, u32[]{:S(2)}) collective-permute-start(bf16[144,512]{1,0:T(8,128)(2,1)S(1)} %get-tuple-element.94), channel_id=1, source_target_pairs={{0,4},{2,6},{4,0},{6,2},{8,12},{10,14},{12,8},{14,10},{1,5},{3,7},... | collective-permute-start | bytes 442376 | tf_op jit(solution)/shard_map/ppermute | solution.py:435
  37.3 6.8 %collective-permute-start.11 = (bf16[144,512]{1,0:T(8,128)(2,1)S(1)}, bf16[144,512]{1,0:T(8,128)(2,1)S(1)}, u32[]{:S(2)}, u32[]{:S(2)}) collective-permute-start(bf16[144,512]{1,0:T(8,128)(2,1)S(1)} %get-tuple-element.95), channel_id=1, source_target_pairs={{0,6},{2,4},{4,2},{6,0},{8,14},{10,12},{12,10},{14,8},{1,7},{3,5},... | collective-permute-start | bytes 442376 | tf_op jit(solution)/shard_map/ppermute | solution.py:435
